TPU v7x, 256 devices: a whole 4x4x8 slice. The times are simulated.
256 devices in a mesh: blk: 16 (over x_lo, y, core), rows: 16 (over x_hi, z).
Axes of the slice: x: 4 (x_hi: 2, x_lo: 2; x = x_hi * 2 + x_lo), y: 4, z: 8, core: 2. Of those that a mesh axis runs over, the one named last changes fastest.
Arguments:
- excitations: float32 [64, 131072], P(None, ('blk', 'rows')), may hold values from -6 to 6
- adjoint_loads: float32 [64, 131072], P(None, ('blk', 'rows')), may hold values from -6 to 6
- near_tiles: bfloat16 [8192, 256, 256], P(('blk', 'rows')), may hold values from -0.125 to 0.125
- tile_rows: int32 [8192], P(('blk', 'rows')), may hold values from 0 to 1
- tile_cols: int32 [8192], P(('blk', 'rows')), may hold values from 0 to 31
- tile_count: int32 [256], P(('blk', 'rows')), may hold values from 4 to 32, as said below
- skeleton_in: bfloat16 [1024, 131072], P(None, ('blk', 'rows')), may hold values from -0.0625 to 0.0625
- skeleton_out: bfloat16 [1024, 131072], P(None, ('blk', 'rows')), may hold values from -0.1875 to 0.1875
- translation: float32 [16, 15, 1024, 1024], P('blk', None, 'rows'), may hold values from -0.046875 to 0.046875
Outputs:
- response: float32 [64, 131072], P(None, ('blk', 'rows'))
- sensitivity: float32 [64, 131072], P(None, ('blk', 'rows'))
Inputs may be any that keep to these rules, and one draw needn't show every extreme that they name: `tile_count`: slots of a device are used from slot 0 on; later slots are no part of the operator.
All inputs are finite; a program needn't handle non-finite values.
Results may differ from a plain program's by a relative error of at most 0.0036.
Values may be sent and summed in bfloat16 or wider, within the bound.
No kernel may reach another device: no remote copies, remote signals or barrier semaphores. Data moves between devices by JAX's collectives and lax.ppermute only.
A program may use at most 128 MiB of HBM per device.

v0:
```python
import jax
import jax.numpy as jnp
from jax import lax
from jax.sharding import PartitionSpec as P

highest = lax.Precision.HIGHEST


def on_device(
    excitations,
    adjoint_loads,
    near_tiles,
    tile_rows,
    tile_cols,
    tile_count,
    skeleton_in,
    skeleton_out,
    translation,
):
    drive_low = excitations.astype(jnp.bfloat16)
    loads_low = adjoint_loads.astype(jnp.bfloat16)
    excite_count = excitations.shape[0]
    panels = excitations.shape[1]
    tile_size = near_tiles.shape[1]
    kernels = translation[0]
    share_width = kernels.shape[1]
    clusters = lax.axis_size("blk")
    cluster = lax.axis_index("blk")
    gathered = lax.all_gather(drive_low, "rows", axis=1, tiled=True)
    column_blocks = gathered.shape[1] // tile_size
    row_blocks = panels // tile_size
    drive_blocks = gathered.reshape(excite_count, column_blocks, tile_size)
    load_blocks = loads_low.reshape(excite_count, row_blocks, tile_size)
    used_slots = tile_count[0]

    def near_group(group_index, carry):
        ahead, behind = carry
        first_slot = group_index * 4
        tile_group = lax.dynamic_slice_in_dim(near_tiles, first_slot, 4, 0)
        row_ids = lax.dynamic_slice_in_dim(tile_rows, first_slot, 4, 0)
        column_ids = lax.dynamic_slice_in_dim(tile_cols, first_slot, 4, 0)
        live_mask = (first_slot + jnp.arange(4, dtype=jnp.int32) < used_slots).astype(jnp.float32)[
            None, :, None
        ]
        source = jnp.take(drive_blocks, column_ids, axis=1)
        target = jnp.take(load_blocks, row_ids, axis=1)
        forward = (
            jnp.einsum("egj,gij->egi", source, tile_group, preferred_element_type=jnp.float32)
            * live_mask
        )
        backward = (
            jnp.einsum("egi,gij->egj", target, tile_group, preferred_element_type=jnp.float32)
            * live_mask
        )
        return (ahead.at[:, row_ids].add(forward), behind.at[:, column_ids].add(backward))

    near_start = (
        jnp.zeros((excite_count, row_blocks, tile_size), jnp.float32),
        jnp.zeros((excite_count, column_blocks, tile_size), jnp.float32),
    )
    near_ahead, near_behind = lax.fori_loop(0, (used_slots + 3) // 4, near_group, near_start)
    contract_panels = (((1,), (1,)), ((), ()))
    charge_part = lax.dot_general(
        drive_low, skeleton_in, contract_panels, preferred_element_type=jnp.float32
    )
    gradient_part = lax.dot_general(
        loads_low, skeleton_out, contract_panels, preferred_element_type=jnp.float32
    )
    charges, gradient_all = lax.psum((charge_part, gradient_part), "rows")
    gradient = lax.dynamic_slice_in_dim(
        gradient_all, lax.axis_index("rows") * share_width, share_width, 1
    )

    def offsets_for(other_ids):
        offset = jnp.remainder(cluster - other_ids, clusters)
        active = (offset != 0).astype(jnp.float32)
        return (jnp.maximum(offset - 1, 0), active)

    charge_piece = lax.all_gather(charges[None], "blk", axis=0, tiled=True)
    span_count = charge_piece.shape[0]
    offset, active = offsets_for(jnp.arange(span_count, dtype=jnp.int32))
    chosen = jnp.take(kernels, offset, axis=0)
    potential = jnp.einsum(
        "cej,ckj->ek", charge_piece * active[:, None, None], chosen, precision=highest
    )
    potential_low = lax.all_gather(potential.astype(jnp.bfloat16), "rows", axis=1, tiled=True)
    far_ahead = jnp.dot(potential_low, skeleton_out, preferred_element_type=jnp.float32)
    offset, active = offsets_for(jnp.arange(lax.axis_size("blk") * 1, dtype=jnp.int32))
    chosen = jnp.take(kernels, offset, axis=0)
    summed = lax.psum_scatter(
        jnp.einsum("ek,ckj->cej", gradient, chosen, precision=highest) * active[:, None, None],
        "blk",
        scatter_dimension=0,
        tiled=True,
    )
    adjoint_low = lax.psum(summed[0], "rows").astype(jnp.bfloat16)
    far_behind = jnp.dot(adjoint_low, skeleton_in, preferred_element_type=jnp.float32)
    near_columns = lax.psum_scatter(
        near_behind.reshape(excite_count, column_blocks * tile_size),
        "rows",
        scatter_dimension=1,
        tiled=True,
    )
    response = near_ahead.reshape(excite_count, panels) + far_ahead
    sensitivity = near_columns + far_behind
    return (response, sensitivity)


def solution(mesh):
    return jax.shard_map(
        on_device,
        mesh=mesh,
        in_specs=(
            P(None, ("blk", "rows")),
            P(None, ("blk", "rows")),
            P(("blk", "rows"), None, None),
            P(("blk", "rows")),
            P(("blk", "rows")),
            P(("blk", "rows")),
            P(None, ("blk", "rows")),
            P(None, ("blk", "rows")),
            P("blk", None, "rows", None),
        ),
        out_specs=(P(None, ("blk", "rows")), P(None, ("blk", "rows"))),
        check_vma=False,
    )
```

profile of v0, /device:TPU:8, one launch (start us, length us, event | category | flops | bytes accessed | tf_op | source)
XLA Modules:
  0.0 574.7 jit_solution(14490784234258708478)
XLA Ops:
  9.2 2.4 convolution_bitcast_fusion
  13.5 159.0 %all-reduce.4.cloned.1.call-done = (f32[1,64,1024]{2,1,0:T(8,128)}, f32[64,1024]{1,0:T(8,128)}) async-done(((f32[1,64,1024]{2,1,0:T(8,128)}, f32[64,1024]{1,0:T(8,128)}), (f32[1,64,1024]{2,1,0:T(8,128)}, f32[64,1024]{1,0:T(8,128)})) %all-reduce.4.cloned.1.call-update) | async-done | bytes 524304 | tf_op jit(solution)/shard_map/psum | solution.py:69
  172.6 4.9 gather_fusion.2
  178.1 10.0 %multiply_bitcast_fusion = f32[16,64,1024]{2,1,0:T(8,128)} fusion(f32[16,64,1024]{2,1,0:T(8,128)} %gather_fusion.2, f32[16]{0:T(128)S(1)} %get-tuple-element.106, pred[16]{0:T(512)(128)(4,1)S(1)} %get-tuple-element.107, f32[64,1024]{1,0:T(8,128)} %get-tuple-element.100, s32[]{:T(128)S(6)} %select_n.53), kind=kOutput, calls=%fused_computation.30 | convolution fusion | flops 807403520 | bytes 8421460 | tf_op jit(solution)/shard_map/ek,ckj->cej/dot_general | solution.py:91
  189.5 59.3 %all-gather.3.cloned.1.call-done = bf16[64,8192]{1,0:T(8,128)(2,1)} async-done(((bf16[64,512]{1,0:T(8,128)(2,1)}), bf16[64,8192]{1,0:T(8,128)(2,1)}) %all-gather.3.cloned.1.call-update) | async-done | bytes 1048592 | tf_op jit(solution)/shard_map/all_gather | solution.py:29
  248.8 2.3 copy.32
  251.4 76.3 %while.12 = (s32[]{:T(128)}, f32[64,2,256]{2,0,1:T(8,128)S(1)}, f32[64,32,256]{2,0,1:T(8,128)S(1)}, s32[]{:T(128)}, s32[32]{0:T(128)}, /*index=5*/bf16[32,256,25...) while((s32[]{:T(128)}, f32[64,2,256]{2,0,1:T(8,128)S(1)}, ...), condition=%wide.region_3.4_spmd, body=%wide.region_0.3_spmd.sunk | while | flops 67504192 | bytes 3940779 | solution.py:61
  252.8 2.0 gather_fusion.1
  257.7 2.4 gather_fusion
  263.7 2.1 gather_fusion.1
  268.6 2.4 gather_fusion
  274.6 2.1 gather_fusion.1
  279.6 2.4 gather_fusion
  285.5 2.1 gather_fusion.1
  290.5 2.4 gather_fusion
  301.3 2.4 gather_fusion
  307.3 2.1 gather_fusion.1
  312.3 2.5 gather_fusion
  318.2 2.1 gather_fusion.1
  323.2 2.4 gather_fusion
  329.4 7.4 %fusion.33 = bf16[64,64]{1,0:T(8,128)(2,1)S(1)} fusion(f32[16,64,1024]{2,1,0:T(8,128)} %gather_fusion.2, pred[16]{0:T(512)(128)(4,1)S(1)} %copy-done.6, f32[16,64,1024]{2,1,0:T(8,128)} %all-gather.5.cloned.1.call-done, f32[16]{0:T(128)S(1)} %copy-done.4), kind=kOutput, calls=%fused_computation.45 | convolution fusion | flops 807407616 | bytes 8396880 | tf_op jit(solution)/shard_map/cej,ckj->ek/dot_general | solution.py:83
  336.9 43.5 %all_gather.11 = bf16[64,1024]{0,1:T(8,128)(2,1)S(1)} all-gather(bf16[64,64]{0,1:T(8,128)(2,1)S(1)} %copy.24), channel_id=1, replica_groups=mesh['blk'=16,'rows'=16] {'rows'}, dimensions={1}, use_global_device_ids=true | all-gather | bytes 139264 | tf_op jit(solution)/shard_map/all_gather | solution.py:86
  381.3 75.2 %all-reduce.5 = bf16[64,1024]{1,0:T(8,128)(2,1)S(1)} all-reduce(f32[64,1024]{1,0:T(8,128)} %bitcast.61), channel_id=1, replica_groups=mesh['blk'=16,'rows'=16] {'rows'}, use_global_device_ids=true, to_apply=%region_8.10 | all-reduce | flops 65536 | bytes 393216 | tf_op jit(solution)/shard_map/psum | solution.py:96
  456.5 109.8 %reduce-scatter.3.cloned.1.call-done = f32[64,512]{1,0:T(8,128)} async-done(((f32[64,8192]{1,0:T(8,128)}), f32[64,512]{1,0:T(8,128)}) %reduce-scatter.3.cloned.1.call-update) | async-done | bytes 131088 | tf_op jit(solution)/shard_map/reduce_scatter | solution.py:98
  (97 shorter events, 56.5 us)
Async XLA Ops:
  7.2 4.4 copy-start
  7.2 165.3 %all-reduce.4.cloned.1.call-start = ((), (), s32[]{:S(2)}) async-start(), calls=%async_computation.6 | async-start | bytes 1048576 | tf_op jit(solution)/shard_map/psum | solution.py:69
  8.2 4.6 copy-start.2
  12.7 236.1 %all-gather.3.cloned.1.call-start = ((), (), s32[]{:S(2)}) async-start(), calls=%async_computation.2 | async-start | bytes 1114112 | tf_op jit(solution)/shard_map/all_gather | solution.py:29
  13.5 315.9 %all-gather.5.cloned.1.call-start = ((), (), s32[]{:S(2)}) async-start(), calls=%async_computation.3 | async-start | bytes 4456448 | tf_op jit(solution)/shard_map/all_gather | solution.py:79
  172.5 208.8 %reduce-scatter.5.cloned.1.call-start = ((), (), s32[]{:S(2)}) async-start(), calls=%async_computation.5 | async-start | bytes 4456448 | tf_op jit(solution)/shard_map/reduce_scatter | solution.py:90
  177.5 0.5 copy-start.3
  177.5 0.6 copy-start.5
  188.2 378.1 %reduce-scatter.3.cloned.1.call-start = ((), (), s32[]{:S(2)}) async-start(), calls=%async_computation.4 | async-start | bytes 2228224 | tf_op jit(solution)/shard_map/reduce_scatter | solution.py:98
  327.7 1.6 copy-start.4
  327.7 1.6 copy-start.6
  329.3 237.0 %copy-start.1 = (bf16[1024,512]{1,0:T(8,128)(2,1)S(1)}, bf16[1024,512]{1,0:T(8,128)(2,1)}, u32[]{:S(2)}) copy-start(bf16[1024,512]{1,0:T(8,128)(2,1)} %param.19) | copy-start | bytes 3145732
Sparse Core Ops, SparseCore 0:
  12.9 159.5 all-reduce.3
  175.9 72.9 all-gather.2
  250.8 35.8 all-gather.4
  289.3 66.4 reduce-scatter.4
  360.0 206.2 reduce-scatter.2
where the time goes:
time: 576 us; the launch traced here: 575 us
  waiting for transfers between devices  329 us (57%)
  blocking collectives  119 us (21%)
  matrix products  42.8 us (7%)
  local copies, waits for them, and re-layouts  41.8 us (7%)
  other arithmetic  27.4 us (5%)
  between operations  14.6 us (3%)
    psum x1, waiting for transfers between devices, on_device(): charges, gradient_all = lax.psum((charge_part, gradient_part), 'rows')  159 us
    reduce_scatter x1, waiting for transfers between devices, on_device(): lax.psum_scatter(near_behind.reshape(excite_count, column_blocks * tile_s...  110 us
    psum x1, blocking collectives, on_device(): adjoint_low = lax.psum(summed[0], 'rows').astype(jnp.bfloat16)  75.2 us
    all_gather x1, waiting for transfers between devices, on_device(): gathered = lax.all_gather(drive_low, 'rows', axis=1, tiled=True)  59.3 us
    all_gather x1, blocking collectives, on_device(): lax.all_gather(potential.astype(jnp.bfloat16), 'rows', axis=1, tiled=True)  43.5 us
    gather x7, local copies, waits for them, and re-layouts, near_group(): source = jnp.take(drive_blocks, column_ids, axis=1)  17.1 us
    gather x7, local copies, waits for them, and re-layouts, near_group(): target = jnp.take(load_blocks, row_ids, axis=1)  14.4 us
  transfers between devices with their start and end apart: 5, of which 3 were waited for; matrix products, arithmetic and copies ran while one was open for 18% of the time, Pallas kernels for 0%

commit v1 on v0

v1 whole, which is shorter than its diff:
```python
import jax
import jax.numpy as jnp
from jax import lax
from jax.experimental import pallas as pl
from jax.experimental.pallas import tpu as pltpu
from jax.sharding import Mesh
from jax.sharding import PartitionSpec as P

BLK = ("xlo", "y", "core")
ROWS = ("xhi", "z")
FACE = ("xlo", "y")
bf16 = jnp.bfloat16
f32 = jnp.float32
LAST = (((1,), (1,)), ((), ()))


def vmem():
    return pl.BlockSpec(memory_space=pltpu.VMEM)


def smem():
    return pl.BlockSpec(memory_space=pltpu.SMEM)


def call(kernel, outs, args, specs=None, scratch=(), flops=10**7, name=None):
    moved = sum(a.size * a.dtype.itemsize for a in args)
    return pl.pallas_call(
        kernel,
        out_shape=[jax.ShapeDtypeStruct(s, d) for s, d in outs],
        in_specs=specs or [vmem()] * len(args),
        out_specs=[vmem()] * len(outs),
        scratch_shapes=list(scratch),
        compiler_params=pltpu.CompilerParams(vmem_limit_bytes=40 * 2**20),
        cost_estimate=pl.CostEstimate(flops=flops, bytes_accessed=moved, transcendentals=0),
        name=name,
    )(*args)


def split(value):
    high = value.astype(bf16)
    return high, (value - high.astype(f32)).astype(bf16)


def dot(a, b):
    return jnp.dot(a, b, preferred_element_type=f32)


def dot_last(a, b):
    return lax.dot_general(a, b, LAST, preferred_element_type=f32)


def put_pieces(ref, value, lead=()):
    for piece in range(16):
        for part in range(4):
            row = piece // 2 * 8
            col = piece % 2 * 512 + part * 128
            ref[(*lead, piece, pl.ds(part * 8, 8), slice(None))] = value[row : row + 8, col : col + 128]


def join_pieces(ref, first):
    rows = []
    for band in range(8):
        blocks = [
            ref[band * 2 + half, first + part * 8 : first + part * 8 + 8, :]
            for half in range(2)
            for part in range(4)
        ]
        rows.append(jnp.concatenate(blocks, axis=1))
    return jnp.concatenate(rows, axis=0)


def prepare(exc_ref, loads_ref, skin_ref, skout_ref, drive_ref, low_ref, msg_ref):
    drive = exc_ref[...].astype(bf16)
    loads = loads_ref[...].astype(bf16)
    for part in range(2):
        drive_ref[part] = drive[:, part * 256 : part * 256 + 256]
        low_ref[part] = loads[:, part * 256 : part * 256 + 256]
    charges = dot_last(drive, skin_ref[...]).astype(bf16).astype(f32)
    twice = jnp.concatenate([loads, loads], axis=0)
    gradient = dot_last(skout_ref[...], twice)
    left = lax.broadcasted_iota(jnp.int32, (32, 128), 1) < 64
    for piece in range(16):
        row = piece // 2 * 8
        for part in range(4):
            col = piece % 2 * 512 + part * 128
            msg_ref[piece, part * 8 : part * 8 + 8, :] = charges[row : row + 8, col : col + 128].astype(bf16)
        k = piece * 64
        msg_ref[piece, 32:64, :] = jnp.where(
            left, gradient[k : k + 32], gradient[k + 32 : k + 64]
        ).astype(bf16)


def cross_core(msg_ref, trans_ref, copies_ref, grad_ref, send_ref):
    total = jnp.sum(msg_ref[...].astype(f32), axis=0)
    share = total[:32].astype(bf16)
    for piece in range(16):
        copies_ref[piece] = share
    packed = total[32:]
    gradient = jnp.concatenate([packed, pltpu.roll(packed, 64, 1)], axis=0)
    gradient = gradient.T[:64]
    grad_ref[...] = gradient
    high, low = split(gradient)
    both = jnp.concatenate([high, low], axis=0)
    cluster = lax.axis_index(BLK)
    other = 1 - lax.axis_index("core")
    for q in range(8):
        lag = lax.rem(cluster - (2 * q + other) + 16, 16)
        t_high, t_low = split(trans_ref[0, lag - 1])
        pair = dot(both, t_high)
        send_ref[q] = (pair[:64] + pair[64:] + dot(high, t_low)).astype(bf16)


def own_core(grad_ref, came_ref, trans_ref, send_ref):
    high, low = split(grad_ref[...])
    both = jnp.concatenate([high, low], axis=0)
    cluster = lax.axis_index(BLK)
    core = lax.axis_index("core")
    for q in range(8):
        lag = lax.rem(cluster - (2 * q + core) + 16, 16)
        t_high, t_low = split(trans_ref[0, jnp.maximum(lag - 1, 0)])
        pair = dot(both, t_high)
        value = pair[:64] + pair[64:] + dot(high, t_low)
        send_ref[q] = (jnp.where(lag == 0, 0.0, value) + came_ref[q].astype(f32)).astype(bf16)


def spread(pieces_ref, out_ref):
    value = join_pieces(pieces_ref, 0)
    for q in range(8):
        out_ref[q] = value


def forward(own_ref, other_ref, adj_ref, trans_ref, pot_ref, msg_ref):
    cluster = lax.axis_index(BLK)
    core = lax.axis_index("core")
    total = jnp.zeros((64, 64), f32)
    for q in range(8):
        for ref, parity in ((own_ref, core), (other_ref, 1 - core)):
            lag = lax.rem(cluster - (2 * q + parity) + 16, 16)
            t_high, t_low = split(trans_ref[0, jnp.maximum(lag - 1, 0)])
            both = jnp.concatenate([t_high, t_low], axis=0)
            pair = dot_last(both, ref[q])
            total = total + jnp.where(lag == 0, 0.0, pair[:64] + pair[64:])
    pot_ref[...] = jnp.concatenate([total[:32], total[32:]], axis=1).astype(bf16)
    put_pieces(msg_ref, jnp.sum(adj_ref[...].astype(f32), axis=0).astype(bf16))


def near(count_ref, rows_ref, cols_ref, tiles_ref, drive_ref, low_ref, adj_ref, ahead_ref, msg_ref, acc, behind):
    acc[...] = jnp.zeros_like(acc)
    behind[...] = jnp.zeros_like(behind)
    count = count_ref[0]
    group = 4

    def step(index, carry):
        results = []
        for part in range(group):
            slot = index * group + part
            live = slot < count
            slot = jnp.minimum(slot, 31)
            row = rows_ref[slot]
            col = cols_ref[slot]
            tile = tiles_ref[slot]
            fwd = dot_last(drive_ref[col], tile)
            bwd = dot(low_ref[row], tile)
            results.append((live, row, col, fwd, bwd))
        for live, row, col, fwd, bwd in results:
            acc[row] += jnp.where(live, fwd, 0.0)
            behind[col] += jnp.where(live, bwd, 0.0)
        return carry

    lax.fori_loop(0, (count + group - 1) // group, step, 0)
    for part in range(2):
        ahead_ref[:, part * 256 : part * 256 + 256] = acc[part]
    for col in range(32):
        for half in range(2):
            msg_ref[col // 2, pl.ds(col % 2 * 128 + half * 64, 64), :] = behind[
                col, :, half * 128 : half * 128 + 128
            ].astype(bf16)
    msg_ref[:, 256:288, :] = adj_ref[...]


def low_shares(near_ref, pot_ref, out_ref):
    adjoint = jnp.sum(near_ref[:, 256:288, :].astype(f32), axis=0).astype(bf16)
    for piece in range(16):
        out_ref[piece, 0:32, :] = adjoint
        out_ref[piece, 32:64, :] = pot_ref[...]


def finish(low_ref, near_ref, ahead_ref, skin_ref, skout_ref, resp_ref, sens_ref):
    adjoint = join_pieces(low_ref, 0)
    packed = jnp.concatenate([low_ref[r, 32:64, :] for r in range(16)], axis=0)
    packed = packed.astype(f32).T.astype(bf16)
    upper = jnp.concatenate([skout_ref[r * 64 : r * 64 + 32, :] for r in range(16)], axis=0)
    lower = jnp.concatenate([skout_ref[r * 64 + 32 : r * 64 + 64, :] for r in range(16)], axis=0)
    resp_ref[...] = ahead_ref[...] + dot(packed[:64], upper) + dot(packed[64:], lower)
    far = dot(adjoint, skin_ref[...])
    for part in range(4):
        value = near_ref[0, part * 64 : part * 64 + 64, :].astype(f32)
        for source in range(1, 16):
            value = value + near_ref[source, part * 64 : part * 64 + 64, :].astype(f32)
        sens_ref[:, part * 128 : part * 128 + 128] = far[:, part * 128 : part * 128 + 128] + value


def swap(value):
    return lax.ppermute(value, "core", [(0, 1), (1, 0)])


def exchange(value, axes):
    return lax.all_to_all(value, axes, 0, 0, tiled=True)


def on_device(exc, loads, tiles, tile_rows, tile_cols, tile_count, skin, skout, trans):
    drive, low, msg = call(
        prepare,
        [((2, 64, 256), bf16), ((2, 64, 256), bf16), ((16, 64, 128), bf16)],
        [exc, loads, skin, skout],
        name="prepare",
    )
    drives = lax.all_gather(drive, ROWS, axis=0, tiled=True)
    msg = exchange(msg, ROWS)
    copies, gradient, send = call(
        cross_core,
        [((16, 32, 128), bf16), ((64, 64), f32), ((8, 64, 1024), bf16)],
        [msg, trans],
        name="cross_core",
    )
    came = swap(send)
    (charges,) = call(spread, [((8, 64, 1024), bf16)], [exchange(copies, ROWS)], name="spread")
    charges = exchange(charges, FACE)
    others = swap(charges)
    (send,) = call(own_core, [((8, 64, 1024), bf16)], [gradient, came, trans], name="own_core")
    adjoint = exchange(send, FACE)
    potential, adjoint = call(
        forward,
        [((32, 128), bf16), ((16, 32, 128), bf16)],
        [charges, others, adjoint, trans],
        name="forward",
    )
    ahead, behind = call(
        near,
        [((64, 512), f32), ((16, 288, 128), bf16)],
        [tile_count, tile_rows, tile_cols, tiles, drives, low, adjoint],
        specs=[smem(), smem(), smem()] + [vmem()] * 4,
        scratch=[pltpu.VMEM((2, 64, 256), f32), pltpu.VMEM((32, 64, 256), f32)],
        name="near",
    )
    behind = exchange(behind, ROWS)
    (shares,) = call(low_shares, [((16, 64, 128), bf16)], [behind, potential], name="low_shares")
    shares = exchange(shares, ROWS)
    return tuple(
        call(
            finish,
            [((64, 512), f32), ((64, 512), f32)],
            [shares, behind, ahead, skin, skout],
            name="finish",
        )
    )


def solution(mesh):
    fine = Mesh(mesh.devices.reshape(2, 4, 2, 2, 8), BLK + ROWS)
    every = BLK + ROWS
    return jax.shard_map(
        on_device,
        mesh=fine,
        in_specs=(
            P(None, every),
            P(None, every),
            P(every, None, None),
            P(every),
            P(every),
            P(every),
            P(None, every),
            P(None, every),
            P(BLK, None, ROWS, None),
        ),
        out_specs=(P(None, every), P(None, every)),
        check_vma=False,
    )
```

time: 576 us -> 201 us (0.35)
  waiting for transfers between devices: 329 us -> 75.4 us
  blocking collectives: 119 us -> 69.3 us
  matrix products: 42.8 us -> 0 us
  local copies, waits for them, and re-layouts: 41.8 us -> 14.1 us
  other arithmetic: 27.4 us -> 0 us
  starting transfers between devices: 0.2 us -> 14.4 us
  Pallas kernels: 0 us -> 11.3 us
    psum x1 -> x0, waiting for transfers between devices: 159 us -> none  [on_device(): charges, gradient_all = lax.psum((charge_part, gradient_part), 'rows')]
    reduce_scatter x2 -> x0, waiting for transfers between devices: 110 us -> none  [the longest x1 110 us: on_device(): lax.psum_scatter(near_behind.reshape(excite_count, column_blocks * tile_s...]
    psum x1 -> x0, blocking collectives: 75.2 us -> none  [on_device(): adjoint_low = lax.psum(summed[0], 'rows').astype(jnp.bfloat16)]
    all_to_all x0 -> x3, blocking collectives: none -> 69.3 us  [exchange(): return lax.all_to_all(value, axes, 0, 0, tiled=True)]
    all_gather x1 -> x0, blocking collectives: 43.5 us -> none  [on_device(): lax.all_gather(potential.astype(jnp.bfloat16), 'rows', axis=1, tiled=True)]
    dot_general x20 -> x0, matrix products: 42.8 us -> none  [the longest x1 10 us: on_device(): jnp.einsum('ek,ckj->cej', gradient, chosen, precision=highest)]
    gather x15 -> x0, local copies, waits for them, and re-layouts: 36.3 us -> none  [the longest x7 17.1 us: near_group(): source = jnp.take(drive_blocks, column_ids, axis=1)]
    all_to_all x0 -> x3, waiting for transfers between devices: none -> 34.7 us  [exchange(): return lax.all_to_all(value, axes, 0, 0, tiled=True)]
  transfers between devices with their start and end apart: 5 -> 6, of which waited for: 3 -> 4; matrix products, arithmetic and copies ran while one was open for 18% -> 0% of each run, Pallas kernels for 0% -> 2%
where the time goes in v1:
time: 201 us; the launch traced here: 199 us
  waiting for transfers between devices  75.4 us (38%)
  blocking collectives  69.3 us (34%)
  between operations  14.8 us (7%)
  starting transfers between devices  14.4 us (7%)
  local copies, waits for them, and re-layouts  14.1 us (7%)
  Pallas kernels  11.3 us (6%)
    all_to_all x3, blocking collectives, exchange(): return lax.all_to_all(value, axes, 0, 0, tiled=True)  69.3 us
    all_gather x1, waiting for transfers between devices, on_device(): drives = lax.all_gather(drive, ROWS, axis=0, tiled=True)  40 us
    all_to_all x3, waiting for transfers between devices, exchange(): return lax.all_to_all(value, axes, 0, 0, tiled=True)  34.7 us
    all_to_all x3, starting transfers between devices, exchange(): return lax.all_to_all(value, axes, 0, 0, tiled=True)  14.3 us
    unnamed x26, local copies, waits for them, and re-layouts  14.1 us
    pallas_call x8, Pallas kernels, call(): pl.pallas_call(kernel, out_shape=[jax.ShapeDtypeStruct(s, d) for s, d in...  11.3 us
  transfers between devices with their start and end apart: 6, of which 4 were waited for; matrix products, arithmetic and copies ran while one was open for 0% of the time, Pallas kernels for 2%

profile of v1, /device:TPU:8, one launch (start us, length us, event | category | flops | bytes accessed | tf_op | source)
XLA Modules:
  0.0 199.1 jit_solution(3551398389558685371)
XLA Ops:
  7.2 1.2 copy-done.3
  8.4 1.2 copy-done.5
  9.6 0.9 copy-done.9
  12.3 22.4 %all_to_all.30.msg_ref = bf16[16,64,128]{2,1,0:T(8,128)(2,1)S(1)} all-to-all(bf16[16,64,128]{2,1,0:T(8,128)(2,1)S(1)} %get-tuple-element.14), channel_id=1, replica_groups=mesh['xlo'=2,'y'=4,'core'=2,'xhi'=2,'z'=8] {'xhi','z'}, dimensions={0} | all-to-all | bytes 524288 | tf_op jit(solution)/shard_map/all_to_all | solution.py:208
  34.7 2.1 %copy-done = f32[1,15,64,1024]{3,2,1,0:T(8,128)S(1)} copy-done((f32[1,15,64,1024]{3,2,1,0:T(8,128)S(1)}, f32[1,15,64,1024]{3,2,1,0:T(8,128)}, u32[]{:S(2)}) %copy-start) | copy-done | bytes 3932184
  36.8 2.0 %cross_core.1 = (bf16[16,32,128]{2,1,0:T(8,128)(2,1)}, f32[64,64]{1,0:T(8,128)S(1)}, bf16[8,64,1024]{2,1,0:T(8,128)(2,1)}) custom-call(bf16[16,64,128]{2,1,0:T(8,128)(2,1)S(1)} %all_to_all.30.msg_ref, f32[1,15,64,1024]{3,2,1,0:T(8,128)S(1)} %copy-done), custom_call_target="tpu_custom_call" | custom-call | flops 10000000 | bytes 4194304 | tf_op jit(solution)/shard_map/cross_core/pallas_call | solution.py:27
  38.9 4.5 %all-to-all-start.1 = ((bf16[16,32,128]{2,1,0:T(8,128)(2,1)}), bf16[16,32,128]{2,1,0:T(8,128)(2,1)S(1)}, u32[]{:S(2)}, u32[]{:S(2)}) async-start(bf16[16,32,128]{2,1,0:T(8,128)(2,1)} %get-tuple-element.15), calls=%async_computation.1 | async-start | bytes 262144 | tf_op jit(solution)/shard_map/all_to_all | solution.py:208
  43.5 10.0 %all-to-all-done.1.pieces_ref = bf16[16,32,128]{2,1,0:T(8,128)(2,1)S(1)} async-done(((bf16[16,32,128]{2,1,0:T(8,128)(2,1)}), bf16[16,32,128]{2,1,0:T(8,128)(2,1)S(1)}, u32[]{:S(2)}, u32[]{:S(2)}) %all-to-all-start.1) | async-done | bytes 131104 | tf_op jit(solution)/shard_map/all_to_all | solution.py:208
  53.5 1.1 spread.1
  54.6 4.9 %all-to-all-start.2 = ((bf16[8,64,1024]{2,1,0:T(8,128)(2,1)}), bf16[8,64,1024]{2,1,0:T(8,128)(2,1)S(1)}, u32[]{:S(2)}, u32[]{:S(2)}) async-start(bf16[8,64,1024]{2,1,0:T(8,128)(2,1)} %spread.1), calls=%async_computation.2 | async-start | bytes 2097152 | tf_op jit(solution)/shard_map/all_to_all | solution.py:208
  60.3 11.0 %all-to-all-done.2.own_ref = bf16[8,64,1024]{2,1,0:T(8,128)(2,1)S(1)} async-done(((bf16[8,64,1024]{2,1,0:T(8,128)(2,1)}), bf16[8,64,1024]{2,1,0:T(8,128)(2,1)S(1)}, u32[]{:S(2)}, u32[]{:S(2)}) %all-to-all-start.2) | async-done | bytes 1048608 | tf_op jit(solution)/shard_map/all_to_all | solution.py:208
  71.3 2.2 %copy-done.1 = f32[1,15,64,1024]{3,2,1,0:T(8,128)S(1)} copy-done((f32[1,15,64,1024]{3,2,1,0:T(8,128)S(1)}, f32[1,15,64,1024]{3,2,1,0:T(8,128)}, u32[]{:S(2)}) %copy-start.1) | copy-done | bytes 3932184
  73.4 1.9 own_core.1
  75.3 4.8 %all-to-all-start.3 = ((bf16[8,64,1024]{2,1,0:T(8,128)(2,1)}), bf16[8,64,1024]{2,1,0:T(8,128)(2,1)S(1)}, u32[]{:S(2)}, u32[]{:S(2)}) async-start(bf16[8,64,1024]{2,1,0:T(8,128)(2,1)} %own_core.1), calls=%async_computation.3 | async-start | bytes 2097152 | tf_op jit(solution)/shard_map/all_to_all | solution.py:208
  80.8 13.7 %all-to-all-done.3.adj_ref = bf16[8,64,1024]{2,1,0:T(8,128)(2,1)S(1)} async-done(((bf16[8,64,1024]{2,1,0:T(8,128)(2,1)}), bf16[8,64,1024]{2,1,0:T(8,128)(2,1)S(1)}, u32[]{:S(2)}, u32[]{:S(2)}) %all-to-all-start.3) | async-done | bytes 1048608 | tf_op jit(solution)/shard_map/all_to_all | solution.py:208
  94.5 2.1 %copy-done.2 = f32[1,15,64,1024]{3,2,1,0:T(8,128)S(1)} copy-done((f32[1,15,64,1024]{3,2,1,0:T(8,128)S(1)}, f32[1,15,64,1024]{3,2,1,0:T(8,128)}, u32[]{:S(2)}) %copy-start.2) | copy-done | bytes 3932184
  96.6 1.4 forward.1
  98.1 40.0 %all-gather.2.cloned.1.call-done.drive_ref = bf16[32,64,256]{2,1,0:T(8,128)(2,1)} async-done(((bf16[2,64,256]{2,1,0:T(8,128)(2,1)}), bf16[32,64,256]{2,1,0:T(8,128)(2,1)}) %all-gather.2.cloned.1.call-update) | async-done | bytes 1048592 | tf_op jit(solution)/shard_map/all_gather | solution.py:218
  138.1 2.2 %copy-done.7 = bf16[32,256,256]{2,1,0:T(8,128)(2,1)S(1)} copy-done((bf16[32,256,256]{2,1,0:T(8,128)(2,1)S(1)}, bf16[32,256,256]{2,1,0:T(8,128)(2,1)}, u32[]{:S(2)}) %copy-start.7) | copy-done | bytes 4194328
  140.3 1.2 copy-done.8
  141.5 2.7 %near.1 = (f32[64,512]{1,0:T(8,128)S(1)}, bf16[16,288,128]{2,1,0:T(8,128)(2,1)S(1)}) custom-call(s32[1]{0:T(128)S(6)} %copy.11.count_ref, s32[32]{0:T(128)S(1)} %copy-done.11, s32[32]{0:T(128)S(1)} %copy-done.12, bf16[32,256,256]{2,1,0:T(8,128)(2,1)S(1)} %copy-done.7, bf16[32,64,256]{2,1,0:T(8,128)(2,1)S(1)} %copy-done.8, ...), custom_call_target="tpu_custom_call" | custom-call | flops 10000000 | bytes 5439748 | tf_op jit(solution)/shard_map/near/pallas_call | solution.py:27
  144.2 33.0 %all_to_all.31.near_ref = bf16[16,288,128]{2,1,0:T(8,128)(2,1)S(1)} all-to-all(bf16[16,288,128]{2,1,0:T(8,128)(2,1)S(1)} %get-tuple-element.19), channel_id=1, replica_groups=mesh['xlo'=2,'y'=4,'core'=2,'xhi'=2,'z'=8] {'xhi','z'}, dimensions={0} | all-to-all | bytes 2359296 | tf_op jit(solution)/shard_map/all_to_all | solution.py:208
  177.2 13.8 %all_to_all.32.low_ref = bf16[16,64,128]{2,1,0:T(8,128)(2,1)S(1)} all-to-all(bf16[16,64,128]{2,1,0:T(8,128)(2,1)S(1)} %low_shares.1), channel_id=1, replica_groups=mesh['xlo'=2,'y'=4,'core'=2,'xhi'=2,'z'=8] {'xhi','z'}, dimensions={0} | all-to-all | bytes 524288 | tf_op jit(solution)/shard_map/all_to_all | solution.py:208
  191.0 1.2 finish.1
  (26 shorter events, 2.6 us)
Async XLA Ops:
  7.2 1.2 copy-start.3
  8.4 1.2 copy-start.5
  9.6 0.9 copy-start.9
  10.5 0.9 copy-start.10
  34.7 2.1 %copy-start = (f32[1,15,64,1024]{3,2,1,0:T(8,128)S(1)}, f32[1,15,64,1024]{3,2,1,0:T(8,128)}, u32[]{:S(2)}) copy-start(f32[1,15,64,1024]{3,2,1,0:T(8,128)} %trans_ref.5) | copy-start | bytes 11796484
  38.9 14.6 %all-to-all-start.1 = ((bf16[16,32,128]{2,1,0:T(8,128)(2,1)}), bf16[16,32,128]{2,1,0:T(8,128)(2,1)S(1)}, u32[]{:S(2)}, u32[]{:S(2)}) async-start(bf16[16,32,128]{2,1,0:T(8,128)(2,1)} %get-tuple-element.15), calls=%async_computation.1 | async-start | bytes 262144 | tf_op jit(solution)/shard_map/all_to_all | solution.py:208
  43.4 27.8 %collective-permute-start.1 = (bf16[8,64,1024]{2,1,0:T(8,128)(2,1)}, bf16[8,64,1024]{2,1,0:T(8,128)(2,1)S(1)}, u32[]{:S(2)}, u32[]{:S(2)}) collective-permute-start(bf16[8,64,1024]{2,1,0:T(8,128)(2,1)} %get-tuple-element.17), channel_id=1, source_target_pairs={{0,16},{16,0},{1,17},{17,1},{2,18},{18,2},{3,19},{19,3},{4,20},{20... | collective-permute-start | bytes 3145736 | tf_op jit(solution)/shard_map/ppermute | solution.py:204
  54.6 16.7 %all-to-all-start.2 = ((bf16[8,64,1024]{2,1,0:T(8,128)(2,1)}), bf16[8,64,1024]{2,1,0:T(8,128)(2,1)S(1)}, u32[]{:S(2)}, u32[]{:S(2)}) async-start(bf16[8,64,1024]{2,1,0:T(8,128)(2,1)} %spread.1), calls=%async_computation.2 | async-start | bytes 2097152 | tf_op jit(solution)/shard_map/all_to_all | solution.py:208
  59.5 78.5 %all-gather.2.cloned.1.call-start = ((), (), s32[]{:S(2)}) async-start(), calls=%async_computation.6 | async-start | bytes 1114112 | tf_op jit(solution)/shard_map/all_gather | solution.py:218
  71.2 23.3 %collective-permute-start = (bf16[8,64,1024]{2,1,0:T(8,128)(2,1)S(1)}, bf16[8,64,1024]{2,1,0:T(8,128)(2,1)S(1)}, u32[]{:S(2)}, u32[]{:S(2)}) collective-permute-start(bf16[8,64,1024]{2,1,0:T(8,128)(2,1)S(1)} %all-to-all-done.2.own_ref), channel_id=1, source_target_pairs={{0,16},{16,0},{1,17},{17,1},{2,18},{18,2},{3,19},{19,3},{4,20},{20... | collective-permute-start | bytes 3145736 | tf_op jit(solution)/shard_map/ppermute | solution.py:204
  71.3 2.2 %copy-start.1 = (f32[1,15,64,1024]{3,2,1,0:T(8,128)S(1)}, f32[1,15,64,1024]{3,2,1,0:T(8,128)}, u32[]{:S(2)}) copy-start(f32[1,15,64,1024]{3,2,1,0:T(8,128)} %trans_ref.5) | copy-start | bytes 11796484
  75.3 19.2 %all-to-all-start.3 = ((bf16[8,64,1024]{2,1,0:T(8,128)(2,1)}), bf16[8,64,1024]{2,1,0:T(8,128)(2,1)S(1)}, u32[]{:S(2)}, u32[]{:S(2)}) async-start(bf16[8,64,1024]{2,1,0:T(8,128)(2,1)} %own_core.1), calls=%async_computation.3 | async-start | bytes 2097152 | tf_op jit(solution)/shard_map/all_to_all | solution.py:208
  80.1 57.9 %copy-start.11 = (s32[32]{0:T(128)S(1)}, s32[32]{0:T(128)}, u32[]{:S(2)}) copy-start(s32[32]{0:T(128)} %rows_ref.1) | copy-start | bytes 388
  80.1 57.9 %copy-start.12 = (s32[32]{0:T(128)S(1)}, s32[32]{0:T(128)}, u32[]{:S(2)}) copy-start(s32[32]{0:T(128)} %cols_ref.1) | copy-start | bytes 388
  94.5 2.1 %copy-start.2 = (f32[1,15,64,1024]{3,2,1,0:T(8,128)S(1)}, f32[1,15,64,1024]{3,2,1,0:T(8,128)}, u32[]{:S(2)}) copy-start(f32[1,15,64,1024]{3,2,1,0:T(8,128)} %trans_ref.5) | copy-start | bytes 11796484
  138.1 2.2 %copy-start.7 = (bf16[32,256,256]{2,1,0:T(8,128)(2,1)S(1)}, bf16[32,256,256]{2,1,0:T(8,128)(2,1)}, u32[]{:S(2)}) copy-start(bf16[32,256,256]{2,1,0:T(8,128)(2,1)} %tiles_ref.1) | copy-start | bytes 12582916
  140.3 1.2 copy-start.8
  141.5 49.5 %copy-start.4 = (bf16[1024,512]{1,0:T(8,128)(2,1)S(1)}, bf16[1024,512]{1,0:T(8,128)(2,1)}, u32[]{:S(2)}) copy-start(bf16[1024,512]{1,0:T(8,128)(2,1)} %skin_ref.3) | copy-start | bytes 3145732
  141.5 49.5 %copy-start.6 = (bf16[1024,512]{1,0:T(8,128)(2,1)S(1)}, bf16[1024,512]{1,0:T(8,128)(2,1)}, u32[]{:S(2)}) copy-start(bf16[1024,512]{1,0:T(8,128)(2,1)} %skout_ref.3) | copy-start | bytes 3145732
Sparse Core Ops, SparseCore 0:
  63.5 74.5 all-gather.1

commit v2 on v1

v2 whole, which is shorter than its diff:
```python
import jax
import jax.numpy as jnp
from jax import lax
from jax.experimental import pallas as pl
from jax.experimental.pallas import tpu as pltpu
from jax.sharding import Mesh
from jax.sharding import PartitionSpec as P

BLK = ("xlo", "y", "core")
ROWS = ("xhi", "z")
FACE = ("xlo", "y")
bf16 = jnp.bfloat16
f32 = jnp.float32
LAST = (((1,), (1,)), ((), ()))


def vmem():
    return pl.BlockSpec(memory_space=pltpu.VMEM)


def smem():
    return pl.BlockSpec(memory_space=pltpu.SMEM)


def hbm():
    return pl.BlockSpec(memory_space=pltpu.HBM)


def call(kernel, outs, args, specs=None, scratch=(), flops=10**7, name=None, room=8, alias=None):
    moved = sum(a.size * a.dtype.itemsize for a in args)
    return pl.pallas_call(
        kernel,
        out_shape=[jax.ShapeDtypeStruct(s, d) for s, d in outs],
        in_specs=specs or [vmem()] * len(args),
        out_specs=[vmem()] * len(outs),
        scratch_shapes=list(scratch),
        compiler_params=pltpu.CompilerParams(vmem_limit_bytes=room * 2**20),
        cost_estimate=pl.CostEstimate(flops=flops, bytes_accessed=moved, transcendentals=0),
        name=name,
        input_output_aliases=alias or {},
    )(*args)


def split(value):
    high = value.astype(bf16)
    return high, (value - high.astype(f32)).astype(bf16)


def dot(a, b):
    return jnp.dot(a, b, preferred_element_type=f32)


def dot_last(a, b):
    return lax.dot_general(a, b, LAST, preferred_element_type=f32)


def join_pieces(ref, first):
    rows = []
    for band in range(8):
        blocks = [
            ref[band * 2 + half, first + part * 8 : first + part * 8 + 8, :]
            for half in range(2)
            for part in range(4)
        ]
        rows.append(jnp.concatenate(blocks, axis=1))
    return jnp.concatenate(rows, axis=0)


def round_panels(exc_ref, loads_ref, drive_ref, low_ref):
    drive = exc_ref[...].astype(bf16)
    loads = loads_ref[...].astype(bf16)
    for part in range(2):
        drive_ref[part] = drive[:, part * 256 : part * 256 + 256]
        low_ref[part] = loads[:, part * 256 : part * 256 + 256]


def prepare(drive_ref, low_ref, skin_hbm, skout_hbm, msg_ref, skin, skout, sems):
    first = pltpu.make_async_copy(skin_hbm, skin, sems.at[0])
    second = pltpu.make_async_copy(skout_hbm, skout, sems.at[1])
    first.start()
    second.start()
    drive = jnp.concatenate([drive_ref[0], drive_ref[1]], axis=1)
    loads = jnp.concatenate([low_ref[0], low_ref[1]], axis=1)
    first.wait()
    charges = dot_last(drive, skin[...])
    for piece in range(16):
        row = piece // 2 * 8
        for part in range(4):
            col = piece % 2 * 512 + part * 128
            msg_ref[piece, part * 8 : part * 8 + 8, :] = charges[row : row + 8, col : col + 128].astype(bf16)
    second.wait()
    gradient = dot_last(skout[...], jnp.concatenate([loads, loads], axis=0))
    left = lax.broadcasted_iota(jnp.int32, (32, 128), 1) < 64
    for piece in range(16):
        k = piece * 64
        msg_ref[piece, 32:64, :] = jnp.where(
            left, gradient[k : k + 32], gradient[k + 32 : k + 64]
        ).astype(bf16)


def lags():
    cluster = lax.axis_index(BLK)
    core = lax.axis_index("core")
    return [
        lax.rem(cluster - (2 * q + parity) + 16, 16) for parity in (1 - core, core) for q in range(8)
    ]


def fetch(trans_hbm, blocks, sems, lag):
    copies = []
    for index in range(16):
        copies.append(
            pltpu.make_async_copy(
                trans_hbm.at[0, jnp.maximum(lag[index] - 1, 0)], blocks.at[index], sems.at[index]
            )
        )
        copies[index].start()
    return copies


def adjoint_terms(msg_ref, trans_hbm, copies_ref, send_ref, keep_ref, blocks, sems):
    lag = lags()
    fetched = fetch(trans_hbm, blocks, sems, lag)
    total = jnp.sum(msg_ref[...].astype(f32), axis=0)
    share = total[:32].astype(bf16)
    for piece in range(16):
        copies_ref[piece] = share
    packed = total[32:]
    gradient = jnp.concatenate([packed, pltpu.roll(packed, 64, 1)], axis=0)
    high, low = split(gradient.T[:64])
    both = jnp.concatenate([high, low], axis=0)
    for index in range(16):
        fetched[index].wait()
        t_high, t_low = split(blocks[index])
        pair = dot(both, t_high)
        value = pair[:64] + pair[64:] + dot(high, t_low)
        if index < 8:
            send_ref[index] = value.astype(bf16)
        else:
            keep_ref[index - 8] = jnp.where(lag[index] == 0, 0.0, value)


def pack(keep_ref, came_ref, pieces_ref, out_ref):
    charges = join_pieces(pieces_ref, 0)
    for q in range(8):
        out_ref[q, 0] = (keep_ref[q] + came_ref[q].astype(f32)).astype(bf16)
        out_ref[q, 1] = charges


def unpack(came_ref, near_ref, msg_ref, charges_ref):
    del near_ref
    total = came_ref[0, 0].astype(f32)
    charges_ref[0] = came_ref[0, 1]
    for q in range(1, 8):
        total = total + came_ref[q, 0].astype(f32)
        charges_ref[q] = came_ref[q, 1]
    for piece in range(16):
        row = piece // 2 * 8
        for part in range(4):
            col = piece % 2 * 512 + part * 128
            msg_ref[piece, 256 + part * 8 : 264 + part * 8, :] = total[row : row + 8, col : col + 128].astype(bf16)


def forward(other_ref, came_ref, trans_hbm, pot_ref, blocks, sems):
    lag = lags()
    fetched = fetch(trans_hbm, blocks, sems, lag)
    total = jnp.zeros((64, 64), f32)
    for index in range(16):
        fetched[index].wait()
        t_high, t_low = split(blocks[index])
        both = jnp.concatenate([t_high, t_low], axis=0)
        charges = other_ref[index] if index < 8 else came_ref[index - 8, 1]
        pair = dot_last(both, charges)
        total = total + jnp.where(lag[index] == 0, 0.0, pair[:64] + pair[64:])
    pot_ref[...] = jnp.concatenate([total[:32], total[32:]], axis=1).astype(bf16)


def near(count_ref, rows_ref, cols_ref, low_ref, tiles_hbm, *refs):
    pieces, (ahead_ref, msg_ref, acc, behind, drives, tiles_ref, piece_sems, tile_sems) = refs[:8], refs[8:]

    def tile_copy(index):
        span = pl.ds(index * 4, 4)
        return pltpu.make_async_copy(tiles_hbm.at[span], tiles_ref.at[span], tile_sems.at[index])

    arriving = [
        pltpu.make_async_copy(pieces[index], drives.at[index], piece_sems.at[index]) for index in range(8)
    ]
    for copy in arriving:
        copy.start()
    for index in range(8):
        tile_copy(index).start()
    acc[...] = jnp.zeros_like(acc)
    behind[...] = jnp.zeros_like(behind)
    count = count_ref[0]
    my_z = lax.axis_index("z")
    my_half = lax.axis_index("xhi")
    group = 4
    for copy in arriving:
        copy.wait()

    def step(index, carry):
        tile_copy(index).wait()
        results = []
        for part in range(group):
            slot = index * group + part
            live = slot < count
            row = rows_ref[slot]
            col = cols_ref[slot]
            owner = col // 2
            hops = lax.rem(my_z - lax.rem(owner, 8) + 8, 8)
            side = lax.rem(owner // 8 + my_half, 2)
            tile = tiles_ref[slot]
            fwd = dot_last(drives[hops, side, lax.rem(col, 2)], tile)
            bwd = dot(low_ref[row], tile)
            results.append((live, row, col, fwd, bwd))
        for live, row, col, fwd, bwd in results:
            acc[row] += jnp.where(live, fwd, 0.0)
            behind[col] += jnp.where(live, bwd, 0.0)
        return carry

    groups = (count + group - 1) // group
    lax.fori_loop(0, groups, step, 0)

    def drain(index, carry):
        tile_copy(index).wait()
        return carry

    lax.fori_loop(groups, 8, drain, 0)
    for part in range(2):
        ahead_ref[:, part * 256 : part * 256 + 256] = acc[part]
    for col in range(32):
        for half in range(2):
            msg_ref[col // 2, pl.ds(col % 2 * 128 + half * 64, 64), :] = behind[
                col, :, half * 128 : half * 128 + 128
            ].astype(bf16)
    msg_ref[:, 256:288, :] = jnp.zeros((16, 32, 128), bf16)


def low_shares(near_ref, pot_ref, out_ref):
    adjoint = jnp.sum(near_ref[:, 256:288, :].astype(f32), axis=0).astype(bf16)
    for piece in range(16):
        out_ref[piece, 0:32, :] = adjoint
        out_ref[piece, 32:64, :] = pot_ref[...]


def finish(low_ref, near_ref, ahead_ref, skin_hbm, skout_hbm, resp_ref, sens_ref, skin_ref, skout_ref, sems):
    first = pltpu.make_async_copy(skout_hbm, skout_ref, sems.at[0])
    second = pltpu.make_async_copy(skin_hbm, skin_ref, sems.at[1])
    first.start()
    second.start()
    adjoint = join_pieces(low_ref, 0)
    packed = jnp.concatenate([low_ref[r, 32:64, :] for r in range(16)], axis=0)
    packed = packed.astype(f32).T.astype(bf16)
    first.wait()
    upper = jnp.concatenate([skout_ref[r * 64 : r * 64 + 32, :] for r in range(16)], axis=0)
    lower = jnp.concatenate([skout_ref[r * 64 + 32 : r * 64 + 64, :] for r in range(16)], axis=0)
    resp_ref[...] = ahead_ref[...] + dot(packed[:64], upper) + dot(packed[64:], lower)
    second.wait()
    far = dot(adjoint, skin_ref[...])
    for part in range(4):
        value = near_ref[0, part * 64 : part * 64 + 64, :].astype(f32)
        for source in range(1, 16):
            value = value + near_ref[source, part * 64 : part * 64 + 64, :].astype(f32)
        sens_ref[:, part * 128 : part * 128 + 128] = far[:, part * 128 : part * 128 + 128] + value


def swap(value):
    return lax.ppermute(value, "core", [(0, 1), (1, 0)])


def exchange(value, axes):
    return lax.all_to_all(value, axes, 0, 0, tiled=True)


def in_hbm(value):
    return pltpu.with_memory_space_constraint(value, pltpu.HBM)


def shift(value, step):
    return lax.ppermute(value, "z", [(i, (i + step) % 8) for i in range(8)])


def tie(*values):
    return lax.optimization_barrier(values)


def on_device(exc, loads, tiles, tile_rows, tile_cols, tile_count, skin, skout, trans):
    tiles, skin, skout, trans = (in_hbm(value) for value in (tiles, skin, skout, trans))
    blocks = [pltpu.VMEM((16, 64, 1024), f32), pltpu.SemaphoreType.DMA((16,))]
    drive, low = call(
        round_panels, [((2, 64, 256), bf16), ((2, 64, 256), bf16)], [exc, loads], name="round_panels"
    )
    mate = lax.ppermute(drive, "xhi", [(0, 1), (1, 0)])
    (msg,) = call(
        prepare,
        [((16, 64, 128), bf16)],
        [drive, low, skin, skout],
        specs=[vmem()] * 2 + [hbm()] * 2,
        scratch=[pltpu.VMEM((1024, 512), bf16)] * 2 + [pltpu.SemaphoreType.DMA((2,))],
        name="prepare",
    )
    here = jnp.stack([drive, mate])
    here, msg = tie(here, msg)
    up1, down1 = shift(here, 1), shift(here, -1)
    msg = exchange(msg, ROWS)
    msg, up1, down1 = tie(msg, up1, down1)
    copies, send, keep = call(
        adjoint_terms,
        [((16, 32, 128), bf16), ((8, 64, 1024), bf16), ((8, 64, 1024), f32)],
        [msg, trans],
        specs=[vmem(), hbm()],
        scratch=blocks,
        name="adjoint_terms",
        room=12,
    )
    came = swap(send)
    up2, down2 = shift(up1, 1), shift(down1, -1)
    copies = exchange(copies, ROWS)
    copies, up2, down2 = tie(copies, up2, down2)
    (both,) = call(pack, [((8, 2, 64, 1024), bf16)], [keep, came, copies], name="pack")
    up3, down3 = shift(up2, 1), shift(down2, -1)
    up4 = shift(up3, 1)
    both = exchange(both, FACE)
    ahead, behind = call(
        near,
        [((64, 512), f32), ((16, 288, 128), bf16)],
        [tile_count, tile_rows, tile_cols, low, tiles, here, up1, up2, up3, up4, down3, down2, down1],
        specs=[smem(), smem(), smem(), vmem()] + [hbm()] * 9,
        scratch=[
            pltpu.VMEM((2, 64, 256), f32),
            pltpu.VMEM((32, 64, 256), f32),
            pltpu.VMEM((8, 2, 2, 64, 256), bf16),
            pltpu.VMEM((32, 256, 256), bf16),
            pltpu.SemaphoreType.DMA((8,)),
            pltpu.SemaphoreType.DMA((8,)),
        ],
        name="near",
        room=16,
    )
    behind, charges = call(
        unpack,
        [((16, 288, 128), bf16), ((8, 64, 1024), bf16)],
        [both, behind],
        alias={1: 0},
        name="unpack",
    )
    others = swap(charges)
    behind = exchange(behind, ROWS)
    (potential,) = call(
        forward,
        [((32, 128), bf16)],
        [others, both, trans],
        specs=[vmem(), vmem(), hbm()],
        scratch=blocks,
        name="forward",
        room=12,
    )
    (shares,) = call(low_shares, [((16, 64, 128), bf16)], [behind, potential], name="low_shares")
    shares = exchange(shares, ROWS)
    return tuple(
        call(
            finish,
            [((64, 512), f32), ((64, 512), f32)],
            [shares, behind, ahead, skin, skout],
            specs=[vmem()] * 3 + [hbm()] * 2,
            scratch=[pltpu.VMEM((1024, 512), bf16)] * 2 + [pltpu.SemaphoreType.DMA((2,))],
            name="finish",
        )
    )


def solution(mesh):
    fine = Mesh(mesh.devices.reshape(2, 4, 2, 2, 8), BLK + ROWS)
    every = BLK + ROWS
    return jax.shard_map(
        on_device,
        mesh=fine,
        in_specs=(
            P(None, every),
            P(None, every),
            P(every, None, None),
            P(every),
            P(every),
            P(every),
            P(None, every),
            P(None, every),
            P(BLK, None, ROWS, None),
        ),
        out_specs=(P(None, every), P(None, every)),
        check_vma=False,
    )
```

time: 201 us -> 147 us (0.73)
  blocking collectives: 69.3 us -> 17 us
  starting transfers between devices: 14.4 us -> 44.1 us
  waiting for transfers between devices: 75.4 us -> 50.3 us
  between operations: 14.8 us -> 1.62 us
  Pallas kernels: 11.3 us -> 22.9 us
  local copies, waits for them, and re-layouts: 14.1 us -> 9.57 us
    all_to_all x3 -> x1, blocking collectives: 69.3 us -> 17 us  [exchange(): return lax.all_to_all(value, axes, 0, 0, tiled=True)]
    all_gather x1 -> x0, waiting for transfers between devices: 40 us -> none  [on_device(): drives = lax.all_gather(drive, ROWS, axis=0, tiled=True)]
    ppermute x0 -> x8, waiting for transfers between devices: none -> 22 us  [the longest x7 22 us: shift(): return lax.ppermute(value, 'z', [(i, (i + step) % 8) for i in range(8)])]
    all_to_all x3 -> x4, starting transfers between devices: 14.3 us -> 30.5 us  [exchange(): return lax.all_to_all(value, axes, 0, 0, tiled=True)]
    ppermute x0 -> x8, starting transfers between devices: none -> 13.3 us  [the longest x7 10.2 us: shift(): return lax.ppermute(value, 'z', [(i, (i + step) % 8) for i in range(8)])]
    pallas_call x8 -> x9, Pallas kernels: 11.3 us -> 22.9 us  [call(): pl.pallas_call(kernel, out_shape=[jax.ShapeDtypeStruct(s, d) for s, d in...]
    all_to_all x3 -> x4, waiting for transfers between devices: 34.7 us -> 25.4 us  [exchange(): return lax.all_to_all(value, axes, 0, 0, tiled=True)]
    unnamed x26 -> x30, local copies, waits for them, and re-layouts: 14.1 us -> 9.57 us
  transfers between devices with their start and end apart: 6 -> 14, of which waited for: 4 -> 8; matrix products, arithmetic and copies ran while one was open for 0% -> 0% of each run, Pallas kernels for 2% -> 10%
where the time goes in v2:
time: 147 us; the launch traced here: 145 us
  waiting for transfers between devices  50.3 us (34%)
  starting transfers between devices  44.1 us (30%)
  Pallas kernels  22.9 us (16%)
  blocking collectives  17 us (12%)
  local copies, waits for them, and re-layouts  9.57 us (7%)
  between operations  1.62 us (1%)
    all_to_all x4, starting transfers between devices, exchange(): return lax.all_to_all(value, axes, 0, 0, tiled=True)  30.5 us
    all_to_all x4, waiting for transfers between devices, exchange(): return lax.all_to_all(value, axes, 0, 0, tiled=True)  25.4 us
    pallas_call x9, Pallas kernels, call(): pl.pallas_call(kernel, out_shape=[jax.ShapeDtypeStruct(s, d) for s, d in...  22.9 us
    ppermute x7, waiting for transfers between devices, shift(): return lax.ppermute(value, 'z', [(i, (i + step) % 8) for i in range(8)])  22 us
    all_to_all x1, blocking collectives, exchange(): return lax.all_to_all(value, axes, 0, 0, tiled=True)  17 us
    ppermute x7, starting transfers between devices, shift(): return lax.ppermute(value, 'z', [(i, (i + step) % 8) for i in range(8)])  10.2 us
    unnamed x30, local copies, waits for them, and re-layouts  9.57 us
    ppermute x1, starting transfers between devices, on_device(): mate = lax.ppermute(drive, 'xhi', [(0, 1), (1, 0)])  3.11 us
  transfers between devices with their start and end apart: 14, of which 8 were waited for; matrix products, arithmetic and copies ran while one was open for 0% of the time, Pallas kernels for 10%

profile of v2, /device:TPU:8, one launch (start us, length us, event | category | flops | bytes accessed | tf_op | source)
XLA Modules:
  0.0 145.4 jit_solution(17148498364500372380)
XLA Ops:
  2.5 3.1 %collective-permute-start = (bf16[2,64,256]{2,1,0:T(8,128)(2,1)S(1)}, bf16[2,64,256]{2,1,0:T(8,128)(2,1)S(1)}, u32[]{:S(2)}, u32[]{:S(2)}) collective-permute-start(bf16[2,64,256]{2,1,0:T(8,128)(2,1)S(1)} %get-tuple-element.19.drive_ref), channel_id=1, source_target_pairs={{0,8},{8,0},{1,9},{9,1},{2,10},{10,2},{3,11},{11,3},{4,12},{12,4},... | collective-permute-start | bytes 196616 | tf_op jit(solution)/shard_map/ppermute | solution.py:293
  5.6 2.8 %prepare.1 = bf16[16,64,128]{2,1,0:T(8,128)(2,1)} custom-call(bf16[2,64,256]{2,1,0:T(8,128)(2,1)S(1)} %get-tuple-element.19.drive_ref, bf16[2,64,256]{2,1,0:T(8,128)(2,1)S(1)} %get-tuple-element.20.low_ref, bf16[1024,512]{1,0:T(8,128)(2,1)} %skin_hbm.3, bf16[1024,512]{1,0:T(8,128)(2,1)} %skout_hbm.3), custom_call_target="tpu_custom_call" | custom-call | flops 10000000 | bytes 2228224 | tf_op jit(solution)/shard_map/prepare/pallas_call | solution.py:31
  8.4 10.9 %all-to-all-start = ((bf16[16,64,128]{2,1,0:T(8,128)(2,1)}), bf16[16,64,128]{2,1,0:T(8,128)(2,1)S(1)}, u32[]{:S(2)}, u32[]{:S(2)}) async-start(bf16[16,64,128]{2,1,0:T(8,128)(2,1)} %prepare.1), calls=%async_computation | async-start | bytes 524288 | tf_op jit(solution)/shard_map/all_to_all | solution.py:272
  19.4 1.9 %collective-permute-start.1 = (bf16[2,2,64,256]{3,2,1,0:T(8,128)(2,1)S(1)}, bf16[2,2,64,256]{3,2,1,0:T(8,128)(2,1)S(1)}, u32[]{:S(2)}, u32[]{:S(2)}) collective-permute-start(bf16[2,2,64,256]{3,2,1,0:T(8,128)(2,1)S(1)} %pad_maximum_fusion.refs_0_), channel_id=1, source_target_pairs={{0,1},{1,2},{2,3},{3,4},{4,5},{5,6},{6,7},{7,0},{8,9},{9,10},{10,1... | collective-permute-start | bytes 393224 | tf_op jit(solution)/shard_map/ppermute | solution.py:280
  21.3 1.4 collective-permute-start.2
  22.7 7.4 %collective-permute-done.1.refs_1_ = bf16[2,2,64,256]{3,2,1,0:T(8,128)(2,1)S(1)} collective-permute-done((bf16[2,2,64,256]{3,2,1,0:T(8,128)(2,1)S(1)}, bf16[2,2,64,256]{3,2,1,0:T(8,128)(2,1)S(1)}, u32[]{:S(2)}, u32[]{:S(2)}) %collective-permute-start.1) | collective-permute-done | bytes 131104 | tf_op jit(solution)/shard_map/ppermute | solution.py:280
  31.4 5.8 %adjoint_terms.1 = (bf16[16,32,128]{2,1,0:T(8,128)(2,1)S(1)}, bf16[8,64,1024]{2,1,0:T(8,128)(2,1)}, f32[8,64,1024]{2,1,0:T(8,128)S(1)}) custom-call(bf16[16,64,128]{2,1,0:T(8,128)(2,1)S(1)} %all-to-all-done.msg_ref, f32[1,15,64,1024]{3,2,1,0:T(8,128)} %trans_hbm.3), custom_call_target="tpu_custom_call" | custom-call | flops 10000000 | bytes 4194304 | tf_op jit(solution)/shard_map/adjoint_terms/pallas_call | solution.py:31
  37.8 6.5 %all-to-all-start.1 = ((bf16[16,32,128]{2,1,0:T(8,128)(2,1)}), bf16[16,32,128]{2,1,0:T(8,128)(2,1)S(1)}, u32[]{:S(2)}, u32[]{:S(2)}) async-start(bf16[16,32,128]{2,1,0:T(8,128)(2,1)} %copy-done.11), calls=%async_computation.1 | async-start | bytes 262144 | tf_op jit(solution)/shard_map/all_to_all | solution.py:272
  44.3 1.9 %collective-permute-start.4 = (bf16[2,2,64,256]{3,2,1,0:T(8,128)(2,1)}, bf16[2,2,64,256]{3,2,1,0:T(8,128)(2,1)S(1)}, u32[]{:S(2)}, u32[]{:S(2)}) collective-permute-start(bf16[2,2,64,256]{3,2,1,0:T(8,128)(2,1)} %copy-done.2), channel_id=1, source_target_pairs={{0,1},{1,2},{2,3},{3,4},{4,5},{5,6},{6,7},{7,0},{8,9},{9,10},{10,1... | collective-permute-start | bytes 393224 | tf_op jit(solution)/shard_map/ppermute | solution.py:280
  46.2 1.4 collective-permute-start.5
  47.6 6.4 %collective-permute-done.4.refs_2_ = bf16[2,2,64,256]{3,2,1,0:T(8,128)(2,1)S(1)} collective-permute-done((bf16[2,2,64,256]{3,2,1,0:T(8,128)(2,1)}, bf16[2,2,64,256]{3,2,1,0:T(8,128)(2,1)S(1)}, u32[]{:S(2)}, u32[]{:S(2)}) %collective-permute-start.4) | collective-permute-done | bytes 131104 | tf_op jit(solution)/shard_map/ppermute | solution.py:280
  56.4 5.1 %all-to-all-start.2 = ((bf16[8,2,64,1024]{3,2,1,0:T(8,128)(2,1)}), bf16[8,2,64,1024]{3,2,1,0:T(8,128)(2,1)S(1)}, u32[]{:S(2)}, u32[]{:S(2)}) async-start(bf16[8,2,64,1024]{3,2,1,0:T(8,128)(2,1)} %copy-done), calls=%async_computation.2 | async-start | bytes 4194304 | tf_op jit(solution)/shard_map/all_to_all | solution.py:272
  61.4 1.5 %collective-permute-start.6 = (bf16[2,2,64,256]{3,2,1,0:T(8,128)(2,1)S(1)}, bf16[2,2,64,256]{3,2,1,0:T(8,128)(2,1)S(1)}, u32[]{:S(2)}, u32[]{:S(2)}) collective-permute-start(bf16[2,2,64,256]{3,2,1,0:T(8,128)(2,1)S(1)} %copy-done.5), channel_id=1, source_target_pairs={{0,1},{1,2},{2,3},{3,4},{4,5},{5,6},{6,7},{7,0},{8,9},{9,10},{10,1... | collective-permute-start | bytes 393224 | tf_op jit(solution)/shard_map/ppermute | solution.py:280
  63.0 1.7 %collective-permute-start.8 = (bf16[2,2,64,256]{3,2,1,0:T(8,128)(2,1)}, bf16[2,2,64,256]{3,2,1,0:T(8,128)(2,1)S(1)}, u32[]{:S(2)}, u32[]{:S(2)}) collective-permute-start(bf16[2,2,64,256]{3,2,1,0:T(8,128)(2,1)} %collective-permute-done.5.refs_6_), channel_id=1, source_target_pairs={{0,7},{1,0},{2,1},{3,2},{4,3},{5,4},{6,5},{7,6},{8,15},{9,8},{10,9... | collective-permute-start | bytes 393224 | tf_op jit(solution)/shard_map/ppermute | solution.py:280
  64.7 2.9 %collective-permute-done.6.refs_3_ = bf16[2,2,64,256]{3,2,1,0:T(8,128)(2,1)S(1)} collective-permute-done((bf16[2,2,64,256]{3,2,1,0:T(8,128)(2,1)S(1)}, bf16[2,2,64,256]{3,2,1,0:T(8,128)(2,1)S(1)}, u32[]{:S(2)}, u32[]{:S(2)}) %collective-permute-start.6) | collective-permute-done | bytes 131104 | tf_op jit(solution)/shard_map/ppermute | solution.py:280
  68.6 5.2 %collective-permute-done.7.refs_4_ = bf16[2,2,64,256]{3,2,1,0:T(8,128)(2,1)S(1)} collective-permute-done((bf16[2,2,64,256]{3,2,1,0:T(8,128)(2,1)S(1)}, bf16[2,2,64,256]{3,2,1,0:T(8,128)(2,1)S(1)}, u32[]{:S(2)}, u32[]{:S(2)}) %collective-permute-start.7) | collective-permute-done | bytes 131104 | tf_op jit(solution)/shard_map/ppermute | solution.py:280
  75.6 5.7 %near.1 = (f32[64,512]{1,0:T(8,128)S(1)}, bf16[16,288,128]{2,1,0:T(8,128)(2,1)S(1)}) custom-call(s32[1]{0:T(128)S(6)} %copy.13.count_ref, s32[32]{0:T(128)S(1)} %copy-done.12, s32[32]{0:T(128)S(1)} %copy-done.13, bf16[2,64,256]{2,1,0:T(8,128)(2,1)S(1)} %get-tuple-element.20.low_ref, bf16[32,256,256]{2,1,0:T(8,128)(2,1)} %tiles_hbm.1, ...), custom_call_target="tpu_custom_call" | custom-call | flops 10000000 | bytes 5308676 | tf_op jit(solution)/shard_map/near/pallas_call | solution.py:31
  82.0 3.8 %all-to-all-done.2.came_ref = bf16[8,2,64,1024]{3,2,1,0:T(8,128)(2,1)S(1)} async-done(((bf16[8,2,64,1024]{3,2,1,0:T(8,128)(2,1)}), bf16[8,2,64,1024]{3,2,1,0:T(8,128)(2,1)S(1)}, u32[]{:S(2)}, u32[]{:S(2)}) %all-to-all-start.2) | async-done | bytes 2097184 | tf_op jit(solution)/shard_map/all_to_all | solution.py:272
  88.1 8.0 %all-to-all-start.3 = ((bf16[16,288,128]{2,1,0:T(8,128)(2,1)}), bf16[16,288,128]{2,1,0:T(8,128)(2,1)S(1)}, u32[]{:S(2)}, u32[]{:S(2)}) async-start(bf16[16,288,128]{2,1,0:T(8,128)(2,1)} %copy-done.1), calls=%async_computation.3 | async-start | bytes 2359296 | tf_op jit(solution)/shard_map/all_to_all | solution.py:272
  96.4 2.9 %collective-permute-done.9.other_ref = bf16[8,64,1024]{2,1,0:T(8,128)(2,1)S(1)} collective-permute-done((bf16[8,64,1024]{2,1,0:T(8,128)(2,1)}, bf16[8,64,1024]{2,1,0:T(8,128)(2,1)S(1)}, u32[]{:S(2)}, u32[]{:S(2)}) %collective-permute-start.9) | collective-permute-done | bytes 1048608 | tf_op jit(solution)/shard_map/ppermute | solution.py:268
  99.2 5.5 %forward.1.pot_ref = bf16[32,128]{1,0:T(8,128)(2,1)S(1)} custom-call(bf16[8,64,1024]{2,1,0:T(8,128)(2,1)S(1)} %collective-permute-done.9.other_ref, bf16[8,2,64,1024]{3,2,1,0:T(8,128)(2,1)S(1)} %all-to-all-done.2.came_ref, f32[1,15,64,1024]{3,2,1,0:T(8,128)} %trans_hbm.3), custom_call_target="tpu_custom_call" | custom-call | flops 10000000 | bytes 7077888 | tf_op jit(solution)/shard_map/forward/pallas_call | solution.py:31
  104.7 20.9 %all-to-all-done.3.near_ref = bf16[16,288,128]{2,1,0:T(8,128)(2,1)S(1)} async-done(((bf16[16,288,128]{2,1,0:T(8,128)(2,1)}), bf16[16,288,128]{2,1,0:T(8,128)(2,1)S(1)}, u32[]{:S(2)}, u32[]{:S(2)}) %all-to-all-start.3) | async-done | bytes 1179680 | tf_op jit(solution)/shard_map/all_to_all | solution.py:272
  125.7 17.0 %all_to_all.25.low_ref = bf16[16,64,128]{2,1,0:T(8,128)(2,1)S(1)} all-to-all(bf16[16,64,128]{2,1,0:T(8,128)(2,1)S(1)} %low_shares.1), channel_id=1, replica_groups=mesh['xlo'=2,'y'=4,'core'=2,'xhi'=2,'z'=8] {'xhi','z'}, dimensions={0} | all-to-all | bytes 524288 | tf_op jit(solution)/shard_map/all_to_all | solution.py:272
  142.7 2.6 %finish.1 = (f32[64,512]{1,0:T(8,128)}, f32[64,512]{1,0:T(8,128)}) custom-call(bf16[16,64,128]{2,1,0:T(8,128)(2,1)S(1)} %all_to_all.25.low_ref, bf16[16,288,128]{2,1,0:T(8,128)(2,1)S(1)} %all-to-all-done.3.near_ref, f32[64,512]{1,0:T(8,128)S(1)} %copy-done.8, bf16[1024,512]{1,0:T(8,128)(2,1)} %skin_hbm.3, bf16[1024,512]{1,0:T(8,128)(2,1)} %skout_hbm.3), custom_call_target="tpu_custom_call" | custom-call | flops 10000000 | bytes 3670016 | tf_op jit(solution)/shard_map/finish/pallas_call | solution.py:31
  (45 shorter events, 11.3 us)
Async XLA Ops:
  0.6 0.9 copy-start.9
  2.5 5.9 %collective-permute-start = (bf16[2,64,256]{2,1,0:T(8,128)(2,1)S(1)}, bf16[2,64,256]{2,1,0:T(8,128)(2,1)S(1)}, u32[]{:S(2)}, u32[]{:S(2)}) collective-permute-start(bf16[2,64,256]{2,1,0:T(8,128)(2,1)S(1)} %get-tuple-element.19.drive_ref), channel_id=1, source_target_pairs={{0,8},{8,0},{1,9},{9,1},{2,10},{10,2},{3,11},{11,3},{4,12},{12,4},... | collective-permute-start | bytes 196616 | tf_op jit(solution)/shard_map/ppermute | solution.py:293
  8.4 22.9 %all-to-all-start = ((bf16[16,64,128]{2,1,0:T(8,128)(2,1)}), bf16[16,64,128]{2,1,0:T(8,128)(2,1)S(1)}, u32[]{:S(2)}, u32[]{:S(2)}) async-start(bf16[16,64,128]{2,1,0:T(8,128)(2,1)} %prepare.1), calls=%async_computation | async-start | bytes 524288 | tf_op jit(solution)/shard_map/all_to_all | solution.py:272
  19.4 10.7 %collective-permute-start.1 = (bf16[2,2,64,256]{3,2,1,0:T(8,128)(2,1)S(1)}, bf16[2,2,64,256]{3,2,1,0:T(8,128)(2,1)S(1)}, u32[]{:S(2)}, u32[]{:S(2)}) collective-permute-start(bf16[2,2,64,256]{3,2,1,0:T(8,128)(2,1)S(1)} %pad_maximum_fusion.refs_0_), channel_id=1, source_target_pairs={{0,1},{1,2},{2,3},{3,4},{4,5},{5,6},{6,7},{7,0},{8,9},{9,10},{10,1... | collective-permute-start | bytes 393224 | tf_op jit(solution)/shard_map/ppermute | solution.py:280
  21.3 9.5 %collective-permute-start.2 = (bf16[2,2,64,256]{3,2,1,0:T(8,128)(2,1)S(1)}, bf16[2,2,64,256]{3,2,1,0:T(8,128)(2,1)}, u32[]{:S(2)}, u32[]{:S(2)}) collective-permute-start(bf16[2,2,64,256]{3,2,1,0:T(8,128)(2,1)S(1)} %pad_maximum_fusion.refs_0_), channel_id=1, source_target_pairs={{0,7},{1,0},{2,1},{3,2},{4,3},{5,4},{6,5},{7,6},{8,15},{9,8},{10,9... | collective-permute-start | bytes 393224 | tf_op jit(solution)/shard_map/ppermute | solution.py:280
  37.8 16.9 %collective-permute-start.3 = (bf16[8,64,1024]{2,1,0:T(8,128)(2,1)}, bf16[8,64,1024]{2,1,0:T(8,128)(2,1)S(1)}, u32[]{:S(2)}, u32[]{:S(2)}) collective-permute-start(bf16[8,64,1024]{2,1,0:T(8,128)(2,1)} %get-tuple-element.25), channel_id=1, source_target_pairs={{0,16},{16,0},{1,17},{17,1},{2,18},{18,2},{3,19},{19,3},{4,20},{20... | collective-permute-start | bytes 3145736 | tf_op jit(solution)/shard_map/ppermute | solution.py:268
  37.8 16.9 %all-to-all-start.1 = ((bf16[16,32,128]{2,1,0:T(8,128)(2,1)}), bf16[16,32,128]{2,1,0:T(8,128)(2,1)S(1)}, u32[]{:S(2)}, u32[]{:S(2)}) async-start(bf16[16,32,128]{2,1,0:T(8,128)(2,1)} %copy-done.11), calls=%async_computation.1 | async-start | bytes 262144 | tf_op jit(solution)/shard_map/all_to_all | solution.py:272
  44.3 9.8 %collective-permute-start.4 = (bf16[2,2,64,256]{3,2,1,0:T(8,128)(2,1)}, bf16[2,2,64,256]{3,2,1,0:T(8,128)(2,1)S(1)}, u32[]{:S(2)}, u32[]{:S(2)}) collective-permute-start(bf16[2,2,64,256]{3,2,1,0:T(8,128)(2,1)} %copy-done.2), channel_id=1, source_target_pairs={{0,1},{1,2},{2,3},{3,4},{4,5},{5,6},{6,7},{7,0},{8,9},{9,10},{10,1... | collective-permute-start | bytes 393224 | tf_op jit(solution)/shard_map/ppermute | solution.py:280
  46.2 8.5 %collective-permute-start.5 = (bf16[2,2,64,256]{3,2,1,0:T(8,128)(2,1)}, bf16[2,2,64,256]{3,2,1,0:T(8,128)(2,1)}, u32[]{:S(2)}, u32[]{:S(2)}) collective-permute-start(bf16[2,2,64,256]{3,2,1,0:T(8,128)(2,1)} %collective-permute-done.2.refs_7_), channel_id=1, source_target_pairs={{0,7},{1,0},{2,1},{3,2},{4,3},{5,4},{6,5},{7,6},{8,15},{9,8},{10,9... | collective-permute-start | bytes 393224 | tf_op jit(solution)/shard_map/ppermute | solution.py:280
  55.0 1.3 copy-start
  56.3 5.1 %copy-start.5 = (bf16[2,2,64,256]{3,2,1,0:T(8,128)(2,1)S(1)}, bf16[2,2,64,256]{3,2,1,0:T(8,128)(2,1)}, u32[]{:S(2)}) copy-start(bf16[2,2,64,256]{3,2,1,0:T(8,128)(2,1)} %copy-done.4) | copy-start | bytes 393220
  56.3 17.4 %copy-start.12 = (s32[32]{0:T(128)S(1)}, s32[32]{0:T(128)}, u32[]{:S(2)}) copy-start(s32[32]{0:T(128)} %rows_ref.1) | copy-start | bytes 388
  56.3 17.5 %copy-start.13 = (s32[32]{0:T(128)S(1)}, s32[32]{0:T(128)}, u32[]{:S(2)}) copy-start(s32[32]{0:T(128)} %cols_ref.1) | copy-start | bytes 388
  56.4 29.5 %all-to-all-start.2 = ((bf16[8,2,64,1024]{3,2,1,0:T(8,128)(2,1)}), bf16[8,2,64,1024]{3,2,1,0:T(8,128)(2,1)S(1)}, u32[]{:S(2)}, u32[]{:S(2)}) async-start(bf16[8,2,64,1024]{3,2,1,0:T(8,128)(2,1)} %copy-done), calls=%async_computation.2 | async-start | bytes 4194304 | tf_op jit(solution)/shard_map/all_to_all | solution.py:272
  61.4 6.2 %collective-permute-start.6 = (bf16[2,2,64,256]{3,2,1,0:T(8,128)(2,1)S(1)}, bf16[2,2,64,256]{3,2,1,0:T(8,128)(2,1)S(1)}, u32[]{:S(2)}, u32[]{:S(2)}) collective-permute-start(bf16[2,2,64,256]{3,2,1,0:T(8,128)(2,1)S(1)} %copy-done.5), channel_id=1, source_target_pairs={{0,1},{1,2},{2,3},{3,4},{4,5},{5,6},{6,7},{7,0},{8,9},{9,10},{10,1... | collective-permute-start | bytes 393224 | tf_op jit(solution)/shard_map/ppermute | solution.py:280
  63.0 5.6 %collective-permute-start.8 = (bf16[2,2,64,256]{3,2,1,0:T(8,128)(2,1)}, bf16[2,2,64,256]{3,2,1,0:T(8,128)(2,1)S(1)}, u32[]{:S(2)}, u32[]{:S(2)}) collective-permute-start(bf16[2,2,64,256]{3,2,1,0:T(8,128)(2,1)} %collective-permute-done.5.refs_6_), channel_id=1, source_target_pairs={{0,7},{1,0},{2,1},{3,2},{4,3},{5,4},{6,5},{7,6},{8,15},{9,8},{10,9... | collective-permute-start | bytes 393224 | tf_op jit(solution)/shard_map/ppermute | solution.py:280
  67.6 6.2 %collective-permute-start.7 = (bf16[2,2,64,256]{3,2,1,0:T(8,128)(2,1)S(1)}, bf16[2,2,64,256]{3,2,1,0:T(8,128)(2,1)S(1)}, u32[]{:S(2)}, u32[]{:S(2)}) collective-permute-start(bf16[2,2,64,256]{3,2,1,0:T(8,128)(2,1)S(1)} %collective-permute-done.6.refs_3_), channel_id=1, source_target_pairs={{0,1},{1,2},{2,3},{3,4},{4,5},{5,6},{6,7},{7,0},{8,9},{9,10},{10,1... | collective-permute-start | bytes 393224 | tf_op jit(solution)/shard_map/ppermute | solution.py:280
  73.8 0.9 copy-start.3
  74.7 0.9 copy-start.6
  86.1 1.0 copy-start.1
  87.1 1.0 copy-start.14
  88.1 37.6 %all-to-all-start.3 = ((bf16[16,288,128]{2,1,0:T(8,128)(2,1)}), bf16[16,288,128]{2,1,0:T(8,128)(2,1)S(1)}, u32[]{:S(2)}, u32[]{:S(2)}) async-start(bf16[16,288,128]{2,1,0:T(8,128)(2,1)} %copy-done.1), calls=%async_computation.3 | async-start | bytes 2359296 | tf_op jit(solution)/shard_map/all_to_all | solution.py:272
  96.1 46.6 %copy-start.8 = (f32[64,512]{1,0:T(8,128)S(1)}, f32[64,512]{1,0:T(8,128)}, u32[]{:S(2)}) copy-start(f32[64,512]{1,0:T(8,128)} %copy-done.7) | copy-start | bytes 393220
  96.1 3.1 %collective-permute-start.9 = (bf16[8,64,1024]{2,1,0:T(8,128)(2,1)}, bf16[8,64,1024]{2,1,0:T(8,128)(2,1)S(1)}, u32[]{:S(2)}, u32[]{:S(2)}) collective-permute-start(bf16[8,64,1024]{2,1,0:T(8,128)(2,1)} %copy-done.14), channel_id=1, source_target_pairs={{0,16},{16,0},{1,17},{17,1},{2,18},{18,2},{3,19},{19,3},{4,20},{20... | collective-permute-start | bytes 3145736 | tf_op jit(solution)/shard_map/ppermute | solution.py:268
  (5 other events, 3.5 us)

commit v3 on v2

v3 whole, which is shorter than its diff:
```python
import jax
import jax.numpy as jnp
from jax import lax
from jax.experimental import pallas as pl
from jax.experimental.pallas import tpu as pltpu
from jax.sharding import Mesh
from jax.sharding import PartitionSpec as P

BLK = ("xlo", "y", "core")
ROWS = ("xhi", "z")
FACE = ("xlo", "y")
bf16 = jnp.bfloat16
f32 = jnp.float32
LAST = (((1,), (1,)), ((), ()))


def vmem():
    return pl.BlockSpec(memory_space=pltpu.VMEM)


def smem():
    return pl.BlockSpec(memory_space=pltpu.SMEM)


def hbm():
    return pl.BlockSpec(memory_space=pltpu.HBM)


def call(kernel, outs, args, specs=None, scratch=(), flops=10**7, name=None, room=8, alias=None):
    moved = sum(a.size * a.dtype.itemsize for a in args)
    return pl.pallas_call(
        kernel,
        out_shape=[jax.ShapeDtypeStruct(s, d) for s, d in outs],
        in_specs=specs or [vmem()] * len(args),
        out_specs=[vmem()] * len(outs),
        scratch_shapes=list(scratch),
        compiler_params=pltpu.CompilerParams(vmem_limit_bytes=room * 2**20),
        cost_estimate=pl.CostEstimate(flops=flops, bytes_accessed=moved, transcendentals=0),
        name=name,
        input_output_aliases=alias or {},
    )(*args)


def split(value):
    high = value.astype(bf16)
    return high, (value - high.astype(f32)).astype(bf16)


def dot(a, b):
    return jnp.dot(a, b, preferred_element_type=f32)


def dot_last(a, b):
    return lax.dot_general(a, b, LAST, preferred_element_type=f32)


def join_pieces(ref, first):
    rows = []
    for band in range(8):
        blocks = [
            ref[band * 2 + half, first + part * 8 : first + part * 8 + 8, :]
            for half in range(2)
            for part in range(4)
        ]
        rows.append(jnp.concatenate(blocks, axis=1))
    return jnp.concatenate(rows, axis=0)


def prepare(exc_hbm, loads_hbm, skin_hbm, skout_hbm, drive_ref, low_ref, msg_ref, exc, loads, skin, skout, sems):
    pairs = ((exc_hbm, exc), (skin_hbm, skin), (loads_hbm, loads), (skout_hbm, skout))
    copies = [pltpu.make_async_copy(src, dst, sems.at[i]) for i, (src, dst) in enumerate(pairs)]
    for copy in copies:
        copy.start()
    copies[0].wait()
    drive = exc[...].astype(bf16)
    for part in range(2):
        drive_ref[part] = drive[:, part * 256 : part * 256 + 256]
    copies[1].wait()
    charges = dot_last(drive, skin[...])
    for piece in range(16):
        row = piece // 2 * 8
        for part in range(4):
            col = piece % 2 * 512 + part * 128
            msg_ref[piece, part * 8 : part * 8 + 8, :] = charges[row : row + 8, col : col + 128].astype(bf16)
    copies[2].wait()
    low = loads[...].astype(bf16)
    for part in range(2):
        low_ref[part] = low[:, part * 256 : part * 256 + 256]
    twice = jnp.concatenate([low, low], axis=0)
    copies[3].wait()
    gradient = dot_last(skout[...], twice)
    left = lax.broadcasted_iota(jnp.int32, (32, 128), 1) < 64
    for piece in range(16):
        k = piece * 64
        high, rest = split(jnp.where(left, gradient[k : k + 32], gradient[k + 32 : k + 64]))
        msg_ref[piece, 32:64, :] = high
        msg_ref[piece, 64:96, :] = rest


def split_translation(trans_hbm, high_ref, low_ref, blocks, sems):
    copies = [pltpu.make_async_copy(trans_hbm.at[0, d], blocks.at[d], sems.at[d]) for d in range(15)]
    for copy in copies:
        copy.start()
    for d in range(15):
        copies[d].wait()
        high, low = split(blocks[d])
        high_ref[d] = high
        low_ref[d] = low


def lags():
    cluster = lax.axis_index(BLK)
    core = lax.axis_index("core")
    return [
        lax.rem(cluster - (2 * q + parity) + 16, 16) for parity in (1 - core, core) for q in range(8)
    ]


def adjoint_terms(msg_ref, high_ref, low_ref, copies_ref, send_ref, keep_ref):
    lag = lags()
    total = jnp.sum(msg_ref[:, 0:32, :].astype(f32), axis=0)
    share = total.astype(bf16)
    for piece in range(16):
        copies_ref[piece] = share
    packed = jnp.sum(msg_ref[:, 32:64, :].astype(f32) + msg_ref[:, 64:96, :].astype(f32), axis=0)
    gradient = jnp.concatenate([packed, pltpu.roll(packed, 64, 1)], axis=0)
    high, low = split(gradient.T[:64])
    both = jnp.concatenate([high, low], axis=0)
    for index in range(16):
        block = jnp.maximum(lag[index] - 1, 0)
        pair = dot(both, high_ref[block])
        value = pair[:64] + pair[64:] + dot(high, low_ref[block])
        if index < 8:
            send_ref[index] = value
        else:
            keep_ref[index - 8] = jnp.where(lag[index] == 0, 0.0, value)


def pack(keep_ref, came_ref, pieces_ref, out_ref):
    charges = join_pieces(pieces_ref, 0)
    for q in range(8):
        out_ref[q, 0] = (keep_ref[q] + came_ref[q]).astype(bf16)
        out_ref[q, 1] = charges


def unpack(came_ref, keep_ref, mate_ref, msg_ref, charges_ref):
    total = came_ref[0, 0].astype(f32)
    charges_ref[0] = came_ref[0, 1]
    for q in range(1, 8):
        total = total + came_ref[q, 0].astype(f32)
        charges_ref[q] = came_ref[q, 1]
    for piece in range(8):
        msg_ref[piece, 0:256, :] = (keep_ref[piece] + mate_ref[piece].astype(f32)).astype(bf16)
        for part in range(8):
            msg_ref[piece, 256 + part * 8 : 264 + part * 8, :] = total[
                piece * 8 : piece * 8 + 8, part * 128 : part * 128 + 128
            ].astype(bf16)


def forward(other_ref, came_ref, high_ref, low_ref, pot_ref):
    lag = lags()
    total = jnp.zeros((64, 64), f32)
    for index in range(16):
        block = jnp.maximum(lag[index] - 1, 0)
        both = jnp.concatenate([high_ref[block], low_ref[block]], axis=0)
        charges = other_ref[index] if index < 8 else came_ref[index - 8, 1]
        pair = dot_last(both, charges)
        total = total + jnp.where(lag[index] == 0, 0.0, pair[:64] + pair[64:])
    pot_ref[...] = jnp.concatenate([total[:32], total[32:]], axis=1).astype(bf16)


def near(count_ref, rows_ref, cols_ref, low_ref, tiles_hbm, *refs):
    pieces, refs = refs[:8], refs[8:]
    ahead_ref, send_ref, keep_ref, acc, behind, drives, tiles_ref, tile_sems, piece_sems = refs

    def tile_copy(index):
        span = pl.ds(index * 4, 4)
        return pltpu.make_async_copy(tiles_hbm.at[span], tiles_ref.at[span], tile_sems.at[index])

    arriving = [
        pltpu.make_async_copy(pieces[index], drives.at[index], piece_sems.at[index]) for index in range(8)
    ]
    for copy in arriving:
        copy.start()
    for index in range(8):
        tile_copy(index).start()
    acc[...] = jnp.zeros_like(acc)
    behind[...] = jnp.zeros_like(behind)
    for copy in arriving:
        copy.wait()
    count = count_ref[0]
    my_z = lax.axis_index("z")
    my_half = lax.axis_index("xhi")
    group = 4

    def step(index, carry):
        tile_copy(index).wait()
        results = []
        for part in range(group):
            slot = index * group + part
            row = rows_ref[slot]
            col = cols_ref[slot]
            owner = col // 2
            hops = lax.rem(my_z - lax.rem(owner, 8) + 8, 8)
            side = lax.rem(owner // 8 + my_half, 2)
            tile = tiles_ref[slot]
            fwd = dot_last(drives[hops, side, lax.rem(col, 2)], tile)
            bwd = dot(low_ref[row], tile)
            results.append((slot < count, row, col, fwd, bwd))
        for live, row, col, fwd, bwd in results:
            acc[row] += jnp.where(live, fwd, 0.0)
            behind[col] += jnp.where(live, bwd, 0.0)
        return carry

    groups = (count + group - 1) // group
    lax.fori_loop(0, groups, step, 0)

    def drain(index, carry):
        tile_copy(index).wait()
        return carry

    lax.fori_loop(groups, 8, drain, 0)
    for part in range(2):
        ahead_ref[:, part * 256 : part * 256 + 256] = acc[part]
    for z in range(8):
        for part in range(4):
            rows = pl.ds(part * 64, 64)
            cols = pl.ds(part % 2 * 128, 128)
            send_ref[z, rows, :] = behind[(1 - my_half) * 16 + 2 * z + part // 2, :, cols].astype(bf16)
            keep_ref[z, rows, :] = behind[my_half * 16 + 2 * z + part // 2, :, cols]


def fold(msg_ref, out_ref):
    out_ref[...] = jnp.sum(msg_ref[:, 256:320, :].astype(f32), axis=0)


def low_shares(mine_ref, mate_ref, pot_ref, mate_pot_ref, out_ref):
    adjoint = (mine_ref[...] + mate_ref[...]).astype(bf16)
    upper = lax.axis_index("xhi") == 1
    pot = pot_ref[...].astype(f32)
    mate_pot = mate_pot_ref[...].astype(f32)
    first = jnp.where(upper, mate_pot, pot).astype(bf16)
    second = jnp.where(upper, pot, mate_pot).astype(bf16)
    for piece in range(8):
        out_ref[piece, 0:64, :] = adjoint
        out_ref[piece, 64:96, :] = first
        out_ref[piece, 96:128, :] = second


def finish(low_ref, near_ref, ahead_ref, skin_ref, skout_ref, resp_ref, sens_ref):
    adjoint = jnp.concatenate(
        [
            jnp.concatenate([low_ref[z, part * 8 : part * 8 + 8, :] for part in range(8)], axis=1)
            for z in range(8)
        ],
        axis=0,
    )
    packed = jnp.concatenate([low_ref[r % 8, 64 + r // 8 * 32 : 96 + r // 8 * 32, :] for r in range(16)], axis=0)
    packed = packed.astype(f32).T.astype(bf16)
    upper = jnp.concatenate([skout_ref[r * 64 : r * 64 + 32, :] for r in range(16)], axis=0)
    lower = jnp.concatenate([skout_ref[r * 64 + 32 : r * 64 + 64, :] for r in range(16)], axis=0)
    resp_ref[...] = ahead_ref[...] + dot(packed[:64], upper) + dot(packed[64:], lower)
    far = dot(adjoint, skin_ref[...])
    for part in range(4):
        value = near_ref[0, part * 64 : part * 64 + 64, :].astype(f32)
        for source in range(1, 8):
            value = value + near_ref[source, part * 64 : part * 64 + 64, :].astype(f32)
        sens_ref[:, part * 128 : part * 128 + 128] = far[:, part * 128 : part * 128 + 128] + value


def swap(value, axis):
    return lax.ppermute(value, axis, [(0, 1), (1, 0)])


def exchange(value, axes):
    return lax.all_to_all(value, axes, 0, 0, tiled=True)


def in_hbm(value):
    return pltpu.with_memory_space_constraint(value, pltpu.HBM)


def shift(value, step):
    return lax.ppermute(value, "z", [(i, (i + step) % 8) for i in range(8)])


def tie(*values):
    return lax.optimization_barrier(values)


def on_device(exc, loads, tiles, tile_rows, tile_cols, tile_count, skin, skout, trans):
    drive, low, msg = call(
        prepare,
        [((2, 64, 256), bf16), ((2, 64, 256), bf16), ((16, 96, 128), bf16)],
        [in_hbm(exc), in_hbm(loads), in_hbm(skin), in_hbm(skout)],
        specs=[hbm()] * 4,
        scratch=[pltpu.VMEM((64, 512), f32)] * 2
        + [pltpu.VMEM((1024, 512), bf16)] * 2
        + [pltpu.SemaphoreType.DMA((4,))],
        name="prepare",
    )
    here = jnp.stack([drive, swap(drive, "xhi")])
    up1, down1 = shift(here, 1), shift(here, -1)
    up2, down2 = shift(up1, 1), shift(down1, -1)
    high, rest = call(
        split_translation,
        [((15, 64, 1024), bf16)] * 2,
        [in_hbm(trans)],
        specs=[hbm()],
        scratch=[pltpu.VMEM((15, 64, 1024), f32), pltpu.SemaphoreType.DMA((15,))],
        name="split_translation",
        room=16,
    )
    msg, up2, down2, high, rest = tie(exchange(msg, ROWS), up2, down2, high, rest)
    copies, send, keep = call(
        adjoint_terms,
        [((16, 32, 128), bf16), ((8, 64, 1024), f32), ((8, 64, 1024), f32)],
        [msg, high, rest],
        name="adjoint_terms",
        room=12,
    )
    came = swap(send, "core")
    up3, down3 = shift(up2, 1), shift(down2, -1)
    up4 = shift(up3, 1)
    copies, up4, down3 = tie(exchange(copies, ROWS), up4, down3)
    (both,) = call(pack, [((8, 2, 64, 1024), bf16)], [keep, came, copies], name="pack")
    both = exchange(both, FACE)
    ahead, send, keep = call(
        near,
        [((64, 512), f32), ((8, 256, 128), bf16), ((8, 256, 128), f32)],
        [tile_count, tile_rows, tile_cols, low, in_hbm(tiles)]
        + [in_hbm(piece) for piece in (here, up1, up2, up3, up4, down3, down2, down1)],
        specs=[smem(), smem(), smem(), vmem()] + [hbm()] * 9,
        scratch=[
            pltpu.VMEM((2, 64, 256), f32),
            pltpu.VMEM((32, 64, 256), f32),
            pltpu.VMEM((8, 2, 2, 64, 256), bf16),
            pltpu.VMEM((32, 256, 256), bf16),
            pltpu.SemaphoreType.DMA((8,)),
            pltpu.SemaphoreType.DMA((8,)),
        ],
        name="near",
        room=16,
    )
    mate = swap(send, "xhi")
    behind, charges = call(
        unpack,
        [((8, 320, 128), bf16), ((8, 64, 1024), bf16)],
        [both, keep, mate],
        name="unpack",
    )
    others = swap(charges, "core")
    behind = exchange(behind, "z")
    (potential,) = call(
        forward,
        [((32, 128), bf16)],
        [others, both, high, rest],
        name="forward",
        room=12,
    )
    mate_pot = swap(potential, "xhi")
    behind, mate_pot = tie(behind, mate_pot)
    (mine,) = call(fold, [((64, 128), f32)], [behind], name="fold")
    (shares,) = call(
        low_shares,
        [((8, 128, 128), bf16)],
        [mine, swap(mine, "xhi"), potential, mate_pot],
        name="low_shares",
    )
    shares = exchange(shares, "z")
    return tuple(
        call(
            finish,
            [((64, 512), f32), ((64, 512), f32)],
            [shares, behind, ahead, skin, skout],
            name="finish",
        )
    )


def solution(mesh):
    fine = Mesh(mesh.devices.reshape(2, 4, 2, 2, 8), BLK + ROWS)
    every = BLK + ROWS
    return jax.shard_map(
        on_device,
        mesh=fine,
        in_specs=(
            P(None, every),
            P(None, every),
            P(every, None, None),
            P(every),
            P(every),
            P(every),
            P(None, every),
            P(None, every),
            P(BLK, None, ROWS, None),
        ),
        out_specs=(P(None, every), P(None, every)),
        check_vma=False,
    )
```

time: 147 us -> 156 us (1.061)
  waiting for transfers between devices: 50.3 us -> 63.4 us
  Pallas kernels: 22.9 us -> 15.1 us
  local copies, waits for them, and re-layouts: 9.57 us -> 16 us
  blocking collectives: 17 us -> 12.9 us
  starting transfers between devices: 44.1 us -> 45.8 us
    ppermute x3 -> x6, waiting for transfers between devices: 2.86 us -> 44.9 us  [swap(): return lax.ppermute(value, axis, [(0, 1), (1, 0)])]
    all_to_all x4, waiting for transfers between devices: 25.4 us -> 8.73 us  [exchange(): return lax.all_to_all(value, axes, 0, 0, tiled=True)]
    ppermute x7, waiting for transfers between devices: 22 us -> 9.73 us  [shift(): return lax.ppermute(value, 'z', [(i, (i + step) % 8) for i in range(8)])]
    pallas_call x9 -> x10, Pallas kernels: 22.9 us -> 15.1 us  [call(): pl.pallas_call(kernel, out_shape=[jax.ShapeDtypeStruct(s, d) for s, d in...]
    unnamed x30 -> x48, local copies, waits for them, and re-layouts: 9.57 us -> 16 us
    all_to_all x1, blocking collectives: 17 us -> 12.9 us  [exchange(): return lax.all_to_all(value, axes, 0, 0, tiled=True)]
    ppermute x3 -> x6, starting transfers between devices: 3.39 us -> 7.2 us  [swap(): return lax.ppermute(value, axis, [(0, 1), (1, 0)])]
    all_to_all x4, starting transfers between devices: 30.5 us -> 28.8 us  [exchange(): return lax.all_to_all(value, axes, 0, 0, tiled=True)]
  transfers between devices with their start and end apart: 14 -> 17, of which waited for: 8 -> 9; matrix products, arithmetic and copies ran while one was open for 0% -> 0% of each run, Pallas kernels for 10% -> 5%
where the time goes in v3:
time: 156 us; the launch traced here: 155 us
  waiting for transfers between devices  63.4 us (41%)
  starting transfers between devices  45.8 us (29%)
  local copies, waits for them, and re-layouts  16 us (10%)
  Pallas kernels  15.1 us (10%)
  blocking collectives  12.9 us (8%)
    ppermute x6, waiting for transfers between devices, swap(): return lax.ppermute(value, axis, [(0, 1), (1, 0)])  44.9 us
    all_to_all x4, starting transfers between devices, exchange(): return lax.all_to_all(value, axes, 0, 0, tiled=True)  28.8 us
    unnamed x48, local copies, waits for them, and re-layouts  16 us
    pallas_call x10, Pallas kernels, call(): pl.pallas_call(kernel, out_shape=[jax.ShapeDtypeStruct(s, d) for s, d in...  15.1 us
    all_to_all x1, blocking collectives, exchange(): return lax.all_to_all(value, axes, 0, 0, tiled=True)  12.9 us
    ppermute x7, starting transfers between devices, shift(): return lax.ppermute(value, 'z', [(i, (i + step) % 8) for i in range(8)])  9.76 us
    ppermute x7, waiting for transfers between devices, shift(): return lax.ppermute(value, 'z', [(i, (i + step) % 8) for i in range(8)])  9.73 us
    all_to_all x4, waiting for transfers between devices, exchange(): return lax.all_to_all(value, axes, 0, 0, tiled=True)  8.73 us
  transfers between devices with their start and end apart: 17, of which 9 were waited for; matrix products, arithmetic and copies ran while one was open for 0% of the time, Pallas kernels for 5%

profile of v3, /device:TPU:8, one launch (start us, length us, event | category | flops | bytes accessed | tf_op | source)
XLA Modules:
  0.0 154.6 jit_solution(12479373166776975270)
XLA Ops:
  0.6 3.0 %prepare.1 = (bf16[2,64,256]{2,1,0:T(8,128)(2,1)S(1)}, bf16[2,64,256]{2,1,0:T(8,128)(2,1)S(1)}, bf16[16,96,128]{2,1,0:T(8,128)(2,1)}) custom-call(f32[64,512]{1,0:T(8,128)} %exc_hbm.1, f32[64,512]{1,0:T(8,128)} %loads_hbm.1, bf16[1024,512]{1,0:T(8,128)(2,1)} %skin_ref.1, bf16[1024,512]{1,0:T(8,128)(2,1)} %skout_ref.1), custom_call_target="tpu_custom_call" | custom-call | flops 10000000 | bytes 2359296 | tf_op jit(solution)/shard_map/prepare/pallas_call | solution.py:31
  3.6 11.0 %all-to-all-start = ((bf16[16,96,128]{2,1,0:T(8,128)(2,1)}), bf16[16,96,128]{2,1,0:T(8,128)(2,1)S(1)}, u32[]{:S(2)}, u32[]{:S(2)}) async-start(bf16[16,96,128]{2,1,0:T(8,128)(2,1)} %get-tuple-element.25), calls=%async_computation | async-start | bytes 786432 | tf_op jit(solution)/shard_map/all_to_all | solution.py:276
  14.6 3.4 %collective-permute-start = (bf16[2,64,256]{2,1,0:T(8,128)(2,1)S(1)}, bf16[2,64,256]{2,1,0:T(8,128)(2,1)S(1)}, u32[]{:S(2)}, u32[]{:S(2)}) collective-permute-start(bf16[2,64,256]{2,1,0:T(8,128)(2,1)S(1)} %get-tuple-element.26), channel_id=1, source_target_pairs={{0,8},{8,0},{1,9},{9,1},{2,10},{10,2},{3,11},{11,3},{4,12},{12,4},... | collective-permute-start | bytes 196616 | tf_op jit(solution)/shard_map/ppermute | solution.py:272
  18.1 3.2 %collective-permute-done = bf16[2,64,256]{2,1,0:T(8,128)(2,1)S(1)} collective-permute-done((bf16[2,64,256]{2,1,0:T(8,128)(2,1)S(1)}, bf16[2,64,256]{2,1,0:T(8,128)(2,1)S(1)}, u32[]{:S(2)}, u32[]{:S(2)}) %collective-permute-start) | collective-permute-done | bytes 65568 | tf_op jit(solution)/shard_map/ppermute | solution.py:272
  23.0 1.7 %collective-permute-start.3 = (bf16[2,2,64,256]{3,2,1,0:T(8,128)(2,1)S(1)}, bf16[2,2,64,256]{3,2,1,0:T(8,128)(2,1)S(1)}, u32[]{:S(2)}, u32[]{:S(2)}) collective-permute-start(bf16[2,2,64,256]{3,2,1,0:T(8,128)(2,1)S(1)} %pad_maximum_fusion.refs_0_), channel_id=1, source_target_pairs={{0,7},{1,0},{2,1},{3,2},{4,3},{5,4},{6,5},{7,6},{8,15},{9,8},{10,9... | collective-permute-start | bytes 393224 | tf_op jit(solution)/shard_map/ppermute | solution.py:284
  24.7 4.7 %collective-permute-done.1.refs_1_ = bf16[2,2,64,256]{3,2,1,0:T(8,128)(2,1)S(1)} collective-permute-done((bf16[2,2,64,256]{3,2,1,0:T(8,128)(2,1)S(1)}, bf16[2,2,64,256]{3,2,1,0:T(8,128)(2,1)S(1)}, u32[]{:S(2)}, u32[]{:S(2)}) %collective-permute-start.1) | collective-permute-done | bytes 131104 | tf_op jit(solution)/shard_map/ppermute | solution.py:284
  29.4 3.2 %collective-permute-start.4 = (bf16[2,2,64,256]{3,2,1,0:T(8,128)(2,1)S(1)}, bf16[2,2,64,256]{3,2,1,0:T(8,128)(2,1)S(1)}, u32[]{:S(2)}, u32[]{:S(2)}) collective-permute-start(bf16[2,2,64,256]{3,2,1,0:T(8,128)(2,1)S(1)} %collective-permute-done.3.refs_7_), channel_id=1, source_target_pairs={{0,7},{1,0},{2,1},{3,2},{4,3},{5,4},{6,5},{7,6},{8,15},{9,8},{10,9... | collective-permute-start | bytes 393224 | tf_op jit(solution)/shard_map/ppermute | solution.py:284
  32.6 2.2 %split_translation.1 = (bf16[15,64,1024]{2,1,0:T(8,128)(2,1)S(1)}, bf16[15,64,1024]{2,1,0:T(8,128)(2,1)S(1)}) custom-call(f32[1,15,64,1024]{3,2,1,0:T(8,128)} %trans_hbm.1), custom_call_target="tpu_custom_call" | custom-call | flops 10000000 | bytes 3932160 | tf_op jit(solution)/shard_map/split_translation/pallas_call | solution.py:31
  36.2 2.3 %copy-done.4 = bf16[15,64,1024]{2,1,0:T(8,128)(2,1)S(1)} copy-done((bf16[15,64,1024]{2,1,0:T(8,128)(2,1)S(1)}, bf16[15,64,1024]{2,1,0:T(8,128)(2,1)}, u32[]{:S(2)}) %copy-start.4) | copy-done | bytes 1966104
  38.5 2.9 %adjoint_terms.1 = (bf16[16,32,128]{2,1,0:T(8,128)(2,1)}, f32[8,64,1024]{2,1,0:T(8,128)}, f32[8,64,1024]{2,1,0:T(8,128)S(1)}) custom-call(bf16[16,96,128]{2,1,0:T(8,128)(2,1)S(1)} %all-to-all-done.msg_ref, bf16[15,64,1024]{2,1,0:T(8,128)(2,1)S(1)} %get-tuple-element.30.high_ref, bf16[15,64,1024]{2,1,0:T(8,128)(2,1)S(1)} %copy-done.4), custom_call_target="tpu_custom_call" | custom-call | flops 10000000 | bytes 4325376 | tf_op jit(solution)/shard_map/adjoint_terms/pallas_call | solution.py:31
  42.8 8.0 %all-to-all-start.1 = ((bf16[16,32,128]{2,1,0:T(8,128)(2,1)}), bf16[16,32,128]{2,1,0:T(8,128)(2,1)S(1)}, u32[]{:S(2)}, u32[]{:S(2)}) async-start(bf16[16,32,128]{2,1,0:T(8,128)(2,1)} %get-tuple-element.34), calls=%async_computation.1 | async-start | bytes 262144 | tf_op jit(solution)/shard_map/all_to_all | solution.py:276
  50.7 3.2 %collective-permute-start.8 = (bf16[2,2,64,256]{3,2,1,0:T(8,128)(2,1)S(1)}, bf16[2,2,64,256]{3,2,1,0:T(8,128)(2,1)S(1)}, u32[]{:S(2)}, u32[]{:S(2)}) collective-permute-start(bf16[2,2,64,256]{3,2,1,0:T(8,128)(2,1)S(1)} %collective-permute-done.4.refs_6_), channel_id=1, source_target_pairs={{0,7},{1,0},{2,1},{3,2},{4,3},{5,4},{6,5},{7,6},{8,15},{9,8},{10,9... | collective-permute-start | bytes 393224 | tf_op jit(solution)/shard_map/ppermute | solution.py:284
  54.0 5.0 %collective-permute-done.8.refs_5_ = bf16[2,2,64,256]{3,2,1,0:T(8,128)(2,1)S(1)} collective-permute-done((bf16[2,2,64,256]{3,2,1,0:T(8,128)(2,1)S(1)}, bf16[2,2,64,256]{3,2,1,0:T(8,128)(2,1)S(1)}, u32[]{:S(2)}, u32[]{:S(2)}) %collective-permute-start.8) | collective-permute-done | bytes 131104 | tf_op jit(solution)/shard_map/ppermute | solution.py:284
  59.0 2.2 %all-to-all-done.1.pieces_ref = bf16[16,32,128]{2,1,0:T(8,128)(2,1)S(1)} async-done(((bf16[16,32,128]{2,1,0:T(8,128)(2,1)}), bf16[16,32,128]{2,1,0:T(8,128)(2,1)S(1)}, u32[]{:S(2)}, u32[]{:S(2)}) %all-to-all-start.1) | async-done | bytes 131104 | tf_op jit(solution)/shard_map/all_to_all | solution.py:276
  64.4 5.1 %all-to-all-start.2 = ((bf16[8,2,64,1024]{3,2,1,0:T(8,128)(2,1)}), bf16[8,2,64,1024]{3,2,1,0:T(8,128)(2,1)S(1)}, u32[]{:S(2)}, u32[]{:S(2)}) async-start(bf16[8,2,64,1024]{3,2,1,0:T(8,128)(2,1)} %copy-done), calls=%async_computation.2 | async-start | bytes 4194304 | tf_op jit(solution)/shard_map/all_to_all | solution.py:276
  70.2 3.9 %near.1 = (f32[64,512]{1,0:T(8,128)S(1)}, bf16[8,256,128]{2,1,0:T(8,128)(2,1)S(1)}, f32[8,256,128]{2,1,0:T(8,128)S(1)}) custom-call(s32[1]{0:T(128)S(6)} %copy.11.count_ref, s32[32]{0:T(128)S(1)} %copy-done.13, s32[32]{0:T(128)S(1)} %copy-done.14, bf16[2,64,256]{2,1,0:T(8,128)(2,1)S(1)} %get-tuple-element.38.low_ref, bf16[32,256,256]{2,1,0:T(8,128)(2,1)} %tiles_hbm.1, ...), custom_call_target="tpu_custom_call" | custom-call | flops 10000000 | bytes 5308676 | tf_op jit(solution)/shard_map/near/pallas_call | solution.py:31
  74.1 3.6 %collective-permute-start.9 = (bf16[8,256,128]{2,1,0:T(8,128)(2,1)S(1)}, bf16[8,256,128]{2,1,0:T(8,128)(2,1)S(1)}, u32[]{:S(2)}, u32[]{:S(2)}) collective-permute-start(bf16[8,256,128]{2,1,0:T(8,128)(2,1)S(1)} %get-tuple-element.42), channel_id=1, source_target_pairs={{0,8},{8,0},{1,9},{9,1},{2,10},{10,2},{3,11},{11,3},{4,12},{12,4},... | collective-permute-start | bytes 1572872 | tf_op jit(solution)/shard_map/ppermute | solution.py:272
  77.7 28.3 %collective-permute-done.9.mate_ref = bf16[8,256,128]{2,1,0:T(8,128)(2,1)S(1)} collective-permute-done((bf16[8,256,128]{2,1,0:T(8,128)(2,1)S(1)}, bf16[8,256,128]{2,1,0:T(8,128)(2,1)S(1)}, u32[]{:S(2)}, u32[]{:S(2)}) %collective-permute-start.9) | collective-permute-done | bytes 524320 | tf_op jit(solution)/shard_map/ppermute | solution.py:272
  110.0 4.7 %all-to-all-start.3 = ((bf16[8,320,128]{2,1,0:T(8,128)(2,1)}), bf16[8,320,128]{2,1,0:T(8,128)(2,1)S(1)}, u32[]{:S(2)}, u32[]{:S(2)}) async-start(bf16[8,320,128]{2,1,0:T(8,128)(2,1)} %copy-done.10), calls=%async_computation.3 | async-start | bytes 1310720 | tf_op jit(solution)/shard_map/all_to_all | solution.py:276
  114.8 2.9 %collective-permute-done.10.other_ref = bf16[8,64,1024]{2,1,0:T(8,128)(2,1)S(1)} collective-permute-done((bf16[8,64,1024]{2,1,0:T(8,128)(2,1)}, bf16[8,64,1024]{2,1,0:T(8,128)(2,1)S(1)}, u32[]{:S(2)}, u32[]{:S(2)}) %collective-permute-start.10) | collective-permute-done | bytes 1048608 | tf_op jit(solution)/shard_map/ppermute | solution.py:272
  122.1 5.1 %collective-permute-done.11.mate_pot_ref = bf16[32,128]{1,0:T(8,128)(2,1)S(1)} collective-permute-done((bf16[32,128]{1,0:T(8,128)(2,1)S(1)}, bf16[32,128]{1,0:T(8,128)(2,1)S(1)}, u32[]{:S(2)}, u32[]{:S(2)}) %collective-permute-start.11) | collective-permute-done | bytes 8224 | tf_op jit(solution)/shard_map/ppermute | solution.py:272
  127.2 6.6 %all-to-all-done.3.msg_ref.near_ref = bf16[8,320,128]{2,1,0:T(8,128)(2,1)S(1)} async-done(((bf16[8,320,128]{2,1,0:T(8,128)(2,1)}), bf16[8,320,128]{2,1,0:T(8,128)(2,1)S(1)}, u32[]{:S(2)}, u32[]{:S(2)}) %all-to-all-start.3) | async-done | bytes 655392 | tf_op jit(solution)/shard_map/all_to_all | solution.py:276
  133.9 5.4 %collective-permute-done.12.mate_ref = f32[64,128]{1,0:T(8,128)S(1)} collective-permute-done((f32[64,128]{1,0:T(8,128)S(1)}, f32[64,128]{1,0:T(8,128)S(1)}, u32[]{:S(2)}, u32[]{:S(2)}) %collective-permute-start.12) | collective-permute-done | bytes 32800 | tf_op jit(solution)/shard_map/ppermute | solution.py:272
  139.4 12.9 %all_to_all.25.low_ref = bf16[8,128,128]{2,1,0:T(8,128)(2,1)S(1)} all-to-all(bf16[8,128,128]{2,1,0:T(8,128)(2,1)S(1)} %low_shares.1), channel_id=1, replica_groups=mesh['xlo'=2,'y'=4,'core'=2,'xhi'=2,'z'=8] {'z'}, dimensions={0} | all-to-all | bytes 524288 | tf_op jit(solution)/shard_map/all_to_all | solution.py:276
  (70 shorter events, 18.6 us)
Async XLA Ops:
  3.6 32.6 %all-to-all-start = ((bf16[16,96,128]{2,1,0:T(8,128)(2,1)}), bf16[16,96,128]{2,1,0:T(8,128)(2,1)S(1)}, u32[]{:S(2)}, u32[]{:S(2)}) async-start(bf16[16,96,128]{2,1,0:T(8,128)(2,1)} %get-tuple-element.25), calls=%async_computation | async-start | bytes 786432 | tf_op jit(solution)/shard_map/all_to_all | solution.py:276
  14.6 6.7 %collective-permute-start = (bf16[2,64,256]{2,1,0:T(8,128)(2,1)S(1)}, bf16[2,64,256]{2,1,0:T(8,128)(2,1)S(1)}, u32[]{:S(2)}, u32[]{:S(2)}) collective-permute-start(bf16[2,64,256]{2,1,0:T(8,128)(2,1)S(1)} %get-tuple-element.26), channel_id=1, source_target_pairs={{0,8},{8,0},{1,9},{9,1},{2,10},{10,2},{3,11},{11,3},{4,12},{12,4},... | collective-permute-start | bytes 196616 | tf_op jit(solution)/shard_map/ppermute | solution.py:272
  21.3 20.1 %copy-start.16 = (bf16[2,2,64,256]{3,2,1,0:T(8,128)(2,1)}, bf16[2,2,64,256]{3,2,1,0:T(8,128)(2,1)S(1)}, u32[]{:S(2)}) copy-start(bf16[2,2,64,256]{3,2,1,0:T(8,128)(2,1)S(1)} %pad_maximum_fusion.refs_0_) | copy-start | bytes 393220
  21.3 8.0 %collective-permute-start.1 = (bf16[2,2,64,256]{3,2,1,0:T(8,128)(2,1)S(1)}, bf16[2,2,64,256]{3,2,1,0:T(8,128)(2,1)S(1)}, u32[]{:S(2)}, u32[]{:S(2)}) collective-permute-start(bf16[2,2,64,256]{3,2,1,0:T(8,128)(2,1)S(1)} %pad_maximum_fusion.refs_0_), channel_id=1, source_target_pairs={{0,1},{1,2},{2,3},{3,4},{4,5},{5,6},{6,7},{7,0},{8,9},{9,10},{10,1... | collective-permute-start | bytes 393224 | tf_op jit(solution)/shard_map/ppermute | solution.py:284
  23.0 6.4 %collective-permute-start.3 = (bf16[2,2,64,256]{3,2,1,0:T(8,128)(2,1)S(1)}, bf16[2,2,64,256]{3,2,1,0:T(8,128)(2,1)S(1)}, u32[]{:S(2)}, u32[]{:S(2)}) collective-permute-start(bf16[2,2,64,256]{3,2,1,0:T(8,128)(2,1)S(1)} %pad_maximum_fusion.refs_0_), channel_id=1, source_target_pairs={{0,7},{1,0},{2,1},{3,2},{4,3},{5,4},{6,5},{7,6},{8,15},{9,8},{10,9... | collective-permute-start | bytes 393224 | tf_op jit(solution)/shard_map/ppermute | solution.py:284
  29.3 12.1 %copy-start.17 = (bf16[2,2,64,256]{3,2,1,0:T(8,128)(2,1)}, bf16[2,2,64,256]{3,2,1,0:T(8,128)(2,1)S(1)}, u32[]{:S(2)}) copy-start(bf16[2,2,64,256]{3,2,1,0:T(8,128)(2,1)S(1)} %collective-permute-done.1.refs_1_) | copy-start | bytes 393220
  29.3 6.8 %collective-permute-start.2 = (bf16[2,2,64,256]{3,2,1,0:T(8,128)(2,1)S(1)}, bf16[2,2,64,256]{3,2,1,0:T(8,128)(2,1)S(1)}, u32[]{:S(2)}, u32[]{:S(2)}) collective-permute-start(bf16[2,2,64,256]{3,2,1,0:T(8,128)(2,1)S(1)} %collective-permute-done.1.refs_1_), channel_id=1, source_target_pairs={{0,1},{1,2},{2,3},{3,4},{4,5},{5,6},{6,7},{7,0},{8,9},{9,10},{10,1... | collective-permute-start | bytes 393224 | tf_op jit(solution)/shard_map/ppermute | solution.py:284
  29.4 12.0 %copy-start.18 = (bf16[2,2,64,256]{3,2,1,0:T(8,128)(2,1)}, bf16[2,2,64,256]{3,2,1,0:T(8,128)(2,1)S(1)}, u32[]{:S(2)}) copy-start(bf16[2,2,64,256]{3,2,1,0:T(8,128)(2,1)S(1)} %collective-permute-done.3.refs_7_) | copy-start | bytes 393220
  29.4 6.8 %collective-permute-start.4 = (bf16[2,2,64,256]{3,2,1,0:T(8,128)(2,1)S(1)}, bf16[2,2,64,256]{3,2,1,0:T(8,128)(2,1)S(1)}, u32[]{:S(2)}, u32[]{:S(2)}) collective-permute-start(bf16[2,2,64,256]{3,2,1,0:T(8,128)(2,1)S(1)} %collective-permute-done.3.refs_7_), channel_id=1, source_target_pairs={{0,7},{1,0},{2,1},{3,2},{4,3},{5,4},{6,5},{7,6},{8,15},{9,8},{10,9... | collective-permute-start | bytes 393224 | tf_op jit(solution)/shard_map/ppermute | solution.py:284
  36.2 6.6 %copy-start.19 = (bf16[2,2,64,256]{3,2,1,0:T(8,128)(2,1)}, bf16[2,2,64,256]{3,2,1,0:T(8,128)(2,1)S(1)}, u32[]{:S(2)}) copy-start(bf16[2,2,64,256]{3,2,1,0:T(8,128)(2,1)S(1)} %collective-permute-done.2.refs_2_) | copy-start | bytes 393220
  36.2 14.6 %copy-start.20 = (bf16[2,2,64,256]{3,2,1,0:T(8,128)(2,1)}, bf16[2,2,64,256]{3,2,1,0:T(8,128)(2,1)S(1)}, u32[]{:S(2)}) copy-start(bf16[2,2,64,256]{3,2,1,0:T(8,128)(2,1)S(1)} %collective-permute-done.4.refs_6_) | copy-start | bytes 393220
  42.8 18.4 %collective-permute-start.5 = (f32[8,64,1024]{2,1,0:T(8,128)}, f32[8,64,1024]{2,1,0:T(8,128)S(1)}, u32[]{:S(2)}, u32[]{:S(2)}) collective-permute-start(f32[8,64,1024]{2,1,0:T(8,128)} %get-tuple-element.33), channel_id=1, source_target_pairs={{0,16},{16,0},{1,17},{17,1},{2,18},{18,2},{3,19},{19,3},{4,20},{20... | collective-permute-start | bytes 6291464 | tf_op jit(solution)/shard_map/ppermute | solution.py:272
  42.8 11.2 %collective-permute-start.6 = (bf16[2,2,64,256]{3,2,1,0:T(8,128)(2,1)S(1)}, bf16[2,2,64,256]{3,2,1,0:T(8,128)(2,1)S(1)}, u32[]{:S(2)}, u32[]{:S(2)}) collective-permute-start(bf16[2,2,64,256]{3,2,1,0:T(8,128)(2,1)S(1)} %collective-permute-done.2.refs_2_), channel_id=1, source_target_pairs={{0,1},{1,2},{2,3},{3,4},{4,5},{5,6},{6,7},{7,0},{8,9},{9,10},{10,1... | collective-permute-start | bytes 393224 | tf_op jit(solution)/shard_map/ppermute | solution.py:284
  42.8 18.4 %all-to-all-start.1 = ((bf16[16,32,128]{2,1,0:T(8,128)(2,1)}), bf16[16,32,128]{2,1,0:T(8,128)(2,1)S(1)}, u32[]{:S(2)}, u32[]{:S(2)}) async-start(bf16[16,32,128]{2,1,0:T(8,128)(2,1)} %get-tuple-element.34), calls=%async_computation.1 | async-start | bytes 262144 | tf_op jit(solution)/shard_map/all_to_all | solution.py:276
  50.7 8.3 %collective-permute-start.8 = (bf16[2,2,64,256]{3,2,1,0:T(8,128)(2,1)S(1)}, bf16[2,2,64,256]{3,2,1,0:T(8,128)(2,1)S(1)}, u32[]{:S(2)}, u32[]{:S(2)}) collective-permute-start(bf16[2,2,64,256]{3,2,1,0:T(8,128)(2,1)S(1)} %collective-permute-done.4.refs_6_), channel_id=1, source_target_pairs={{0,7},{1,0},{2,1},{3,2},{4,3},{5,4},{6,5},{7,6},{8,15},{9,8},{10,9... | collective-permute-start | bytes 393224 | tf_op jit(solution)/shard_map/ppermute | solution.py:284
  54.0 9.1 %copy-start.21 = (bf16[2,2,64,256]{3,2,1,0:T(8,128)(2,1)}, bf16[2,2,64,256]{3,2,1,0:T(8,128)(2,1)S(1)}, u32[]{:S(2)}) copy-start(bf16[2,2,64,256]{3,2,1,0:T(8,128)(2,1)S(1)} %collective-permute-done.6.refs_3_) | copy-start | bytes 393220
  54.0 7.2 %collective-permute-start.7 = (bf16[2,2,64,256]{3,2,1,0:T(8,128)(2,1)S(1)}, bf16[2,2,64,256]{3,2,1,0:T(8,128)(2,1)S(1)}, u32[]{:S(2)}, u32[]{:S(2)}) collective-permute-start(bf16[2,2,64,256]{3,2,1,0:T(8,128)(2,1)S(1)} %collective-permute-done.6.refs_3_), channel_id=1, source_target_pairs={{0,1},{1,2},{2,3},{3,4},{4,5},{5,6},{6,7},{7,0},{8,9},{9,10},{10,1... | collective-permute-start | bytes 393224 | tf_op jit(solution)/shard_map/ppermute | solution.py:284
  64.4 42.4 %all-to-all-start.2 = ((bf16[8,2,64,1024]{3,2,1,0:T(8,128)(2,1)}), bf16[8,2,64,1024]{3,2,1,0:T(8,128)(2,1)S(1)}, u32[]{:S(2)}, u32[]{:S(2)}) async-start(bf16[8,2,64,1024]{3,2,1,0:T(8,128)(2,1)} %copy-done), calls=%async_computation.2 | async-start | bytes 4194304 | tf_op jit(solution)/shard_map/all_to_all | solution.py:276
  74.1 31.9 %collective-permute-start.9 = (bf16[8,256,128]{2,1,0:T(8,128)(2,1)S(1)}, bf16[8,256,128]{2,1,0:T(8,128)(2,1)S(1)}, u32[]{:S(2)}, u32[]{:S(2)}) collective-permute-start(bf16[8,256,128]{2,1,0:T(8,128)(2,1)S(1)} %get-tuple-element.42), channel_id=1, source_target_pairs={{0,8},{8,0},{1,9},{9,1},{2,10},{10,2},{3,11},{11,3},{4,12},{12,4},... | collective-permute-start | bytes 1572872 | tf_op jit(solution)/shard_map/ppermute | solution.py:272
  110.0 23.8 %all-to-all-start.3 = ((bf16[8,320,128]{2,1,0:T(8,128)(2,1)}), bf16[8,320,128]{2,1,0:T(8,128)(2,1)S(1)}, u32[]{:S(2)}, u32[]{:S(2)}) async-start(bf16[8,320,128]{2,1,0:T(8,128)(2,1)} %copy-done.10), calls=%async_computation.3 | async-start | bytes 1310720 | tf_op jit(solution)/shard_map/all_to_all | solution.py:276
  114.7 2.9 %collective-permute-start.10 = (bf16[8,64,1024]{2,1,0:T(8,128)(2,1)}, bf16[8,64,1024]{2,1,0:T(8,128)(2,1)S(1)}, u32[]{:S(2)}, u32[]{:S(2)}) collective-permute-start(bf16[8,64,1024]{2,1,0:T(8,128)(2,1)} %copy-done.15), channel_id=1, source_target_pairs={{0,16},{16,0},{1,17},{17,1},{2,18},{18,2},{3,19},{19,3},{4,20},{20... | collective-permute-start | bytes 3145736 | tf_op jit(solution)/shard_map/ppermute | solution.py:272
  122.0 30.2 %copy-start.6 = (bf16[1024,512]{1,0:T(8,128)(2,1)S(1)}, bf16[1024,512]{1,0:T(8,128)(2,1)}, u32[]{:S(2)}) copy-start(bf16[1024,512]{1,0:T(8,128)(2,1)} %skin_ref.1) | copy-start | bytes 3145732
  122.0 5.2 %collective-permute-start.11 = (bf16[32,128]{1,0:T(8,128)(2,1)S(1)}, bf16[32,128]{1,0:T(8,128)(2,1)S(1)}, u32[]{:S(2)}, u32[]{:S(2)}) collective-permute-start(bf16[32,128]{1,0:T(8,128)(2,1)S(1)} %forward.1.pot_ref), channel_id=1, source_target_pairs={{0,8},{8,0},{1,9},{9,1},{2,10},{10,2},{3,11},{11,3},{4,12},{12,4},... | collective-permute-start | bytes 24584 | tf_op jit(solution)/shard_map/ppermute | solution.py:272
  133.8 5.5 %collective-permute-start.12 = (f32[64,128]{1,0:T(8,128)S(1)}, f32[64,128]{1,0:T(8,128)S(1)}, u32[]{:S(2)}, u32[]{:S(2)}) collective-permute-start(f32[64,128]{1,0:T(8,128)S(1)} %fold.1.mine_ref), channel_id=1, source_target_pairs={{0,8},{8,0},{1,9},{9,1},{2,10},{10,2},{3,11},{11,3},{4,12},{12,4},... | collective-permute-start | bytes 98312 | tf_op jit(solution)/shard_map/ppermute | solution.py:272
  (17 other events, 38.8 us)

commit v4 on v3

--- a/solution.py
+++ b/solution.py
@@ -26,7 +26,7 @@
     return pl.BlockSpec(memory_space=pltpu.HBM)
 
 
-def call(kernel, outs, args, specs=None, scratch=(), flops=10**7, name=None, room=8, alias=None):
+def call(kernel, outs, args, specs=None, scratch=(), flops=10**7, name=None):
     moved = sum(a.size * a.dtype.itemsize for a in args)
     return pl.pallas_call(
         kernel,
@@ -34,10 +34,9 @@
         in_specs=specs or [vmem()] * len(args),
         out_specs=[vmem()] * len(outs),
         scratch_shapes=list(scratch),
-        compiler_params=pltpu.CompilerParams(vmem_limit_bytes=room * 2**20),
+        compiler_params=pltpu.CompilerParams(vmem_limit_bytes=20 * 2**20),
         cost_estimate=pl.CostEstimate(flops=flops, bytes_accessed=moved, transcendentals=0),
         name=name,
-        input_output_aliases=alias or {},
     )(*args)
 
 
@@ -97,74 +96,90 @@
         msg_ref[piece, 64:96, :] = rest
 
 
-def split_translation(trans_hbm, high_ref, low_ref, blocks, sems):
+def split_translation(trans_hbm, out_ref, blocks, sems):
     copies = [pltpu.make_async_copy(trans_hbm.at[0, d], blocks.at[d], sems.at[d]) for d in range(15)]
     for copy in copies:
         copy.start()
     for d in range(15):
         copies[d].wait()
         high, low = split(blocks[d])
-        high_ref[d] = high
-        low_ref[d] = low
-
-
-def lags():
+        out_ref[d, :64] = high
+        out_ref[d, 64:] = low
+
+
+def lags(parity):
     cluster = lax.axis_index(BLK)
-    core = lax.axis_index("core")
-    return [
-        lax.rem(cluster - (2 * q + parity) + 16, 16) for parity in (1 - core, core) for q in range(8)
-    ]
-
-
-def adjoint_terms(msg_ref, high_ref, low_ref, copies_ref, send_ref, keep_ref):
-    lag = lags()
-    total = jnp.sum(msg_ref[:, 0:32, :].astype(f32), axis=0)
-    share = total.astype(bf16)
+    return [lax.rem(cluster - (2 * q + parity) + 16, 16) for q in range(8)]
+
+
+def fetch(parts_hbm, blocks, sems, lag):
+    copies = []
+    for index, behind in enumerate(lag):
+        source = parts_hbm.at[jnp.maximum(behind - 1, 0)]
+        copies.append(pltpu.make_async_copy(source, blocks.at[index], sems.at[index]))
+        copies[index].start()
+    return copies
+
+
+def term(both, block):
+    pair = dot(both, block[:64])
+    return pair[:64] + pair[64:] + dot(both[:64], block[64:])
+
+
+def other_terms(msg_ref, parts_hbm, copies_ref, grad_ref, send_ref, blocks, sems):
+    fetched = fetch(parts_hbm, blocks, sems, lags(1 - lax.axis_index("core")))
+    share = jnp.sum(msg_ref[:, 0:32, :].astype(f32), axis=0).astype(bf16)
     for piece in range(16):
         copies_ref[piece] = share
     packed = jnp.sum(msg_ref[:, 32:64, :].astype(f32) + msg_ref[:, 64:96, :].astype(f32), axis=0)
     gradient = jnp.concatenate([packed, pltpu.roll(packed, 64, 1)], axis=0)
     high, low = split(gradient.T[:64])
     both = jnp.concatenate([high, low], axis=0)
-    for index in range(16):
-        block = jnp.maximum(lag[index] - 1, 0)
-        pair = dot(both, high_ref[block])
-        value = pair[:64] + pair[64:] + dot(high, low_ref[block])
-        if index < 8:
-            send_ref[index] = value
-        else:
-            keep_ref[index - 8] = jnp.where(lag[index] == 0, 0.0, value)
-
-
-def pack(keep_ref, came_ref, pieces_ref, out_ref):
+    grad_ref[...] = both
+    for index in range(8):
+        fetched[index].wait()
+        send_ref[index] = term(both, blocks[index])
+
+
+def own_terms(grad_ref, came_ref, parts_hbm, out_ref, blocks, sems):
+    lag = lags(lax.axis_index("core"))
+    fetched = fetch(parts_hbm, blocks, sems, lag)
+    both = grad_ref[...]
+    for index in range(8):
+        fetched[index].wait()
+        value = jnp.where(lag[index] == 0, 0.0, term(both, blocks[index]))
+        out_ref[index] = (value + came_ref[index]).astype(bf16)
+
+
+def pack(own_ref, pieces_ref, out_ref):
     charges = join_pieces(pieces_ref, 0)
     for q in range(8):
-        out_ref[q, 0] = (keep_ref[q] + came_ref[q]).astype(bf16)
+        out_ref[q, 0] = own_ref[q]
         out_ref[q, 1] = charges
 
 
-def unpack(came_ref, keep_ref, mate_ref, msg_ref, charges_ref):
+def unpack(came_ref, msg_ref, charges_ref):
     total = came_ref[0, 0].astype(f32)
     charges_ref[0] = came_ref[0, 1]
     for q in range(1, 8):
         total = total + came_ref[q, 0].astype(f32)
         charges_ref[q] = came_ref[q, 1]
     for piece in range(8):
-        msg_ref[piece, 0:256, :] = (keep_ref[piece] + mate_ref[piece].astype(f32)).astype(bf16)
         for part in range(8):
-            msg_ref[piece, 256 + part * 8 : 264 + part * 8, :] = total[
+            msg_ref[piece, part * 8 : part * 8 + 8, :] = total[
                 piece * 8 : piece * 8 + 8, part * 128 : part * 128 + 128
             ].astype(bf16)
 
 
-def forward(other_ref, came_ref, high_ref, low_ref, pot_ref):
-    lag = lags()
+def forward(other_ref, came_ref, parts_hbm, pot_ref, blocks, sems):
+    core = lax.axis_index("core")
+    lag = lags(1 - core) + lags(core)
+    fetched = fetch(parts_hbm, blocks, sems, lag)
     total = jnp.zeros((64, 64), f32)
     for index in range(16):
-        block = jnp.maximum(lag[index] - 1, 0)
-        both = jnp.concatenate([high_ref[block], low_ref[block]], axis=0)
         charges = other_ref[index] if index < 8 else came_ref[index - 8, 1]
-        pair = dot_last(both, charges)
+        fetched[index].wait()
+        pair = dot_last(blocks[index], charges)
         total = total + jnp.where(lag[index] == 0, 0.0, pair[:64] + pair[64:])
     pot_ref[...] = jnp.concatenate([total[:32], total[32:]], axis=1).astype(bf16)
 
@@ -231,10 +246,10 @@
 
 
 def fold(msg_ref, out_ref):
-    out_ref[...] = jnp.sum(msg_ref[:, 256:320, :].astype(f32), axis=0)
-
-
-def low_shares(mine_ref, mate_ref, pot_ref, mate_pot_ref, out_ref):
+    out_ref[...] = jnp.sum(msg_ref[...].astype(f32), axis=0)
+
+
+def last_message(mine_ref, mate_ref, pot_ref, mate_pot_ref, keep_ref, mate_near_ref, out_ref):
     adjoint = (mine_ref[...] + mate_ref[...]).astype(bf16)
     upper = lax.axis_index("xhi") == 1
     pot = pot_ref[...].astype(f32)
@@ -245,27 +260,36 @@
         out_ref[piece, 0:64, :] = adjoint
         out_ref[piece, 64:96, :] = first
         out_ref[piece, 96:128, :] = second
-
-
-def finish(low_ref, near_ref, ahead_ref, skin_ref, skout_ref, resp_ref, sens_ref):
+        out_ref[piece, 128:384, :] = (keep_ref[piece] + mate_near_ref[piece].astype(f32)).astype(bf16)
+
+
+def finish(msg_ref, ahead_ref, skin_hbm, skout_hbm, resp_ref, sens_ref, skin_ref, skout_ref, sems):
+    first = pltpu.make_async_copy(skin_hbm, skin_ref, sems.at[0])
+    second = pltpu.make_async_copy(skout_hbm, skout_ref, sems.at[1])
+    first.start()
+    second.start()
     adjoint = jnp.concatenate(
         [
-            jnp.concatenate([low_ref[z, part * 8 : part * 8 + 8, :] for part in range(8)], axis=1)
+            jnp.concatenate([msg_ref[z, part * 8 : part * 8 + 8, :] for part in range(8)], axis=1)
             for z in range(8)
         ],
         axis=0,
     )
-    packed = jnp.concatenate([low_ref[r % 8, 64 + r // 8 * 32 : 96 + r // 8 * 32, :] for r in range(16)], axis=0)
+    packed = jnp.concatenate([msg_ref[r % 8, 64 + r // 8 * 32 : 96 + r // 8 * 32, :] for r in range(16)], axis=0)
     packed = packed.astype(f32).T.astype(bf16)
+    near_sums = []
+    for part in range(4):
+        rows = slice(128 + part * 64, 192 + part * 64)
+        value = msg_ref[0, rows, :].astype(f32)
+        for source in range(1, 8):
+            value = value + msg_ref[source, rows, :].astype(f32)
+        near_sums.append(value)
+    first.wait()
+    sens_ref[...] = dot(adjoint, skin_ref[...]) + jnp.concatenate(near_sums, axis=1)
+    second.wait()
     upper = jnp.concatenate([skout_ref[r * 64 : r * 64 + 32, :] for r in range(16)], axis=0)
     lower = jnp.concatenate([skout_ref[r * 64 + 32 : r * 64 + 64, :] for r in range(16)], axis=0)
     resp_ref[...] = ahead_ref[...] + dot(packed[:64], upper) + dot(packed[64:], lower)
-    far = dot(adjoint, skin_ref[...])
-    for part in range(4):
-        value = near_ref[0, part * 64 : part * 64 + 64, :].astype(f32)
-        for source in range(1, 8):
-            value = value + near_ref[source, part * 64 : part * 64 + 64, :].astype(f32)
-        sens_ref[:, part * 128 : part * 128 + 128] = far[:, part * 128 : part * 128 + 128] + value
 
 
 def swap(value, axis):
@@ -299,32 +323,41 @@
         + [pltpu.SemaphoreType.DMA((4,))],
         name="prepare",
     )
-    here = jnp.stack([drive, swap(drive, "xhi")])
-    up1, down1 = shift(here, 1), shift(here, -1)
-    up2, down2 = shift(up1, 1), shift(down1, -1)
-    high, rest = call(
+    mate = swap(drive, "xhi")
+    (parts,) = call(
         split_translation,
-        [((15, 64, 1024), bf16)] * 2,
+        [((15, 128, 1024), bf16)],
         [in_hbm(trans)],
         specs=[hbm()],
         scratch=[pltpu.VMEM((15, 64, 1024), f32), pltpu.SemaphoreType.DMA((15,))],
         name="split_translation",
-        room=16,
-    )
-    msg, up2, down2, high, rest = tie(exchange(msg, ROWS), up2, down2, high, rest)
-    copies, send, keep = call(
-        adjoint_terms,
-        [((16, 32, 128), bf16), ((8, 64, 1024), f32), ((8, 64, 1024), f32)],
-        [msg, high, rest],
-        name="adjoint_terms",
-        room=12,
-    )
-    came = swap(send, "core")
+    )
+    parts = in_hbm(parts)
+    msg, mate, parts = tie(exchange(msg, ROWS), mate, parts)
+    blocks = [pltpu.VMEM((8, 128, 1024), bf16), pltpu.SemaphoreType.DMA((8,))]
+    copies, gradient, send = call(
+        other_terms,
+        [((16, 32, 128), bf16), ((128, 64), bf16), ((8, 64, 1024), f32)],
+        [msg, parts],
+        specs=[vmem(), hbm()],
+        scratch=blocks,
+        name="other_terms",
+    )
+    here = jnp.stack([drive, mate])
+    up1, down1 = shift(here, 1), shift(here, -1)
+    (own,) = call(
+        own_terms,
+        [((8, 64, 1024), bf16)],
+        [gradient, swap(send, "core"), parts],
+        specs=[vmem(), vmem(), hbm()],
+        scratch=blocks,
+        name="own_terms",
+    )
+    copies, up1, down1, own = tie(exchange(copies, ROWS), up1, down1, own)
+    (both,) = call(pack, [((8, 2, 64, 1024), bf16)], [own, copies], name="pack")
+    up2, down2 = shift(up1, 1), shift(down1, -1)
     up3, down3 = shift(up2, 1), shift(down2, -1)
     up4 = shift(up3, 1)
-    copies, up4, down3 = tie(exchange(copies, ROWS), up4, down3)
-    (both,) = call(pack, [((8, 2, 64, 1024), bf16)], [keep, came, copies], name="pack")
-    both = exchange(both, FACE)
     ahead, send, keep = call(
         near,
         [((64, 512), f32), ((8, 256, 128), bf16), ((8, 256, 128), f32)],
@@ -340,39 +373,40 @@
             pltpu.SemaphoreType.DMA((8,)),
         ],
         name="near",
-        room=16,
-    )
-    mate = swap(send, "xhi")
-    behind, charges = call(
+    )
+    both, ahead, send, keep = tie(exchange(both, FACE), ahead, send, keep)
+    mate_near = swap(send, "xhi")
+    adjoint, charges = call(
         unpack,
-        [((8, 320, 128), bf16), ((8, 64, 1024), bf16)],
-        [both, keep, mate],
+        [((8, 64, 128), bf16), ((8, 64, 1024), bf16)],
+        [both],
         name="unpack",
     )
     others = swap(charges, "core")
-    behind = exchange(behind, "z")
     (potential,) = call(
         forward,
         [((32, 128), bf16)],
-        [others, both, high, rest],
+        [others, both, parts],
+        specs=[vmem(), vmem(), hbm()],
+        scratch=[pltpu.VMEM((16, 128, 1024), bf16), pltpu.SemaphoreType.DMA((16,))],
         name="forward",
-        room=12,
     )
     mate_pot = swap(potential, "xhi")
-    behind, mate_pot = tie(behind, mate_pot)
-    (mine,) = call(fold, [((64, 128), f32)], [behind], name="fold")
-    (shares,) = call(
-        low_shares,
-        [((8, 128, 128), bf16)],
-        [mine, swap(mine, "xhi"), potential, mate_pot],
-        name="low_shares",
-    )
-    shares = exchange(shares, "z")
+    adjoint, mate_pot = tie(exchange(adjoint, "z"), mate_pot)
+    (mine,) = call(fold, [((64, 128), f32)], [adjoint], name="fold")
+    (last,) = call(
+        last_message,
+        [((8, 384, 128), bf16)],
+        [mine, swap(mine, "xhi"), potential, mate_pot, keep, mate_near],
+        name="last_message",
+    )
     return tuple(
         call(
             finish,
             [((64, 512), f32), ((64, 512), f32)],
-            [shares, behind, ahead, skin, skout],
+            [exchange(last, "z"), ahead, in_hbm(skin), in_hbm(skout)],
+            specs=[vmem()] * 2 + [hbm()] * 2,
+            scratch=[pltpu.VMEM((1024, 512), bf16)] * 2 + [pltpu.SemaphoreType.DMA((2,))],
             name="finish",
         )
     )

time: 156 us -> 140 us (0.90)
  waiting for transfers between devices: 63.4 us -> 31.8 us
  blocking collectives: 12.9 us -> 27.6 us
  Pallas kernels: 15.1 us -> 28.8 us
  local copies, waits for them, and re-layouts: 16 us -> 4.53 us
    ppermute x6, waiting for transfers between devices: 44.9 us -> 7.54 us  [swap(): return lax.ppermute(value, axis, [(0, 1), (1, 0)])]
    all_to_all x1, blocking collectives: 12.9 us -> 27.6 us  [exchange(): return lax.all_to_all(value, axes, 0, 0, tiled=True)]
    pallas_call x10 -> x11, Pallas kernels: 15.1 us -> 28.8 us  [call(): pl.pallas_call(kernel, out_shape=[jax.ShapeDtypeStruct(s, d) for s, d in...]
    unnamed x48 -> x24, local copies, waits for them, and re-layouts: 16 us -> 4.53 us
    ppermute x7, waiting for transfers between devices: 9.73 us -> 15 us  [shift(): return lax.ppermute(value, 'z', [(i, (i + step) % 8) for i in range(8)])]
    all_to_all x4, starting transfers between devices: 28.8 us -> 25.6 us  [exchange(): return lax.all_to_all(value, axes, 0, 0, tiled=True)]
    ppermute x6, starting transfers between devices: 7.2 us -> 9.48 us  [swap(): return lax.ppermute(value, axis, [(0, 1), (1, 0)])]
  transfers between devices with their start and end apart: 17 -> 17, of which waited for: 9 -> 10; matrix products, arithmetic and copies ran while one was open for 0% -> 0% of each run, Pallas kernels for 5% -> 12%
where the time goes in v4:
time: 140 us; the launch traced here: 139 us
  starting transfers between devices  44.8 us (32%)
  waiting for transfers between devices  31.8 us (23%)
  Pallas kernels  28.8 us (21%)
  blocking collectives  27.6 us (20%)
  local copies, waits for them, and re-layouts  4.53 us (3%)
  between operations  1.62 us (1%)
    pallas_call x11, Pallas kernels, call(): pl.pallas_call(kernel, out_shape=[jax.ShapeDtypeStruct(s, d) for s, d in...  28.8 us
    all_to_all x1, blocking collectives, exchange(): return lax.all_to_all(value, axes, 0, 0, tiled=True)  27.6 us
    all_to_all x4, starting transfers between devices, exchange(): return lax.all_to_all(value, axes, 0, 0, tiled=True)  25.6 us
    ppermute x7, waiting for transfers between devices, shift(): return lax.ppermute(value, 'z', [(i, (i + step) % 8) for i in range(8)])  15 us
    ppermute x7, starting transfers between devices, shift(): return lax.ppermute(value, 'z', [(i, (i + step) % 8) for i in range(8)])  9.69 us
    ppermute x6, starting transfers between devices, swap(): return lax.ppermute(value, axis, [(0, 1), (1, 0)])  9.48 us
    all_to_all x4, waiting for transfers between devices, exchange(): return lax.all_to_all(value, axes, 0, 0, tiled=True)  9.25 us
    ppermute x6, waiting for transfers between devices, swap(): return lax.ppermute(value, axis, [(0, 1), (1, 0)])  7.54 us
  transfers between devices with their start and end apart: 17, of which 10 were waited for; matrix products, arithmetic and copies ran while one was open for 0% of the time, Pallas kernels for 12%

profile of v4, /device:TPU:8, one launch (start us, length us, event | category | flops | bytes accessed | tf_op | source)
XLA Modules:
  0.0 139.1 jit_solution(9367175806033541583)
XLA Ops:
  0.6 3.0 %prepare.1 = (bf16[2,64,256]{2,1,0:T(8,128)(2,1)S(1)}, bf16[2,64,256]{2,1,0:T(8,128)(2,1)S(1)}, bf16[16,96,128]{2,1,0:T(8,128)(2,1)}) custom-call(f32[64,512]{1,0:T(8,128)} %exc_hbm.1, f32[64,512]{1,0:T(8,128)} %loads_hbm.1, bf16[1024,512]{1,0:T(8,128)(2,1)} %skin_hbm.3, bf16[1024,512]{1,0:T(8,128)(2,1)} %skout_hbm.3), custom_call_target="tpu_custom_call" | custom-call | flops 10000000 | bytes 2359296 | tf_op jit(solution)/shard_map/prepare/pallas_call | solution.py:31
  3.6 11.0 %all-to-all-start = ((bf16[16,96,128]{2,1,0:T(8,128)(2,1)}), bf16[16,96,128]{2,1,0:T(8,128)(2,1)S(1)}, u32[]{:S(2)}, u32[]{:S(2)}) async-start(bf16[16,96,128]{2,1,0:T(8,128)(2,1)} %get-tuple-element.26), calls=%async_computation | async-start | bytes 786432 | tf_op jit(solution)/shard_map/all_to_all | solution.py:300
  14.7 3.4 %collective-permute-start = (bf16[2,64,256]{2,1,0:T(8,128)(2,1)S(1)}, bf16[2,64,256]{2,1,0:T(8,128)(2,1)S(1)}, u32[]{:S(2)}, u32[]{:S(2)}) collective-permute-start(bf16[2,64,256]{2,1,0:T(8,128)(2,1)S(1)} %get-tuple-element.27), channel_id=1, source_target_pairs={{0,8},{8,0},{1,9},{9,1},{2,10},{10,2},{3,11},{11,3},{4,12},{12,4},... | collective-permute-start | bytes 196616 | tf_op jit(solution)/shard_map/ppermute | solution.py:296
  18.1 2.2 %split_translation.1.parts_hbm = bf16[15,128,1024]{2,1,0:T(8,128)(2,1)S(1)} custom-call(f32[1,15,64,1024]{3,2,1,0:T(8,128)} %trans_hbm.1), custom_call_target="tpu_custom_call" | custom-call | flops 10000000 | bytes 3932160 | tf_op jit(solution)/shard_map/split_translation/pallas_call | solution.py:31
  22.2 6.6 %all-to-all-done.msg_ref = bf16[16,96,128]{2,1,0:T(8,128)(2,1)S(1)} async-done(((bf16[16,96,128]{2,1,0:T(8,128)(2,1)}), bf16[16,96,128]{2,1,0:T(8,128)(2,1)S(1)}, u32[]{:S(2)}, u32[]{:S(2)}) %all-to-all-start) | async-done | bytes 393248 | tf_op jit(solution)/shard_map/all_to_all | solution.py:300
  28.8 4.3 %other_terms.1 = (bf16[16,32,128]{2,1,0:T(8,128)(2,1)}, bf16[128,64]{1,0:T(8,128)(2,1)S(1)}, f32[8,64,1024]{2,1,0:T(8,128)}) custom-call(bf16[16,96,128]{2,1,0:T(8,128)(2,1)S(1)} %all-to-all-done.msg_ref, bf16[15,128,1024]{2,1,0:T(8,128)(2,1)} %copy-done), custom_call_target="tpu_custom_call" | custom-call | flops 10000000 | bytes 4325376 | tf_op jit(solution)/shard_map/other_terms/pallas_call | solution.py:31
  33.2 4.8 %all-to-all-start.1 = ((bf16[16,32,128]{2,1,0:T(8,128)(2,1)}), bf16[16,32,128]{2,1,0:T(8,128)(2,1)S(1)}, u32[]{:S(2)}, u32[]{:S(2)}) async-start(bf16[16,32,128]{2,1,0:T(8,128)(2,1)} %get-tuple-element.30), calls=%async_computation.1 | async-start | bytes 262144 | tf_op jit(solution)/shard_map/all_to_all | solution.py:300
  38.1 3.2 %collective-permute-start.2 = (bf16[2,2,64,256]{3,2,1,0:T(8,128)(2,1)S(1)}, bf16[2,2,64,256]{3,2,1,0:T(8,128)(2,1)S(1)}, u32[]{:S(2)}, u32[]{:S(2)}) collective-permute-start(bf16[2,2,64,256]{3,2,1,0:T(8,128)(2,1)S(1)} %pad_maximum_fusion.refs_0_), channel_id=1, source_target_pairs={{0,7},{1,0},{2,1},{3,2},{4,3},{5,4},{6,5},{7,6},{8,15},{9,8},{10,9... | collective-permute-start | bytes 393224 | tf_op jit(solution)/shard_map/ppermute | solution.py:308
  41.3 3.0 %own_terms.1.own_ref = bf16[8,64,1024]{2,1,0:T(8,128)(2,1)S(1)} custom-call(bf16[128,64]{1,0:T(8,128)(2,1)S(1)} %get-tuple-element.32.grad_ref, f32[8,64,1024]{2,1,0:T(8,128)S(1)} %collective-permute-done.3.came_ref, bf16[15,128,1024]{2,1,0:T(8,128)(2,1)} %copy-done), custom_call_target="tpu_custom_call" | custom-call | flops 10000000 | bytes 6045696 | tf_op jit(solution)/shard_map/own_terms/pallas_call | solution.py:31
  44.3 2.3 %collective-permute-done.2.refs_7_ = bf16[2,2,64,256]{3,2,1,0:T(8,128)(2,1)S(1)} collective-permute-done((bf16[2,2,64,256]{3,2,1,0:T(8,128)(2,1)S(1)}, bf16[2,2,64,256]{3,2,1,0:T(8,128)(2,1)S(1)}, u32[]{:S(2)}, u32[]{:S(2)}) %collective-permute-start.2) | collective-permute-done | bytes 131104 | tf_op jit(solution)/shard_map/ppermute | solution.py:308
  49.9 5.1 %all-to-all-start.2 = ((bf16[8,2,64,1024]{3,2,1,0:T(8,128)(2,1)}), bf16[8,2,64,1024]{3,2,1,0:T(8,128)(2,1)S(1)}, u32[]{:S(2)}, u32[]{:S(2)}) async-start(bf16[8,2,64,1024]{3,2,1,0:T(8,128)(2,1)} %copy-done.1), calls=%async_computation.2 | async-start | bytes 4194304 | tf_op jit(solution)/shard_map/all_to_all | solution.py:300
  58.3 3.1 %collective-permute-done.4.refs_2_ = bf16[2,2,64,256]{3,2,1,0:T(8,128)(2,1)S(1)} collective-permute-done((bf16[2,2,64,256]{3,2,1,0:T(8,128)(2,1)}, bf16[2,2,64,256]{3,2,1,0:T(8,128)(2,1)S(1)}, u32[]{:S(2)}, u32[]{:S(2)}) %collective-permute-start.4) | collective-permute-done | bytes 131104 | tf_op jit(solution)/shard_map/ppermute | solution.py:308
  61.8 2.8 %collective-permute-start.8 = (bf16[2,2,64,256]{3,2,1,0:T(8,128)(2,1)S(1)}, bf16[2,2,64,256]{3,2,1,0:T(8,128)(2,1)S(1)}, u32[]{:S(2)}, u32[]{:S(2)}) collective-permute-start(bf16[2,2,64,256]{3,2,1,0:T(8,128)(2,1)S(1)} %collective-permute-done.7.refs_6_), channel_id=1, source_target_pairs={{0,7},{1,0},{2,1},{3,2},{4,3},{5,4},{6,5},{7,6},{8,15},{9,8},{10,9... | collective-permute-start | bytes 393224 | tf_op jit(solution)/shard_map/ppermute | solution.py:308
  64.7 2.9 %collective-permute-done.5.refs_3_ = bf16[2,2,64,256]{3,2,1,0:T(8,128)(2,1)S(1)} collective-permute-done((bf16[2,2,64,256]{3,2,1,0:T(8,128)(2,1)S(1)}, bf16[2,2,64,256]{3,2,1,0:T(8,128)(2,1)S(1)}, u32[]{:S(2)}, u32[]{:S(2)}) %collective-permute-start.5) | collective-permute-done | bytes 131104 | tf_op jit(solution)/shard_map/ppermute | solution.py:308
  68.3 5.5 %collective-permute-done.6.refs_4_ = bf16[2,2,64,256]{3,2,1,0:T(8,128)(2,1)S(1)} collective-permute-done((bf16[2,2,64,256]{3,2,1,0:T(8,128)(2,1)S(1)}, bf16[2,2,64,256]{3,2,1,0:T(8,128)(2,1)S(1)}, u32[]{:S(2)}, u32[]{:S(2)}) %collective-permute-start.6) | collective-permute-done | bytes 131104 | tf_op jit(solution)/shard_map/ppermute | solution.py:308
  74.4 4.6 %near.1 = (f32[64,512]{1,0:T(8,128)S(1)}, bf16[8,256,128]{2,1,0:T(8,128)(2,1)}, f32[8,256,128]{2,1,0:T(8,128)S(1)}) custom-call(s32[1]{0:T(128)S(6)} %copy.11.count_ref, s32[32]{0:T(128)S(1)} %copy-done.2, s32[32]{0:T(128)S(1)} %copy-done.3, bf16[2,64,256]{2,1,0:T(8,128)(2,1)S(1)} %get-tuple-element.36.low_ref, bf16[32,256,256]{2,1,0:T(8,128)(2,1)} %tiles_hbm.1, ...), custom_call_target="tpu_custom_call" | custom-call | flops 10000000 | bytes 5308676 | tf_op jit(solution)/shard_map/near/pallas_call | solution.py:31
  80.5 5.1 %collective-permute-start.12 = (bf16[8,256,128]{2,1,0:T(8,128)(2,1)}, bf16[8,256,128]{2,1,0:T(8,128)(2,1)}, u32[]{:S(2)}, u32[]{:S(2)}) collective-permute-start(bf16[8,256,128]{2,1,0:T(8,128)(2,1)} %get-tuple-element.48), channel_id=1, source_target_pairs={{0,8},{8,0},{1,9},{9,1},{2,10},{10,2},{3,11},{11,3},{4,12},{12,4},... | collective-permute-start | bytes 1572872 | tf_op jit(solution)/shard_map/ppermute | solution.py:296
  85.6 4.6 %all-to-all-start.3 = ((bf16[8,64,128]{2,1,0:T(8,128)(2,1)}), bf16[8,64,128]{2,1,0:T(8,128)(2,1)S(1)}, u32[]{:S(2)}, u32[]{:S(2)}) async-start(bf16[8,64,128]{2,1,0:T(8,128)(2,1)} %get-tuple-element.43), calls=%async_computation.3 | async-start | bytes 262144 | tf_op jit(solution)/shard_map/all_to_all | solution.py:300
  90.2 6.6 %forward.1.pot_ref = bf16[32,128]{1,0:T(8,128)(2,1)S(1)} custom-call(bf16[8,64,1024]{2,1,0:T(8,128)(2,1)} %collective-permute-done.9.other_ref, bf16[8,2,64,1024]{3,2,1,0:T(8,128)(2,1)S(1)} %all-to-all-done.2.came_ref, bf16[15,128,1024]{2,1,0:T(8,128)(2,1)} %copy-done), custom_call_target="tpu_custom_call" | custom-call | flops 10000000 | bytes 7077888 | tf_op jit(solution)/shard_map/forward/pallas_call | solution.py:31
  97.3 2.4 %all-to-all-done.3.msg_ref = bf16[8,64,128]{2,1,0:T(8,128)(2,1)S(1)} async-done(((bf16[8,64,128]{2,1,0:T(8,128)(2,1)}), bf16[8,64,128]{2,1,0:T(8,128)(2,1)S(1)}, u32[]{:S(2)}, u32[]{:S(2)}) %all-to-all-start.3) | async-done | bytes 131104 | tf_op jit(solution)/shard_map/all_to_all | solution.py:300
  99.7 2.4 %collective-permute-done.10.mate_pot_ref = bf16[32,128]{1,0:T(8,128)(2,1)S(1)} collective-permute-done((bf16[32,128]{1,0:T(8,128)(2,1)S(1)}, bf16[32,128]{1,0:T(8,128)(2,1)S(1)}, u32[]{:S(2)}, u32[]{:S(2)}) %collective-permute-start.10) | collective-permute-done | bytes 8224 | tf_op jit(solution)/shard_map/ppermute | solution.py:296
  102.6 5.1 %collective-permute-done.11.mate_ref = f32[64,128]{1,0:T(8,128)S(1)} collective-permute-done((f32[64,128]{1,0:T(8,128)S(1)}, f32[64,128]{1,0:T(8,128)S(1)}, u32[]{:S(2)}, u32[]{:S(2)}) %collective-permute-start.11) | collective-permute-done | bytes 32800 | tf_op jit(solution)/shard_map/ppermute | solution.py:296
  108.8 27.6 %all_to_all.25.msg_ref = bf16[8,384,128]{2,1,0:T(8,128)(2,1)S(1)} all-to-all(bf16[8,384,128]{2,1,0:T(8,128)(2,1)S(1)} %last_message.1), channel_id=1, replica_groups=mesh['xlo'=2,'y'=4,'core'=2,'xhi'=2,'z'=8] {'z'}, dimensions={0} | all-to-all | bytes 1572864 | tf_op jit(solution)/shard_map/all_to_all | solution.py:300
  136.4 2.5 %finish.1 = (f32[64,512]{1,0:T(8,128)}, f32[64,512]{1,0:T(8,128)}) custom-call(bf16[8,384,128]{2,1,0:T(8,128)(2,1)S(1)} %all_to_all.25.msg_ref, f32[64,512]{1,0:T(8,128)S(1)} %get-tuple-element.49.ahead_ref, bf16[1024,512]{1,0:T(8,128)(2,1)} %skin_hbm.3, bf16[1024,512]{1,0:T(8,128)(2,1)} %skout_hbm.3), custom_call_target="tpu_custom_call" | custom-call | flops 10000000 | bytes 3014656 | tf_op jit(solution)/shard_map/finish/pallas_call | solution.py:31
  (47 shorter events, 13.0 us)
Async XLA Ops:
  3.6 25.2 %all-to-all-start = ((bf16[16,96,128]{2,1,0:T(8,128)(2,1)}), bf16[16,96,128]{2,1,0:T(8,128)(2,1)S(1)}, u32[]{:S(2)}, u32[]{:S(2)}) async-start(bf16[16,96,128]{2,1,0:T(8,128)(2,1)} %get-tuple-element.26), calls=%async_computation | async-start | bytes 786432 | tf_op jit(solution)/shard_map/all_to_all | solution.py:300
  14.7 7.5 %collective-permute-start = (bf16[2,64,256]{2,1,0:T(8,128)(2,1)S(1)}, bf16[2,64,256]{2,1,0:T(8,128)(2,1)S(1)}, u32[]{:S(2)}, u32[]{:S(2)}) collective-permute-start(bf16[2,64,256]{2,1,0:T(8,128)(2,1)S(1)} %get-tuple-element.27), channel_id=1, source_target_pairs={{0,8},{8,0},{1,9},{9,1},{2,10},{10,2},{3,11},{11,3},{4,12},{12,4},... | collective-permute-start | bytes 196616 | tf_op jit(solution)/shard_map/ppermute | solution.py:296
  33.1 8.2 %collective-permute-start.3 = (f32[8,64,1024]{2,1,0:T(8,128)}, f32[8,64,1024]{2,1,0:T(8,128)S(1)}, u32[]{:S(2)}, u32[]{:S(2)}) collective-permute-start(f32[8,64,1024]{2,1,0:T(8,128)} %get-tuple-element.33), channel_id=1, source_target_pairs={{0,16},{16,0},{1,17},{17,1},{2,18},{18,2},{3,19},{19,3},{4,20},{20... | collective-permute-start | bytes 6291464 | tf_op jit(solution)/shard_map/ppermute | solution.py:296
  33.2 15.2 %all-to-all-start.1 = ((bf16[16,32,128]{2,1,0:T(8,128)(2,1)}), bf16[16,32,128]{2,1,0:T(8,128)(2,1)S(1)}, u32[]{:S(2)}, u32[]{:S(2)}) async-start(bf16[16,32,128]{2,1,0:T(8,128)(2,1)} %get-tuple-element.30), calls=%async_computation.1 | async-start | bytes 262144 | tf_op jit(solution)/shard_map/all_to_all | solution.py:300
  38.1 6.2 %copy-start.4 = (bf16[2,2,64,256]{3,2,1,0:T(8,128)(2,1)}, bf16[2,2,64,256]{3,2,1,0:T(8,128)(2,1)S(1)}, u32[]{:S(2)}) copy-start(bf16[2,2,64,256]{3,2,1,0:T(8,128)(2,1)S(1)} %pad_maximum_fusion.refs_0_) | copy-start | bytes 393220
  38.1 8.5 %collective-permute-start.2 = (bf16[2,2,64,256]{3,2,1,0:T(8,128)(2,1)S(1)}, bf16[2,2,64,256]{3,2,1,0:T(8,128)(2,1)S(1)}, u32[]{:S(2)}, u32[]{:S(2)}) collective-permute-start(bf16[2,2,64,256]{3,2,1,0:T(8,128)(2,1)S(1)} %pad_maximum_fusion.refs_0_), channel_id=1, source_target_pairs={{0,7},{1,0},{2,1},{3,2},{4,3},{5,4},{6,5},{7,6},{8,15},{9,8},{10,9... | collective-permute-start | bytes 393224 | tf_op jit(solution)/shard_map/ppermute | solution.py:308
  41.3 7.1 %collective-permute-start.1 = (bf16[2,2,64,256]{3,2,1,0:T(8,128)(2,1)S(1)}, bf16[2,2,64,256]{3,2,1,0:T(8,128)(2,1)}, u32[]{:S(2)}, u32[]{:S(2)}) collective-permute-start(bf16[2,2,64,256]{3,2,1,0:T(8,128)(2,1)S(1)} %pad_maximum_fusion.refs_0_), channel_id=1, source_target_pairs={{0,1},{1,2},{2,3},{3,4},{4,5},{5,6},{6,7},{7,0},{8,9},{9,10},{10,1... | collective-permute-start | bytes 393224 | tf_op jit(solution)/shard_map/ppermute | solution.py:308
  49.9 6.7 %copy-start.6 = (bf16[2,2,64,256]{3,2,1,0:T(8,128)(2,1)S(1)}, bf16[2,2,64,256]{3,2,1,0:T(8,128)(2,1)}, u32[]{:S(2)}) copy-start(bf16[2,2,64,256]{3,2,1,0:T(8,128)(2,1)} %copy-done.5) | copy-start | bytes 393220
  49.9 24.5 %copy-start.2 = (s32[32]{0:T(128)S(1)}, s32[32]{0:T(128)}, u32[]{:S(2)}) copy-start(s32[32]{0:T(128)} %rows_ref.1) | copy-start | bytes 388
  49.9 24.5 %copy-start.3 = (s32[32]{0:T(128)S(1)}, s32[32]{0:T(128)}, u32[]{:S(2)}) copy-start(s32[32]{0:T(128)} %cols_ref.1) | copy-start | bytes 388
  49.9 29.4 %all-to-all-start.2 = ((bf16[8,2,64,1024]{3,2,1,0:T(8,128)(2,1)}), bf16[8,2,64,1024]{3,2,1,0:T(8,128)(2,1)S(1)}, u32[]{:S(2)}, u32[]{:S(2)}) async-start(bf16[8,2,64,1024]{3,2,1,0:T(8,128)(2,1)} %copy-done.1), calls=%async_computation.2 | async-start | bytes 4194304 | tf_op jit(solution)/shard_map/all_to_all | solution.py:300
  55.0 6.4 %collective-permute-start.4 = (bf16[2,2,64,256]{3,2,1,0:T(8,128)(2,1)}, bf16[2,2,64,256]{3,2,1,0:T(8,128)(2,1)S(1)}, u32[]{:S(2)}, u32[]{:S(2)}) collective-permute-start(bf16[2,2,64,256]{3,2,1,0:T(8,128)(2,1)} %collective-permute-done.1.refs_1_), channel_id=1, source_target_pairs={{0,1},{1,2},{2,3},{3,4},{4,5},{5,6},{6,7},{7,0},{8,9},{9,10},{10,1... | collective-permute-start | bytes 393224 | tf_op jit(solution)/shard_map/ppermute | solution.py:308
  56.6 5.2 %collective-permute-start.7 = (bf16[2,2,64,256]{3,2,1,0:T(8,128)(2,1)S(1)}, bf16[2,2,64,256]{3,2,1,0:T(8,128)(2,1)S(1)}, u32[]{:S(2)}, u32[]{:S(2)}) collective-permute-start(bf16[2,2,64,256]{3,2,1,0:T(8,128)(2,1)S(1)} %copy-done.6), channel_id=1, source_target_pairs={{0,7},{1,0},{2,1},{3,2},{4,3},{5,4},{6,5},{7,6},{8,15},{9,8},{10,9... | collective-permute-start | bytes 393224 | tf_op jit(solution)/shard_map/ppermute | solution.py:308
  61.4 12.4 %copy-start.7 = (bf16[2,2,64,256]{3,2,1,0:T(8,128)(2,1)}, bf16[2,2,64,256]{3,2,1,0:T(8,128)(2,1)S(1)}, u32[]{:S(2)}) copy-start(bf16[2,2,64,256]{3,2,1,0:T(8,128)(2,1)S(1)} %collective-permute-done.4.refs_2_) | copy-start | bytes 393220
  61.4 6.2 %collective-permute-start.5 = (bf16[2,2,64,256]{3,2,1,0:T(8,128)(2,1)S(1)}, bf16[2,2,64,256]{3,2,1,0:T(8,128)(2,1)S(1)}, u32[]{:S(2)}, u32[]{:S(2)}) collective-permute-start(bf16[2,2,64,256]{3,2,1,0:T(8,128)(2,1)S(1)} %collective-permute-done.4.refs_2_), channel_id=1, source_target_pairs={{0,1},{1,2},{2,3},{3,4},{4,5},{5,6},{6,7},{7,0},{8,9},{9,10},{10,1... | collective-permute-start | bytes 393224 | tf_op jit(solution)/shard_map/ppermute | solution.py:308
  61.8 12.0 %copy-start.8 = (bf16[2,2,64,256]{3,2,1,0:T(8,128)(2,1)}, bf16[2,2,64,256]{3,2,1,0:T(8,128)(2,1)S(1)}, u32[]{:S(2)}) copy-start(bf16[2,2,64,256]{3,2,1,0:T(8,128)(2,1)S(1)} %collective-permute-done.7.refs_6_) | copy-start | bytes 393220
  61.8 6.4 %collective-permute-start.8 = (bf16[2,2,64,256]{3,2,1,0:T(8,128)(2,1)S(1)}, bf16[2,2,64,256]{3,2,1,0:T(8,128)(2,1)S(1)}, u32[]{:S(2)}, u32[]{:S(2)}) collective-permute-start(bf16[2,2,64,256]{3,2,1,0:T(8,128)(2,1)S(1)} %collective-permute-done.7.refs_6_), channel_id=1, source_target_pairs={{0,7},{1,0},{2,1},{3,2},{4,3},{5,4},{6,5},{7,6},{8,15},{9,8},{10,9... | collective-permute-start | bytes 393224 | tf_op jit(solution)/shard_map/ppermute | solution.py:308
  67.6 6.2 %copy-start.9 = (bf16[2,2,64,256]{3,2,1,0:T(8,128)(2,1)}, bf16[2,2,64,256]{3,2,1,0:T(8,128)(2,1)S(1)}, u32[]{:S(2)}) copy-start(bf16[2,2,64,256]{3,2,1,0:T(8,128)(2,1)S(1)} %collective-permute-done.5.refs_3_) | copy-start | bytes 393220
  67.6 6.2 %collective-permute-start.6 = (bf16[2,2,64,256]{3,2,1,0:T(8,128)(2,1)S(1)}, bf16[2,2,64,256]{3,2,1,0:T(8,128)(2,1)S(1)}, u32[]{:S(2)}, u32[]{:S(2)}) collective-permute-start(bf16[2,2,64,256]{3,2,1,0:T(8,128)(2,1)S(1)} %collective-permute-done.5.refs_3_), channel_id=1, source_target_pairs={{0,1},{1,2},{2,3},{3,4},{4,5},{5,6},{6,7},{7,0},{8,9},{9,10},{10,1... | collective-permute-start | bytes 393224 | tf_op jit(solution)/shard_map/ppermute | solution.py:308
  80.5 9.8 %collective-permute-start.9 = (bf16[8,64,1024]{2,1,0:T(8,128)(2,1)}, bf16[8,64,1024]{2,1,0:T(8,128)(2,1)}, u32[]{:S(2)}, u32[]{:S(2)}) collective-permute-start(bf16[8,64,1024]{2,1,0:T(8,128)(2,1)} %get-tuple-element.44), channel_id=1, source_target_pairs={{0,16},{16,0},{1,17},{17,1},{2,18},{18,2},{3,19},{19,3},{4,20},{20... | collective-permute-start | bytes 3145736 | tf_op jit(solution)/shard_map/ppermute | solution.py:296
  80.5 22.1 %collective-permute-start.12 = (bf16[8,256,128]{2,1,0:T(8,128)(2,1)}, bf16[8,256,128]{2,1,0:T(8,128)(2,1)}, u32[]{:S(2)}, u32[]{:S(2)}) collective-permute-start(bf16[8,256,128]{2,1,0:T(8,128)(2,1)} %get-tuple-element.48), channel_id=1, source_target_pairs={{0,8},{8,0},{1,9},{9,1},{2,10},{10,2},{3,11},{11,3},{4,12},{12,4},... | collective-permute-start | bytes 1572872 | tf_op jit(solution)/shard_map/ppermute | solution.py:296
  85.6 14.1 %all-to-all-start.3 = ((bf16[8,64,128]{2,1,0:T(8,128)(2,1)}), bf16[8,64,128]{2,1,0:T(8,128)(2,1)S(1)}, u32[]{:S(2)}, u32[]{:S(2)}) async-start(bf16[8,64,128]{2,1,0:T(8,128)(2,1)} %get-tuple-element.43), calls=%async_computation.3 | async-start | bytes 262144 | tf_op jit(solution)/shard_map/all_to_all | solution.py:300
  96.9 5.2 %collective-permute-start.10 = (bf16[32,128]{1,0:T(8,128)(2,1)S(1)}, bf16[32,128]{1,0:T(8,128)(2,1)S(1)}, u32[]{:S(2)}, u32[]{:S(2)}) collective-permute-start(bf16[32,128]{1,0:T(8,128)(2,1)S(1)} %forward.1.pot_ref), channel_id=1, source_target_pairs={{0,8},{8,0},{1,9},{9,1},{2,10},{10,2},{3,11},{11,3},{4,12},{12,4},... | collective-permute-start | bytes 24584 | tf_op jit(solution)/shard_map/ppermute | solution.py:296
  102.1 5.5 %collective-permute-start.11 = (f32[64,128]{1,0:T(8,128)S(1)}, f32[64,128]{1,0:T(8,128)S(1)}, u32[]{:S(2)}, u32[]{:S(2)}) collective-permute-start(f32[64,128]{1,0:T(8,128)S(1)} %fold.1.mine_ref), channel_id=1, source_target_pairs={{0,8},{8,0},{1,9},{9,1},{2,10},{10,2},{3,11},{11,3},{4,12},{12,4},... | collective-permute-start | bytes 98312 | tf_op jit(solution)/shard_map/ppermute | solution.py:296
  (5 other events, 10.1 us)

commit v5 on v4

--- a/solution.py
+++ b/solution.py
@@ -26,8 +26,7 @@
     return pl.BlockSpec(memory_space=pltpu.HBM)
 
 
-def call(kernel, outs, args, specs=None, scratch=(), flops=10**7, name=None):
-    moved = sum(a.size * a.dtype.itemsize for a in args)
+def call(kernel, outs, args, specs=None, scratch=(), name=None):
     return pl.pallas_call(
         kernel,
         out_shape=[jax.ShapeDtypeStruct(s, d) for s, d in outs],
@@ -35,7 +34,7 @@
         out_specs=[vmem()] * len(outs),
         scratch_shapes=list(scratch),
         compiler_params=pltpu.CompilerParams(vmem_limit_bytes=20 * 2**20),
-        cost_estimate=pl.CostEstimate(flops=flops, bytes_accessed=moved, transcendentals=0),
+        cost_estimate=pl.CostEstimate(flops=1000, bytes_accessed=1000, transcendentals=0),
         name=name,
     )(*args)
 
@@ -126,16 +125,20 @@
     return pair[:64] + pair[64:] + dot(both[:64], block[64:])
 
 
-def other_terms(msg_ref, parts_hbm, copies_ref, grad_ref, send_ref, blocks, sems):
-    fetched = fetch(parts_hbm, blocks, sems, lags(1 - lax.axis_index("core")))
+def shares(msg_ref, copies_ref, grad_ref):
     share = jnp.sum(msg_ref[:, 0:32, :].astype(f32), axis=0).astype(bf16)
     for piece in range(16):
         copies_ref[piece] = share
     packed = jnp.sum(msg_ref[:, 32:64, :].astype(f32) + msg_ref[:, 64:96, :].astype(f32), axis=0)
     gradient = jnp.concatenate([packed, pltpu.roll(packed, 64, 1)], axis=0)
     high, low = split(gradient.T[:64])
-    both = jnp.concatenate([high, low], axis=0)
-    grad_ref[...] = both
+    grad_ref[:64] = high
+    grad_ref[64:] = low
+
+
+def other_terms(grad_ref, parts_hbm, send_ref, blocks, sems):
+    fetched = fetch(parts_hbm, blocks, sems, lags(1 - lax.axis_index("core")))
+    both = grad_ref[...]
     for index in range(8):
         fetched[index].wait()
         send_ref[index] = term(both, blocks[index])
@@ -186,7 +189,8 @@
 
 def near(count_ref, rows_ref, cols_ref, low_ref, tiles_hbm, *refs):
     pieces, refs = refs[:8], refs[8:]
-    ahead_ref, send_ref, keep_ref, acc, behind, drives, tiles_ref, tile_sems, piece_sems = refs
+    (ahead_ref, far_up, far_down), refs = refs[:3], refs[3:]
+    own_refs, (acc, behind, drives, tiles_ref, tile_sems, piece_sems) = refs[:6], refs[6:]
 
     def tile_copy(index):
         span = pl.ds(index * 4, 4)
@@ -237,19 +241,37 @@
     lax.fori_loop(groups, 8, drain, 0)
     for part in range(2):
         ahead_ref[:, part * 256 : part * 256 + 256] = acc[part]
-    for z in range(8):
-        for part in range(4):
-            rows = pl.ds(part * 64, 64)
-            cols = pl.ds(part % 2 * 128, 128)
-            send_ref[z, rows, :] = behind[(1 - my_half) * 16 + 2 * z + part // 2, :, cols].astype(bf16)
-            keep_ref[z, rows, :] = behind[my_half * 16 + 2 * z + part // 2, :, cols]
+    for ref, offset in zip((far_up, far_down, *own_refs), (4, -3, 3, -2, 2, -1, 1, 0)):
+        owner_z = lax.rem(my_z + offset + 8, 8)
+        for half in range(2):
+            for part in range(4):
+                value = behind[half * 16 + 2 * owner_z + part // 2, :, part % 2 * 128 : part % 2 * 128 + 128]
+                rows = slice(half * 256 + part * 64, half * 256 + part * 64 + 64)
+                ref[rows, :] = value.astype(ref.dtype)
+
+
+def add_two(up_ref, own_up_ref, down_ref, own_down_ref, up_out, down_out):
+    up_out[...] = (up_ref[...].astype(f32) + own_up_ref[...]).astype(bf16)
+    down_out[...] = (down_ref[...].astype(f32) + own_down_ref[...]).astype(bf16)
+
+
+def add_last(up_ref, own_up_ref, down_ref, own_ref, up_out, sum_out):
+    up_out[...] = (up_ref[...].astype(f32) + own_up_ref[...]).astype(bf16)
+    sum_out[...] = down_ref[...].astype(f32) + own_ref[...]
+
+
+def close_ring(up_ref, sum_ref, keep_ref, send_ref):
+    mine = pl.multiple_of(lax.axis_index("xhi") * 256, 256)
+    mates = 256 - mine
+    keep_ref[...] = up_ref[pl.ds(mine, 256), :].astype(f32) + sum_ref[pl.ds(mine, 256), :]
+    send_ref[...] = up_ref[pl.ds(mates, 256), :].astype(f32) + sum_ref[pl.ds(mates, 256), :]
 
 
 def fold(msg_ref, out_ref):
     out_ref[...] = jnp.sum(msg_ref[...].astype(f32), axis=0)
 
 
-def last_message(mine_ref, mate_ref, pot_ref, mate_pot_ref, keep_ref, mate_near_ref, out_ref):
+def last_message(mine_ref, mate_ref, pot_ref, mate_pot_ref, out_ref):
     adjoint = (mine_ref[...] + mate_ref[...]).astype(bf16)
     upper = lax.axis_index("xhi") == 1
     pot = pot_ref[...].astype(f32)
@@ -260,10 +282,9 @@
         out_ref[piece, 0:64, :] = adjoint
         out_ref[piece, 64:96, :] = first
         out_ref[piece, 96:128, :] = second
-        out_ref[piece, 128:384, :] = (keep_ref[piece] + mate_near_ref[piece].astype(f32)).astype(bf16)
-
-
-def finish(msg_ref, ahead_ref, skin_hbm, skout_hbm, resp_ref, sens_ref, skin_ref, skout_ref, sems):
+
+
+def finish(msg_ref, ahead_ref, keep_ref, mate_ref, skin_hbm, skout_hbm, resp_ref, sens_ref, skin_ref, skout_ref, sems):
     first = pltpu.make_async_copy(skin_hbm, skin_ref, sems.at[0])
     second = pltpu.make_async_copy(skout_hbm, skout_ref, sems.at[1])
     first.start()
@@ -277,15 +298,11 @@
     )
     packed = jnp.concatenate([msg_ref[r % 8, 64 + r // 8 * 32 : 96 + r // 8 * 32, :] for r in range(16)], axis=0)
     packed = packed.astype(f32).T.astype(bf16)
-    near_sums = []
-    for part in range(4):
-        rows = slice(128 + part * 64, 192 + part * 64)
-        value = msg_ref[0, rows, :].astype(f32)
-        for source in range(1, 8):
-            value = value + msg_ref[source, rows, :].astype(f32)
-        near_sums.append(value)
+    near_sum = keep_ref[...] + mate_ref[...]
     first.wait()
-    sens_ref[...] = dot(adjoint, skin_ref[...]) + jnp.concatenate(near_sums, axis=1)
+    sens_ref[...] = dot(adjoint, skin_ref[...]) + jnp.concatenate(
+        [near_sum[part * 64 : part * 64 + 64] for part in range(4)], axis=1
+    )
     second.wait()
     upper = jnp.concatenate([skout_ref[r * 64 : r * 64 + 32, :] for r in range(16)], axis=0)
     lower = jnp.concatenate([skout_ref[r * 64 + 32 : r * 64 + 64, :] for r in range(16)], axis=0)
@@ -333,18 +350,21 @@
         name="split_translation",
     )
     parts = in_hbm(parts)
-    msg, mate, parts = tie(exchange(msg, ROWS), mate, parts)
+    here = jnp.stack([drive, mate])
+    up1, down1 = shift(here, 1), shift(here, -1)
+    msg, up1, down1, parts = tie(exchange(msg, ROWS), up1, down1, parts)
+    copies, gradient = call(
+        shares, [((16, 32, 128), bf16), ((128, 64), bf16)], [msg], name="shares"
+    )
     blocks = [pltpu.VMEM((8, 128, 1024), bf16), pltpu.SemaphoreType.DMA((8,))]
-    copies, gradient, send = call(
+    (send,) = call(
         other_terms,
-        [((16, 32, 128), bf16), ((128, 64), bf16), ((8, 64, 1024), f32)],
-        [msg, parts],
+        [((8, 64, 1024), f32)],
+        [gradient, parts],
         specs=[vmem(), hbm()],
         scratch=blocks,
         name="other_terms",
     )
-    here = jnp.stack([drive, mate])
-    up1, down1 = shift(here, 1), shift(here, -1)
     (own,) = call(
         own_terms,
         [((8, 64, 1024), bf16)],
@@ -353,14 +373,15 @@
         scratch=blocks,
         name="own_terms",
     )
-    copies, up1, down1, own = tie(exchange(copies, ROWS), up1, down1, own)
-    (both,) = call(pack, [((8, 2, 64, 1024), bf16)], [own, copies], name="pack")
     up2, down2 = shift(up1, 1), shift(down1, -1)
     up3, down3 = shift(up2, 1), shift(down2, -1)
     up4 = shift(up3, 1)
-    ahead, send, keep = call(
+    copies, up4, down3, own = tie(exchange(copies, ROWS), up4, down3, own)
+    (both,) = call(pack, [((8, 2, 64, 1024), bf16)], [own, copies], name="pack")
+    chunk = (512, 128)
+    ahead, ring_up, ring_down, own3, own_2, own2, own_1, own1, own0 = call(
         near,
-        [((64, 512), f32), ((8, 256, 128), bf16), ((8, 256, 128), f32)],
+        [((64, 512), f32), (chunk, bf16), (chunk, bf16)] + [(chunk, f32)] * 6,
         [tile_count, tile_rows, tile_cols, low, in_hbm(tiles)]
         + [in_hbm(piece) for piece in (here, up1, up2, up3, up4, down3, down2, down1)],
         specs=[smem(), smem(), smem(), vmem()] + [hbm()] * 9,
@@ -374,7 +395,22 @@
         ],
         name="near",
     )
-    both, ahead, send, keep = tie(exchange(both, FACE), ahead, send, keep)
+    for own_up, own_down in ((own3, own_2), (own2, own_1)):
+        ring_up, ring_down = call(
+            add_two,
+            [(chunk, bf16)] * 2,
+            [shift(ring_up, 1), own_up, shift(ring_down, -1), own_down],
+            name="add_two",
+        )
+    ring_up, near_sum = call(
+        add_last,
+        [(chunk, bf16), (chunk, f32)],
+        [shift(ring_up, 1), own1, shift(ring_down, -1), own0],
+        name="add_last",
+    )
+    ring_up = shift(ring_up, 1)
+    both, ahead, ring_up, near_sum = tie(exchange(both, FACE), ahead, ring_up, near_sum)
+    keep, send = call(close_ring, [((256, 128), f32)] * 2, [ring_up, near_sum], name="close_ring")
     mate_near = swap(send, "xhi")
     adjoint, charges = call(
         unpack,
@@ -392,20 +428,20 @@
         name="forward",
     )
     mate_pot = swap(potential, "xhi")
-    adjoint, mate_pot = tie(exchange(adjoint, "z"), mate_pot)
+    adjoint, mate_pot, mate_near = tie(exchange(adjoint, "z"), mate_pot, mate_near)
     (mine,) = call(fold, [((64, 128), f32)], [adjoint], name="fold")
     (last,) = call(
         last_message,
-        [((8, 384, 128), bf16)],
-        [mine, swap(mine, "xhi"), potential, mate_pot, keep, mate_near],
+        [((8, 128, 128), bf16)],
+        [mine, swap(mine, "xhi"), potential, mate_pot],
         name="last_message",
     )
     return tuple(
         call(
             finish,
             [((64, 512), f32), ((64, 512), f32)],
-            [exchange(last, "z"), ahead, in_hbm(skin), in_hbm(skout)],
-            specs=[vmem()] * 2 + [hbm()] * 2,
+            [exchange(last, "z"), ahead, keep, mate_near, in_hbm(skin), in_hbm(skout)],
+            specs=[vmem()] * 4 + [hbm()] * 2,
             scratch=[pltpu.VMEM((1024, 512), bf16)] * 2 + [pltpu.SemaphoreType.DMA((2,))],
             name="finish",
         )

time: 140 us -> 152 us (1.086)
  starting transfers between devices: 44.8 us -> 56.7 us
  blocking collectives: 27.6 us -> 17.4 us
  waiting for transfers between devices: 31.8 us -> 40.5 us
  local copies, waits for them, and re-layouts: 4.53 us -> 7.3 us
  Pallas kernels: 28.8 us -> 26.4 us
    ppermute x7 -> x14, starting transfers between devices: 9.69 us -> 21.1 us  [shift(): return lax.ppermute(value, 'z', [(i, (i + step) % 8) for i in range(8)])]
    all_to_all x1, blocking collectives: 27.6 us -> 17.4 us  [exchange(): return lax.all_to_all(value, axes, 0, 0, tiled=True)]
    ppermute x7 -> x14, waiting for transfers between devices: 15 us -> 23.5 us  [shift(): return lax.ppermute(value, 'z', [(i, (i + step) % 8) for i in range(8)])]
    ppermute x6, waiting for transfers between devices: 7.54 us -> 12.6 us  [swap(): return lax.ppermute(value, axis, [(0, 1), (1, 0)])]
    all_to_all x4, waiting for transfers between devices: 9.25 us -> 4.43 us  [exchange(): return lax.all_to_all(value, axes, 0, 0, tiled=True)]
    unnamed x24 -> x34, local copies, waits for them, and re-layouts: 4.53 us -> 7.3 us
    pallas_call x11 -> x16, Pallas kernels: 28.8 us -> 26.4 us  [call(): pl.pallas_call(kernel, out_shape=[jax.ShapeDtypeStruct(s, d) for s, d in...]
    all_to_all x4, starting transfers between devices: 25.6 us -> 28 us  [exchange(): return lax.all_to_all(value, axes, 0, 0, tiled=True)]
  transfers between devices with their start and end apart: 17 -> 24, of which waited for: 10 -> 13; matrix products, arithmetic and copies ran while one was open for 0% -> 0% of each run, Pallas kernels for 12% -> 10%
where the time goes in v5:
time: 152 us; the launch traced here: 150 us
  starting transfers between devices  56.7 us (37%)
  waiting for transfers between devices  40.5 us (27%)
  Pallas kernels  26.4 us (17%)
  blocking collectives  17.4 us (11%)
  local copies, waits for them, and re-layouts  7.3 us (5%)
  between operations  1.72 us (1%)
    all_to_all x4, starting transfers between devices, exchange(): return lax.all_to_all(value, axes, 0, 0, tiled=True)  28 us
    pallas_call x16, Pallas kernels, call(): pl.pallas_call(kernel, out_shape=[jax.ShapeDtypeStruct(s, d) for s, d in...  26.4 us
    ppermute x14, waiting for transfers between devices, shift(): return lax.ppermute(value, 'z', [(i, (i + step) % 8) for i in range(8)])  23.5 us
    ppermute x14, starting transfers between devices, shift(): return lax.ppermute(value, 'z', [(i, (i + step) % 8) for i in range(8)])  21.1 us
    all_to_all x1, blocking collectives, exchange(): return lax.all_to_all(value, axes, 0, 0, tiled=True)  17.4 us
    ppermute x6, waiting for transfers between devices, swap(): return lax.ppermute(value, axis, [(0, 1), (1, 0)])  12.6 us
    ppermute x6, starting transfers between devices, swap(): return lax.ppermute(value, axis, [(0, 1), (1, 0)])  7.61 us
    unnamed x34, local copies, waits for them, and re-layouts  7.3 us
  transfers between devices with their start and end apart: 24, of which 13 were waited for; matrix products, arithmetic and copies ran while one was open for 0% of the time, Pallas kernels for 10%

profile of v5, /device:TPU:8, one launch (start us, length us, event | category | flops | bytes accessed | tf_op | source)
XLA Modules:
  0.0 150.0 jit_solution(13772251646604517428)
XLA Ops:
  0.6 3.0 %prepare.1 = (bf16[2,64,256]{2,1,0:T(8,128)(2,1)S(1)}, bf16[2,64,256]{2,1,0:T(8,128)(2,1)S(1)}, bf16[16,96,128]{2,1,0:T(8,128)(2,1)}) custom-call(f32[64,512]{1,0:T(8,128)} %exc_hbm.1, f32[64,512]{1,0:T(8,128)} %loads_hbm.1, bf16[1024,512]{1,0:T(8,128)(2,1)} %skin_hbm.3, bf16[1024,512]{1,0:T(8,128)(2,1)} %skout_hbm.3), custom_call_target="tpu_custom_call" | custom-call | flops 1000 | bytes 1000 | tf_op jit(solution)/shard_map/prepare/pallas_call | solution.py:30
  3.6 11.0 %all-to-all-start = ((bf16[16,96,128]{2,1,0:T(8,128)(2,1)}), bf16[16,96,128]{2,1,0:T(8,128)(2,1)S(1)}, u32[]{:S(2)}, u32[]{:S(2)}) async-start(bf16[16,96,128]{2,1,0:T(8,128)(2,1)} %get-tuple-element.41), calls=%async_computation | async-start | bytes 786432 | tf_op jit(solution)/shard_map/all_to_all | solution.py:317
  14.7 3.4 %collective-permute-start = (bf16[2,64,256]{2,1,0:T(8,128)(2,1)S(1)}, bf16[2,64,256]{2,1,0:T(8,128)(2,1)S(1)}, u32[]{:S(2)}, u32[]{:S(2)}) collective-permute-start(bf16[2,64,256]{2,1,0:T(8,128)(2,1)S(1)} %get-tuple-element.42), channel_id=1, source_target_pairs={{0,8},{8,0},{1,9},{9,1},{2,10},{10,2},{3,11},{11,3},{4,12},{12,4},... | collective-permute-start | bytes 196616 | tf_op jit(solution)/shard_map/ppermute | solution.py:313
  18.1 3.2 %collective-permute-done = bf16[2,64,256]{2,1,0:T(8,128)(2,1)S(1)} collective-permute-done((bf16[2,64,256]{2,1,0:T(8,128)(2,1)S(1)}, bf16[2,64,256]{2,1,0:T(8,128)(2,1)S(1)}, u32[]{:S(2)}, u32[]{:S(2)}) %collective-permute-start) | collective-permute-done | bytes 65568 | tf_op jit(solution)/shard_map/ppermute | solution.py:313
  30.4 4.3 %other_terms.1 = f32[8,64,1024]{2,1,0:T(8,128)} custom-call(bf16[128,64]{1,0:T(8,128)(2,1)S(1)} %get-tuple-element.47.grad_ref, bf16[15,128,1024]{2,1,0:T(8,128)(2,1)} %copy-done), custom_call_target="tpu_custom_call" | custom-call | flops 1000 | bytes 1000 | tf_op jit(solution)/shard_map/other_terms/pallas_call | solution.py:30
  38.2 3.8 %collective-permute-done.3.refs_2_ = bf16[2,2,64,256]{3,2,1,0:T(8,128)(2,1)S(1)} collective-permute-done((bf16[2,2,64,256]{3,2,1,0:T(8,128)(2,1)S(1)}, bf16[2,2,64,256]{3,2,1,0:T(8,128)(2,1)S(1)}, u32[]{:S(2)}, u32[]{:S(2)}) %collective-permute-start.3) | collective-permute-done | bytes 131104 | tf_op jit(solution)/shard_map/ppermute | solution.py:325
  42.4 8.5 %all-to-all-start.1 = ((bf16[16,32,128]{2,1,0:T(8,128)(2,1)}), bf16[16,32,128]{2,1,0:T(8,128)(2,1)S(1)}, u32[]{:S(2)}, u32[]{:S(2)}) async-start(bf16[16,32,128]{2,1,0:T(8,128)(2,1)} %get-tuple-element.44), calls=%async_computation.1 | async-start | bytes 262144 | tf_op jit(solution)/shard_map/all_to_all | solution.py:317
  50.9 3.2 %collective-permute-start.7 = (bf16[2,2,64,256]{3,2,1,0:T(8,128)(2,1)}, bf16[2,2,64,256]{3,2,1,0:T(8,128)(2,1)}, u32[]{:S(2)}, u32[]{:S(2)}) collective-permute-start(bf16[2,2,64,256]{3,2,1,0:T(8,128)(2,1)} %collective-permute-done.6.refs_6_), channel_id=1, source_target_pairs={{0,7},{1,0},{2,1},{3,2},{4,3},{5,4},{6,5},{7,6},{8,15},{9,8},{10,9... | collective-permute-start | bytes 393224 | tf_op jit(solution)/shard_map/ppermute | solution.py:325
  54.2 3.0 %own_terms.1.own_ref = bf16[8,64,1024]{2,1,0:T(8,128)(2,1)S(1)} custom-call(bf16[128,64]{1,0:T(8,128)(2,1)S(1)} %get-tuple-element.47.grad_ref, f32[8,64,1024]{2,1,0:T(8,128)S(1)} %collective-permute-done.8.came_ref, bf16[15,128,1024]{2,1,0:T(8,128)(2,1)} %copy-done), custom_call_target="tpu_custom_call" | custom-call | flops 1000 | bytes 1000 | tf_op jit(solution)/shard_map/own_terms/pallas_call | solution.py:30
  57.2 4.1 %all-to-all-done.1.pieces_ref = bf16[16,32,128]{2,1,0:T(8,128)(2,1)S(1)} async-done(((bf16[16,32,128]{2,1,0:T(8,128)(2,1)}), bf16[16,32,128]{2,1,0:T(8,128)(2,1)S(1)}, u32[]{:S(2)}, u32[]{:S(2)}) %all-to-all-start.1) | async-done | bytes 131104 | tf_op jit(solution)/shard_map/all_to_all | solution.py:317
  62.9 5.1 %all-to-all-start.2 = ((bf16[8,2,64,1024]{3,2,1,0:T(8,128)(2,1)}), bf16[8,2,64,1024]{3,2,1,0:T(8,128)(2,1)S(1)}, u32[]{:S(2)}, u32[]{:S(2)}) async-start(bf16[8,2,64,1024]{3,2,1,0:T(8,128)(2,1)} %copy-done.1), calls=%async_computation.2 | async-start | bytes 4194304 | tf_op jit(solution)/shard_map/all_to_all | solution.py:317
  68.7 3.6 %near.1 = (f32[64,512]{1,0:T(8,128)S(1)}, bf16[512,128]{1,0:T(8,128)(2,1)S(1)}, bf16[512,128]{1,0:T(8,128)(2,1)S(1)}, f32[512,128]{1,0:T(8,128)S(1)}, f32[512,12...) custom-call(s32[1]{0:T(128)S(6)} %copy.11.count_ref, ...), custom_call_target="tpu_custom_call" | custom-call | flops 1000 | bytes 1000 | tf_op jit(solution)/shard_map/near/pallas_call | solution.py:30
  76.4 2.7 %collective-permute-done.10.down_ref = bf16[512,128]{1,0:T(8,128)(2,1)S(1)} collective-permute-done((bf16[512,128]{1,0:T(8,128)(2,1)S(1)}, bf16[512,128]{1,0:T(8,128)(2,1)S(1)}, u32[]{:S(2)}, u32[]{:S(2)}) %collective-permute-start.10) | collective-permute-done | bytes 131104 | tf_op jit(solution)/shard_map/ppermute | solution.py:325
  83.9 3.4 %collective-permute-done.11.up_ref = bf16[512,128]{1,0:T(8,128)(2,1)S(1)} collective-permute-done((bf16[512,128]{1,0:T(8,128)(2,1)S(1)}, bf16[512,128]{1,0:T(8,128)(2,1)S(1)}, u32[]{:S(2)}, u32[]{:S(2)}) %collective-permute-start.11) | collective-permute-done | bytes 131104 | tf_op jit(solution)/shard_map/ppermute | solution.py:325
  89.2 3.2 %collective-permute-start.14 = (bf16[512,128]{1,0:T(8,128)(2,1)S(1)}, bf16[512,128]{1,0:T(8,128)(2,1)S(1)}, u32[]{:S(2)}, u32[]{:S(2)}) collective-permute-start(bf16[512,128]{1,0:T(8,128)(2,1)S(1)} %get-tuple-element.65), channel_id=1, source_target_pairs={{0,7},{1,0},{2,1},{3,2},{4,3},{5,4},{6,5},{7,6},{8,15},{9,8},{10,9... | collective-permute-start | bytes 393224 | tf_op jit(solution)/shard_map/ppermute | solution.py:325
  92.4 3.6 %collective-permute-done.13.up_ref = bf16[512,128]{1,0:T(8,128)(2,1)S(1)} collective-permute-done((bf16[512,128]{1,0:T(8,128)(2,1)S(1)}, bf16[512,128]{1,0:T(8,128)(2,1)S(1)}, u32[]{:S(2)}, u32[]{:S(2)}) %collective-permute-start.13) | collective-permute-done | bytes 131104 | tf_op jit(solution)/shard_map/ppermute | solution.py:325
  96.2 6.2 %collective-permute-done.15.up_ref = bf16[512,128]{1,0:T(8,128)(2,1)S(1)} collective-permute-done((bf16[512,128]{1,0:T(8,128)(2,1)S(1)}, bf16[512,128]{1,0:T(8,128)(2,1)S(1)}, u32[]{:S(2)}, u32[]{:S(2)}) %collective-permute-start.15) | collective-permute-done | bytes 131104 | tf_op jit(solution)/shard_map/ppermute | solution.py:325
  104.2 3.4 %all-to-all-start.3 = ((bf16[8,64,128]{2,1,0:T(8,128)(2,1)}), bf16[8,64,128]{2,1,0:T(8,128)(2,1)S(1)}, u32[]{:S(2)}, u32[]{:S(2)}) async-start(bf16[8,64,128]{2,1,0:T(8,128)(2,1)} %copy-done.4), calls=%async_computation.3 | async-start | bytes 262144 | tf_op jit(solution)/shard_map/all_to_all | solution.py:317
  108.5 3.3 %collective-permute-start.18 = (f32[256,128]{1,0:T(8,128)S(1)}, f32[256,128]{1,0:T(8,128)S(1)}, u32[]{:S(2)}, u32[]{:S(2)}) collective-permute-start(f32[256,128]{1,0:T(8,128)S(1)} %get-tuple-element.74), channel_id=1, source_target_pairs={{0,8},{8,0},{1,9},{9,1},{2,10},{10,2},{3,11},{11,3},{4,12},{12,4},... | collective-permute-start | bytes 393224 | tf_op jit(solution)/shard_map/ppermute | solution.py:313
  111.8 5.4 %forward.1.pot_ref = bf16[32,128]{1,0:T(8,128)(2,1)S(1)} custom-call(bf16[8,64,1024]{2,1,0:T(8,128)(2,1)S(1)} %collective-permute-done.16.other_ref, bf16[8,2,64,1024]{3,2,1,0:T(8,128)(2,1)S(1)} %all-to-all-done.2.came_ref, bf16[15,128,1024]{2,1,0:T(8,128)(2,1)} %copy-done), custom_call_target="tpu_custom_call" | custom-call | flops 1000 | bytes 1000 | tf_op jit(solution)/shard_map/forward/pallas_call | solution.py:30
  118.3 4.2 %collective-permute-done.17.mate_pot_ref = bf16[32,128]{1,0:T(8,128)(2,1)S(1)} collective-permute-done((bf16[32,128]{1,0:T(8,128)(2,1)S(1)}, bf16[32,128]{1,0:T(8,128)(2,1)S(1)}, u32[]{:S(2)}, u32[]{:S(2)}) %collective-permute-start.17) | collective-permute-done | bytes 8224 | tf_op jit(solution)/shard_map/ppermute | solution.py:313
  122.9 5.1 %collective-permute-done.19.mate_ref = f32[64,128]{1,0:T(8,128)S(1)} collective-permute-done((f32[64,128]{1,0:T(8,128)S(1)}, f32[64,128]{1,0:T(8,128)S(1)}, u32[]{:S(2)}, u32[]{:S(2)}) %collective-permute-start.19) | collective-permute-done | bytes 32800 | tf_op jit(solution)/shard_map/ppermute | solution.py:313
  128.1 17.4 %all_to_all.25.msg_ref = bf16[8,128,128]{2,1,0:T(8,128)(2,1)S(1)} all-to-all(bf16[8,128,128]{2,1,0:T(8,128)(2,1)S(1)} %last_message.1), channel_id=1, replica_groups=mesh['xlo'=2,'y'=4,'core'=2,'xhi'=2,'z'=8] {'z'}, dimensions={0} | all-to-all | bytes 524288 | tf_op jit(solution)/shard_map/all_to_all | solution.py:317
  147.3 2.5 %finish.1 = (f32[64,512]{1,0:T(8,128)}, f32[64,512]{1,0:T(8,128)}) custom-call(bf16[8,128,128]{2,1,0:T(8,128)(2,1)S(1)} %all_to_all.25.msg_ref, f32[64,512]{1,0:T(8,128)S(1)} %copy-done.6, f32[256,128]{1,0:T(8,128)S(1)} %copy-done.8, f32[256,128]{1,0:T(8,128)S(1)} %copy-done.10, bf16[1024,512]{1,0:T(8,128)(2,1)} %skin_hbm.3, bf16[1024,512]{1,0:T(8,128)(2,1)} %skout_hbm.3), custom_call_target="tpu_custom_call" | custom-call | flops 1000 | bytes 1000 | tf_op jit(solution)/shard_map/finish/pallas_call | solution.py:30
  (76 shorter events, 31.4 us)
Async XLA Ops:
  3.6 26.0 %all-to-all-start = ((bf16[16,96,128]{2,1,0:T(8,128)(2,1)}), bf16[16,96,128]{2,1,0:T(8,128)(2,1)S(1)}, u32[]{:S(2)}, u32[]{:S(2)}) async-start(bf16[16,96,128]{2,1,0:T(8,128)(2,1)} %get-tuple-element.41), calls=%async_computation | async-start | bytes 786432 | tf_op jit(solution)/shard_map/all_to_all | solution.py:317
  14.7 6.7 %collective-permute-start = (bf16[2,64,256]{2,1,0:T(8,128)(2,1)S(1)}, bf16[2,64,256]{2,1,0:T(8,128)(2,1)S(1)}, u32[]{:S(2)}, u32[]{:S(2)}) collective-permute-start(bf16[2,64,256]{2,1,0:T(8,128)(2,1)S(1)} %get-tuple-element.42), channel_id=1, source_target_pairs={{0,8},{8,0},{1,9},{9,1},{2,10},{10,2},{3,11},{11,3},{4,12},{12,4},... | collective-permute-start | bytes 196616 | tf_op jit(solution)/shard_map/ppermute | solution.py:313
  21.4 8.0 %collective-permute-start.1 = (bf16[2,2,64,256]{3,2,1,0:T(8,128)(2,1)S(1)}, bf16[2,2,64,256]{3,2,1,0:T(8,128)(2,1)S(1)}, u32[]{:S(2)}, u32[]{:S(2)}) collective-permute-start(bf16[2,2,64,256]{3,2,1,0:T(8,128)(2,1)S(1)} %pad_maximum_fusion.refs_0_), channel_id=1, source_target_pairs={{0,1},{1,2},{2,3},{3,4},{4,5},{5,6},{6,7},{7,0},{8,9},{9,10},{10,1... | collective-permute-start | bytes 393224 | tf_op jit(solution)/shard_map/ppermute | solution.py:325
  23.0 6.4 %collective-permute-start.2 = (bf16[2,2,64,256]{3,2,1,0:T(8,128)(2,1)S(1)}, bf16[2,2,64,256]{3,2,1,0:T(8,128)(2,1)S(1)}, u32[]{:S(2)}, u32[]{:S(2)}) collective-permute-start(bf16[2,2,64,256]{3,2,1,0:T(8,128)(2,1)S(1)} %pad_maximum_fusion.refs_0_), channel_id=1, source_target_pairs={{0,7},{1,0},{2,1},{3,2},{4,3},{5,4},{6,5},{7,6},{8,15},{9,8},{10,9... | collective-permute-start | bytes 393224 | tf_op jit(solution)/shard_map/ppermute | solution.py:325
  34.8 19.4 %collective-permute-start.8 = (f32[8,64,1024]{2,1,0:T(8,128)}, f32[8,64,1024]{2,1,0:T(8,128)S(1)}, u32[]{:S(2)}, u32[]{:S(2)}) collective-permute-start(f32[8,64,1024]{2,1,0:T(8,128)} %other_terms.1), channel_id=1, source_target_pairs={{0,16},{16,0},{1,17},{17,1},{2,18},{18,2},{3,19},{19,3},{4,20},{20... | collective-permute-start | bytes 6291464 | tf_op jit(solution)/shard_map/ppermute | solution.py:313
  34.9 7.2 %collective-permute-start.3 = (bf16[2,2,64,256]{3,2,1,0:T(8,128)(2,1)S(1)}, bf16[2,2,64,256]{3,2,1,0:T(8,128)(2,1)S(1)}, u32[]{:S(2)}, u32[]{:S(2)}) collective-permute-start(bf16[2,2,64,256]{3,2,1,0:T(8,128)(2,1)S(1)} %collective-permute-done.1.refs_1_), channel_id=1, source_target_pairs={{0,1},{1,2},{2,3},{3,4},{4,5},{5,6},{6,7},{7,0},{8,9},{9,10},{10,1... | collective-permute-start | bytes 393224 | tf_op jit(solution)/shard_map/ppermute | solution.py:325
  36.6 14.3 %collective-permute-start.6 = (bf16[2,2,64,256]{3,2,1,0:T(8,128)(2,1)S(1)}, bf16[2,2,64,256]{3,2,1,0:T(8,128)(2,1)}, u32[]{:S(2)}, u32[]{:S(2)}) collective-permute-start(bf16[2,2,64,256]{3,2,1,0:T(8,128)(2,1)S(1)} %collective-permute-done.2.refs_7_), channel_id=1, source_target_pairs={{0,7},{1,0},{2,1},{3,2},{4,3},{5,4},{6,5},{7,6},{8,15},{9,8},{10,9... | collective-permute-start | bytes 393224 | tf_op jit(solution)/shard_map/ppermute | solution.py:325
  42.0 12.1 %collective-permute-start.4 = (bf16[2,2,64,256]{3,2,1,0:T(8,128)(2,1)S(1)}, bf16[2,2,64,256]{3,2,1,0:T(8,128)(2,1)}, u32[]{:S(2)}, u32[]{:S(2)}) collective-permute-start(bf16[2,2,64,256]{3,2,1,0:T(8,128)(2,1)S(1)} %collective-permute-done.3.refs_2_), channel_id=1, source_target_pairs={{0,1},{1,2},{2,3},{3,4},{4,5},{5,6},{6,7},{7,0},{8,9},{9,10},{10,1... | collective-permute-start | bytes 393224 | tf_op jit(solution)/shard_map/ppermute | solution.py:325
  42.4 18.9 %all-to-all-start.1 = ((bf16[16,32,128]{2,1,0:T(8,128)(2,1)}), bf16[16,32,128]{2,1,0:T(8,128)(2,1)S(1)}, u32[]{:S(2)}, u32[]{:S(2)}) async-start(bf16[16,32,128]{2,1,0:T(8,128)(2,1)} %get-tuple-element.44), calls=%async_computation.1 | async-start | bytes 262144 | tf_op jit(solution)/shard_map/all_to_all | solution.py:317
  50.9 10.4 %collective-permute-start.7 = (bf16[2,2,64,256]{3,2,1,0:T(8,128)(2,1)}, bf16[2,2,64,256]{3,2,1,0:T(8,128)(2,1)}, u32[]{:S(2)}, u32[]{:S(2)}) collective-permute-start(bf16[2,2,64,256]{3,2,1,0:T(8,128)(2,1)} %collective-permute-done.6.refs_6_), channel_id=1, source_target_pairs={{0,7},{1,0},{2,1},{3,2},{4,3},{5,4},{6,5},{7,6},{8,15},{9,8},{10,9... | collective-permute-start | bytes 393224 | tf_op jit(solution)/shard_map/ppermute | solution.py:325
  54.1 7.2 %collective-permute-start.5 = (bf16[2,2,64,256]{3,2,1,0:T(8,128)(2,1)}, bf16[2,2,64,256]{3,2,1,0:T(8,128)(2,1)}, u32[]{:S(2)}, u32[]{:S(2)}) collective-permute-start(bf16[2,2,64,256]{3,2,1,0:T(8,128)(2,1)} %collective-permute-done.4.refs_3_), channel_id=1, source_target_pairs={{0,1},{1,2},{2,3},{3,4},{4,5},{5,6},{6,7},{7,0},{8,9},{9,10},{10,1... | collective-permute-start | bytes 393224 | tf_op jit(solution)/shard_map/ppermute | solution.py:325
  62.9 39.4 %all-to-all-start.2 = ((bf16[8,2,64,1024]{3,2,1,0:T(8,128)(2,1)}), bf16[8,2,64,1024]{3,2,1,0:T(8,128)(2,1)S(1)}, u32[]{:S(2)}, u32[]{:S(2)}) async-start(bf16[8,2,64,1024]{3,2,1,0:T(8,128)(2,1)} %copy-done.1), calls=%async_computation.2 | async-start | bytes 4194304 | tf_op jit(solution)/shard_map/all_to_all | solution.py:317
  72.2 6.9 %collective-permute-start.10 = (bf16[512,128]{1,0:T(8,128)(2,1)S(1)}, bf16[512,128]{1,0:T(8,128)(2,1)S(1)}, u32[]{:S(2)}, u32[]{:S(2)}) collective-permute-start(bf16[512,128]{1,0:T(8,128)(2,1)S(1)} %get-tuple-element.57), channel_id=1, source_target_pairs={{0,7},{1,0},{2,1},{3,2},{4,3},{5,4},{6,5},{7,6},{8,15},{9,8},{10,9... | collective-permute-start | bytes 393224 | tf_op jit(solution)/shard_map/ppermute | solution.py:325
  74.4 6.2 %collective-permute-start.9 = (bf16[512,128]{1,0:T(8,128)(2,1)S(1)}, bf16[512,128]{1,0:T(8,128)(2,1)S(1)}, u32[]{:S(2)}, u32[]{:S(2)}) collective-permute-start(bf16[512,128]{1,0:T(8,128)(2,1)S(1)} %get-tuple-element.55), channel_id=1, source_target_pairs={{0,1},{1,2},{2,3},{3,4},{4,5},{5,6},{6,7},{7,0},{8,9},{9,10},{10,1... | collective-permute-start | bytes 393224 | tf_op jit(solution)/shard_map/ppermute | solution.py:325
  80.6 6.7 %collective-permute-start.11 = (bf16[512,128]{1,0:T(8,128)(2,1)S(1)}, bf16[512,128]{1,0:T(8,128)(2,1)S(1)}, u32[]{:S(2)}, u32[]{:S(2)}) collective-permute-start(bf16[512,128]{1,0:T(8,128)(2,1)S(1)} %get-tuple-element.59), channel_id=1, source_target_pairs={{0,1},{1,2},{2,3},{3,4},{4,5},{5,6},{6,7},{7,0},{8,9},{9,10},{10,1... | collective-permute-start | bytes 393224 | tf_op jit(solution)/shard_map/ppermute | solution.py:325
  82.8 6.2 %collective-permute-start.12 = (bf16[512,128]{1,0:T(8,128)(2,1)S(1)}, bf16[512,128]{1,0:T(8,128)(2,1)S(1)}, u32[]{:S(2)}, u32[]{:S(2)}) collective-permute-start(bf16[512,128]{1,0:T(8,128)(2,1)S(1)} %get-tuple-element.61), channel_id=1, source_target_pairs={{0,7},{1,0},{2,1},{3,2},{4,3},{5,4},{6,5},{7,6},{8,15},{9,8},{10,9... | collective-permute-start | bytes 393224 | tf_op jit(solution)/shard_map/ppermute | solution.py:325
  89.1 6.9 %collective-permute-start.13 = (bf16[512,128]{1,0:T(8,128)(2,1)S(1)}, bf16[512,128]{1,0:T(8,128)(2,1)S(1)}, u32[]{:S(2)}, u32[]{:S(2)}) collective-permute-start(bf16[512,128]{1,0:T(8,128)(2,1)S(1)} %get-tuple-element.63), channel_id=1, source_target_pairs={{0,1},{1,2},{2,3},{3,4},{4,5},{5,6},{6,7},{7,0},{8,9},{9,10},{10,1... | collective-permute-start | bytes 393224 | tf_op jit(solution)/shard_map/ppermute | solution.py:325
  89.2 6.9 %collective-permute-start.14 = (bf16[512,128]{1,0:T(8,128)(2,1)S(1)}, bf16[512,128]{1,0:T(8,128)(2,1)S(1)}, u32[]{:S(2)}, u32[]{:S(2)}) collective-permute-start(bf16[512,128]{1,0:T(8,128)(2,1)S(1)} %get-tuple-element.65), channel_id=1, source_target_pairs={{0,7},{1,0},{2,1},{3,2},{4,3},{5,4},{6,5},{7,6},{8,15},{9,8},{10,9... | collective-permute-start | bytes 393224 | tf_op jit(solution)/shard_map/ppermute | solution.py:325
  96.1 6.3 %collective-permute-start.15 = (bf16[512,128]{1,0:T(8,128)(2,1)S(1)}, bf16[512,128]{1,0:T(8,128)(2,1)S(1)}, u32[]{:S(2)}, u32[]{:S(2)}) collective-permute-start(bf16[512,128]{1,0:T(8,128)(2,1)S(1)} %get-tuple-element.67), channel_id=1, source_target_pairs={{0,1},{1,2},{2,3},{3,4},{4,5},{5,6},{6,7},{7,0},{8,9},{9,10},{10,1... | collective-permute-start | bytes 393224 | tf_op jit(solution)/shard_map/ppermute | solution.py:325
  104.2 7.7 %collective-permute-start.16 = (bf16[8,64,1024]{2,1,0:T(8,128)(2,1)}, bf16[8,64,1024]{2,1,0:T(8,128)(2,1)S(1)}, u32[]{:S(2)}, u32[]{:S(2)}) collective-permute-start(bf16[8,64,1024]{2,1,0:T(8,128)(2,1)} %get-tuple-element.71), channel_id=1, source_target_pairs={{0,16},{16,0},{1,17},{17,1},{2,18},{18,2},{3,19},{19,3},{4,20},{20... | collective-permute-start | bytes 3145736 | tf_op jit(solution)/shard_map/ppermute | solution.py:313
  104.2 14.1 %all-to-all-start.3 = ((bf16[8,64,128]{2,1,0:T(8,128)(2,1)}), bf16[8,64,128]{2,1,0:T(8,128)(2,1)S(1)}, u32[]{:S(2)}, u32[]{:S(2)}) async-start(bf16[8,64,128]{2,1,0:T(8,128)(2,1)} %copy-done.4), calls=%async_computation.3 | async-start | bytes 262144 | tf_op jit(solution)/shard_map/all_to_all | solution.py:317
  108.5 9.2 %collective-permute-start.18 = (f32[256,128]{1,0:T(8,128)S(1)}, f32[256,128]{1,0:T(8,128)S(1)}, u32[]{:S(2)}, u32[]{:S(2)}) collective-permute-start(f32[256,128]{1,0:T(8,128)S(1)} %get-tuple-element.74), channel_id=1, source_target_pairs={{0,8},{8,0},{1,9},{9,1},{2,10},{10,2},{3,11},{11,3},{4,12},{12,4},... | collective-permute-start | bytes 393224 | tf_op jit(solution)/shard_map/ppermute | solution.py:313
  117.3 5.2 %collective-permute-start.17 = (bf16[32,128]{1,0:T(8,128)(2,1)S(1)}, bf16[32,128]{1,0:T(8,128)(2,1)S(1)}, u32[]{:S(2)}, u32[]{:S(2)}) collective-permute-start(bf16[32,128]{1,0:T(8,128)(2,1)S(1)} %forward.1.pot_ref), channel_id=1, source_target_pairs={{0,8},{8,0},{1,9},{9,1},{2,10},{10,2},{3,11},{11,3},{4,12},{12,4},... | collective-permute-start | bytes 24584 | tf_op jit(solution)/shard_map/ppermute | solution.py:313
  122.5 5.5 %collective-permute-start.19 = (f32[64,128]{1,0:T(8,128)S(1)}, f32[64,128]{1,0:T(8,128)S(1)}, u32[]{:S(2)}, u32[]{:S(2)}) collective-permute-start(f32[64,128]{1,0:T(8,128)S(1)} %fold.1.mine_ref), channel_id=1, source_target_pairs={{0,8},{8,0},{1,9},{9,1},{2,10},{10,2},{3,11},{11,3},{4,12},{12,4},... | collective-permute-start | bytes 98312 | tf_op jit(solution)/shard_map/ppermute | solution.py:313
  (17 other events, 107.5 us)

commit v6 on v5

--- a/solution.py
+++ b/solution.py
@@ -26,16 +26,17 @@
     return pl.BlockSpec(memory_space=pltpu.HBM)
 
 
-def call(kernel, outs, args, specs=None, scratch=(), name=None):
+def call(kernel, outs, args, specs=None, out_specs=None, scratch=(), alias=None, name=None):
     return pl.pallas_call(
         kernel,
         out_shape=[jax.ShapeDtypeStruct(s, d) for s, d in outs],
         in_specs=specs or [vmem()] * len(args),
-        out_specs=[vmem()] * len(outs),
+        out_specs=out_specs or [vmem()] * len(outs),
         scratch_shapes=list(scratch),
         compiler_params=pltpu.CompilerParams(vmem_limit_bytes=20 * 2**20),
         cost_estimate=pl.CostEstimate(flops=1000, bytes_accessed=1000, transcendentals=0),
         name=name,
+        input_output_aliases=alias or {},
     )(*args)
 
 
@@ -161,17 +162,21 @@
         out_ref[q, 1] = charges
 
 
-def unpack(came_ref, msg_ref, charges_ref):
+def unpack(came_ref, near_hbm, msg_hbm, charges_ref, rows, sem):
+    del near_hbm
     total = came_ref[0, 0].astype(f32)
-    charges_ref[0] = came_ref[0, 1]
     for q in range(1, 8):
         total = total + came_ref[q, 0].astype(f32)
-        charges_ref[q] = came_ref[q, 1]
     for piece in range(8):
         for part in range(8):
-            msg_ref[piece, part * 8 : part * 8 + 8, :] = total[
+            rows[piece, part * 8 : part * 8 + 8, :] = total[
                 piece * 8 : piece * 8 + 8, part * 128 : part * 128 + 128
             ].astype(bf16)
+    copy = pltpu.make_async_copy(rows, msg_hbm.at[:, pl.ds(512, 64), :], sem)
+    copy.start()
+    for q in range(8):
+        charges_ref[q] = came_ref[q, 1]
+    copy.wait()
 
 
 def forward(other_ref, came_ref, parts_hbm, pot_ref, blocks, sems):
@@ -189,8 +194,7 @@
 
 def near(count_ref, rows_ref, cols_ref, low_ref, tiles_hbm, *refs):
     pieces, refs = refs[:8], refs[8:]
-    (ahead_ref, far_up, far_down), refs = refs[:3], refs[3:]
-    own_refs, (acc, behind, drives, tiles_ref, tile_sems, piece_sems) = refs[:6], refs[6:]
+    ahead_ref, msg_ref, acc, behind, drives, tiles_ref, tile_sems, piece_sems = refs
 
     def tile_copy(index):
         span = pl.ds(index * 4, 4)
@@ -241,34 +245,34 @@
     lax.fori_loop(groups, 8, drain, 0)
     for part in range(2):
         ahead_ref[:, part * 256 : part * 256 + 256] = acc[part]
-    for ref, offset in zip((far_up, far_down, *own_refs), (4, -3, 3, -2, 2, -1, 1, 0)):
-        owner_z = lax.rem(my_z + offset + 8, 8)
+    for z in range(8):
         for half in range(2):
             for part in range(4):
-                value = behind[half * 16 + 2 * owner_z + part // 2, :, part % 2 * 128 : part % 2 * 128 + 128]
                 rows = slice(half * 256 + part * 64, half * 256 + part * 64 + 64)
-                ref[rows, :] = value.astype(ref.dtype)
-
-
-def add_two(up_ref, own_up_ref, down_ref, own_down_ref, up_out, down_out):
-    up_out[...] = (up_ref[...].astype(f32) + own_up_ref[...]).astype(bf16)
-    down_out[...] = (down_ref[...].astype(f32) + own_down_ref[...]).astype(bf16)
-
-
-def add_last(up_ref, own_up_ref, down_ref, own_ref, up_out, sum_out):
-    up_out[...] = (up_ref[...].astype(f32) + own_up_ref[...]).astype(bf16)
-    sum_out[...] = down_ref[...].astype(f32) + own_ref[...]
-
-
-def close_ring(up_ref, sum_ref, keep_ref, send_ref):
+                value = behind[half * 16 + 2 * z + part // 2, :, part % 2 * 128 : part % 2 * 128 + 128]
+                msg_ref[z, rows, :] = value.astype(bf16)
+
+
+def fold(msg_ref, out_ref):
+    out_ref[...] = jnp.sum(msg_ref[:, 512:576, :].astype(f32), axis=0)
+
+
+def fold_near(msg_ref, keep_ref, send_ref):
     mine = pl.multiple_of(lax.axis_index("xhi") * 256, 256)
-    mates = 256 - mine
-    keep_ref[...] = up_ref[pl.ds(mine, 256), :].astype(f32) + sum_ref[pl.ds(mine, 256), :]
-    send_ref[...] = up_ref[pl.ds(mates, 256), :].astype(f32) + sum_ref[pl.ds(mates, 256), :]
-
-
-def fold(msg_ref, out_ref):
-    out_ref[...] = jnp.sum(msg_ref[...].astype(f32), axis=0)
+    for ref, first in ((keep_ref, mine), (send_ref, 256 - mine)):
+        value = msg_ref[0, pl.ds(first, 256), :].astype(f32)
+        for source in range(1, 8):
+            value = value + msg_ref[source, pl.ds(first, 256), :].astype(f32)
+        ref[...] = value
+
+
+def stage(skin_hbm, skout_hbm, skin_ref, skout_ref, sems):
+    first = pltpu.make_async_copy(skin_hbm, skin_ref, sems.at[0])
+    second = pltpu.make_async_copy(skout_hbm, skout_ref, sems.at[1])
+    first.start()
+    second.start()
+    first.wait()
+    second.wait()
 
 
 def last_message(mine_ref, mate_ref, pot_ref, mate_pot_ref, out_ref):
@@ -284,11 +288,7 @@
         out_ref[piece, 96:128, :] = second
 
 
-def finish(msg_ref, ahead_ref, keep_ref, mate_ref, skin_hbm, skout_hbm, resp_ref, sens_ref, skin_ref, skout_ref, sems):
-    first = pltpu.make_async_copy(skin_hbm, skin_ref, sems.at[0])
-    second = pltpu.make_async_copy(skout_hbm, skout_ref, sems.at[1])
-    first.start()
-    second.start()
+def finish(msg_ref, ahead_ref, keep_ref, mate_ref, skin_ref, skout_ref, resp_ref, sens_ref):
     adjoint = jnp.concatenate(
         [
             jnp.concatenate([msg_ref[z, part * 8 : part * 8 + 8, :] for part in range(8)], axis=1)
@@ -299,11 +299,9 @@
     packed = jnp.concatenate([msg_ref[r % 8, 64 + r // 8 * 32 : 96 + r // 8 * 32, :] for r in range(16)], axis=0)
     packed = packed.astype(f32).T.astype(bf16)
     near_sum = keep_ref[...] + mate_ref[...]
-    first.wait()
     sens_ref[...] = dot(adjoint, skin_ref[...]) + jnp.concatenate(
         [near_sum[part * 64 : part * 64 + 64] for part in range(4)], axis=1
     )
-    second.wait()
     upper = jnp.concatenate([skout_ref[r * 64 : r * 64 + 32, :] for r in range(16)], axis=0)
     lower = jnp.concatenate([skout_ref[r * 64 + 32 : r * 64 + 64, :] for r in range(16)], axis=0)
     resp_ref[...] = ahead_ref[...] + dot(packed[:64], upper) + dot(packed[64:], lower)
@@ -373,15 +371,14 @@
         scratch=blocks,
         name="own_terms",
     )
+    copies, own = tie(exchange(copies, ROWS), own)
+    (both,) = call(pack, [((8, 2, 64, 1024), bf16)], [own, copies], name="pack")
     up2, down2 = shift(up1, 1), shift(down1, -1)
     up3, down3 = shift(up2, 1), shift(down2, -1)
     up4 = shift(up3, 1)
-    copies, up4, down3, own = tie(exchange(copies, ROWS), up4, down3, own)
-    (both,) = call(pack, [((8, 2, 64, 1024), bf16)], [own, copies], name="pack")
-    chunk = (512, 128)
-    ahead, ring_up, ring_down, own3, own_2, own2, own_1, own1, own0 = call(
+    ahead, behind = call(
         near,
-        [((64, 512), f32), (chunk, bf16), (chunk, bf16)] + [(chunk, f32)] * 6,
+        [((64, 512), f32), ((8, 576, 128), bf16)],
         [tile_count, tile_rows, tile_cols, low, in_hbm(tiles)]
         + [in_hbm(piece) for piece in (here, up1, up2, up3, up4, down3, down2, down1)],
         specs=[smem(), smem(), smem(), vmem()] + [hbm()] * 9,
@@ -395,27 +392,16 @@
         ],
         name="near",
     )
-    for own_up, own_down in ((own3, own_2), (own2, own_1)):
-        ring_up, ring_down = call(
-            add_two,
-            [(chunk, bf16)] * 2,
-            [shift(ring_up, 1), own_up, shift(ring_down, -1), own_down],
-            name="add_two",
-        )
-    ring_up, near_sum = call(
-        add_last,
-        [(chunk, bf16), (chunk, f32)],
-        [shift(ring_up, 1), own1, shift(ring_down, -1), own0],
-        name="add_last",
-    )
-    ring_up = shift(ring_up, 1)
-    both, ahead, ring_up, near_sum = tie(exchange(both, FACE), ahead, ring_up, near_sum)
-    keep, send = call(close_ring, [((256, 128), f32)] * 2, [ring_up, near_sum], name="close_ring")
-    mate_near = swap(send, "xhi")
-    adjoint, charges = call(
+    behind = in_hbm(behind)
+    both, ahead, behind = tie(exchange(both, FACE), ahead, behind)
+    behind, charges = call(
         unpack,
-        [((8, 64, 128), bf16), ((8, 64, 1024), bf16)],
-        [both],
+        [((8, 576, 128), bf16), ((8, 64, 1024), bf16)],
+        [both, behind],
+        specs=[vmem(), hbm()],
+        out_specs=[hbm(), vmem()],
+        scratch=[pltpu.VMEM((8, 64, 128), bf16), pltpu.SemaphoreType.DMA],
+        alias={1: 0},
         name="unpack",
     )
     others = swap(charges, "core")
@@ -428,21 +414,30 @@
         name="forward",
     )
     mate_pot = swap(potential, "xhi")
-    adjoint, mate_pot, mate_near = tie(exchange(adjoint, "z"), mate_pot, mate_near)
-    (mine,) = call(fold, [((64, 128), f32)], [adjoint], name="fold")
+    behind, mate_pot = tie(exchange(behind, "z"), mate_pot)
+    (mine,) = call(fold, [((64, 128), f32)], [behind], name="fold")
     (last,) = call(
         last_message,
         [((8, 128, 128), bf16)],
         [mine, swap(mine, "xhi"), potential, mate_pot],
         name="last_message",
     )
+    keep, send = call(fold_near, [((256, 128), f32)] * 2, [behind], name="fold_near")
+    mate_near = swap(send, "xhi")
+    staged = call(
+        stage,
+        [((1024, 512), bf16)] * 2,
+        [in_hbm(skin), in_hbm(skout)],
+        specs=[hbm()] * 2,
+        scratch=[pltpu.SemaphoreType.DMA((2,))],
+        name="stage",
+    )
+    last, mate_near, *staged = tie(exchange(last, "z"), mate_near, *staged)
     return tuple(
         call(
             finish,
             [((64, 512), f32), ((64, 512), f32)],
-            [exchange(last, "z"), ahead, keep, mate_near, in_hbm(skin), in_hbm(skout)],
-            specs=[vmem()] * 4 + [hbm()] * 2,
-            scratch=[pltpu.VMEM((1024, 512), bf16)] * 2 + [pltpu.SemaphoreType.DMA((2,))],
+            [last, ahead, keep, mate_near, *staged],
             name="finish",
         )
     )

time: 152 us -> 146 us (0.961)
  blocking collectives: 17.4 us -> 0 us
  waiting for transfers between devices: 40.5 us -> 55.9 us
  starting transfers between devices: 56.7 us -> 49.7 us
  Pallas kernels: 26.4 us -> 28.3 us
    all_to_all x4 -> x5, waiting for transfers between devices: 4.43 us -> 26.8 us  [exchange(): return lax.all_to_all(value, axes, 0, 0, tiled=True)]
    all_to_all x1 -> x0, blocking collectives: 17.4 us -> none  [exchange(): return lax.all_to_all(value, axes, 0, 0, tiled=True)]
    ppermute x14 -> x7, starting transfers between devices: 21.1 us -> 9.48 us  [shift(): return lax.ppermute(value, 'z', [(i, (i + step) % 8) for i in range(8)])]
    ppermute x14 -> x7, waiting for transfers between devices: 23.5 us -> 12.3 us  [shift(): return lax.ppermute(value, 'z', [(i, (i + step) % 8) for i in range(8)])]
    ppermute x6, waiting for transfers between devices: 12.6 us -> 16.9 us  [swap(): return lax.ppermute(value, axis, [(0, 1), (1, 0)])]
    all_to_all x4 -> x5, starting transfers between devices: 28 us -> 31.5 us  [exchange(): return lax.all_to_all(value, axes, 0, 0, tiled=True)]
    pallas_call x16 -> x14, Pallas kernels: 26.4 us -> 28.3 us  [call(): pl.pallas_call(kernel, out_shape=[jax.ShapeDtypeStruct(s, d) for s, d in...]
    unnamed x34 -> x40, local copies, waits for them, and re-layouts: 7.3 us -> 8.39 us
  transfers between devices with their start and end apart: 24 -> 18, of which waited for: 13 -> 14; matrix products, arithmetic and copies ran while one was open for 0% -> 0% of each run, Pallas kernels for 10% -> 12%
where the time goes in v6:
time: 146 us; the launch traced here: 144 us
  waiting for transfers between devices  55.9 us (38%)
  starting transfers between devices  49.7 us (34%)
  Pallas kernels  28.3 us (19%)
  local copies, waits for them, and re-layouts  8.39 us (6%)
  between operations  1.56 us (1%)
    all_to_all x5, starting transfers between devices, exchange(): return lax.all_to_all(value, axes, 0, 0, tiled=True)  31.5 us
    pallas_call x14, Pallas kernels, call(): pl.pallas_call(kernel, out_shape=[jax.ShapeDtypeStruct(s, d) for s, d in...  28.3 us
    all_to_all x5, waiting for transfers between devices, exchange(): return lax.all_to_all(value, axes, 0, 0, tiled=True)  26.8 us
    ppermute x6, waiting for transfers between devices, swap(): return lax.ppermute(value, axis, [(0, 1), (1, 0)])  16.9 us
    ppermute x7, waiting for transfers between devices, shift(): return lax.ppermute(value, 'z', [(i, (i + step) % 8) for i in range(8)])  12.3 us
    ppermute x7, starting transfers between devices, shift(): return lax.ppermute(value, 'z', [(i, (i + step) % 8) for i in range(8)])  9.48 us
    ppermute x6, starting transfers between devices, swap(): return lax.ppermute(value, axis, [(0, 1), (1, 0)])  8.72 us
    unnamed x40, local copies, waits for them, and re-layouts  8.39 us
  transfers between devices with their start and end apart: 18, of which 14 were waited for; matrix products, arithmetic and copies ran while one was open for 0% of the time, Pallas kernels for 12%

profile of v6, /device:TPU:8, one launch (start us, length us, event | category | flops | bytes accessed | tf_op | source)
XLA Modules:
  0.0 143.9 jit_solution(12081424563002425489)
XLA Ops:
  0.6 3.0 %prepare.1 = (bf16[2,64,256]{2,1,0:T(8,128)(2,1)S(1)}, bf16[2,64,256]{2,1,0:T(8,128)(2,1)S(1)}, bf16[16,96,128]{2,1,0:T(8,128)(2,1)}) custom-call(f32[64,512]{1,0:T(8,128)} %exc_hbm.1, f32[64,512]{1,0:T(8,128)} %loads_hbm.1, bf16[1024,512]{1,0:T(8,128)(2,1)} %skin_hbm.3, bf16[1024,512]{1,0:T(8,128)(2,1)} %skout_hbm.3), custom_call_target="tpu_custom_call" | custom-call | flops 1000 | bytes 1000 | tf_op jit(solution)/shard_map/prepare/pallas_call | solution.py:30
  3.6 11.0 %all-to-all-start = ((bf16[16,96,128]{2,1,0:T(8,128)(2,1)}), bf16[16,96,128]{2,1,0:T(8,128)(2,1)S(1)}, u32[]{:S(2)}, u32[]{:S(2)}) async-start(bf16[16,96,128]{2,1,0:T(8,128)(2,1)} %get-tuple-element.30), calls=%async_computation | async-start | bytes 786432 | tf_op jit(solution)/shard_map/all_to_all | solution.py:315
  14.7 3.4 %collective-permute-start = (bf16[2,64,256]{2,1,0:T(8,128)(2,1)S(1)}, bf16[2,64,256]{2,1,0:T(8,128)(2,1)S(1)}, u32[]{:S(2)}, u32[]{:S(2)}) collective-permute-start(bf16[2,64,256]{2,1,0:T(8,128)(2,1)S(1)} %get-tuple-element.31), channel_id=1, source_target_pairs={{0,8},{8,0},{1,9},{9,1},{2,10},{10,2},{3,11},{11,3},{4,12},{12,4},... | collective-permute-start | bytes 196616 | tf_op jit(solution)/shard_map/ppermute | solution.py:311
  18.1 3.2 %collective-permute-done = bf16[2,64,256]{2,1,0:T(8,128)(2,1)S(1)} collective-permute-done((bf16[2,64,256]{2,1,0:T(8,128)(2,1)S(1)}, bf16[2,64,256]{2,1,0:T(8,128)(2,1)S(1)}, u32[]{:S(2)}, u32[]{:S(2)}) %collective-permute-start) | collective-permute-done | bytes 65568 | tf_op jit(solution)/shard_map/ppermute | solution.py:311
  24.7 2.2 %split_translation.1.parts_hbm = bf16[15,128,1024]{2,1,0:T(8,128)(2,1)S(1)} custom-call(f32[1,15,64,1024]{3,2,1,0:T(8,128)} %trans_hbm.1), custom_call_target="tpu_custom_call" | custom-call | flops 1000 | bytes 1000 | tf_op jit(solution)/shard_map/split_translation/pallas_call | solution.py:30
  30.4 4.3 %other_terms.1 = f32[8,64,1024]{2,1,0:T(8,128)} custom-call(bf16[128,64]{1,0:T(8,128)(2,1)S(1)} %get-tuple-element.34.grad_ref, bf16[15,128,1024]{2,1,0:T(8,128)(2,1)} %copy-done), custom_call_target="tpu_custom_call" | custom-call | flops 1000 | bytes 1000 | tf_op jit(solution)/shard_map/other_terms/pallas_call | solution.py:30
  34.9 8.3 %all-to-all-start.1 = ((bf16[16,32,128]{2,1,0:T(8,128)(2,1)}), bf16[16,32,128]{2,1,0:T(8,128)(2,1)S(1)}, u32[]{:S(2)}, u32[]{:S(2)}) async-start(bf16[16,32,128]{2,1,0:T(8,128)(2,1)} %get-tuple-element.33), calls=%async_computation.1 | async-start | bytes 262144 | tf_op jit(solution)/shard_map/all_to_all | solution.py:315
  43.2 3.0 %own_terms.1.own_ref = bf16[8,64,1024]{2,1,0:T(8,128)(2,1)S(1)} custom-call(bf16[128,64]{1,0:T(8,128)(2,1)S(1)} %get-tuple-element.34.grad_ref, f32[8,64,1024]{2,1,0:T(8,128)S(1)} %collective-permute-done.3.came_ref, bf16[15,128,1024]{2,1,0:T(8,128)(2,1)} %copy-done), custom_call_target="tpu_custom_call" | custom-call | flops 1000 | bytes 1000 | tf_op jit(solution)/shard_map/own_terms/pallas_call | solution.py:30
  46.2 7.2 %all-to-all-done.1.pieces_ref = bf16[16,32,128]{2,1,0:T(8,128)(2,1)S(1)} async-done(((bf16[16,32,128]{2,1,0:T(8,128)(2,1)}), bf16[16,32,128]{2,1,0:T(8,128)(2,1)S(1)}, u32[]{:S(2)}, u32[]{:S(2)}) %all-to-all-start.1) | async-done | bytes 131104 | tf_op jit(solution)/shard_map/all_to_all | solution.py:315
  55.0 5.1 %all-to-all-start.2 = ((bf16[8,2,64,1024]{3,2,1,0:T(8,128)(2,1)}), bf16[8,2,64,1024]{3,2,1,0:T(8,128)(2,1)S(1)}, u32[]{:S(2)}, u32[]{:S(2)}) async-start(bf16[8,2,64,1024]{3,2,1,0:T(8,128)(2,1)} %copy-done.1), calls=%async_computation.2 | async-start | bytes 4194304 | tf_op jit(solution)/shard_map/all_to_all | solution.py:315
  63.3 2.9 %collective-permute-done.4.refs_2_ = bf16[2,2,64,256]{3,2,1,0:T(8,128)(2,1)S(1)} collective-permute-done((bf16[2,2,64,256]{3,2,1,0:T(8,128)(2,1)S(1)}, bf16[2,2,64,256]{3,2,1,0:T(8,128)(2,1)S(1)}, u32[]{:S(2)}, u32[]{:S(2)}) %collective-permute-start.4) | collective-permute-done | bytes 131104 | tf_op jit(solution)/shard_map/ppermute | solution.py:323
  67.1 2.4 %collective-permute-start.8 = (bf16[2,2,64,256]{3,2,1,0:T(8,128)(2,1)S(1)}, bf16[2,2,64,256]{3,2,1,0:T(8,128)(2,1)S(1)}, u32[]{:S(2)}, u32[]{:S(2)}) collective-permute-start(bf16[2,2,64,256]{3,2,1,0:T(8,128)(2,1)S(1)} %collective-permute-done.7.refs_6_), channel_id=1, source_target_pairs={{0,7},{1,0},{2,1},{3,2},{4,3},{5,4},{6,5},{7,6},{8,15},{9,8},{10,9... | collective-permute-start | bytes 393224 | tf_op jit(solution)/shard_map/ppermute | solution.py:323
  69.5 2.9 %collective-permute-done.5.refs_3_ = bf16[2,2,64,256]{3,2,1,0:T(8,128)(2,1)S(1)} collective-permute-done((bf16[2,2,64,256]{3,2,1,0:T(8,128)(2,1)S(1)}, bf16[2,2,64,256]{3,2,1,0:T(8,128)(2,1)S(1)}, u32[]{:S(2)}, u32[]{:S(2)}) %collective-permute-start.5) | collective-permute-done | bytes 131104 | tf_op jit(solution)/shard_map/ppermute | solution.py:323
  73.1 5.5 %collective-permute-done.6.refs_4_ = bf16[2,2,64,256]{3,2,1,0:T(8,128)(2,1)S(1)} collective-permute-done((bf16[2,2,64,256]{3,2,1,0:T(8,128)(2,1)S(1)}, bf16[2,2,64,256]{3,2,1,0:T(8,128)(2,1)S(1)}, u32[]{:S(2)}, u32[]{:S(2)}) %collective-permute-start.6) | collective-permute-done | bytes 131104 | tf_op jit(solution)/shard_map/ppermute | solution.py:323
  79.3 5.0 %near.1 = (f32[64,512]{1,0:T(8,128)S(1)}, bf16[8,576,128]{2,1,0:T(8,128)(2,1)S(1)}) custom-call(s32[1]{0:T(128)S(6)} %copy.13.count_ref, s32[32]{0:T(128)S(1)} %copy-done.7, s32[32]{0:T(128)S(1)} %copy-done.8, bf16[2,64,256]{2,1,0:T(8,128)(2,1)S(1)} %get-tuple-element.38.low_ref, bf16[32,256,256]{2,1,0:T(8,128)(2,1)} %tiles_hbm.1, ...), custom_call_target="tpu_custom_call" | custom-call | flops 1000 | bytes 1000 | tf_op jit(solution)/shard_map/near/pallas_call | solution.py:30
  87.8 3.6 %all-to-all-start.3 = ((bf16[8,576,128]{2,1,0:T(8,128)(2,1)}), bf16[8,576,128]{2,1,0:T(8,128)(2,1)S(1)}, u32[]{:S(2)}, u32[]{:S(2)}) async-start(bf16[8,576,128]{2,1,0:T(8,128)(2,1)} %get-tuple-element.45), calls=%async_computation.3 | async-start | bytes 2359296 | tf_op jit(solution)/shard_map/all_to_all | solution.py:315
  91.7 2.9 %collective-permute-done.9.other_ref = bf16[8,64,1024]{2,1,0:T(8,128)(2,1)S(1)} collective-permute-done((bf16[8,64,1024]{2,1,0:T(8,128)(2,1)}, bf16[8,64,1024]{2,1,0:T(8,128)(2,1)S(1)}, u32[]{:S(2)}, u32[]{:S(2)}) %collective-permute-start.9) | collective-permute-done | bytes 1048608 | tf_op jit(solution)/shard_map/ppermute | solution.py:311
  94.5 5.4 %forward.1.pot_ref = bf16[32,128]{1,0:T(8,128)(2,1)S(1)} custom-call(bf16[8,64,1024]{2,1,0:T(8,128)(2,1)S(1)} %collective-permute-done.9.other_ref, bf16[8,2,64,1024]{3,2,1,0:T(8,128)(2,1)S(1)} %all-to-all-done.2.came_ref, bf16[15,128,1024]{2,1,0:T(8,128)(2,1)} %copy-done), custom_call_target="tpu_custom_call" | custom-call | flops 1000 | bytes 1000 | tf_op jit(solution)/shard_map/forward/pallas_call | solution.py:30
  101.5 3.7 %collective-permute-done.10.mate_pot_ref = bf16[32,128]{1,0:T(8,128)(2,1)S(1)} collective-permute-done((bf16[32,128]{1,0:T(8,128)(2,1)S(1)}, bf16[32,128]{1,0:T(8,128)(2,1)S(1)}, u32[]{:S(2)}, u32[]{:S(2)}) %collective-permute-start.10) | collective-permute-done | bytes 8224 | tf_op jit(solution)/shard_map/ppermute | solution.py:311
  105.2 15.6 %all-to-all-done.3.msg_ref = bf16[8,576,128]{2,1,0:T(8,128)(2,1)S(1)} async-done(((bf16[8,576,128]{2,1,0:T(8,128)(2,1)}), bf16[8,576,128]{2,1,0:T(8,128)(2,1)S(1)}, u32[]{:S(2)}, u32[]{:S(2)}) %all-to-all-start.3) | async-done | bytes 1179680 | tf_op jit(solution)/shard_map/all_to_all | solution.py:315
  122.6 3.8 %collective-permute-done.11.mate_ref = f32[64,128]{1,0:T(8,128)S(1)} collective-permute-done((f32[64,128]{1,0:T(8,128)S(1)}, f32[64,128]{1,0:T(8,128)S(1)}, u32[]{:S(2)}, u32[]{:S(2)}) %collective-permute-start.11) | collective-permute-done | bytes 32800 | tf_op jit(solution)/shard_map/ppermute | solution.py:311
  127.1 3.4 %all-to-all-start.4 = ((bf16[8,128,128]{2,1,0:T(8,128)(2,1)}), bf16[8,128,128]{2,1,0:T(8,128)(2,1)S(1)}, u32[]{:S(2)}, u32[]{:S(2)}) async-start(bf16[8,128,128]{2,1,0:T(8,128)(2,1)} %last_message.1), calls=%async_computation.4 | async-start | bytes 524288 | tf_op jit(solution)/shard_map/all_to_all | solution.py:315
  134.0 3.3 %collective-permute-done.12.mate_ref = f32[256,128]{1,0:T(8,128)S(1)} collective-permute-done((f32[256,128]{1,0:T(8,128)S(1)}, f32[256,128]{1,0:T(8,128)S(1)}, u32[]{:S(2)}, u32[]{:S(2)}) %collective-permute-start.12) | collective-permute-done | bytes 131104 | tf_op jit(solution)/shard_map/ppermute | solution.py:311
  137.2 3.7 %all-to-all-done.4.msg_ref = bf16[8,128,128]{2,1,0:T(8,128)(2,1)S(1)} async-done(((bf16[8,128,128]{2,1,0:T(8,128)(2,1)}), bf16[8,128,128]{2,1,0:T(8,128)(2,1)S(1)}, u32[]{:S(2)}, u32[]{:S(2)}) %all-to-all-start.4) | async-done | bytes 262176 | tf_op jit(solution)/shard_map/all_to_all | solution.py:315
  (67 shorter events, 27.4 us)
Async XLA Ops:
  3.6 26.0 %all-to-all-start = ((bf16[16,96,128]{2,1,0:T(8,128)(2,1)}), bf16[16,96,128]{2,1,0:T(8,128)(2,1)S(1)}, u32[]{:S(2)}, u32[]{:S(2)}) async-start(bf16[16,96,128]{2,1,0:T(8,128)(2,1)} %get-tuple-element.30), calls=%async_computation | async-start | bytes 786432 | tf_op jit(solution)/shard_map/all_to_all | solution.py:315
  14.7 6.7 %collective-permute-start = (bf16[2,64,256]{2,1,0:T(8,128)(2,1)S(1)}, bf16[2,64,256]{2,1,0:T(8,128)(2,1)S(1)}, u32[]{:S(2)}, u32[]{:S(2)}) collective-permute-start(bf16[2,64,256]{2,1,0:T(8,128)(2,1)S(1)} %get-tuple-element.31), channel_id=1, source_target_pairs={{0,8},{8,0},{1,9},{9,1},{2,10},{10,2},{3,11},{11,3},{4,12},{12,4},... | collective-permute-start | bytes 196616 | tf_op jit(solution)/shard_map/ppermute | solution.py:311
  21.4 8.0 %collective-permute-start.1 = (bf16[2,2,64,256]{3,2,1,0:T(8,128)(2,1)S(1)}, bf16[2,2,64,256]{3,2,1,0:T(8,128)(2,1)S(1)}, u32[]{:S(2)}, u32[]{:S(2)}) collective-permute-start(bf16[2,2,64,256]{3,2,1,0:T(8,128)(2,1)S(1)} %pad_maximum_fusion.refs_0_), channel_id=1, source_target_pairs={{0,1},{1,2},{2,3},{3,4},{4,5},{5,6},{6,7},{7,0},{8,9},{9,10},{10,1... | collective-permute-start | bytes 393224 | tf_op jit(solution)/shard_map/ppermute | solution.py:323
  23.0 6.4 %collective-permute-start.2 = (bf16[2,2,64,256]{3,2,1,0:T(8,128)(2,1)S(1)}, bf16[2,2,64,256]{3,2,1,0:T(8,128)(2,1)S(1)}, u32[]{:S(2)}, u32[]{:S(2)}) collective-permute-start(bf16[2,2,64,256]{3,2,1,0:T(8,128)(2,1)S(1)} %pad_maximum_fusion.refs_0_), channel_id=1, source_target_pairs={{0,7},{1,0},{2,1},{3,2},{4,3},{5,4},{6,5},{7,6},{8,15},{9,8},{10,9... | collective-permute-start | bytes 393224 | tf_op jit(solution)/shard_map/ppermute | solution.py:323
  34.8 8.5 %collective-permute-start.3 = (f32[8,64,1024]{2,1,0:T(8,128)}, f32[8,64,1024]{2,1,0:T(8,128)S(1)}, u32[]{:S(2)}, u32[]{:S(2)}) collective-permute-start(f32[8,64,1024]{2,1,0:T(8,128)} %other_terms.1), channel_id=1, source_target_pairs={{0,16},{16,0},{1,17},{17,1},{2,18},{18,2},{3,19},{19,3},{4,20},{20... | collective-permute-start | bytes 6291464 | tf_op jit(solution)/shard_map/ppermute | solution.py:311
  34.9 18.5 %all-to-all-start.1 = ((bf16[16,32,128]{2,1,0:T(8,128)(2,1)}), bf16[16,32,128]{2,1,0:T(8,128)(2,1)S(1)}, u32[]{:S(2)}, u32[]{:S(2)}) async-start(bf16[16,32,128]{2,1,0:T(8,128)(2,1)} %get-tuple-element.33), calls=%async_computation.1 | async-start | bytes 262144 | tf_op jit(solution)/shard_map/all_to_all | solution.py:315
  55.0 6.8 %copy-start.14 = (bf16[2,2,64,256]{3,2,1,0:T(8,128)(2,1)S(1)}, bf16[2,2,64,256]{3,2,1,0:T(8,128)(2,1)}, u32[]{:S(2)}) copy-start(bf16[2,2,64,256]{3,2,1,0:T(8,128)(2,1)} %copy-done.13) | copy-start | bytes 393220
  55.0 24.3 %copy-start.7 = (s32[32]{0:T(128)S(1)}, s32[32]{0:T(128)}, u32[]{:S(2)}) copy-start(s32[32]{0:T(128)} %rows_ref.1) | copy-start | bytes 388
  55.0 24.3 %copy-start.8 = (s32[32]{0:T(128)S(1)}, s32[32]{0:T(128)}, u32[]{:S(2)}) copy-start(s32[32]{0:T(128)} %cols_ref.1) | copy-start | bytes 388
  55.0 31.0 %all-to-all-start.2 = ((bf16[8,2,64,1024]{3,2,1,0:T(8,128)(2,1)}), bf16[8,2,64,1024]{3,2,1,0:T(8,128)(2,1)S(1)}, u32[]{:S(2)}, u32[]{:S(2)}) async-start(bf16[8,2,64,1024]{3,2,1,0:T(8,128)(2,1)} %copy-done.1), calls=%async_computation.2 | async-start | bytes 4194304 | tf_op jit(solution)/shard_map/all_to_all | solution.py:315
  60.1 6.2 %collective-permute-start.4 = (bf16[2,2,64,256]{3,2,1,0:T(8,128)(2,1)S(1)}, bf16[2,2,64,256]{3,2,1,0:T(8,128)(2,1)S(1)}, u32[]{:S(2)}, u32[]{:S(2)}) collective-permute-start(bf16[2,2,64,256]{3,2,1,0:T(8,128)(2,1)S(1)} %copy-done.12), channel_id=1, source_target_pairs={{0,1},{1,2},{2,3},{3,4},{4,5},{5,6},{6,7},{7,0},{8,9},{9,10},{10,1... | collective-permute-start | bytes 393224 | tf_op jit(solution)/shard_map/ppermute | solution.py:323
  61.8 5.3 %collective-permute-start.7 = (bf16[2,2,64,256]{3,2,1,0:T(8,128)(2,1)S(1)}, bf16[2,2,64,256]{3,2,1,0:T(8,128)(2,1)S(1)}, u32[]{:S(2)}, u32[]{:S(2)}) collective-permute-start(bf16[2,2,64,256]{3,2,1,0:T(8,128)(2,1)S(1)} %copy-done.14), channel_id=1, source_target_pairs={{0,7},{1,0},{2,1},{3,2},{4,3},{5,4},{6,5},{7,6},{8,15},{9,8},{10,9... | collective-permute-start | bytes 393224 | tf_op jit(solution)/shard_map/ppermute | solution.py:323
  66.3 12.4 %copy-start.15 = (bf16[2,2,64,256]{3,2,1,0:T(8,128)(2,1)}, bf16[2,2,64,256]{3,2,1,0:T(8,128)(2,1)S(1)}, u32[]{:S(2)}) copy-start(bf16[2,2,64,256]{3,2,1,0:T(8,128)(2,1)S(1)} %collective-permute-done.4.refs_2_) | copy-start | bytes 393220
  66.3 6.2 %collective-permute-start.5 = (bf16[2,2,64,256]{3,2,1,0:T(8,128)(2,1)S(1)}, bf16[2,2,64,256]{3,2,1,0:T(8,128)(2,1)S(1)}, u32[]{:S(2)}, u32[]{:S(2)}) collective-permute-start(bf16[2,2,64,256]{3,2,1,0:T(8,128)(2,1)S(1)} %collective-permute-done.4.refs_2_), channel_id=1, source_target_pairs={{0,1},{1,2},{2,3},{3,4},{4,5},{5,6},{6,7},{7,0},{8,9},{9,10},{10,1... | collective-permute-start | bytes 393224 | tf_op jit(solution)/shard_map/ppermute | solution.py:323
  67.1 11.5 %copy-start.16 = (bf16[2,2,64,256]{3,2,1,0:T(8,128)(2,1)}, bf16[2,2,64,256]{3,2,1,0:T(8,128)(2,1)S(1)}, u32[]{:S(2)}) copy-start(bf16[2,2,64,256]{3,2,1,0:T(8,128)(2,1)S(1)} %collective-permute-done.7.refs_6_) | copy-start | bytes 393220
  67.1 6.0 %collective-permute-start.8 = (bf16[2,2,64,256]{3,2,1,0:T(8,128)(2,1)S(1)}, bf16[2,2,64,256]{3,2,1,0:T(8,128)(2,1)S(1)}, u32[]{:S(2)}, u32[]{:S(2)}) collective-permute-start(bf16[2,2,64,256]{3,2,1,0:T(8,128)(2,1)S(1)} %collective-permute-done.7.refs_6_), channel_id=1, source_target_pairs={{0,7},{1,0},{2,1},{3,2},{4,3},{5,4},{6,5},{7,6},{8,15},{9,8},{10,9... | collective-permute-start | bytes 393224 | tf_op jit(solution)/shard_map/ppermute | solution.py:323
  72.5 6.2 %copy-start.17 = (bf16[2,2,64,256]{3,2,1,0:T(8,128)(2,1)}, bf16[2,2,64,256]{3,2,1,0:T(8,128)(2,1)S(1)}, u32[]{:S(2)}) copy-start(bf16[2,2,64,256]{3,2,1,0:T(8,128)(2,1)S(1)} %collective-permute-done.5.refs_3_) | copy-start | bytes 393220
  72.5 6.2 %collective-permute-start.6 = (bf16[2,2,64,256]{3,2,1,0:T(8,128)(2,1)S(1)}, bf16[2,2,64,256]{3,2,1,0:T(8,128)(2,1)S(1)}, u32[]{:S(2)}, u32[]{:S(2)}) collective-permute-start(bf16[2,2,64,256]{3,2,1,0:T(8,128)(2,1)S(1)} %collective-permute-done.5.refs_3_), channel_id=1, source_target_pairs={{0,1},{1,2},{2,3},{3,4},{4,5},{5,6},{6,7},{7,0},{8,9},{9,10},{10,1... | collective-permute-start | bytes 393224 | tf_op jit(solution)/shard_map/ppermute | solution.py:323
  87.8 33.0 %all-to-all-start.3 = ((bf16[8,576,128]{2,1,0:T(8,128)(2,1)}), bf16[8,576,128]{2,1,0:T(8,128)(2,1)S(1)}, u32[]{:S(2)}, u32[]{:S(2)}) async-start(bf16[8,576,128]{2,1,0:T(8,128)(2,1)} %get-tuple-element.45), calls=%async_computation.3 | async-start | bytes 2359296 | tf_op jit(solution)/shard_map/all_to_all | solution.py:315
  91.4 3.1 %collective-permute-start.9 = (bf16[8,64,1024]{2,1,0:T(8,128)(2,1)}, bf16[8,64,1024]{2,1,0:T(8,128)(2,1)S(1)}, u32[]{:S(2)}, u32[]{:S(2)}) collective-permute-start(bf16[8,64,1024]{2,1,0:T(8,128)(2,1)} %copy-done.9), channel_id=1, source_target_pairs={{0,16},{16,0},{1,17},{17,1},{2,18},{18,2},{3,19},{19,3},{4,20},{20... | collective-permute-start | bytes 3145736 | tf_op jit(solution)/shard_map/ppermute | solution.py:311
  100.0 5.2 %collective-permute-start.10 = (bf16[32,128]{1,0:T(8,128)(2,1)S(1)}, bf16[32,128]{1,0:T(8,128)(2,1)S(1)}, u32[]{:S(2)}, u32[]{:S(2)}) collective-permute-start(bf16[32,128]{1,0:T(8,128)(2,1)S(1)} %forward.1.pot_ref), channel_id=1, source_target_pairs={{0,8},{8,0},{1,9},{9,1},{2,10},{10,2},{3,11},{11,3},{4,12},{12,4},... | collective-permute-start | bytes 24584 | tf_op jit(solution)/shard_map/ppermute | solution.py:311
  120.9 5.5 %collective-permute-start.11 = (f32[64,128]{1,0:T(8,128)S(1)}, f32[64,128]{1,0:T(8,128)S(1)}, u32[]{:S(2)}, u32[]{:S(2)}) collective-permute-start(f32[64,128]{1,0:T(8,128)S(1)} %fold.1.mine_ref), channel_id=1, source_target_pairs={{0,8},{8,0},{1,9},{9,1},{2,10},{10,2},{3,11},{11,3},{4,12},{12,4},... | collective-permute-start | bytes 98312 | tf_op jit(solution)/shard_map/ppermute | solution.py:311
  127.1 13.8 %all-to-all-start.4 = ((bf16[8,128,128]{2,1,0:T(8,128)(2,1)}), bf16[8,128,128]{2,1,0:T(8,128)(2,1)S(1)}, u32[]{:S(2)}, u32[]{:S(2)}) async-start(bf16[8,128,128]{2,1,0:T(8,128)(2,1)} %last_message.1), calls=%async_computation.4 | async-start | bytes 524288 | tf_op jit(solution)/shard_map/all_to_all | solution.py:315
  130.7 6.6 %collective-permute-start.12 = (f32[256,128]{1,0:T(8,128)S(1)}, f32[256,128]{1,0:T(8,128)S(1)}, u32[]{:S(2)}, u32[]{:S(2)}) collective-permute-start(f32[256,128]{1,0:T(8,128)S(1)} %get-tuple-element.49), channel_id=1, source_target_pairs={{0,8},{8,0},{1,9},{9,1},{2,10},{10,2},{3,11},{11,3},{4,12},{12,4},... | collective-permute-start | bytes 393224 | tf_op jit(solution)/shard_map/ppermute | solution.py:311
  (14 other events, 38.7 us)

commit v7 on v4

--- a/solution.py
+++ b/solution.py
@@ -26,8 +26,7 @@
     return pl.BlockSpec(memory_space=pltpu.HBM)
 
 
-def call(kernel, outs, args, specs=None, scratch=(), flops=10**7, name=None):
-    moved = sum(a.size * a.dtype.itemsize for a in args)
+def call(kernel, outs, args, specs=None, scratch=(), name=None):
     return pl.pallas_call(
         kernel,
         out_shape=[jax.ShapeDtypeStruct(s, d) for s, d in outs],
@@ -35,7 +34,7 @@
         out_specs=[vmem()] * len(outs),
         scratch_shapes=list(scratch),
         compiler_params=pltpu.CompilerParams(vmem_limit_bytes=20 * 2**20),
-        cost_estimate=pl.CostEstimate(flops=flops, bytes_accessed=moved, transcendentals=0),
+        cost_estimate=pl.CostEstimate(flops=1000, bytes_accessed=1000, transcendentals=0),
         name=name,
     )(*args)
 
@@ -164,11 +163,11 @@
     for q in range(1, 8):
         total = total + came_ref[q, 0].astype(f32)
         charges_ref[q] = came_ref[q, 1]
-    for piece in range(8):
-        for part in range(8):
-            msg_ref[piece, part * 8 : part * 8 + 8, :] = total[
-                piece * 8 : piece * 8 + 8, part * 128 : part * 128 + 128
-            ].astype(bf16)
+    for piece in range(16):
+        row = piece // 2 * 8
+        for part in range(4):
+            col = piece % 2 * 512 + part * 128
+            msg_ref[piece, part * 8 : part * 8 + 8, :] = total[row : row + 8, col : col + 128].astype(bf16)
 
 
 def forward(other_ref, came_ref, parts_hbm, pot_ref, blocks, sems):
@@ -237,56 +236,42 @@
     lax.fori_loop(groups, 8, drain, 0)
     for part in range(2):
         ahead_ref[:, part * 256 : part * 256 + 256] = acc[part]
-    for z in range(8):
-        for part in range(4):
-            rows = pl.ds(part * 64, 64)
-            cols = pl.ds(part % 2 * 128, 128)
-            send_ref[z, rows, :] = behind[(1 - my_half) * 16 + 2 * z + part // 2, :, cols].astype(bf16)
-            keep_ref[z, rows, :] = behind[my_half * 16 + 2 * z + part // 2, :, cols]
-
-
-def fold(msg_ref, out_ref):
-    out_ref[...] = jnp.sum(msg_ref[...].astype(f32), axis=0)
-
-
-def last_message(mine_ref, mate_ref, pot_ref, mate_pot_ref, keep_ref, mate_near_ref, out_ref):
-    adjoint = (mine_ref[...] + mate_ref[...]).astype(bf16)
-    upper = lax.axis_index("xhi") == 1
-    pot = pot_ref[...].astype(f32)
-    mate_pot = mate_pot_ref[...].astype(f32)
-    first = jnp.where(upper, mate_pot, pot).astype(bf16)
-    second = jnp.where(upper, pot, mate_pot).astype(bf16)
-    for piece in range(8):
-        out_ref[piece, 0:64, :] = adjoint
-        out_ref[piece, 64:96, :] = first
-        out_ref[piece, 96:128, :] = second
-        out_ref[piece, 128:384, :] = (keep_ref[piece] + mate_near_ref[piece].astype(f32)).astype(bf16)
-
-
-def finish(msg_ref, ahead_ref, skin_hbm, skout_hbm, resp_ref, sens_ref, skin_ref, skout_ref, sems):
-    first = pltpu.make_async_copy(skin_hbm, skin_ref, sems.at[0])
-    second = pltpu.make_async_copy(skout_hbm, skout_ref, sems.at[1])
-    first.start()
-    second.start()
-    adjoint = jnp.concatenate(
-        [
-            jnp.concatenate([msg_ref[z, part * 8 : part * 8 + 8, :] for part in range(8)], axis=1)
-            for z in range(8)
-        ],
-        axis=0,
-    )
-    packed = jnp.concatenate([msg_ref[r % 8, 64 + r // 8 * 32 : 96 + r // 8 * 32, :] for r in range(16)], axis=0)
+    for target in range(16):
+        for part in range(2):
+            rows = slice(part * 64, part * 64 + 64)
+            cols = slice(part * 128, part * 128 + 128)
+            send_ref[target, rows, :] = behind[2 * target + 1 - my_half, :, cols].astype(bf16)
+            keep_ref[target, rows, :] = behind[2 * target + my_half, :, cols]
+
+
+def last_message(adj_ref, pot_ref, keep_ref, mate_ref, out_ref):
+    adjoint = jnp.sum(adj_ref[...].astype(f32), axis=0).astype(bf16)
+    for piece in range(16):
+        out_ref[piece, 0:32, :] = adjoint
+        out_ref[piece, 32:64, :] = pot_ref[...]
+        out_ref[piece, 64:192, :] = (keep_ref[piece] + mate_ref[piece].astype(f32)).astype(bf16)
+
+
+def stage(*refs):
+    sources, targets, sems = refs[:3], refs[3:6], refs[6]
+    copies = [pltpu.make_async_copy(sources[i], targets[i], sems.at[i]) for i in range(3)]
+    for copy in copies:
+        copy.start()
+    for copy in copies:
+        copy.wait()
+
+
+def finish(msg_ref, skin_ref, skout_ref, ahead_ref, resp_ref, sens_ref):
+    adjoint = join_pieces(msg_ref, 0)
+    packed = jnp.concatenate([msg_ref[r, 32:64, :] for r in range(16)], axis=0)
     packed = packed.astype(f32).T.astype(bf16)
     near_sums = []
-    for part in range(4):
-        rows = slice(128 + part * 64, 192 + part * 64)
-        value = msg_ref[0, rows, :].astype(f32)
-        for source in range(1, 8):
-            value = value + msg_ref[source, rows, :].astype(f32)
-        near_sums.append(value)
-    first.wait()
+    for block in range(2):
+        value = msg_ref[block * 8, 64:192, :].astype(f32)
+        for z in range(1, 8):
+            value = value + msg_ref[block * 8 + z, 64:192, :].astype(f32)
+        near_sums += [value[:64], value[64:]]
     sens_ref[...] = dot(adjoint, skin_ref[...]) + jnp.concatenate(near_sums, axis=1)
-    second.wait()
     upper = jnp.concatenate([skout_ref[r * 64 : r * 64 + 32, :] for r in range(16)], axis=0)
     lower = jnp.concatenate([skout_ref[r * 64 + 32 : r * 64 + 64, :] for r in range(16)], axis=0)
     resp_ref[...] = ahead_ref[...] + dot(packed[:64], upper) + dot(packed[64:], lower)
@@ -360,7 +345,7 @@
     up4 = shift(up3, 1)
     ahead, send, keep = call(
         near,
-        [((64, 512), f32), ((8, 256, 128), bf16), ((8, 256, 128), f32)],
+        [((64, 512), f32), ((16, 128, 128), bf16), ((16, 128, 128), f32)],
         [tile_count, tile_rows, tile_cols, low, in_hbm(tiles)]
         + [in_hbm(piece) for piece in (here, up1, up2, up3, up4, down3, down2, down1)],
         specs=[smem(), smem(), smem(), vmem()] + [hbm()] * 9,
@@ -378,7 +363,7 @@
     mate_near = swap(send, "xhi")
     adjoint, charges = call(
         unpack,
-        [((8, 64, 128), bf16), ((8, 64, 1024), bf16)],
+        [((16, 32, 128), bf16), ((8, 64, 1024), bf16)],
         [both],
         name="unpack",
     )
@@ -391,25 +376,23 @@
         scratch=[pltpu.VMEM((16, 128, 1024), bf16), pltpu.SemaphoreType.DMA((16,))],
         name="forward",
     )
-    mate_pot = swap(potential, "xhi")
-    adjoint, mate_pot = tie(exchange(adjoint, "z"), mate_pot)
-    (mine,) = call(fold, [((64, 128), f32)], [adjoint], name="fold")
+    adjoint, potential, mate_near = tie(exchange(adjoint, ROWS), potential, mate_near)
     (last,) = call(
         last_message,
-        [((8, 384, 128), bf16)],
-        [mine, swap(mine, "xhi"), potential, mate_pot, keep, mate_near],
+        [((16, 192, 128), bf16)],
+        [adjoint, potential, keep, mate_near],
         name="last_message",
     )
-    return tuple(
-        call(
-            finish,
-            [((64, 512), f32), ((64, 512), f32)],
-            [exchange(last, "z"), ahead, in_hbm(skin), in_hbm(skout)],
-            specs=[vmem()] * 2 + [hbm()] * 2,
-            scratch=[pltpu.VMEM((1024, 512), bf16)] * 2 + [pltpu.SemaphoreType.DMA((2,))],
-            name="finish",
-        )
-    )
+    staged = call(
+        stage,
+        [((1024, 512), bf16), ((1024, 512), bf16), ((64, 512), f32)],
+        [in_hbm(skin), in_hbm(skout), in_hbm(ahead)],
+        specs=[hbm()] * 3,
+        scratch=[pltpu.SemaphoreType.DMA((3,))],
+        name="stage",
+    )
+    last, *staged = tie(exchange(last, ROWS), *staged)
+    return tuple(call(finish, [((64, 512), f32), ((64, 512), f32)], [last, *staged], name="finish"))
 
 
 def solution(mesh):

time: 140 us -> 134 us (0.957)
  blocking collectives: 27.6 us -> 0 us
  waiting for transfers between devices: 31.8 us -> 46.3 us
  starting transfers between devices: 44.8 us -> 47.9 us
  Pallas kernels: 28.8 us -> 31.3 us
    all_to_all x1 -> x0, blocking collectives: 27.6 us -> none  [exchange(): return lax.all_to_all(value, axes, 0, 0, tiled=True)]
    all_to_all x4 -> x5, waiting for transfers between devices: 9.25 us -> 31.3 us  [exchange(): return lax.all_to_all(value, axes, 0, 0, tiled=True)]
    ppermute x6 -> x4, waiting for transfers between devices: 7.54 us -> 0.01 us  [swap(): return lax.ppermute(value, axis, [(0, 1), (1, 0)])]
    all_to_all x4 -> x5, starting transfers between devices: 25.6 us -> 32.2 us  [exchange(): return lax.all_to_all(value, axes, 0, 0, tiled=True)]
    ppermute x6 -> x4, starting transfers between devices: 9.48 us -> 6.01 us  [swap(): return lax.ppermute(value, axis, [(0, 1), (1, 0)])]
    pallas_call x11, Pallas kernels: 28.8 us -> 31.3 us  [call(): pl.pallas_call(kernel, out_shape=[jax.ShapeDtypeStruct(s, d) for s, d in...]
    unnamed x24 -> x26, local copies, waits for them, and re-layouts: 4.53 us -> 5.15 us
  transfers between devices with their start and end apart: 17 -> 16, of which waited for: 10 -> 8; matrix products, arithmetic and copies ran while one was open for 0% -> 0% of each run, Pallas kernels for 12% -> 15%
where the time goes in v7:
time: 134 us; the launch traced here: 132 us
  starting transfers between devices  47.9 us (36%)
  waiting for transfers between devices  46.3 us (35%)
  Pallas kernels  31.3 us (23%)
  local copies, waits for them, and re-layouts  5.15 us (4%)
  between operations  1.49 us (1%)
    all_to_all x5, starting transfers between devices, exchange(): return lax.all_to_all(value, axes, 0, 0, tiled=True)  32.2 us
    pallas_call x11, Pallas kernels, call(): pl.pallas_call(kernel, out_shape=[jax.ShapeDtypeStruct(s, d) for s, d in...  31.3 us
    all_to_all x5, waiting for transfers between devices, exchange(): return lax.all_to_all(value, axes, 0, 0, tiled=True)  31.3 us
    ppermute x7, waiting for transfers between devices, shift(): return lax.ppermute(value, 'z', [(i, (i + step) % 8) for i in range(8)])  15 us
    ppermute x7, starting transfers between devices, shift(): return lax.ppermute(value, 'z', [(i, (i + step) % 8) for i in range(8)])  9.69 us
    ppermute x4, starting transfers between devices, swap(): return lax.ppermute(value, axis, [(0, 1), (1, 0)])  6.01 us
    unnamed x26, local copies, waits for them, and re-layouts  5.15 us
  transfers between devices with their start and end apart: 16, of which 8 were waited for; matrix products, arithmetic and copies ran while one was open for 0% of the time, Pallas kernels for 15%

profile of v7, /device:TPU:8, one launch (start us, length us, event | category | flops | bytes accessed | tf_op | source)
XLA Modules:
  0.0 132.1 jit_solution(9814799659163793154)
XLA Ops:
  0.6 3.0 %prepare.1 = (bf16[2,64,256]{2,1,0:T(8,128)(2,1)S(1)}, bf16[2,64,256]{2,1,0:T(8,128)(2,1)S(1)}, bf16[16,96,128]{2,1,0:T(8,128)(2,1)}) custom-call(f32[64,512]{1,0:T(8,128)} %exc_hbm.1, f32[64,512]{1,0:T(8,128)} %loads_hbm.1, bf16[1024,512]{1,0:T(8,128)(2,1)} %refs_0_.1, bf16[1024,512]{1,0:T(8,128)(2,1)} %refs_1_.1), custom_call_target="tpu_custom_call" | custom-call | flops 1000 | bytes 1000 | tf_op jit(solution)/shard_map/prepare/pallas_call | solution.py:30
  3.6 11.0 %all-to-all-start = ((bf16[16,96,128]{2,1,0:T(8,128)(2,1)}), bf16[16,96,128]{2,1,0:T(8,128)(2,1)S(1)}, u32[]{:S(2)}, u32[]{:S(2)}) async-start(bf16[16,96,128]{2,1,0:T(8,128)(2,1)} %get-tuple-element.34), calls=%async_computation | async-start | bytes 786432 | tf_op jit(solution)/shard_map/all_to_all | solution.py:285
  14.7 3.4 %collective-permute-start = (bf16[2,64,256]{2,1,0:T(8,128)(2,1)S(1)}, bf16[2,64,256]{2,1,0:T(8,128)(2,1)S(1)}, u32[]{:S(2)}, u32[]{:S(2)}) collective-permute-start(bf16[2,64,256]{2,1,0:T(8,128)(2,1)S(1)} %get-tuple-element.35), channel_id=1, source_target_pairs={{0,8},{8,0},{1,9},{9,1},{2,10},{10,2},{3,11},{11,3},{4,12},{12,4},... | collective-permute-start | bytes 196616 | tf_op jit(solution)/shard_map/ppermute | solution.py:281
  18.1 2.2 %split_translation.1.parts_hbm = bf16[15,128,1024]{2,1,0:T(8,128)(2,1)S(1)} custom-call(f32[1,15,64,1024]{3,2,1,0:T(8,128)} %trans_hbm.1), custom_call_target="tpu_custom_call" | custom-call | flops 1000 | bytes 1000 | tf_op jit(solution)/shard_map/split_translation/pallas_call | solution.py:30
  20.3 1.9 %copy-done = bf16[15,128,1024]{2,1,0:T(8,128)(2,1)} copy-done((bf16[15,128,1024]{2,1,0:T(8,128)(2,1)}, bf16[15,128,1024]{2,1,0:T(8,128)(2,1)S(1)}, u32[]{:S(2)}) %copy-start) | copy-done | bytes 3932184
  22.2 6.6 %all-to-all-done.msg_ref = bf16[16,96,128]{2,1,0:T(8,128)(2,1)S(1)} async-done(((bf16[16,96,128]{2,1,0:T(8,128)(2,1)}), bf16[16,96,128]{2,1,0:T(8,128)(2,1)S(1)}, u32[]{:S(2)}, u32[]{:S(2)}) %all-to-all-start) | async-done | bytes 393248 | tf_op jit(solution)/shard_map/all_to_all | solution.py:285
  28.8 4.3 %other_terms.1 = (bf16[16,32,128]{2,1,0:T(8,128)(2,1)}, bf16[128,64]{1,0:T(8,128)(2,1)S(1)}, f32[8,64,1024]{2,1,0:T(8,128)}) custom-call(bf16[16,96,128]{2,1,0:T(8,128)(2,1)S(1)} %all-to-all-done.msg_ref, bf16[15,128,1024]{2,1,0:T(8,128)(2,1)} %copy-done), custom_call_target="tpu_custom_call" | custom-call | flops 1000 | bytes 1000 | tf_op jit(solution)/shard_map/other_terms/pallas_call | solution.py:30
  33.2 4.9 %all-to-all-start.1 = ((bf16[16,32,128]{2,1,0:T(8,128)(2,1)}), bf16[16,32,128]{2,1,0:T(8,128)(2,1)S(1)}, u32[]{:S(2)}, u32[]{:S(2)}) async-start(bf16[16,32,128]{2,1,0:T(8,128)(2,1)} %get-tuple-element.38), calls=%async_computation.1 | async-start | bytes 262144 | tf_op jit(solution)/shard_map/all_to_all | solution.py:285
  38.1 3.2 %collective-permute-start.2 = (bf16[2,2,64,256]{3,2,1,0:T(8,128)(2,1)S(1)}, bf16[2,2,64,256]{3,2,1,0:T(8,128)(2,1)S(1)}, u32[]{:S(2)}, u32[]{:S(2)}) collective-permute-start(bf16[2,2,64,256]{3,2,1,0:T(8,128)(2,1)S(1)} %pad_maximum_fusion.refs_0_), channel_id=1, source_target_pairs={{0,7},{1,0},{2,1},{3,2},{4,3},{5,4},{6,5},{7,6},{8,15},{9,8},{10,9... | collective-permute-start | bytes 393224 | tf_op jit(solution)/shard_map/ppermute | solution.py:293
  41.3 3.0 %own_terms.1.own_ref = bf16[8,64,1024]{2,1,0:T(8,128)(2,1)S(1)} custom-call(bf16[128,64]{1,0:T(8,128)(2,1)S(1)} %get-tuple-element.40.grad_ref, f32[8,64,1024]{2,1,0:T(8,128)S(1)} %collective-permute-done.3.came_ref, bf16[15,128,1024]{2,1,0:T(8,128)(2,1)} %copy-done), custom_call_target="tpu_custom_call" | custom-call | flops 1000 | bytes 1000 | tf_op jit(solution)/shard_map/own_terms/pallas_call | solution.py:30
  44.3 2.3 %collective-permute-done.2.refs_7_ = bf16[2,2,64,256]{3,2,1,0:T(8,128)(2,1)S(1)} collective-permute-done((bf16[2,2,64,256]{3,2,1,0:T(8,128)(2,1)S(1)}, bf16[2,2,64,256]{3,2,1,0:T(8,128)(2,1)S(1)}, u32[]{:S(2)}, u32[]{:S(2)}) %collective-permute-start.2) | collective-permute-done | bytes 131104 | tf_op jit(solution)/shard_map/ppermute | solution.py:293
  49.9 5.1 %all-to-all-start.2 = ((bf16[8,2,64,1024]{3,2,1,0:T(8,128)(2,1)}), bf16[8,2,64,1024]{3,2,1,0:T(8,128)(2,1)S(1)}, u32[]{:S(2)}, u32[]{:S(2)}) async-start(bf16[8,2,64,1024]{3,2,1,0:T(8,128)(2,1)} %copy-done.1), calls=%async_computation.2 | async-start | bytes 4194304 | tf_op jit(solution)/shard_map/all_to_all | solution.py:285
  58.2 3.1 %collective-permute-done.4.refs_2_ = bf16[2,2,64,256]{3,2,1,0:T(8,128)(2,1)S(1)} collective-permute-done((bf16[2,2,64,256]{3,2,1,0:T(8,128)(2,1)}, bf16[2,2,64,256]{3,2,1,0:T(8,128)(2,1)S(1)}, u32[]{:S(2)}, u32[]{:S(2)}) %collective-permute-start.4) | collective-permute-done | bytes 131104 | tf_op jit(solution)/shard_map/ppermute | solution.py:293
  61.8 2.8 %collective-permute-start.8 = (bf16[2,2,64,256]{3,2,1,0:T(8,128)(2,1)S(1)}, bf16[2,2,64,256]{3,2,1,0:T(8,128)(2,1)S(1)}, u32[]{:S(2)}, u32[]{:S(2)}) collective-permute-start(bf16[2,2,64,256]{3,2,1,0:T(8,128)(2,1)S(1)} %collective-permute-done.7.refs_6_), channel_id=1, source_target_pairs={{0,7},{1,0},{2,1},{3,2},{4,3},{5,4},{6,5},{7,6},{8,15},{9,8},{10,9... | collective-permute-start | bytes 393224 | tf_op jit(solution)/shard_map/ppermute | solution.py:293
  64.6 2.9 %collective-permute-done.5.refs_3_ = bf16[2,2,64,256]{3,2,1,0:T(8,128)(2,1)S(1)} collective-permute-done((bf16[2,2,64,256]{3,2,1,0:T(8,128)(2,1)S(1)}, bf16[2,2,64,256]{3,2,1,0:T(8,128)(2,1)S(1)}, u32[]{:S(2)}, u32[]{:S(2)}) %collective-permute-start.5) | collective-permute-done | bytes 131104 | tf_op jit(solution)/shard_map/ppermute | solution.py:293
  68.2 5.5 %collective-permute-done.6.refs_4_ = bf16[2,2,64,256]{3,2,1,0:T(8,128)(2,1)S(1)} collective-permute-done((bf16[2,2,64,256]{3,2,1,0:T(8,128)(2,1)S(1)}, bf16[2,2,64,256]{3,2,1,0:T(8,128)(2,1)S(1)}, u32[]{:S(2)}, u32[]{:S(2)}) %collective-permute-start.6) | collective-permute-done | bytes 131104 | tf_op jit(solution)/shard_map/ppermute | solution.py:293
  74.4 6.1 %near.1 = (f32[64,512]{1,0:T(8,128)S(1)}, bf16[16,128,128]{2,1,0:T(8,128)(2,1)}, f32[16,128,128]{2,1,0:T(8,128)S(1)}) custom-call(s32[1]{0:T(128)S(6)} %copy.11.count_ref, s32[32]{0:T(128)S(1)} %copy-done.3, s32[32]{0:T(128)S(1)} %copy-done.4, bf16[2,64,256]{2,1,0:T(8,128)(2,1)S(1)} %get-tuple-element.44.low_ref, bf16[32,256,256]{2,1,0:T(8,128)(2,1)} %tiles_hbm.1, ...), custom_call_target="tpu_custom_call" | custom-call | flops 1000 | bytes 1000 | tf_op jit(solution)/shard_map/near/pallas_call | solution.py:30
  82.3 2.5 %collective-permute-start.10 = (bf16[16,128,128]{2,1,0:T(8,128)(2,1)}, bf16[16,128,128]{2,1,0:T(8,128)(2,1)}, u32[]{:S(2)}, u32[]{:S(2)}) collective-permute-start(bf16[16,128,128]{2,1,0:T(8,128)(2,1)} %get-tuple-element.53), channel_id=1, source_target_pairs={{0,8},{8,0},{1,9},{9,1},{2,10},{10,2},{3,11},{11,3},{4,12},{12,4},... | collective-permute-start | bytes 1572872 | tf_op jit(solution)/shard_map/ppermute | solution.py:281
  84.8 4.6 %all-to-all-start.3 = ((bf16[16,32,128]{2,1,0:T(8,128)(2,1)}), bf16[16,32,128]{2,1,0:T(8,128)(2,1)S(1)}, u32[]{:S(2)}, u32[]{:S(2)}) async-start(bf16[16,32,128]{2,1,0:T(8,128)(2,1)} %get-tuple-element.51), calls=%async_computation.3 | async-start | bytes 262144 | tf_op jit(solution)/shard_map/all_to_all | solution.py:285
  89.4 6.6 %forward.1.pot_ref = bf16[32,128]{1,0:T(8,128)(2,1)S(1)} custom-call(bf16[8,64,1024]{2,1,0:T(8,128)(2,1)} %collective-permute-done.9.other_ref, bf16[8,2,64,1024]{3,2,1,0:T(8,128)(2,1)S(1)} %all-to-all-done.2.came_ref, bf16[15,128,1024]{2,1,0:T(8,128)(2,1)} %copy-done), custom_call_target="tpu_custom_call" | custom-call | flops 1000 | bytes 1000 | tf_op jit(solution)/shard_map/forward/pallas_call | solution.py:30
  96.1 3.7 %all-to-all-done.3.adj_ref = bf16[16,32,128]{2,1,0:T(8,128)(2,1)S(1)} async-done(((bf16[16,32,128]{2,1,0:T(8,128)(2,1)}), bf16[16,32,128]{2,1,0:T(8,128)(2,1)S(1)}, u32[]{:S(2)}, u32[]{:S(2)}) %all-to-all-start.3) | async-done | bytes 131104 | tf_op jit(solution)/shard_map/all_to_all | solution.py:285
  99.8 2.0 %last_message.1 = bf16[16,192,128]{2,1,0:T(8,128)(2,1)} custom-call(bf16[16,32,128]{2,1,0:T(8,128)(2,1)S(1)} %all-to-all-done.3.adj_ref, bf16[32,128]{1,0:T(8,128)(2,1)S(1)} %forward.1.pot_ref, f32[16,128,128]{2,1,0:T(8,128)S(1)} %get-tuple-element.56.keep_ref, bf16[16,128,128]{2,1,0:T(8,128)(2,1)} %collective-permute-done.10.mate_ref), custom_call_target="tpu_custom_call" | custom-call | flops 1000 | bytes 1000 | tf_op jit(solution)/shard_map/last_message/pallas_call | solution.py:30
  101.8 6.6 %all-to-all-start.4 = ((bf16[16,192,128]{2,1,0:T(8,128)(2,1)}), bf16[16,192,128]{2,1,0:T(8,128)(2,1)S(1)}, u32[]{:S(2)}, u32[]{:S(2)}) async-start(bf16[16,192,128]{2,1,0:T(8,128)(2,1)} %last_message.1), calls=%async_computation.4 | async-start | bytes 1572864 | tf_op jit(solution)/shard_map/all_to_all | solution.py:285
  109.9 21.0 %all-to-all-done.4.msg_ref = bf16[16,192,128]{2,1,0:T(8,128)(2,1)S(1)} async-done(((bf16[16,192,128]{2,1,0:T(8,128)(2,1)}), bf16[16,192,128]{2,1,0:T(8,128)(2,1)S(1)}, u32[]{:S(2)}, u32[]{:S(2)}) %all-to-all-start.4) | async-done | bytes 786464 | tf_op jit(solution)/shard_map/all_to_all | solution.py:285
  (46 shorter events, 12.3 us)
Async XLA Ops:
  3.6 25.2 %all-to-all-start = ((bf16[16,96,128]{2,1,0:T(8,128)(2,1)}), bf16[16,96,128]{2,1,0:T(8,128)(2,1)S(1)}, u32[]{:S(2)}, u32[]{:S(2)}) async-start(bf16[16,96,128]{2,1,0:T(8,128)(2,1)} %get-tuple-element.34), calls=%async_computation | async-start | bytes 786432 | tf_op jit(solution)/shard_map/all_to_all | solution.py:285
  14.7 7.5 %collective-permute-start = (bf16[2,64,256]{2,1,0:T(8,128)(2,1)S(1)}, bf16[2,64,256]{2,1,0:T(8,128)(2,1)S(1)}, u32[]{:S(2)}, u32[]{:S(2)}) collective-permute-start(bf16[2,64,256]{2,1,0:T(8,128)(2,1)S(1)} %get-tuple-element.35), channel_id=1, source_target_pairs={{0,8},{8,0},{1,9},{9,1},{2,10},{10,2},{3,11},{11,3},{4,12},{12,4},... | collective-permute-start | bytes 196616 | tf_op jit(solution)/shard_map/ppermute | solution.py:281
  33.1 8.2 %collective-permute-start.3 = (f32[8,64,1024]{2,1,0:T(8,128)}, f32[8,64,1024]{2,1,0:T(8,128)S(1)}, u32[]{:S(2)}, u32[]{:S(2)}) collective-permute-start(f32[8,64,1024]{2,1,0:T(8,128)} %get-tuple-element.41), channel_id=1, source_target_pairs={{0,16},{16,0},{1,17},{17,1},{2,18},{18,2},{3,19},{19,3},{4,20},{20... | collective-permute-start | bytes 6291464 | tf_op jit(solution)/shard_map/ppermute | solution.py:281
  33.2 15.2 %all-to-all-start.1 = ((bf16[16,32,128]{2,1,0:T(8,128)(2,1)}), bf16[16,32,128]{2,1,0:T(8,128)(2,1)S(1)}, u32[]{:S(2)}, u32[]{:S(2)}) async-start(bf16[16,32,128]{2,1,0:T(8,128)(2,1)} %get-tuple-element.38), calls=%async_computation.1 | async-start | bytes 262144 | tf_op jit(solution)/shard_map/all_to_all | solution.py:285
  38.1 6.2 %copy-start.5 = (bf16[2,2,64,256]{3,2,1,0:T(8,128)(2,1)}, bf16[2,2,64,256]{3,2,1,0:T(8,128)(2,1)S(1)}, u32[]{:S(2)}) copy-start(bf16[2,2,64,256]{3,2,1,0:T(8,128)(2,1)S(1)} %pad_maximum_fusion.refs_0_) | copy-start | bytes 393220
  38.1 8.5 %collective-permute-start.2 = (bf16[2,2,64,256]{3,2,1,0:T(8,128)(2,1)S(1)}, bf16[2,2,64,256]{3,2,1,0:T(8,128)(2,1)S(1)}, u32[]{:S(2)}, u32[]{:S(2)}) collective-permute-start(bf16[2,2,64,256]{3,2,1,0:T(8,128)(2,1)S(1)} %pad_maximum_fusion.refs_0_), channel_id=1, source_target_pairs={{0,7},{1,0},{2,1},{3,2},{4,3},{5,4},{6,5},{7,6},{8,15},{9,8},{10,9... | collective-permute-start | bytes 393224 | tf_op jit(solution)/shard_map/ppermute | solution.py:293
  41.3 7.1 %collective-permute-start.1 = (bf16[2,2,64,256]{3,2,1,0:T(8,128)(2,1)S(1)}, bf16[2,2,64,256]{3,2,1,0:T(8,128)(2,1)}, u32[]{:S(2)}, u32[]{:S(2)}) collective-permute-start(bf16[2,2,64,256]{3,2,1,0:T(8,128)(2,1)S(1)} %pad_maximum_fusion.refs_0_), channel_id=1, source_target_pairs={{0,1},{1,2},{2,3},{3,4},{4,5},{5,6},{6,7},{7,0},{8,9},{9,10},{10,1... | collective-permute-start | bytes 393224 | tf_op jit(solution)/shard_map/ppermute | solution.py:293
  49.9 6.7 %copy-start.7 = (bf16[2,2,64,256]{3,2,1,0:T(8,128)(2,1)S(1)}, bf16[2,2,64,256]{3,2,1,0:T(8,128)(2,1)}, u32[]{:S(2)}) copy-start(bf16[2,2,64,256]{3,2,1,0:T(8,128)(2,1)} %copy-done.6) | copy-start | bytes 393220
  49.9 24.5 %copy-start.3 = (s32[32]{0:T(128)S(1)}, s32[32]{0:T(128)}, u32[]{:S(2)}) copy-start(s32[32]{0:T(128)} %rows_ref.1) | copy-start | bytes 388
  49.9 24.5 %copy-start.4 = (s32[32]{0:T(128)S(1)}, s32[32]{0:T(128)}, u32[]{:S(2)}) copy-start(s32[32]{0:T(128)} %cols_ref.1) | copy-start | bytes 388
  49.9 31.2 %all-to-all-start.2 = ((bf16[8,2,64,1024]{3,2,1,0:T(8,128)(2,1)}), bf16[8,2,64,1024]{3,2,1,0:T(8,128)(2,1)S(1)}, u32[]{:S(2)}, u32[]{:S(2)}) async-start(bf16[8,2,64,1024]{3,2,1,0:T(8,128)(2,1)} %copy-done.1), calls=%async_computation.2 | async-start | bytes 4194304 | tf_op jit(solution)/shard_map/all_to_all | solution.py:285
  55.0 6.4 %collective-permute-start.4 = (bf16[2,2,64,256]{3,2,1,0:T(8,128)(2,1)}, bf16[2,2,64,256]{3,2,1,0:T(8,128)(2,1)S(1)}, u32[]{:S(2)}, u32[]{:S(2)}) collective-permute-start(bf16[2,2,64,256]{3,2,1,0:T(8,128)(2,1)} %collective-permute-done.1.refs_1_), channel_id=1, source_target_pairs={{0,1},{1,2},{2,3},{3,4},{4,5},{5,6},{6,7},{7,0},{8,9},{9,10},{10,1... | collective-permute-start | bytes 393224 | tf_op jit(solution)/shard_map/ppermute | solution.py:293
  56.6 5.2 %collective-permute-start.7 = (bf16[2,2,64,256]{3,2,1,0:T(8,128)(2,1)S(1)}, bf16[2,2,64,256]{3,2,1,0:T(8,128)(2,1)S(1)}, u32[]{:S(2)}, u32[]{:S(2)}) collective-permute-start(bf16[2,2,64,256]{3,2,1,0:T(8,128)(2,1)S(1)} %copy-done.7), channel_id=1, source_target_pairs={{0,7},{1,0},{2,1},{3,2},{4,3},{5,4},{6,5},{7,6},{8,15},{9,8},{10,9... | collective-permute-start | bytes 393224 | tf_op jit(solution)/shard_map/ppermute | solution.py:293
  61.4 12.4 %copy-start.8 = (bf16[2,2,64,256]{3,2,1,0:T(8,128)(2,1)}, bf16[2,2,64,256]{3,2,1,0:T(8,128)(2,1)S(1)}, u32[]{:S(2)}) copy-start(bf16[2,2,64,256]{3,2,1,0:T(8,128)(2,1)S(1)} %collective-permute-done.4.refs_2_) | copy-start | bytes 393220
  61.4 6.2 %collective-permute-start.5 = (bf16[2,2,64,256]{3,2,1,0:T(8,128)(2,1)S(1)}, bf16[2,2,64,256]{3,2,1,0:T(8,128)(2,1)S(1)}, u32[]{:S(2)}, u32[]{:S(2)}) collective-permute-start(bf16[2,2,64,256]{3,2,1,0:T(8,128)(2,1)S(1)} %collective-permute-done.4.refs_2_), channel_id=1, source_target_pairs={{0,1},{1,2},{2,3},{3,4},{4,5},{5,6},{6,7},{7,0},{8,9},{9,10},{10,1... | collective-permute-start | bytes 393224 | tf_op jit(solution)/shard_map/ppermute | solution.py:293
  61.8 12.0 %copy-start.9 = (bf16[2,2,64,256]{3,2,1,0:T(8,128)(2,1)}, bf16[2,2,64,256]{3,2,1,0:T(8,128)(2,1)S(1)}, u32[]{:S(2)}) copy-start(bf16[2,2,64,256]{3,2,1,0:T(8,128)(2,1)S(1)} %collective-permute-done.7.refs_6_) | copy-start | bytes 393220
  61.8 6.4 %collective-permute-start.8 = (bf16[2,2,64,256]{3,2,1,0:T(8,128)(2,1)S(1)}, bf16[2,2,64,256]{3,2,1,0:T(8,128)(2,1)S(1)}, u32[]{:S(2)}, u32[]{:S(2)}) collective-permute-start(bf16[2,2,64,256]{3,2,1,0:T(8,128)(2,1)S(1)} %collective-permute-done.7.refs_6_), channel_id=1, source_target_pairs={{0,7},{1,0},{2,1},{3,2},{4,3},{5,4},{6,5},{7,6},{8,15},{9,8},{10,9... | collective-permute-start | bytes 393224 | tf_op jit(solution)/shard_map/ppermute | solution.py:293
  67.6 6.2 %copy-start.10 = (bf16[2,2,64,256]{3,2,1,0:T(8,128)(2,1)}, bf16[2,2,64,256]{3,2,1,0:T(8,128)(2,1)S(1)}, u32[]{:S(2)}) copy-start(bf16[2,2,64,256]{3,2,1,0:T(8,128)(2,1)S(1)} %collective-permute-done.5.refs_3_) | copy-start | bytes 393220
  67.6 6.2 %collective-permute-start.6 = (bf16[2,2,64,256]{3,2,1,0:T(8,128)(2,1)S(1)}, bf16[2,2,64,256]{3,2,1,0:T(8,128)(2,1)S(1)}, u32[]{:S(2)}, u32[]{:S(2)}) collective-permute-start(bf16[2,2,64,256]{3,2,1,0:T(8,128)(2,1)S(1)} %collective-permute-done.5.refs_3_), channel_id=1, source_target_pairs={{0,1},{1,2},{2,3},{3,4},{4,5},{5,6},{6,7},{7,0},{8,9},{9,10},{10,1... | collective-permute-start | bytes 393224 | tf_op jit(solution)/shard_map/ppermute | solution.py:293
  68.2 5.5 %copy-start.11 = (bf16[2,2,64,256]{3,2,1,0:T(8,128)(2,1)}, bf16[2,2,64,256]{3,2,1,0:T(8,128)(2,1)S(1)}, u32[]{:S(2)}) copy-start(bf16[2,2,64,256]{3,2,1,0:T(8,128)(2,1)S(1)} %collective-permute-done.8.refs_5_) | copy-start | bytes 393220
  82.3 7.1 %collective-permute-start.9 = (bf16[8,64,1024]{2,1,0:T(8,128)(2,1)}, bf16[8,64,1024]{2,1,0:T(8,128)(2,1)}, u32[]{:S(2)}, u32[]{:S(2)}) collective-permute-start(bf16[8,64,1024]{2,1,0:T(8,128)(2,1)} %get-tuple-element.52), channel_id=1, source_target_pairs={{0,16},{16,0},{1,17},{17,1},{2,18},{18,2},{3,19},{19,3},{4,20},{20... | collective-permute-start | bytes 3145736 | tf_op jit(solution)/shard_map/ppermute | solution.py:281
  82.3 17.5 %collective-permute-start.10 = (bf16[16,128,128]{2,1,0:T(8,128)(2,1)}, bf16[16,128,128]{2,1,0:T(8,128)(2,1)}, u32[]{:S(2)}, u32[]{:S(2)}) collective-permute-start(bf16[16,128,128]{2,1,0:T(8,128)(2,1)} %get-tuple-element.53), channel_id=1, source_target_pairs={{0,8},{8,0},{1,9},{9,1},{2,10},{10,2},{3,11},{11,3},{4,12},{12,4},... | collective-permute-start | bytes 1572872 | tf_op jit(solution)/shard_map/ppermute | solution.py:281
  84.8 15.0 %all-to-all-start.3 = ((bf16[16,32,128]{2,1,0:T(8,128)(2,1)}), bf16[16,32,128]{2,1,0:T(8,128)(2,1)S(1)}, u32[]{:S(2)}, u32[]{:S(2)}) async-start(bf16[16,32,128]{2,1,0:T(8,128)(2,1)} %get-tuple-element.51), calls=%async_computation.3 | async-start | bytes 262144 | tf_op jit(solution)/shard_map/all_to_all | solution.py:285
  101.8 29.2 %all-to-all-start.4 = ((bf16[16,192,128]{2,1,0:T(8,128)(2,1)}), bf16[16,192,128]{2,1,0:T(8,128)(2,1)S(1)}, u32[]{:S(2)}, u32[]{:S(2)}) async-start(bf16[16,192,128]{2,1,0:T(8,128)(2,1)} %last_message.1), calls=%async_computation.4 | async-start | bytes 1572864 | tf_op jit(solution)/shard_map/all_to_all | solution.py:285
  (5 other events, 5.2 us)

commit v8 on v7

--- a/solution.py
+++ b/solution.py
@@ -185,7 +185,7 @@
 
 def near(count_ref, rows_ref, cols_ref, low_ref, tiles_hbm, *refs):
     pieces, refs = refs[:8], refs[8:]
-    ahead_ref, send_ref, keep_ref, acc, behind, drives, tiles_ref, tile_sems, piece_sems = refs
+    ahead_ref, keep_ref, across_ref, beside_ref, both_ref, acc, behind, drives, tiles_ref, tile_sems, piece_sems = refs
 
     def tile_copy(index):
         span = pl.ds(index * 4, 4)
@@ -236,20 +236,24 @@
     lax.fori_loop(groups, 8, drain, 0)
     for part in range(2):
         ahead_ref[:, part * 256 : part * 256 + 256] = acc[part]
+    parity = lax.rem(my_z, 2)
+    mine = pl.ds(pl.multiple_of(parity * 128, 128), 128)
+    theirs = pl.ds(pl.multiple_of((1 - parity) * 128, 128), 128)
     for target in range(16):
-        for part in range(2):
-            rows = slice(part * 64, part * 64 + 64)
-            cols = slice(part * 128, part * 128 + 128)
-            send_ref[target, rows, :] = behind[2 * target + 1 - my_half, :, cols].astype(bf16)
-            keep_ref[target, rows, :] = behind[2 * target + my_half, :, cols]
-
-
-def last_message(adj_ref, pot_ref, keep_ref, mate_ref, out_ref):
+        keep_ref[target] = behind[2 * target + my_half, :, mine]
+        across_ref[target] = behind[2 * target + 1 - my_half, :, mine].astype(bf16)
+        beside_ref[target] = behind[2 * target + my_half, :, theirs].astype(bf16)
+        both_ref[target] = behind[2 * target + 1 - my_half, :, theirs].astype(bf16)
+
+
+def last_message(adj_ref, pot_ref, keep_ref, across_ref, beside_ref, both_ref, out_ref):
     adjoint = jnp.sum(adj_ref[...].astype(f32), axis=0).astype(bf16)
     for piece in range(16):
         out_ref[piece, 0:32, :] = adjoint
         out_ref[piece, 32:64, :] = pot_ref[...]
-        out_ref[piece, 64:192, :] = (keep_ref[piece] + mate_ref[piece].astype(f32)).astype(bf16)
+        near_sum = keep_ref[piece] + across_ref[piece].astype(f32)
+        near_sum = near_sum + beside_ref[piece].astype(f32) + both_ref[piece].astype(f32)
+        out_ref[piece, 64:128, :] = near_sum.astype(bf16)
 
 
 def stage(*refs):
@@ -267,10 +271,11 @@
     packed = packed.astype(f32).T.astype(bf16)
     near_sums = []
     for block in range(2):
-        value = msg_ref[block * 8, 64:192, :].astype(f32)
-        for z in range(1, 8):
-            value = value + msg_ref[block * 8 + z, 64:192, :].astype(f32)
-        near_sums += [value[:64], value[64:]]
+        for parity in range(2):
+            value = msg_ref[block * 8 + parity, 64:128, :].astype(f32)
+            for z in range(parity + 2, 8, 2):
+                value = value + msg_ref[block * 8 + z, 64:128, :].astype(f32)
+            near_sums.append(value)
     sens_ref[...] = dot(adjoint, skin_ref[...]) + jnp.concatenate(near_sums, axis=1)
     upper = jnp.concatenate([skout_ref[r * 64 : r * 64 + 32, :] for r in range(16)], axis=0)
     lower = jnp.concatenate([skout_ref[r * 64 + 32 : r * 64 + 64, :] for r in range(16)], axis=0)
@@ -343,9 +348,9 @@
     up2, down2 = shift(up1, 1), shift(down1, -1)
     up3, down3 = shift(up2, 1), shift(down2, -1)
     up4 = shift(up3, 1)
-    ahead, send, keep = call(
+    ahead, keep, *quarters = call(
         near,
-        [((64, 512), f32), ((16, 128, 128), bf16), ((16, 128, 128), f32)],
+        [((64, 512), f32), ((16, 64, 128), f32)] + [((16, 64, 128), bf16)] * 3,
         [tile_count, tile_rows, tile_cols, low, in_hbm(tiles)]
         + [in_hbm(piece) for piece in (here, up1, up2, up3, up4, down3, down2, down1)],
         specs=[smem(), smem(), smem(), vmem()] + [hbm()] * 9,
@@ -359,8 +364,11 @@
         ],
         name="near",
     )
-    both, ahead, send, keep = tie(exchange(both, FACE), ahead, send, keep)
-    mate_near = swap(send, "xhi")
+    both, ahead = tie(exchange(both, FACE), ahead)
+    quarters = [
+        lax.ppermute(value, ROWS, [(i, i ^ mask) for i in range(16)])
+        for value, mask in zip(quarters, (8, 1, 9))
+    ]
     adjoint, charges = call(
         unpack,
         [((16, 32, 128), bf16), ((8, 64, 1024), bf16)],
@@ -376,11 +384,11 @@
         scratch=[pltpu.VMEM((16, 128, 1024), bf16), pltpu.SemaphoreType.DMA((16,))],
         name="forward",
     )
-    adjoint, potential, mate_near = tie(exchange(adjoint, ROWS), potential, mate_near)
+    adjoint, potential, *quarters = tie(exchange(adjoint, ROWS), potential, *quarters)
     (last,) = call(
         last_message,
-        [((16, 192, 128), bf16)],
-        [adjoint, potential, keep, mate_near],
+        [((16, 128, 128), bf16)],
+        [adjoint, potential, keep, *quarters],
         name="last_message",
     )
     staged = call(

time: 134 us -> 133 us (level)
  waiting for transfers between devices: 46.3 us -> 40.1 us
  starting transfers between devices: 47.9 us -> 53.7 us
  Pallas kernels: 31.3 us -> 28.7 us
  local copies, waits for them, and re-layouts: 5.15 us -> 7.67 us
    all_to_all x5, waiting for transfers between devices: 31.3 us -> 24.2 us  [exchange(): return lax.all_to_all(value, axes, 0, 0, tiled=True)]
    ppermute x0 -> x3, starting transfers between devices: none -> 6.13 us  [on_device(): lax.ppermute(value, ROWS, [(i, i ^ mask) for i in range(16)])]
    pallas_call x11, Pallas kernels: 31.3 us -> 28.7 us  [call(): pl.pallas_call(kernel, out_shape=[jax.ShapeDtypeStruct(s, d) for s, d in...]
    unnamed x26 -> x32, local copies, waits for them, and re-layouts: 5.15 us -> 7.67 us
    ppermute x4 -> x3, starting transfers between devices: 6.01 us -> 3.53 us  [swap(): return lax.ppermute(value, axis, [(0, 1), (1, 0)])]
    all_to_all x5, starting transfers between devices: 32.2 us -> 34.3 us  [exchange(): return lax.all_to_all(value, axes, 0, 0, tiled=True)]
  transfers between devices with their start and end apart: 16 -> 18, of which waited for: 8 -> 9; matrix products, arithmetic and copies ran while one was open for 0% -> 0% of each run, Pallas kernels for 15% -> 13%
where the time goes in v8:
time: 133 us; the launch traced here: 132 us
  starting transfers between devices  53.7 us (40%)
  waiting for transfers between devices  40.1 us (30%)
  Pallas kernels  28.7 us (22%)
  local copies, waits for them, and re-layouts  7.67 us (6%)
  between operations  1.51 us (1%)
    all_to_all x5, starting transfers between devices, exchange(): return lax.all_to_all(value, axes, 0, 0, tiled=True)  34.3 us
    pallas_call x11, Pallas kernels, call(): pl.pallas_call(kernel, out_shape=[jax.ShapeDtypeStruct(s, d) for s, d in...  28.7 us
    all_to_all x5, waiting for transfers between devices, exchange(): return lax.all_to_all(value, axes, 0, 0, tiled=True)  24.2 us
    ppermute x7, waiting for transfers between devices, shift(): return lax.ppermute(value, 'z', [(i, (i + step) % 8) for i in range(8)])  15 us
    ppermute x7, starting transfers between devices, shift(): return lax.ppermute(value, 'z', [(i, (i + step) % 8) for i in range(8)])  9.69 us
    unnamed x32, local copies, waits for them, and re-layouts  7.67 us
    ppermute x3, starting transfers between devices, on_device(): lax.ppermute(value, ROWS, [(i, i ^ mask) for i in range(16)])  6.13 us
    ppermute x3, starting transfers between devices, swap(): return lax.ppermute(value, axis, [(0, 1), (1, 0)])  3.53 us
  transfers between devices with their start and end apart: 18, of which 9 were waited for; matrix products, arithmetic and copies ran while one was open for 0% of the time, Pallas kernels for 13%

profile of v8, /device:TPU:8, one launch (start us, length us, event | category | flops | bytes accessed | tf_op | source)
XLA Modules:
  0.0 131.7 jit_solution(15816052693541445864)
XLA Ops:
  0.6 3.0 %prepare.1 = (bf16[2,64,256]{2,1,0:T(8,128)(2,1)S(1)}, bf16[2,64,256]{2,1,0:T(8,128)(2,1)S(1)}, bf16[16,96,128]{2,1,0:T(8,128)(2,1)}) custom-call(f32[64,512]{1,0:T(8,128)} %exc_hbm.1, f32[64,512]{1,0:T(8,128)} %loads_hbm.1, bf16[1024,512]{1,0:T(8,128)(2,1)} %refs_0_.1, bf16[1024,512]{1,0:T(8,128)(2,1)} %refs_1_.1), custom_call_target="tpu_custom_call" | custom-call | flops 1000 | bytes 1000 | tf_op jit(solution)/shard_map/prepare/pallas_call | solution.py:30
  3.6 11.0 %all-to-all-start = ((bf16[16,96,128]{2,1,0:T(8,128)(2,1)}), bf16[16,96,128]{2,1,0:T(8,128)(2,1)S(1)}, u32[]{:S(2)}, u32[]{:S(2)}) async-start(bf16[16,96,128]{2,1,0:T(8,128)(2,1)} %get-tuple-element.36), calls=%async_computation | async-start | bytes 786432 | tf_op jit(solution)/shard_map/all_to_all | solution.py:290
  14.7 3.4 %collective-permute-start = (bf16[2,64,256]{2,1,0:T(8,128)(2,1)S(1)}, bf16[2,64,256]{2,1,0:T(8,128)(2,1)S(1)}, u32[]{:S(2)}, u32[]{:S(2)}) collective-permute-start(bf16[2,64,256]{2,1,0:T(8,128)(2,1)S(1)} %get-tuple-element.37), channel_id=1, source_target_pairs={{0,8},{8,0},{1,9},{9,1},{2,10},{10,2},{3,11},{11,3},{4,12},{12,4},... | collective-permute-start | bytes 196616 | tf_op jit(solution)/shard_map/ppermute | solution.py:286
  18.1 2.2 %split_translation.1.parts_hbm = bf16[15,128,1024]{2,1,0:T(8,128)(2,1)S(1)} custom-call(f32[1,15,64,1024]{3,2,1,0:T(8,128)} %trans_hbm.1), custom_call_target="tpu_custom_call" | custom-call | flops 1000 | bytes 1000 | tf_op jit(solution)/shard_map/split_translation/pallas_call | solution.py:30
  20.3 1.9 %copy-done = bf16[15,128,1024]{2,1,0:T(8,128)(2,1)} copy-done((bf16[15,128,1024]{2,1,0:T(8,128)(2,1)}, bf16[15,128,1024]{2,1,0:T(8,128)(2,1)S(1)}, u32[]{:S(2)}) %copy-start) | copy-done | bytes 3932184
  22.2 6.6 %all-to-all-done.msg_ref = bf16[16,96,128]{2,1,0:T(8,128)(2,1)S(1)} async-done(((bf16[16,96,128]{2,1,0:T(8,128)(2,1)}), bf16[16,96,128]{2,1,0:T(8,128)(2,1)S(1)}, u32[]{:S(2)}, u32[]{:S(2)}) %all-to-all-start) | async-done | bytes 393248 | tf_op jit(solution)/shard_map/all_to_all | solution.py:290
  28.8 4.3 %other_terms.1 = (bf16[16,32,128]{2,1,0:T(8,128)(2,1)}, bf16[128,64]{1,0:T(8,128)(2,1)S(1)}, f32[8,64,1024]{2,1,0:T(8,128)}) custom-call(bf16[16,96,128]{2,1,0:T(8,128)(2,1)S(1)} %all-to-all-done.msg_ref, bf16[15,128,1024]{2,1,0:T(8,128)(2,1)} %copy-done), custom_call_target="tpu_custom_call" | custom-call | flops 1000 | bytes 1000 | tf_op jit(solution)/shard_map/other_terms/pallas_call | solution.py:30
  33.2 4.8 %all-to-all-start.1 = ((bf16[16,32,128]{2,1,0:T(8,128)(2,1)}), bf16[16,32,128]{2,1,0:T(8,128)(2,1)S(1)}, u32[]{:S(2)}, u32[]{:S(2)}) async-start(bf16[16,32,128]{2,1,0:T(8,128)(2,1)} %get-tuple-element.40), calls=%async_computation.1 | async-start | bytes 262144 | tf_op jit(solution)/shard_map/all_to_all | solution.py:290
  38.1 3.2 %collective-permute-start.2 = (bf16[2,2,64,256]{3,2,1,0:T(8,128)(2,1)S(1)}, bf16[2,2,64,256]{3,2,1,0:T(8,128)(2,1)S(1)}, u32[]{:S(2)}, u32[]{:S(2)}) collective-permute-start(bf16[2,2,64,256]{3,2,1,0:T(8,128)(2,1)S(1)} %pad_maximum_fusion.refs_0_), channel_id=1, source_target_pairs={{0,7},{1,0},{2,1},{3,2},{4,3},{5,4},{6,5},{7,6},{8,15},{9,8},{10,9... | collective-permute-start | bytes 393224 | tf_op jit(solution)/shard_map/ppermute | solution.py:298
  41.3 3.0 %own_terms.1.own_ref = bf16[8,64,1024]{2,1,0:T(8,128)(2,1)S(1)} custom-call(bf16[128,64]{1,0:T(8,128)(2,1)S(1)} %get-tuple-element.42.grad_ref, f32[8,64,1024]{2,1,0:T(8,128)S(1)} %collective-permute-done.3.came_ref, bf16[15,128,1024]{2,1,0:T(8,128)(2,1)} %copy-done), custom_call_target="tpu_custom_call" | custom-call | flops 1000 | bytes 1000 | tf_op jit(solution)/shard_map/own_terms/pallas_call | solution.py:30
  44.3 2.3 %collective-permute-done.2.refs_7_ = bf16[2,2,64,256]{3,2,1,0:T(8,128)(2,1)S(1)} collective-permute-done((bf16[2,2,64,256]{3,2,1,0:T(8,128)(2,1)S(1)}, bf16[2,2,64,256]{3,2,1,0:T(8,128)(2,1)S(1)}, u32[]{:S(2)}, u32[]{:S(2)}) %collective-permute-start.2) | collective-permute-done | bytes 131104 | tf_op jit(solution)/shard_map/ppermute | solution.py:298
  49.9 5.1 %all-to-all-start.2 = ((bf16[8,2,64,1024]{3,2,1,0:T(8,128)(2,1)}), bf16[8,2,64,1024]{3,2,1,0:T(8,128)(2,1)S(1)}, u32[]{:S(2)}, u32[]{:S(2)}) async-start(bf16[8,2,64,1024]{3,2,1,0:T(8,128)(2,1)} %copy-done.1), calls=%async_computation.2 | async-start | bytes 4194304 | tf_op jit(solution)/shard_map/all_to_all | solution.py:290
  58.3 3.1 %collective-permute-done.4.refs_2_ = bf16[2,2,64,256]{3,2,1,0:T(8,128)(2,1)S(1)} collective-permute-done((bf16[2,2,64,256]{3,2,1,0:T(8,128)(2,1)}, bf16[2,2,64,256]{3,2,1,0:T(8,128)(2,1)S(1)}, u32[]{:S(2)}, u32[]{:S(2)}) %collective-permute-start.4) | collective-permute-done | bytes 131104 | tf_op jit(solution)/shard_map/ppermute | solution.py:298
  61.8 2.8 %collective-permute-start.8 = (bf16[2,2,64,256]{3,2,1,0:T(8,128)(2,1)S(1)}, bf16[2,2,64,256]{3,2,1,0:T(8,128)(2,1)S(1)}, u32[]{:S(2)}, u32[]{:S(2)}) collective-permute-start(bf16[2,2,64,256]{3,2,1,0:T(8,128)(2,1)S(1)} %collective-permute-done.7.refs_6_), channel_id=1, source_target_pairs={{0,7},{1,0},{2,1},{3,2},{4,3},{5,4},{6,5},{7,6},{8,15},{9,8},{10,9... | collective-permute-start | bytes 393224 | tf_op jit(solution)/shard_map/ppermute | solution.py:298
  64.7 2.9 %collective-permute-done.5.refs_3_ = bf16[2,2,64,256]{3,2,1,0:T(8,128)(2,1)S(1)} collective-permute-done((bf16[2,2,64,256]{3,2,1,0:T(8,128)(2,1)S(1)}, bf16[2,2,64,256]{3,2,1,0:T(8,128)(2,1)S(1)}, u32[]{:S(2)}, u32[]{:S(2)}) %collective-permute-start.5) | collective-permute-done | bytes 131104 | tf_op jit(solution)/shard_map/ppermute | solution.py:298
  68.3 5.5 %collective-permute-done.6.refs_4_ = bf16[2,2,64,256]{3,2,1,0:T(8,128)(2,1)S(1)} collective-permute-done((bf16[2,2,64,256]{3,2,1,0:T(8,128)(2,1)S(1)}, bf16[2,2,64,256]{3,2,1,0:T(8,128)(2,1)S(1)}, u32[]{:S(2)}, u32[]{:S(2)}) %collective-permute-start.6) | collective-permute-done | bytes 131104 | tf_op jit(solution)/shard_map/ppermute | solution.py:298
  74.4 4.8 %near.1 = (f32[64,512]{1,0:T(8,128)S(1)}, f32[16,64,128]{2,1,0:T(8,128)S(1)}, bf16[16,64,128]{2,1,0:T(8,128)(2,1)}, bf16[16,64,128]{2,1,0:T(8,128)(2,1)}, bf16[16,64,128]{2,1,0:T(8,128)(2,1)}) custom-call(s32[1]{0:T(128)S(6)} %copy.11.count_ref, s32[32]{0:T(128)S(1)} %copy-done.6, s32[32]{0:T(128)S(1)} %copy-done.7, ...), custom_call_target="tpu_custom_call" | custom-call | flops 1000 | bytes 1000 | tf_op jit(solution)/shard_map/near/pallas_call | solution.py:30
  82.5 4.7 %collective-permute-start.10 = (bf16[16,64,128]{2,1,0:T(8,128)(2,1)}, bf16[16,64,128]{2,1,0:T(8,128)(2,1)S(1)}, u32[]{:S(2)}, u32[]{:S(2)}) collective-permute-start(bf16[16,64,128]{2,1,0:T(8,128)(2,1)} %get-tuple-element.53), channel_id=1, source_target_pairs={{0,8},{1,9},{2,10},{3,11},{4,12},{5,13},{6,14},{7,15},{8,0},{9,1},... | collective-permute-start | bytes 786440 | tf_op jit(solution)/shard_map/ppermute | solution.py:369
  88.6 7.0 %all-to-all-start.3 = ((bf16[16,32,128]{2,1,0:T(8,128)(2,1)}), bf16[16,32,128]{2,1,0:T(8,128)(2,1)S(1)}, u32[]{:S(2)}, u32[]{:S(2)}) async-start(bf16[16,32,128]{2,1,0:T(8,128)(2,1)} %copy-done.5), calls=%async_computation.3 | async-start | bytes 262144 | tf_op jit(solution)/shard_map/all_to_all | solution.py:290
  95.6 5.4 %forward.1.pot_ref = bf16[32,128]{1,0:T(8,128)(2,1)S(1)} custom-call(bf16[8,64,1024]{2,1,0:T(8,128)(2,1)S(1)} %collective-permute-done.9.other_ref, bf16[8,2,64,1024]{3,2,1,0:T(8,128)(2,1)S(1)} %all-to-all-done.2.came_ref, bf16[15,128,1024]{2,1,0:T(8,128)(2,1)} %copy-done), custom_call_target="tpu_custom_call" | custom-call | flops 1000 | bytes 1000 | tf_op jit(solution)/shard_map/forward/pallas_call | solution.py:30
  102.0 3.7 %all-to-all-done.3.adj_ref = bf16[16,32,128]{2,1,0:T(8,128)(2,1)S(1)} async-done(((bf16[16,32,128]{2,1,0:T(8,128)(2,1)}), bf16[16,32,128]{2,1,0:T(8,128)(2,1)S(1)}, u32[]{:S(2)}, u32[]{:S(2)}) %all-to-all-start.3) | async-done | bytes 131104 | tf_op jit(solution)/shard_map/all_to_all | solution.py:290
  106.7 1.9 %last_message.1 = bf16[16,128,128]{2,1,0:T(8,128)(2,1)} custom-call(bf16[16,32,128]{2,1,0:T(8,128)(2,1)S(1)} %all-to-all-done.3.adj_ref, bf16[32,128]{1,0:T(8,128)(2,1)S(1)} %forward.1.pot_ref, f32[16,64,128]{2,1,0:T(8,128)S(1)} %copy-done.3, bf16[16,64,128]{2,1,0:T(8,128)(2,1)S(1)} %collective-permute-done.10.across_ref, ...), custom_call_target="tpu_custom_call" | custom-call | flops 1000 | bytes 1000 | tf_op jit(solution)/shard_map/last_message/pallas_call | solution.py:30
  108.6 6.4 %all-to-all-start.4 = ((bf16[16,128,128]{2,1,0:T(8,128)(2,1)}), bf16[16,128,128]{2,1,0:T(8,128)(2,1)S(1)}, u32[]{:S(2)}, u32[]{:S(2)}) async-start(bf16[16,128,128]{2,1,0:T(8,128)(2,1)} %last_message.1), calls=%async_computation.4 | async-start | bytes 1048576 | tf_op jit(solution)/shard_map/all_to_all | solution.py:290
  116.6 13.9 %all-to-all-done.4.msg_ref = bf16[16,128,128]{2,1,0:T(8,128)(2,1)S(1)} async-done(((bf16[16,128,128]{2,1,0:T(8,128)(2,1)}), bf16[16,128,128]{2,1,0:T(8,128)(2,1)S(1)}, u32[]{:S(2)}, u32[]{:S(2)}) %all-to-all-start.4) | async-done | bytes 524320 | tf_op jit(solution)/shard_map/all_to_all | solution.py:290
  (56 shorter events, 17.2 us)
Async XLA Ops:
  3.6 25.2 %all-to-all-start = ((bf16[16,96,128]{2,1,0:T(8,128)(2,1)}), bf16[16,96,128]{2,1,0:T(8,128)(2,1)S(1)}, u32[]{:S(2)}, u32[]{:S(2)}) async-start(bf16[16,96,128]{2,1,0:T(8,128)(2,1)} %get-tuple-element.36), calls=%async_computation | async-start | bytes 786432 | tf_op jit(solution)/shard_map/all_to_all | solution.py:290
  14.7 7.5 %collective-permute-start = (bf16[2,64,256]{2,1,0:T(8,128)(2,1)S(1)}, bf16[2,64,256]{2,1,0:T(8,128)(2,1)S(1)}, u32[]{:S(2)}, u32[]{:S(2)}) collective-permute-start(bf16[2,64,256]{2,1,0:T(8,128)(2,1)S(1)} %get-tuple-element.37), channel_id=1, source_target_pairs={{0,8},{8,0},{1,9},{9,1},{2,10},{10,2},{3,11},{11,3},{4,12},{12,4},... | collective-permute-start | bytes 196616 | tf_op jit(solution)/shard_map/ppermute | solution.py:286
  33.1 8.2 %collective-permute-start.3 = (f32[8,64,1024]{2,1,0:T(8,128)}, f32[8,64,1024]{2,1,0:T(8,128)S(1)}, u32[]{:S(2)}, u32[]{:S(2)}) collective-permute-start(f32[8,64,1024]{2,1,0:T(8,128)} %get-tuple-element.43), channel_id=1, source_target_pairs={{0,16},{16,0},{1,17},{17,1},{2,18},{18,2},{3,19},{19,3},{4,20},{20... | collective-permute-start | bytes 6291464 | tf_op jit(solution)/shard_map/ppermute | solution.py:286
  33.2 15.2 %all-to-all-start.1 = ((bf16[16,32,128]{2,1,0:T(8,128)(2,1)}), bf16[16,32,128]{2,1,0:T(8,128)(2,1)S(1)}, u32[]{:S(2)}, u32[]{:S(2)}) async-start(bf16[16,32,128]{2,1,0:T(8,128)(2,1)} %get-tuple-element.40), calls=%async_computation.1 | async-start | bytes 262144 | tf_op jit(solution)/shard_map/all_to_all | solution.py:290
  38.1 6.2 %copy-start.8 = (bf16[2,2,64,256]{3,2,1,0:T(8,128)(2,1)}, bf16[2,2,64,256]{3,2,1,0:T(8,128)(2,1)S(1)}, u32[]{:S(2)}) copy-start(bf16[2,2,64,256]{3,2,1,0:T(8,128)(2,1)S(1)} %pad_maximum_fusion.refs_0_) | copy-start | bytes 393220
  38.1 8.5 %collective-permute-start.2 = (bf16[2,2,64,256]{3,2,1,0:T(8,128)(2,1)S(1)}, bf16[2,2,64,256]{3,2,1,0:T(8,128)(2,1)S(1)}, u32[]{:S(2)}, u32[]{:S(2)}) collective-permute-start(bf16[2,2,64,256]{3,2,1,0:T(8,128)(2,1)S(1)} %pad_maximum_fusion.refs_0_), channel_id=1, source_target_pairs={{0,7},{1,0},{2,1},{3,2},{4,3},{5,4},{6,5},{7,6},{8,15},{9,8},{10,9... | collective-permute-start | bytes 393224 | tf_op jit(solution)/shard_map/ppermute | solution.py:298
  41.3 7.1 %collective-permute-start.1 = (bf16[2,2,64,256]{3,2,1,0:T(8,128)(2,1)S(1)}, bf16[2,2,64,256]{3,2,1,0:T(8,128)(2,1)}, u32[]{:S(2)}, u32[]{:S(2)}) collective-permute-start(bf16[2,2,64,256]{3,2,1,0:T(8,128)(2,1)S(1)} %pad_maximum_fusion.refs_0_), channel_id=1, source_target_pairs={{0,1},{1,2},{2,3},{3,4},{4,5},{5,6},{6,7},{7,0},{8,9},{9,10},{10,1... | collective-permute-start | bytes 393224 | tf_op jit(solution)/shard_map/ppermute | solution.py:298
  49.9 6.7 %copy-start.10 = (bf16[2,2,64,256]{3,2,1,0:T(8,128)(2,1)S(1)}, bf16[2,2,64,256]{3,2,1,0:T(8,128)(2,1)}, u32[]{:S(2)}) copy-start(bf16[2,2,64,256]{3,2,1,0:T(8,128)(2,1)} %copy-done.9) | copy-start | bytes 393220
  49.9 24.5 %copy-start.6 = (s32[32]{0:T(128)S(1)}, s32[32]{0:T(128)}, u32[]{:S(2)}) copy-start(s32[32]{0:T(128)} %rows_ref.1) | copy-start | bytes 388
  49.9 24.5 %copy-start.7 = (s32[32]{0:T(128)S(1)}, s32[32]{0:T(128)}, u32[]{:S(2)}) copy-start(s32[32]{0:T(128)} %cols_ref.1) | copy-start | bytes 388
  49.9 30.7 %all-to-all-start.2 = ((bf16[8,2,64,1024]{3,2,1,0:T(8,128)(2,1)}), bf16[8,2,64,1024]{3,2,1,0:T(8,128)(2,1)S(1)}, u32[]{:S(2)}, u32[]{:S(2)}) async-start(bf16[8,2,64,1024]{3,2,1,0:T(8,128)(2,1)} %copy-done.1), calls=%async_computation.2 | async-start | bytes 4194304 | tf_op jit(solution)/shard_map/all_to_all | solution.py:290
  55.0 6.4 %collective-permute-start.4 = (bf16[2,2,64,256]{3,2,1,0:T(8,128)(2,1)}, bf16[2,2,64,256]{3,2,1,0:T(8,128)(2,1)S(1)}, u32[]{:S(2)}, u32[]{:S(2)}) collective-permute-start(bf16[2,2,64,256]{3,2,1,0:T(8,128)(2,1)} %collective-permute-done.1.refs_1_), channel_id=1, source_target_pairs={{0,1},{1,2},{2,3},{3,4},{4,5},{5,6},{6,7},{7,0},{8,9},{9,10},{10,1... | collective-permute-start | bytes 393224 | tf_op jit(solution)/shard_map/ppermute | solution.py:298
  56.6 5.2 %collective-permute-start.7 = (bf16[2,2,64,256]{3,2,1,0:T(8,128)(2,1)S(1)}, bf16[2,2,64,256]{3,2,1,0:T(8,128)(2,1)S(1)}, u32[]{:S(2)}, u32[]{:S(2)}) collective-permute-start(bf16[2,2,64,256]{3,2,1,0:T(8,128)(2,1)S(1)} %copy-done.10), channel_id=1, source_target_pairs={{0,7},{1,0},{2,1},{3,2},{4,3},{5,4},{6,5},{7,6},{8,15},{9,8},{10,9... | collective-permute-start | bytes 393224 | tf_op jit(solution)/shard_map/ppermute | solution.py:298
  61.4 12.4 %copy-start.11 = (bf16[2,2,64,256]{3,2,1,0:T(8,128)(2,1)}, bf16[2,2,64,256]{3,2,1,0:T(8,128)(2,1)S(1)}, u32[]{:S(2)}) copy-start(bf16[2,2,64,256]{3,2,1,0:T(8,128)(2,1)S(1)} %collective-permute-done.4.refs_2_) | copy-start | bytes 393220
  61.4 6.2 %collective-permute-start.5 = (bf16[2,2,64,256]{3,2,1,0:T(8,128)(2,1)S(1)}, bf16[2,2,64,256]{3,2,1,0:T(8,128)(2,1)S(1)}, u32[]{:S(2)}, u32[]{:S(2)}) collective-permute-start(bf16[2,2,64,256]{3,2,1,0:T(8,128)(2,1)S(1)} %collective-permute-done.4.refs_2_), channel_id=1, source_target_pairs={{0,1},{1,2},{2,3},{3,4},{4,5},{5,6},{6,7},{7,0},{8,9},{9,10},{10,1... | collective-permute-start | bytes 393224 | tf_op jit(solution)/shard_map/ppermute | solution.py:298
  61.8 12.0 %copy-start.12 = (bf16[2,2,64,256]{3,2,1,0:T(8,128)(2,1)}, bf16[2,2,64,256]{3,2,1,0:T(8,128)(2,1)S(1)}, u32[]{:S(2)}) copy-start(bf16[2,2,64,256]{3,2,1,0:T(8,128)(2,1)S(1)} %collective-permute-done.7.refs_6_) | copy-start | bytes 393220
  61.8 6.4 %collective-permute-start.8 = (bf16[2,2,64,256]{3,2,1,0:T(8,128)(2,1)S(1)}, bf16[2,2,64,256]{3,2,1,0:T(8,128)(2,1)S(1)}, u32[]{:S(2)}, u32[]{:S(2)}) collective-permute-start(bf16[2,2,64,256]{3,2,1,0:T(8,128)(2,1)S(1)} %collective-permute-done.7.refs_6_), channel_id=1, source_target_pairs={{0,7},{1,0},{2,1},{3,2},{4,3},{5,4},{6,5},{7,6},{8,15},{9,8},{10,9... | collective-permute-start | bytes 393224 | tf_op jit(solution)/shard_map/ppermute | solution.py:298
  67.6 6.2 %collective-permute-start.6 = (bf16[2,2,64,256]{3,2,1,0:T(8,128)(2,1)S(1)}, bf16[2,2,64,256]{3,2,1,0:T(8,128)(2,1)S(1)}, u32[]{:S(2)}, u32[]{:S(2)}) collective-permute-start(bf16[2,2,64,256]{3,2,1,0:T(8,128)(2,1)S(1)} %collective-permute-done.5.refs_3_), channel_id=1, source_target_pairs={{0,1},{1,2},{2,3},{3,4},{4,5},{5,6},{6,7},{7,0},{8,9},{9,10},{10,1... | collective-permute-start | bytes 393224 | tf_op jit(solution)/shard_map/ppermute | solution.py:298
  82.5 13.1 %collective-permute-start.9 = (bf16[8,64,1024]{2,1,0:T(8,128)(2,1)}, bf16[8,64,1024]{2,1,0:T(8,128)(2,1)S(1)}, u32[]{:S(2)}, u32[]{:S(2)}) collective-permute-start(bf16[8,64,1024]{2,1,0:T(8,128)(2,1)} %get-tuple-element.52), channel_id=1, source_target_pairs={{0,16},{16,0},{1,17},{17,1},{2,18},{18,2},{3,19},{19,3},{4,20},{20... | collective-permute-start | bytes 3145736 | tf_op jit(solution)/shard_map/ppermute | solution.py:286
  82.5 18.6 %collective-permute-start.10 = (bf16[16,64,128]{2,1,0:T(8,128)(2,1)}, bf16[16,64,128]{2,1,0:T(8,128)(2,1)S(1)}, u32[]{:S(2)}, u32[]{:S(2)}) collective-permute-start(bf16[16,64,128]{2,1,0:T(8,128)(2,1)} %get-tuple-element.53), channel_id=1, source_target_pairs={{0,8},{1,9},{2,10},{3,11},{4,12},{5,13},{6,14},{7,15},{8,0},{9,1},... | collective-permute-start | bytes 786440 | tf_op jit(solution)/shard_map/ppermute | solution.py:369
  87.1 13.9 %collective-permute-start.11 = (bf16[16,64,128]{2,1,0:T(8,128)(2,1)}, bf16[16,64,128]{2,1,0:T(8,128)(2,1)}, u32[]{:S(2)}, u32[]{:S(2)}) collective-permute-start(bf16[16,64,128]{2,1,0:T(8,128)(2,1)} %get-tuple-element.54), channel_id=1, source_target_pairs={{0,1},{1,0},{2,3},{3,2},{4,5},{5,4},{6,7},{7,6},{8,9},{9,8},{10,11... | collective-permute-start | bytes 786440 | tf_op jit(solution)/shard_map/ppermute | solution.py:369
  87.1 14.8 %collective-permute-start.12 = (bf16[16,64,128]{2,1,0:T(8,128)(2,1)}, bf16[16,64,128]{2,1,0:T(8,128)(2,1)}, u32[]{:S(2)}, u32[]{:S(2)}) collective-permute-start(bf16[16,64,128]{2,1,0:T(8,128)(2,1)} %get-tuple-element.55), channel_id=1, source_target_pairs={{0,9},{1,8},{2,11},{3,10},{4,13},{5,12},{6,15},{7,14},{8,1},{9,0},... | collective-permute-start | bytes 786440 | tf_op jit(solution)/shard_map/ppermute | solution.py:369
  88.6 17.0 %all-to-all-start.3 = ((bf16[16,32,128]{2,1,0:T(8,128)(2,1)}), bf16[16,32,128]{2,1,0:T(8,128)(2,1)S(1)}, u32[]{:S(2)}, u32[]{:S(2)}) async-start(bf16[16,32,128]{2,1,0:T(8,128)(2,1)} %copy-done.5), calls=%async_computation.3 | async-start | bytes 262144 | tf_op jit(solution)/shard_map/all_to_all | solution.py:290
  108.6 22.0 %all-to-all-start.4 = ((bf16[16,128,128]{2,1,0:T(8,128)(2,1)}), bf16[16,128,128]{2,1,0:T(8,128)(2,1)S(1)}, u32[]{:S(2)}, u32[]{:S(2)}) async-start(bf16[16,128,128]{2,1,0:T(8,128)(2,1)} %last_message.1), calls=%async_computation.4 | async-start | bytes 1048576 | tf_op jit(solution)/shard_map/all_to_all | solution.py:290
  (10 other events, 19.4 us)

commit v9 on v8

--- a/solution.py
+++ b/solution.py
@@ -157,12 +157,10 @@
         out_ref[q, 1] = charges
 
 
-def unpack(came_ref, msg_ref, charges_ref):
+def unpack(came_ref, msg_ref):
     total = came_ref[0, 0].astype(f32)
-    charges_ref[0] = came_ref[0, 1]
     for q in range(1, 8):
         total = total + came_ref[q, 0].astype(f32)
-        charges_ref[q] = came_ref[q, 1]
     for piece in range(16):
         row = piece // 2 * 8
         for part in range(4):
@@ -176,7 +174,7 @@
     fetched = fetch(parts_hbm, blocks, sems, lag)
     total = jnp.zeros((64, 64), f32)
     for index in range(16):
-        charges = other_ref[index] if index < 8 else came_ref[index - 8, 1]
+        charges = other_ref[index, 1] if index < 8 else came_ref[index - 8, 1]
         fetched[index].wait()
         pair = dot_last(blocks[index], charges)
         total = total + jnp.where(lag[index] == 0, 0.0, pair[:64] + pair[64:])
@@ -240,18 +238,22 @@
     mine = pl.ds(pl.multiple_of(parity * 128, 128), 128)
     theirs = pl.ds(pl.multiple_of((1 - parity) * 128, 128), 128)
     for target in range(16):
-        keep_ref[target] = behind[2 * target + my_half, :, mine]
+        keep_ref[target] = behind[2 * target + my_half, :, mine].astype(bf16)
         across_ref[target] = behind[2 * target + 1 - my_half, :, mine].astype(bf16)
         beside_ref[target] = behind[2 * target + my_half, :, theirs].astype(bf16)
         both_ref[target] = behind[2 * target + 1 - my_half, :, theirs].astype(bf16)
 
 
-def last_message(adj_ref, pot_ref, keep_ref, across_ref, beside_ref, both_ref, out_ref):
+def last_message(adj_ref, pot_ref, keep_hbm, across_ref, beside_ref, both_ref, out_ref, keep_ref, sem):
+    copy = pltpu.make_async_copy(keep_hbm, keep_ref, sem)
+    copy.start()
     adjoint = jnp.sum(adj_ref[...].astype(f32), axis=0).astype(bf16)
     for piece in range(16):
         out_ref[piece, 0:32, :] = adjoint
         out_ref[piece, 32:64, :] = pot_ref[...]
-        near_sum = keep_ref[piece] + across_ref[piece].astype(f32)
+    copy.wait()
+    for piece in range(16):
+        near_sum = keep_ref[piece].astype(f32) + across_ref[piece].astype(f32)
         near_sum = near_sum + beside_ref[piece].astype(f32) + both_ref[piece].astype(f32)
         out_ref[piece, 64:128, :] = near_sum.astype(bf16)
 
@@ -350,7 +352,7 @@
     up4 = shift(up3, 1)
     ahead, keep, *quarters = call(
         near,
-        [((64, 512), f32), ((16, 64, 128), f32)] + [((16, 64, 128), bf16)] * 3,
+        [((64, 512), f32)] + [((16, 64, 128), bf16)] * 4,
         [tile_count, tile_rows, tile_cols, low, in_hbm(tiles)]
         + [in_hbm(piece) for piece in (here, up1, up2, up3, up4, down3, down2, down1)],
         specs=[smem(), smem(), smem(), vmem()] + [hbm()] * 9,
@@ -369,13 +371,8 @@
         lax.ppermute(value, ROWS, [(i, i ^ mask) for i in range(16)])
         for value, mask in zip(quarters, (8, 1, 9))
     ]
-    adjoint, charges = call(
-        unpack,
-        [((16, 32, 128), bf16), ((8, 64, 1024), bf16)],
-        [both],
-        name="unpack",
-    )
-    others = swap(charges, "core")
+    (adjoint,) = call(unpack, [((16, 32, 128), bf16)], [both], name="unpack")
+    others = swap(both, "core")
     (potential,) = call(
         forward,
         [((32, 128), bf16)],
@@ -388,7 +385,9 @@
     (last,) = call(
         last_message,
         [((16, 128, 128), bf16)],
-        [adjoint, potential, keep, *quarters],
+        [adjoint, potential, in_hbm(keep), *quarters],
+        specs=[vmem()] * 2 + [hbm()] + [vmem()] * 3,
+        scratch=[pltpu.VMEM((16, 64, 128), bf16), pltpu.SemaphoreType.DMA],
         name="last_message",
     )
     staged = call(

time: 133 us -> 131 us (0.985)
  local copies, waits for them, and re-layouts: 7.67 us -> 5.85 us
    unnamed x32 -> x28, local copies, waits for them, and re-layouts: 7.67 us -> 5.85 us
  transfers between devices with their start and end apart: 18 -> 18, of which waited for: 9 -> 9; matrix products, arithmetic and copies ran while one was open for 0% -> 0% of each run, Pallas kernels for 13% -> 15%
where the time goes in v9:
time: 131 us; the launch traced here: 130 us
  starting transfers between devices  54 us (41%)
  waiting for transfers between devices  39 us (30%)
  Pallas kernels  29.8 us (23%)
  local copies, waits for them, and re-layouts  5.85 us (4%)
  between operations  1.52 us (1%)
    all_to_all x5, starting transfers between devices, exchange(): return lax.all_to_all(value, axes, 0, 0, tiled=True)  34.9 us
    pallas_call x11, Pallas kernels, call(): pl.pallas_call(kernel, out_shape=[jax.ShapeDtypeStruct(s, d) for s, d in...  29.8 us
    all_to_all x5, waiting for transfers between devices, exchange(): return lax.all_to_all(value, axes, 0, 0, tiled=True)  24.1 us
    ppermute x7, waiting for transfers between devices, shift(): return lax.ppermute(value, 'z', [(i, (i + step) % 8) for i in range(8)])  14.9 us
    ppermute x7, starting transfers between devices, shift(): return lax.ppermute(value, 'z', [(i, (i + step) % 8) for i in range(8)])  9.66 us
    ppermute x3, starting transfers between devices, on_device(): lax.ppermute(value, ROWS, [(i, i ^ mask) for i in range(16)])  5.9 us
    unnamed x28, local copies, waits for them, and re-layouts  5.85 us
    ppermute x3, starting transfers between devices, swap(): return lax.ppermute(value, axis, [(0, 1), (1, 0)])  3.53 us
  transfers between devices with their start and end apart: 18, of which 9 were waited for; matrix products, arithmetic and copies ran while one was open for 0% of the time, Pallas kernels for 15%

profile of v9, /device:TPU:8, one launch (start us, length us, event | category | flops | bytes accessed | tf_op | source)
XLA Modules:
  0.0 130.2 jit_solution(14563324105539164197)
XLA Ops:
  0.6 3.0 %prepare.1 = (bf16[2,64,256]{2,1,0:T(8,128)(2,1)S(1)}, bf16[2,64,256]{2,1,0:T(8,128)(2,1)S(1)}, bf16[16,96,128]{2,1,0:T(8,128)(2,1)}) custom-call(f32[64,512]{1,0:T(8,128)} %exc_hbm.1, f32[64,512]{1,0:T(8,128)} %loads_hbm.1, bf16[1024,512]{1,0:T(8,128)(2,1)} %refs_0_.1, bf16[1024,512]{1,0:T(8,128)(2,1)} %refs_1_.1), custom_call_target="tpu_custom_call" | custom-call | flops 1000 | bytes 1000 | tf_op jit(solution)/shard_map/prepare/pallas_call | solution.py:30
  3.6 11.0 %all-to-all-start = ((bf16[16,96,128]{2,1,0:T(8,128)(2,1)}), bf16[16,96,128]{2,1,0:T(8,128)(2,1)S(1)}, u32[]{:S(2)}, u32[]{:S(2)}) async-start(bf16[16,96,128]{2,1,0:T(8,128)(2,1)} %get-tuple-element.34), calls=%async_computation | async-start | bytes 786432 | tf_op jit(solution)/shard_map/all_to_all | solution.py:292
  14.7 3.4 %collective-permute-start = (bf16[2,64,256]{2,1,0:T(8,128)(2,1)S(1)}, bf16[2,64,256]{2,1,0:T(8,128)(2,1)S(1)}, u32[]{:S(2)}, u32[]{:S(2)}) collective-permute-start(bf16[2,64,256]{2,1,0:T(8,128)(2,1)S(1)} %get-tuple-element.35), channel_id=1, source_target_pairs={{0,8},{8,0},{1,9},{9,1},{2,10},{10,2},{3,11},{11,3},{4,12},{12,4},... | collective-permute-start | bytes 196616 | tf_op jit(solution)/shard_map/ppermute | solution.py:288
  18.1 2.2 %split_translation.1.parts_hbm = bf16[15,128,1024]{2,1,0:T(8,128)(2,1)S(1)} custom-call(f32[1,15,64,1024]{3,2,1,0:T(8,128)} %trans_hbm.1), custom_call_target="tpu_custom_call" | custom-call | flops 1000 | bytes 1000 | tf_op jit(solution)/shard_map/split_translation/pallas_call | solution.py:30
  22.2 6.6 %all-to-all-done.msg_ref = bf16[16,96,128]{2,1,0:T(8,128)(2,1)S(1)} async-done(((bf16[16,96,128]{2,1,0:T(8,128)(2,1)}), bf16[16,96,128]{2,1,0:T(8,128)(2,1)S(1)}, u32[]{:S(2)}, u32[]{:S(2)}) %all-to-all-start) | async-done | bytes 393248 | tf_op jit(solution)/shard_map/all_to_all | solution.py:292
  28.8 4.3 %other_terms.1 = (bf16[16,32,128]{2,1,0:T(8,128)(2,1)}, bf16[128,64]{1,0:T(8,128)(2,1)S(1)}, f32[8,64,1024]{2,1,0:T(8,128)}) custom-call(bf16[16,96,128]{2,1,0:T(8,128)(2,1)S(1)} %all-to-all-done.msg_ref, bf16[15,128,1024]{2,1,0:T(8,128)(2,1)} %copy-done), custom_call_target="tpu_custom_call" | custom-call | flops 1000 | bytes 1000 | tf_op jit(solution)/shard_map/other_terms/pallas_call | solution.py:30
  33.2 4.9 %all-to-all-start.1 = ((bf16[16,32,128]{2,1,0:T(8,128)(2,1)}), bf16[16,32,128]{2,1,0:T(8,128)(2,1)S(1)}, u32[]{:S(2)}, u32[]{:S(2)}) async-start(bf16[16,32,128]{2,1,0:T(8,128)(2,1)} %get-tuple-element.38), calls=%async_computation.1 | async-start | bytes 262144 | tf_op jit(solution)/shard_map/all_to_all | solution.py:292
  38.1 2.0 %collective-permute-start.1 = (bf16[2,2,64,256]{3,2,1,0:T(8,128)(2,1)S(1)}, bf16[2,2,64,256]{3,2,1,0:T(8,128)(2,1)S(1)}, u32[]{:S(2)}, u32[]{:S(2)}) collective-permute-start(bf16[2,2,64,256]{3,2,1,0:T(8,128)(2,1)S(1)} %pad_maximum_fusion.refs_0_), channel_id=1, source_target_pairs={{0,1},{1,2},{2,3},{3,4},{4,5},{5,6},{6,7},{7,0},{8,9},{9,10},{10,1... | collective-permute-start | bytes 393224 | tf_op jit(solution)/shard_map/ppermute | solution.py:300
  41.4 3.0 %own_terms.1.own_ref = bf16[8,64,1024]{2,1,0:T(8,128)(2,1)S(1)} custom-call(bf16[128,64]{1,0:T(8,128)(2,1)S(1)} %get-tuple-element.40.grad_ref, f32[8,64,1024]{2,1,0:T(8,128)S(1)} %collective-permute-done.3.came_ref, bf16[15,128,1024]{2,1,0:T(8,128)(2,1)} %copy-done), custom_call_target="tpu_custom_call" | custom-call | flops 1000 | bytes 1000 | tf_op jit(solution)/shard_map/own_terms/pallas_call | solution.py:30
  44.4 3.4 %collective-permute-done.1.refs_1_ = bf16[2,2,64,256]{3,2,1,0:T(8,128)(2,1)S(1)} collective-permute-done((bf16[2,2,64,256]{3,2,1,0:T(8,128)(2,1)S(1)}, bf16[2,2,64,256]{3,2,1,0:T(8,128)(2,1)S(1)}, u32[]{:S(2)}, u32[]{:S(2)}) %collective-permute-start.1) | collective-permute-done | bytes 131104 | tf_op jit(solution)/shard_map/ppermute | solution.py:300
  50.1 5.1 %all-to-all-start.2 = ((bf16[8,2,64,1024]{3,2,1,0:T(8,128)(2,1)}), bf16[8,2,64,1024]{3,2,1,0:T(8,128)(2,1)S(1)}, u32[]{:S(2)}, u32[]{:S(2)}) async-start(bf16[8,2,64,1024]{3,2,1,0:T(8,128)(2,1)} %copy-done.1), calls=%async_computation.2 | async-start | bytes 4194304 | tf_op jit(solution)/shard_map/all_to_all | solution.py:292
  56.6 1.9 %collective-permute-start.7 = (bf16[2,2,64,256]{3,2,1,0:T(8,128)(2,1)}, bf16[2,2,64,256]{3,2,1,0:T(8,128)(2,1)S(1)}, u32[]{:S(2)}, u32[]{:S(2)}) collective-permute-start(bf16[2,2,64,256]{3,2,1,0:T(8,128)(2,1)} %collective-permute-done.2.refs_7_), channel_id=1, source_target_pairs={{0,7},{1,0},{2,1},{3,2},{4,3},{5,4},{6,5},{7,6},{8,15},{9,8},{10,9... | collective-permute-start | bytes 393224 | tf_op jit(solution)/shard_map/ppermute | solution.py:300
  58.4 2.9 %collective-permute-done.4.refs_2_ = bf16[2,2,64,256]{3,2,1,0:T(8,128)(2,1)S(1)} collective-permute-done((bf16[2,2,64,256]{3,2,1,0:T(8,128)(2,1)S(1)}, bf16[2,2,64,256]{3,2,1,0:T(8,128)(2,1)S(1)}, u32[]{:S(2)}, u32[]{:S(2)}) %collective-permute-start.4) | collective-permute-done | bytes 131104 | tf_op jit(solution)/shard_map/ppermute | solution.py:300
  61.9 2.9 %collective-permute-start.8 = (bf16[2,2,64,256]{3,2,1,0:T(8,128)(2,1)S(1)}, bf16[2,2,64,256]{3,2,1,0:T(8,128)(2,1)S(1)}, u32[]{:S(2)}, u32[]{:S(2)}) collective-permute-start(bf16[2,2,64,256]{3,2,1,0:T(8,128)(2,1)S(1)} %collective-permute-done.7.refs_6_), channel_id=1, source_target_pairs={{0,7},{1,0},{2,1},{3,2},{4,3},{5,4},{6,5},{7,6},{8,15},{9,8},{10,9... | collective-permute-start | bytes 393224 | tf_op jit(solution)/shard_map/ppermute | solution.py:300
  64.8 2.7 %collective-permute-done.5.refs_3_ = bf16[2,2,64,256]{3,2,1,0:T(8,128)(2,1)S(1)} collective-permute-done((bf16[2,2,64,256]{3,2,1,0:T(8,128)(2,1)S(1)}, bf16[2,2,64,256]{3,2,1,0:T(8,128)(2,1)S(1)}, u32[]{:S(2)}, u32[]{:S(2)}) %collective-permute-start.5) | collective-permute-done | bytes 131104 | tf_op jit(solution)/shard_map/ppermute | solution.py:300
  68.2 5.5 %collective-permute-done.6.refs_4_ = bf16[2,2,64,256]{3,2,1,0:T(8,128)(2,1)S(1)} collective-permute-done((bf16[2,2,64,256]{3,2,1,0:T(8,128)(2,1)S(1)}, bf16[2,2,64,256]{3,2,1,0:T(8,128)(2,1)S(1)}, u32[]{:S(2)}, u32[]{:S(2)}) %collective-permute-start.6) | collective-permute-done | bytes 131104 | tf_op jit(solution)/shard_map/ppermute | solution.py:300
  74.4 4.8 %near.1 = (f32[64,512]{1,0:T(8,128)S(1)}, bf16[16,64,128]{2,1,0:T(8,128)(2,1)S(1)}, bf16[16,64,128]{2,1,0:T(8,128)(2,1)}, bf16[16,64,128]{2,1,0:T(8,128)(2,1)}, bf16[16,64,128]{2,1,0:T(8,128)(2,1)}) custom-call(s32[1]{0:T(128)S(6)} %copy.11.count_ref, s32[32]{0:T(128)S(1)} %copy-done.4, s32[32]{0:T(128)S(1)} %copy-done.5, ...), custom_call_target="tpu_custom_call" | custom-call | flops 1000 | bytes 1000 | tf_op jit(solution)/shard_map/near/pallas_call | solution.py:30
  80.6 4.2 %collective-permute-start.10 = (bf16[16,64,128]{2,1,0:T(8,128)(2,1)}, bf16[16,64,128]{2,1,0:T(8,128)(2,1)S(1)}, u32[]{:S(2)}, u32[]{:S(2)}) collective-permute-start(bf16[16,64,128]{2,1,0:T(8,128)(2,1)} %get-tuple-element.49), channel_id=1, source_target_pairs={{0,8},{1,9},{2,10},{3,11},{4,12},{5,13},{6,14},{7,15},{8,0},{9,1},... | collective-permute-start | bytes 786440 | tf_op jit(solution)/shard_map/ppermute | solution.py:371
  87.3 7.3 %all-to-all-start.3 = ((bf16[16,32,128]{2,1,0:T(8,128)(2,1)}), bf16[16,32,128]{2,1,0:T(8,128)(2,1)S(1)}, u32[]{:S(2)}, u32[]{:S(2)}) async-start(bf16[16,32,128]{2,1,0:T(8,128)(2,1)} %unpack.1), calls=%async_computation.3 | async-start | bytes 262144 | tf_op jit(solution)/shard_map/all_to_all | solution.py:292
  94.6 7.0 %forward.1.pot_ref = bf16[32,128]{1,0:T(8,128)(2,1)S(1)} custom-call(bf16[8,2,64,1024]{3,2,1,0:T(8,128)(2,1)} %collective-permute-done.9.other_ref, bf16[8,2,64,1024]{3,2,1,0:T(8,128)(2,1)S(1)} %all-to-all-done.2.came_ref, bf16[15,128,1024]{2,1,0:T(8,128)(2,1)} %copy-done), custom_call_target="tpu_custom_call" | custom-call | flops 1000 | bytes 1000 | tf_op jit(solution)/shard_map/forward/pallas_call | solution.py:30
  101.7 3.0 %all-to-all-done.3.adj_ref = bf16[16,32,128]{2,1,0:T(8,128)(2,1)S(1)} async-done(((bf16[16,32,128]{2,1,0:T(8,128)(2,1)}), bf16[16,32,128]{2,1,0:T(8,128)(2,1)S(1)}, u32[]{:S(2)}, u32[]{:S(2)}) %all-to-all-start.3) | async-done | bytes 131104 | tf_op jit(solution)/shard_map/all_to_all | solution.py:292
  104.7 1.9 %last_message.1 = bf16[16,128,128]{2,1,0:T(8,128)(2,1)} custom-call(bf16[16,32,128]{2,1,0:T(8,128)(2,1)S(1)} %all-to-all-done.3.adj_ref, bf16[32,128]{1,0:T(8,128)(2,1)S(1)} %forward.1.pot_ref, bf16[16,64,128]{2,1,0:T(8,128)(2,1)} %copy-done.2, bf16[16,64,128]{2,1,0:T(8,128)(2,1)S(1)} %collective-permute-done.10.across_ref, ...), custom_call_target="tpu_custom_call" | custom-call | flops 1000 | bytes 1000 | tf_op jit(solution)/shard_map/last_message/pallas_call | solution.py:30
  106.6 6.6 %all-to-all-start.4 = ((bf16[16,128,128]{2,1,0:T(8,128)(2,1)}), bf16[16,128,128]{2,1,0:T(8,128)(2,1)S(1)}, u32[]{:S(2)}, u32[]{:S(2)}) async-start(bf16[16,128,128]{2,1,0:T(8,128)(2,1)} %last_message.1), calls=%async_computation.4 | async-start | bytes 1048576 | tf_op jit(solution)/shard_map/all_to_all | solution.py:292
  114.8 14.3 %all-to-all-done.4.msg_ref = bf16[16,128,128]{2,1,0:T(8,128)(2,1)S(1)} async-done(((bf16[16,128,128]{2,1,0:T(8,128)(2,1)}), bf16[16,128,128]{2,1,0:T(8,128)(2,1)S(1)}, u32[]{:S(2)}, u32[]{:S(2)}) %all-to-all-start.4) | async-done | bytes 524320 | tf_op jit(solution)/shard_map/all_to_all | solution.py:292
  (52 shorter events, 14.7 us)
Async XLA Ops:
  3.6 25.2 %all-to-all-start = ((bf16[16,96,128]{2,1,0:T(8,128)(2,1)}), bf16[16,96,128]{2,1,0:T(8,128)(2,1)S(1)}, u32[]{:S(2)}, u32[]{:S(2)}) async-start(bf16[16,96,128]{2,1,0:T(8,128)(2,1)} %get-tuple-element.34), calls=%async_computation | async-start | bytes 786432 | tf_op jit(solution)/shard_map/all_to_all | solution.py:292
  14.7 7.5 %collective-permute-start = (bf16[2,64,256]{2,1,0:T(8,128)(2,1)S(1)}, bf16[2,64,256]{2,1,0:T(8,128)(2,1)S(1)}, u32[]{:S(2)}, u32[]{:S(2)}) collective-permute-start(bf16[2,64,256]{2,1,0:T(8,128)(2,1)S(1)} %get-tuple-element.35), channel_id=1, source_target_pairs={{0,8},{8,0},{1,9},{9,1},{2,10},{10,2},{3,11},{11,3},{4,12},{12,4},... | collective-permute-start | bytes 196616 | tf_op jit(solution)/shard_map/ppermute | solution.py:288
  33.1 8.3 %collective-permute-start.3 = (f32[8,64,1024]{2,1,0:T(8,128)}, f32[8,64,1024]{2,1,0:T(8,128)S(1)}, u32[]{:S(2)}, u32[]{:S(2)}) collective-permute-start(f32[8,64,1024]{2,1,0:T(8,128)} %get-tuple-element.41), channel_id=1, source_target_pairs={{0,16},{16,0},{1,17},{17,1},{2,18},{18,2},{3,19},{19,3},{4,20},{20... | collective-permute-start | bytes 6291464 | tf_op jit(solution)/shard_map/ppermute | solution.py:288
  33.2 15.4 %all-to-all-start.1 = ((bf16[16,32,128]{2,1,0:T(8,128)(2,1)}), bf16[16,32,128]{2,1,0:T(8,128)(2,1)S(1)}, u32[]{:S(2)}, u32[]{:S(2)}) async-start(bf16[16,32,128]{2,1,0:T(8,128)(2,1)} %get-tuple-element.38), calls=%async_computation.1 | async-start | bytes 262144 | tf_op jit(solution)/shard_map/all_to_all | solution.py:292
  38.1 6.3 %copy-start.6 = (bf16[2,2,64,256]{3,2,1,0:T(8,128)(2,1)}, bf16[2,2,64,256]{3,2,1,0:T(8,128)(2,1)S(1)}, u32[]{:S(2)}) copy-start(bf16[2,2,64,256]{3,2,1,0:T(8,128)(2,1)S(1)} %pad_maximum_fusion.refs_0_) | copy-start | bytes 393220
  38.1 9.7 %collective-permute-start.1 = (bf16[2,2,64,256]{3,2,1,0:T(8,128)(2,1)S(1)}, bf16[2,2,64,256]{3,2,1,0:T(8,128)(2,1)S(1)}, u32[]{:S(2)}, u32[]{:S(2)}) collective-permute-start(bf16[2,2,64,256]{3,2,1,0:T(8,128)(2,1)S(1)} %pad_maximum_fusion.refs_0_), channel_id=1, source_target_pairs={{0,1},{1,2},{2,3},{3,4},{4,5},{5,6},{6,7},{7,0},{8,9},{9,10},{10,1... | collective-permute-start | bytes 393224 | tf_op jit(solution)/shard_map/ppermute | solution.py:300
  40.1 8.4 %collective-permute-start.2 = (bf16[2,2,64,256]{3,2,1,0:T(8,128)(2,1)S(1)}, bf16[2,2,64,256]{3,2,1,0:T(8,128)(2,1)}, u32[]{:S(2)}, u32[]{:S(2)}) collective-permute-start(bf16[2,2,64,256]{3,2,1,0:T(8,128)(2,1)S(1)} %pad_maximum_fusion.refs_0_), channel_id=1, source_target_pairs={{0,7},{1,0},{2,1},{3,2},{4,3},{5,4},{6,5},{7,6},{8,15},{9,8},{10,9... | collective-permute-start | bytes 393224 | tf_op jit(solution)/shard_map/ppermute | solution.py:300
  50.1 24.3 %copy-start.4 = (s32[32]{0:T(128)S(1)}, s32[32]{0:T(128)}, u32[]{:S(2)}) copy-start(s32[32]{0:T(128)} %rows_ref.1) | copy-start | bytes 388
  50.1 24.3 %copy-start.5 = (s32[32]{0:T(128)S(1)}, s32[32]{0:T(128)}, u32[]{:S(2)}) copy-start(s32[32]{0:T(128)} %cols_ref.1) | copy-start | bytes 388
  50.1 30.4 %all-to-all-start.2 = ((bf16[8,2,64,1024]{3,2,1,0:T(8,128)(2,1)}), bf16[8,2,64,1024]{3,2,1,0:T(8,128)(2,1)S(1)}, u32[]{:S(2)}, u32[]{:S(2)}) async-start(bf16[8,2,64,1024]{3,2,1,0:T(8,128)(2,1)} %copy-done.1), calls=%async_computation.2 | async-start | bytes 4194304 | tf_op jit(solution)/shard_map/all_to_all | solution.py:292
  55.2 6.2 %collective-permute-start.4 = (bf16[2,2,64,256]{3,2,1,0:T(8,128)(2,1)S(1)}, bf16[2,2,64,256]{3,2,1,0:T(8,128)(2,1)S(1)}, u32[]{:S(2)}, u32[]{:S(2)}) collective-permute-start(bf16[2,2,64,256]{3,2,1,0:T(8,128)(2,1)S(1)} %copy-done.8), channel_id=1, source_target_pairs={{0,1},{1,2},{2,3},{3,4},{4,5},{5,6},{6,7},{7,0},{8,9},{9,10},{10,1... | collective-permute-start | bytes 393224 | tf_op jit(solution)/shard_map/ppermute | solution.py:300
  56.6 5.3 %collective-permute-start.7 = (bf16[2,2,64,256]{3,2,1,0:T(8,128)(2,1)}, bf16[2,2,64,256]{3,2,1,0:T(8,128)(2,1)S(1)}, u32[]{:S(2)}, u32[]{:S(2)}) collective-permute-start(bf16[2,2,64,256]{3,2,1,0:T(8,128)(2,1)} %collective-permute-done.2.refs_7_), channel_id=1, source_target_pairs={{0,7},{1,0},{2,1},{3,2},{4,3},{5,4},{6,5},{7,6},{8,15},{9,8},{10,9... | collective-permute-start | bytes 393224 | tf_op jit(solution)/shard_map/ppermute | solution.py:300
  61.4 12.4 %copy-start.9 = (bf16[2,2,64,256]{3,2,1,0:T(8,128)(2,1)}, bf16[2,2,64,256]{3,2,1,0:T(8,128)(2,1)S(1)}, u32[]{:S(2)}) copy-start(bf16[2,2,64,256]{3,2,1,0:T(8,128)(2,1)S(1)} %collective-permute-done.4.refs_2_) | copy-start | bytes 393220
  61.4 6.2 %collective-permute-start.5 = (bf16[2,2,64,256]{3,2,1,0:T(8,128)(2,1)S(1)}, bf16[2,2,64,256]{3,2,1,0:T(8,128)(2,1)S(1)}, u32[]{:S(2)}, u32[]{:S(2)}) collective-permute-start(bf16[2,2,64,256]{3,2,1,0:T(8,128)(2,1)S(1)} %collective-permute-done.4.refs_2_), channel_id=1, source_target_pairs={{0,1},{1,2},{2,3},{3,4},{4,5},{5,6},{6,7},{7,0},{8,9},{9,10},{10,1... | collective-permute-start | bytes 393224 | tf_op jit(solution)/shard_map/ppermute | solution.py:300
  61.9 11.9 %copy-start.10 = (bf16[2,2,64,256]{3,2,1,0:T(8,128)(2,1)}, bf16[2,2,64,256]{3,2,1,0:T(8,128)(2,1)S(1)}, u32[]{:S(2)}) copy-start(bf16[2,2,64,256]{3,2,1,0:T(8,128)(2,1)S(1)} %collective-permute-done.7.refs_6_) | copy-start | bytes 393220
  61.9 6.3 %collective-permute-start.8 = (bf16[2,2,64,256]{3,2,1,0:T(8,128)(2,1)S(1)}, bf16[2,2,64,256]{3,2,1,0:T(8,128)(2,1)S(1)}, u32[]{:S(2)}, u32[]{:S(2)}) collective-permute-start(bf16[2,2,64,256]{3,2,1,0:T(8,128)(2,1)S(1)} %collective-permute-done.7.refs_6_), channel_id=1, source_target_pairs={{0,7},{1,0},{2,1},{3,2},{4,3},{5,4},{6,5},{7,6},{8,15},{9,8},{10,9... | collective-permute-start | bytes 393224 | tf_op jit(solution)/shard_map/ppermute | solution.py:300
  67.6 6.2 %copy-start.11 = (bf16[2,2,64,256]{3,2,1,0:T(8,128)(2,1)}, bf16[2,2,64,256]{3,2,1,0:T(8,128)(2,1)S(1)}, u32[]{:S(2)}) copy-start(bf16[2,2,64,256]{3,2,1,0:T(8,128)(2,1)S(1)} %collective-permute-done.5.refs_3_) | copy-start | bytes 393220
  67.6 6.2 %collective-permute-start.6 = (bf16[2,2,64,256]{3,2,1,0:T(8,128)(2,1)S(1)}, bf16[2,2,64,256]{3,2,1,0:T(8,128)(2,1)S(1)}, u32[]{:S(2)}, u32[]{:S(2)}) collective-permute-start(bf16[2,2,64,256]{3,2,1,0:T(8,128)(2,1)S(1)} %collective-permute-done.5.refs_3_), channel_id=1, source_target_pairs={{0,1},{1,2},{2,3},{3,4},{4,5},{5,6},{6,7},{7,0},{8,9},{9,10},{10,1... | collective-permute-start | bytes 393224 | tf_op jit(solution)/shard_map/ppermute | solution.py:300
  80.6 14.0 %collective-permute-start.9 = (bf16[8,2,64,1024]{3,2,1,0:T(8,128)(2,1)S(1)}, bf16[8,2,64,1024]{3,2,1,0:T(8,128)(2,1)}, u32[]{:S(2)}, u32[]{:S(2)}) collective-permute-start(bf16[8,2,64,1024]{3,2,1,0:T(8,128)(2,1)S(1)} %all-to-all-done.2.came_ref), channel_id=1, source_target_pairs={{0,16},{16,0},{1,17},{17,1},{2,18},{18,2},{3,19},{19,3},{4,20},{20... | collective-permute-start | bytes 6291464 | tf_op jit(solution)/shard_map/ppermute | solution.py:288
  80.6 21.1 %collective-permute-start.10 = (bf16[16,64,128]{2,1,0:T(8,128)(2,1)}, bf16[16,64,128]{2,1,0:T(8,128)(2,1)S(1)}, u32[]{:S(2)}, u32[]{:S(2)}) collective-permute-start(bf16[16,64,128]{2,1,0:T(8,128)(2,1)} %get-tuple-element.49), channel_id=1, source_target_pairs={{0,8},{1,9},{2,10},{3,11},{4,12},{5,13},{6,14},{7,15},{8,0},{9,1},... | collective-permute-start | bytes 786440 | tf_op jit(solution)/shard_map/ppermute | solution.py:371
  84.7 16.9 %collective-permute-start.11 = (bf16[16,64,128]{2,1,0:T(8,128)(2,1)}, bf16[16,64,128]{2,1,0:T(8,128)(2,1)S(1)}, u32[]{:S(2)}, u32[]{:S(2)}) collective-permute-start(bf16[16,64,128]{2,1,0:T(8,128)(2,1)} %get-tuple-element.50), channel_id=1, source_target_pairs={{0,1},{1,0},{2,3},{3,2},{4,5},{5,4},{6,7},{7,6},{8,9},{9,8},{10,11... | collective-permute-start | bytes 786440 | tf_op jit(solution)/shard_map/ppermute | solution.py:371
  84.7 16.9 %collective-permute-start.12 = (bf16[16,64,128]{2,1,0:T(8,128)(2,1)}, bf16[16,64,128]{2,1,0:T(8,128)(2,1)S(1)}, u32[]{:S(2)}, u32[]{:S(2)}) collective-permute-start(bf16[16,64,128]{2,1,0:T(8,128)(2,1)} %get-tuple-element.51), channel_id=1, source_target_pairs={{0,9},{1,8},{2,11},{3,10},{4,13},{5,12},{6,15},{7,14},{8,1},{9,0},... | collective-permute-start | bytes 786440 | tf_op jit(solution)/shard_map/ppermute | solution.py:371
  87.3 17.4 %all-to-all-start.3 = ((bf16[16,32,128]{2,1,0:T(8,128)(2,1)}), bf16[16,32,128]{2,1,0:T(8,128)(2,1)S(1)}, u32[]{:S(2)}, u32[]{:S(2)}) async-start(bf16[16,32,128]{2,1,0:T(8,128)(2,1)} %unpack.1), calls=%async_computation.3 | async-start | bytes 262144 | tf_op jit(solution)/shard_map/all_to_all | solution.py:292
  106.6 22.5 %all-to-all-start.4 = ((bf16[16,128,128]{2,1,0:T(8,128)(2,1)}), bf16[16,128,128]{2,1,0:T(8,128)(2,1)S(1)}, u32[]{:S(2)}, u32[]{:S(2)}) async-start(bf16[16,128,128]{2,1,0:T(8,128)(2,1)} %last_message.1), calls=%async_computation.4 | async-start | bytes 1048576 | tf_op jit(solution)/shard_map/all_to_all | solution.py:292
  (8 other events, 16.5 us)

commit v10 on v9

--- a/solution.py
+++ b/solution.py
@@ -168,15 +168,13 @@
             msg_ref[piece, part * 8 : part * 8 + 8, :] = total[row : row + 8, col : col + 128].astype(bf16)
 
 
-def forward(other_ref, came_ref, parts_hbm, pot_ref, blocks, sems):
+def forward(other_ref, came_ref, parts_ref, pot_ref):
     core = lax.axis_index("core")
     lag = lags(1 - core) + lags(core)
-    fetched = fetch(parts_hbm, blocks, sems, lag)
     total = jnp.zeros((64, 64), f32)
     for index in range(16):
         charges = other_ref[index, 1] if index < 8 else came_ref[index - 8, 1]
-        fetched[index].wait()
-        pair = dot_last(blocks[index], charges)
+        pair = dot_last(parts_ref[jnp.maximum(lag[index] - 1, 0)], charges)
         total = total + jnp.where(lag[index] == 0, 0.0, pair[:64] + pair[64:])
     pot_ref[...] = jnp.concatenate([total[:32], total[32:]], axis=1).astype(bf16)
 
@@ -324,13 +322,12 @@
         scratch=[pltpu.VMEM((15, 64, 1024), f32), pltpu.SemaphoreType.DMA((15,))],
         name="split_translation",
     )
-    parts = in_hbm(parts)
     msg, mate, parts = tie(exchange(msg, ROWS), mate, parts)
     blocks = [pltpu.VMEM((8, 128, 1024), bf16), pltpu.SemaphoreType.DMA((8,))]
     copies, gradient, send = call(
         other_terms,
         [((16, 32, 128), bf16), ((128, 64), bf16), ((8, 64, 1024), f32)],
-        [msg, parts],
+        [msg, in_hbm(parts)],
         specs=[vmem(), hbm()],
         scratch=blocks,
         name="other_terms",
@@ -340,7 +337,7 @@
     (own,) = call(
         own_terms,
         [((8, 64, 1024), bf16)],
-        [gradient, swap(send, "core"), parts],
+        [gradient, swap(send, "core"), in_hbm(parts)],
         specs=[vmem(), vmem(), hbm()],
         scratch=blocks,
         name="own_terms",
@@ -377,8 +374,6 @@
         forward,
         [((32, 128), bf16)],
         [others, both, parts],
-        specs=[vmem(), vmem(), hbm()],
-        scratch=[pltpu.VMEM((16, 128, 1024), bf16), pltpu.SemaphoreType.DMA((16,))],
         name="forward",
     )
     adjoint, potential, *quarters = tie(exchange(adjoint, ROWS), potential, *quarters)

time: 131 us -> 130 us (level)
  starting transfers between devices: 54 us -> 50.9 us
  Pallas kernels: 29.8 us -> 27.2 us
  local copies, waits for them, and re-layouts: 5.85 us -> 7.95 us
  waiting for transfers between devices: 39 us -> 41 us
    pallas_call x11, Pallas kernels: 29.8 us -> 27.2 us  [call(): pl.pallas_call(kernel, out_shape=[jax.ShapeDtypeStruct(s, d) for s, d in...]
    all_to_all x5, starting transfers between devices: 34.9 us -> 32.7 us  [exchange(): return lax.all_to_all(value, axes, 0, 0, tiled=True)]
    unnamed x28 -> x30, local copies, waits for them, and re-layouts: 5.85 us -> 7.95 us
    all_to_all x5, waiting for transfers between devices: 24.1 us -> 26.1 us  [exchange(): return lax.all_to_all(value, axes, 0, 0, tiled=True)]
  transfers between devices with their start and end apart: 18 -> 18, of which waited for: 9 -> 9; matrix products, arithmetic and copies ran while one was open for 0% -> 0% of each run, Pallas kernels for 15% -> 13%
where the time goes in v10:
time: 130 us; the launch traced here: 129 us
  starting transfers between devices  50.9 us (39%)
  waiting for transfers between devices  41 us (32%)
  Pallas kernels  27.2 us (21%)
  local copies, waits for them, and re-layouts  7.95 us (6%)
  between operations  1.52 us (1%)
    all_to_all x5, starting transfers between devices, exchange(): return lax.all_to_all(value, axes, 0, 0, tiled=True)  32.7 us
    pallas_call x11, Pallas kernels, call(): pl.pallas_call(kernel, out_shape=[jax.ShapeDtypeStruct(s, d) for s, d in...  27.2 us
    all_to_all x5, waiting for transfers between devices, exchange(): return lax.all_to_all(value, axes, 0, 0, tiled=True)  26.1 us
    ppermute x7, waiting for transfers between devices, shift(): return lax.ppermute(value, 'z', [(i, (i + step) % 8) for i in range(8)])  14.9 us
    ppermute x7, starting transfers between devices, shift(): return lax.ppermute(value, 'z', [(i, (i + step) % 8) for i in range(8)])  9.66 us
    unnamed x30, local copies, waits for them, and re-layouts  7.95 us
    ppermute x3, starting transfers between devices, on_device(): lax.ppermute(value, ROWS, [(i, i ^ mask) for i in range(16)])  4.99 us
    ppermute x3, starting transfers between devices, swap(): return lax.ppermute(value, axis, [(0, 1), (1, 0)])  3.53 us
  transfers between devices with their start and end apart: 18, of which 9 were waited for; matrix products, arithmetic and copies ran while one was open for 0% of the time, Pallas kernels for 13%

profile of v10, /device:TPU:8, one launch (start us, length us, event | category | flops | bytes accessed | tf_op | source)
XLA Modules:
  0.0 128.6 jit_solution(15065316034533026490)
XLA Ops:
  0.6 3.0 %prepare.1 = (bf16[2,64,256]{2,1,0:T(8,128)(2,1)S(1)}, bf16[2,64,256]{2,1,0:T(8,128)(2,1)S(1)}, bf16[16,96,128]{2,1,0:T(8,128)(2,1)}) custom-call(f32[64,512]{1,0:T(8,128)} %exc_hbm.1, f32[64,512]{1,0:T(8,128)} %loads_hbm.1, bf16[1024,512]{1,0:T(8,128)(2,1)} %refs_0_.1, bf16[1024,512]{1,0:T(8,128)(2,1)} %refs_1_.1), custom_call_target="tpu_custom_call" | custom-call | flops 1000 | bytes 1000 | tf_op jit(solution)/shard_map/prepare/pallas_call | solution.py:30
  3.6 11.0 %all-to-all-start = ((bf16[16,96,128]{2,1,0:T(8,128)(2,1)}), bf16[16,96,128]{2,1,0:T(8,128)(2,1)S(1)}, u32[]{:S(2)}, u32[]{:S(2)}) async-start(bf16[16,96,128]{2,1,0:T(8,128)(2,1)} %get-tuple-element.34), calls=%async_computation | async-start | bytes 786432 | tf_op jit(solution)/shard_map/all_to_all | solution.py:290
  14.7 3.4 %collective-permute-start = (bf16[2,64,256]{2,1,0:T(8,128)(2,1)S(1)}, bf16[2,64,256]{2,1,0:T(8,128)(2,1)S(1)}, u32[]{:S(2)}, u32[]{:S(2)}) collective-permute-start(bf16[2,64,256]{2,1,0:T(8,128)(2,1)S(1)} %get-tuple-element.35), channel_id=1, source_target_pairs={{0,8},{8,0},{1,9},{9,1},{2,10},{10,2},{3,11},{11,3},{4,12},{12,4},... | collective-permute-start | bytes 196616 | tf_op jit(solution)/shard_map/ppermute | solution.py:286
  18.1 2.2 %split_translation.1.parts_hbm.parts_ref = bf16[15,128,1024]{2,1,0:T(8,128)(2,1)S(1)} custom-call(f32[1,15,64,1024]{3,2,1,0:T(8,128)} %trans_hbm.1), custom_call_target="tpu_custom_call" | custom-call | flops 1000 | bytes 1000 | tf_op jit(solution)/shard_map/split_translation/pallas_call | solution.py:30
  22.2 6.6 %all-to-all-done.msg_ref = bf16[16,96,128]{2,1,0:T(8,128)(2,1)S(1)} async-done(((bf16[16,96,128]{2,1,0:T(8,128)(2,1)}), bf16[16,96,128]{2,1,0:T(8,128)(2,1)S(1)}, u32[]{:S(2)}, u32[]{:S(2)}) %all-to-all-start) | async-done | bytes 393248 | tf_op jit(solution)/shard_map/all_to_all | solution.py:290
  28.8 4.3 %other_terms.1 = (bf16[16,32,128]{2,1,0:T(8,128)(2,1)}, bf16[128,64]{1,0:T(8,128)(2,1)S(1)}, f32[8,64,1024]{2,1,0:T(8,128)}) custom-call(bf16[16,96,128]{2,1,0:T(8,128)(2,1)S(1)} %all-to-all-done.msg_ref, bf16[15,128,1024]{2,1,0:T(8,128)(2,1)} %copy-done), custom_call_target="tpu_custom_call" | custom-call | flops 1000 | bytes 1000 | tf_op jit(solution)/shard_map/other_terms/pallas_call | solution.py:30
  33.2 4.8 %all-to-all-start.1 = ((bf16[16,32,128]{2,1,0:T(8,128)(2,1)}), bf16[16,32,128]{2,1,0:T(8,128)(2,1)S(1)}, u32[]{:S(2)}, u32[]{:S(2)}) async-start(bf16[16,32,128]{2,1,0:T(8,128)(2,1)} %get-tuple-element.38), calls=%async_computation.1 | async-start | bytes 262144 | tf_op jit(solution)/shard_map/all_to_all | solution.py:290
  38.1 2.0 %collective-permute-start.1 = (bf16[2,2,64,256]{3,2,1,0:T(8,128)(2,1)S(1)}, bf16[2,2,64,256]{3,2,1,0:T(8,128)(2,1)S(1)}, u32[]{:S(2)}, u32[]{:S(2)}) collective-permute-start(bf16[2,2,64,256]{3,2,1,0:T(8,128)(2,1)S(1)} %pad_maximum_fusion.refs_0_), channel_id=1, source_target_pairs={{0,1},{1,2},{2,3},{3,4},{4,5},{5,6},{6,7},{7,0},{8,9},{9,10},{10,1... | collective-permute-start | bytes 393224 | tf_op jit(solution)/shard_map/ppermute | solution.py:298
  41.4 3.0 %own_terms.1.own_ref = bf16[8,64,1024]{2,1,0:T(8,128)(2,1)S(1)} custom-call(bf16[128,64]{1,0:T(8,128)(2,1)S(1)} %get-tuple-element.40.grad_ref, f32[8,64,1024]{2,1,0:T(8,128)S(1)} %collective-permute-done.3.came_ref, bf16[15,128,1024]{2,1,0:T(8,128)(2,1)} %copy-done), custom_call_target="tpu_custom_call" | custom-call | flops 1000 | bytes 1000 | tf_op jit(solution)/shard_map/own_terms/pallas_call | solution.py:30
  44.4 3.4 %collective-permute-done.1.refs_1_ = bf16[2,2,64,256]{3,2,1,0:T(8,128)(2,1)S(1)} collective-permute-done((bf16[2,2,64,256]{3,2,1,0:T(8,128)(2,1)S(1)}, bf16[2,2,64,256]{3,2,1,0:T(8,128)(2,1)S(1)}, u32[]{:S(2)}, u32[]{:S(2)}) %collective-permute-start.1) | collective-permute-done | bytes 131104 | tf_op jit(solution)/shard_map/ppermute | solution.py:298
  50.2 5.1 %all-to-all-start.2 = ((bf16[8,2,64,1024]{3,2,1,0:T(8,128)(2,1)}), bf16[8,2,64,1024]{3,2,1,0:T(8,128)(2,1)S(1)}, u32[]{:S(2)}, u32[]{:S(2)}) async-start(bf16[8,2,64,1024]{3,2,1,0:T(8,128)(2,1)} %copy-done.2), calls=%async_computation.2 | async-start | bytes 4194304 | tf_op jit(solution)/shard_map/all_to_all | solution.py:290
  58.5 2.9 %collective-permute-done.4.refs_2_ = bf16[2,2,64,256]{3,2,1,0:T(8,128)(2,1)S(1)} collective-permute-done((bf16[2,2,64,256]{3,2,1,0:T(8,128)(2,1)S(1)}, bf16[2,2,64,256]{3,2,1,0:T(8,128)(2,1)S(1)}, u32[]{:S(2)}, u32[]{:S(2)}) %collective-permute-start.4) | collective-permute-done | bytes 131104 | tf_op jit(solution)/shard_map/ppermute | solution.py:298
  61.9 2.9 %collective-permute-start.8 = (bf16[2,2,64,256]{3,2,1,0:T(8,128)(2,1)S(1)}, bf16[2,2,64,256]{3,2,1,0:T(8,128)(2,1)S(1)}, u32[]{:S(2)}, u32[]{:S(2)}) collective-permute-start(bf16[2,2,64,256]{3,2,1,0:T(8,128)(2,1)S(1)} %collective-permute-done.7.refs_6_), channel_id=1, source_target_pairs={{0,7},{1,0},{2,1},{3,2},{4,3},{5,4},{6,5},{7,6},{8,15},{9,8},{10,9... | collective-permute-start | bytes 393224 | tf_op jit(solution)/shard_map/ppermute | solution.py:298
  64.9 2.7 %collective-permute-done.5.refs_3_ = bf16[2,2,64,256]{3,2,1,0:T(8,128)(2,1)S(1)} collective-permute-done((bf16[2,2,64,256]{3,2,1,0:T(8,128)(2,1)S(1)}, bf16[2,2,64,256]{3,2,1,0:T(8,128)(2,1)S(1)}, u32[]{:S(2)}, u32[]{:S(2)}) %collective-permute-start.5) | collective-permute-done | bytes 131104 | tf_op jit(solution)/shard_map/ppermute | solution.py:298
  68.3 5.5 %collective-permute-done.6.refs_4_ = bf16[2,2,64,256]{3,2,1,0:T(8,128)(2,1)S(1)} collective-permute-done((bf16[2,2,64,256]{3,2,1,0:T(8,128)(2,1)S(1)}, bf16[2,2,64,256]{3,2,1,0:T(8,128)(2,1)S(1)}, u32[]{:S(2)}, u32[]{:S(2)}) %collective-permute-start.6) | collective-permute-done | bytes 131104 | tf_op jit(solution)/shard_map/ppermute | solution.py:298
  74.4 6.2 %near.1 = (f32[64,512]{1,0:T(8,128)S(1)}, bf16[16,64,128]{2,1,0:T(8,128)(2,1)S(1)}, bf16[16,64,128]{2,1,0:T(8,128)(2,1)}, bf16[16,64,128]{2,1,0:T(8,128)(2,1)}, bf16[16,64,128]{2,1,0:T(8,128)(2,1)}) custom-call(s32[1]{0:T(128)S(6)} %copy.11.count_ref, s32[32]{0:T(128)S(1)} %copy-done.5, s32[32]{0:T(128)S(1)} %copy-done.6, ...), custom_call_target="tpu_custom_call" | custom-call | flops 1000 | bytes 1000 | tf_op jit(solution)/shard_map/near/pallas_call | solution.py:30
  82.0 2.3 %collective-permute-start.10 = (bf16[16,64,128]{2,1,0:T(8,128)(2,1)}, bf16[16,64,128]{2,1,0:T(8,128)(2,1)S(1)}, u32[]{:S(2)}, u32[]{:S(2)}) collective-permute-start(bf16[16,64,128]{2,1,0:T(8,128)(2,1)} %get-tuple-element.49), channel_id=1, source_target_pairs={{0,8},{1,9},{2,10},{3,11},{4,12},{5,13},{6,14},{7,15},{8,0},{9,1},... | collective-permute-start | bytes 786440 | tf_op jit(solution)/shard_map/ppermute | solution.py:368
  84.4 2.6 %collective-permute-start.12 = (bf16[16,64,128]{2,1,0:T(8,128)(2,1)}, bf16[16,64,128]{2,1,0:T(8,128)(2,1)S(1)}, u32[]{:S(2)}, u32[]{:S(2)}) collective-permute-start(bf16[16,64,128]{2,1,0:T(8,128)(2,1)} %get-tuple-element.51), channel_id=1, source_target_pairs={{0,9},{1,8},{2,11},{3,10},{4,13},{5,12},{6,15},{7,14},{8,1},{9,0},... | collective-permute-start | bytes 786440 | tf_op jit(solution)/shard_map/ppermute | solution.py:368
  87.8 7.1 %all-to-all-start.3 = ((bf16[16,32,128]{2,1,0:T(8,128)(2,1)}), bf16[16,32,128]{2,1,0:T(8,128)(2,1)S(1)}, u32[]{:S(2)}, u32[]{:S(2)}) async-start(bf16[16,32,128]{2,1,0:T(8,128)(2,1)} %unpack.1), calls=%async_computation.3 | async-start | bytes 262144 | tf_op jit(solution)/shard_map/all_to_all | solution.py:290
  95.0 2.1 %copy-done.1 = bf16[15,128,1024]{2,1,0:T(8,128)(2,1)S(1)} copy-done((bf16[15,128,1024]{2,1,0:T(8,128)(2,1)S(1)}, bf16[15,128,1024]{2,1,0:T(8,128)(2,1)}, u32[]{:S(2)}) %copy-start.1) | copy-done | bytes 3932184
  97.1 2.9 %forward.1.pot_ref = bf16[32,128]{1,0:T(8,128)(2,1)S(1)} custom-call(bf16[8,2,64,1024]{3,2,1,0:T(8,128)(2,1)} %collective-permute-done.9.other_ref, bf16[8,2,64,1024]{3,2,1,0:T(8,128)(2,1)S(1)} %all-to-all-done.2.came_ref, bf16[15,128,1024]{2,1,0:T(8,128)(2,1)S(1)} %copy-done.1), custom_call_target="tpu_custom_call" | custom-call | flops 1000 | bytes 1000 | tf_op jit(solution)/shard_map/forward/pallas_call | solution.py:30
  100.0 5.0 %all-to-all-done.3.adj_ref = bf16[16,32,128]{2,1,0:T(8,128)(2,1)S(1)} async-done(((bf16[16,32,128]{2,1,0:T(8,128)(2,1)}), bf16[16,32,128]{2,1,0:T(8,128)(2,1)S(1)}, u32[]{:S(2)}, u32[]{:S(2)}) %all-to-all-start.3) | async-done | bytes 131104 | tf_op jit(solution)/shard_map/all_to_all | solution.py:290
  106.9 4.6 %all-to-all-start.4 = ((bf16[16,128,128]{2,1,0:T(8,128)(2,1)}), bf16[16,128,128]{2,1,0:T(8,128)(2,1)S(1)}, u32[]{:S(2)}, u32[]{:S(2)}) async-start(bf16[16,128,128]{2,1,0:T(8,128)(2,1)} %last_message.1), calls=%async_computation.4 | async-start | bytes 1048576 | tf_op jit(solution)/shard_map/all_to_all | solution.py:290
  113.1 14.3 %all-to-all-done.4.msg_ref = bf16[16,128,128]{2,1,0:T(8,128)(2,1)S(1)} async-done(((bf16[16,128,128]{2,1,0:T(8,128)(2,1)}), bf16[16,128,128]{2,1,0:T(8,128)(2,1)S(1)}, u32[]{:S(2)}, u32[]{:S(2)}) %all-to-all-start.4) | async-done | bytes 524320 | tf_op jit(solution)/shard_map/all_to_all | solution.py:290
  (54 shorter events, 16.7 us)
Async XLA Ops:
  3.6 25.2 %all-to-all-start = ((bf16[16,96,128]{2,1,0:T(8,128)(2,1)}), bf16[16,96,128]{2,1,0:T(8,128)(2,1)S(1)}, u32[]{:S(2)}, u32[]{:S(2)}) async-start(bf16[16,96,128]{2,1,0:T(8,128)(2,1)} %get-tuple-element.34), calls=%async_computation | async-start | bytes 786432 | tf_op jit(solution)/shard_map/all_to_all | solution.py:290
  14.7 7.5 %collective-permute-start = (bf16[2,64,256]{2,1,0:T(8,128)(2,1)S(1)}, bf16[2,64,256]{2,1,0:T(8,128)(2,1)S(1)}, u32[]{:S(2)}, u32[]{:S(2)}) collective-permute-start(bf16[2,64,256]{2,1,0:T(8,128)(2,1)S(1)} %get-tuple-element.35), channel_id=1, source_target_pairs={{0,8},{8,0},{1,9},{9,1},{2,10},{10,2},{3,11},{11,3},{4,12},{12,4},... | collective-permute-start | bytes 196616 | tf_op jit(solution)/shard_map/ppermute | solution.py:286
  33.1 8.3 %collective-permute-start.3 = (f32[8,64,1024]{2,1,0:T(8,128)}, f32[8,64,1024]{2,1,0:T(8,128)S(1)}, u32[]{:S(2)}, u32[]{:S(2)}) collective-permute-start(f32[8,64,1024]{2,1,0:T(8,128)} %get-tuple-element.41), channel_id=1, source_target_pairs={{0,16},{16,0},{1,17},{17,1},{2,18},{18,2},{3,19},{19,3},{4,20},{20... | collective-permute-start | bytes 6291464 | tf_op jit(solution)/shard_map/ppermute | solution.py:286
  33.2 15.4 %all-to-all-start.1 = ((bf16[16,32,128]{2,1,0:T(8,128)(2,1)}), bf16[16,32,128]{2,1,0:T(8,128)(2,1)S(1)}, u32[]{:S(2)}, u32[]{:S(2)}) async-start(bf16[16,32,128]{2,1,0:T(8,128)(2,1)} %get-tuple-element.38), calls=%async_computation.1 | async-start | bytes 262144 | tf_op jit(solution)/shard_map/all_to_all | solution.py:290
  38.1 6.3 %copy-start.7 = (bf16[2,2,64,256]{3,2,1,0:T(8,128)(2,1)}, bf16[2,2,64,256]{3,2,1,0:T(8,128)(2,1)S(1)}, u32[]{:S(2)}) copy-start(bf16[2,2,64,256]{3,2,1,0:T(8,128)(2,1)S(1)} %pad_maximum_fusion.refs_0_) | copy-start | bytes 393220
  38.1 9.7 %collective-permute-start.1 = (bf16[2,2,64,256]{3,2,1,0:T(8,128)(2,1)S(1)}, bf16[2,2,64,256]{3,2,1,0:T(8,128)(2,1)S(1)}, u32[]{:S(2)}, u32[]{:S(2)}) collective-permute-start(bf16[2,2,64,256]{3,2,1,0:T(8,128)(2,1)S(1)} %pad_maximum_fusion.refs_0_), channel_id=1, source_target_pairs={{0,1},{1,2},{2,3},{3,4},{4,5},{5,6},{6,7},{7,0},{8,9},{9,10},{10,1... | collective-permute-start | bytes 393224 | tf_op jit(solution)/shard_map/ppermute | solution.py:298
  40.1 8.4 %collective-permute-start.2 = (bf16[2,2,64,256]{3,2,1,0:T(8,128)(2,1)S(1)}, bf16[2,2,64,256]{3,2,1,0:T(8,128)(2,1)}, u32[]{:S(2)}, u32[]{:S(2)}) collective-permute-start(bf16[2,2,64,256]{3,2,1,0:T(8,128)(2,1)S(1)} %pad_maximum_fusion.refs_0_), channel_id=1, source_target_pairs={{0,7},{1,0},{2,1},{3,2},{4,3},{5,4},{6,5},{7,6},{8,15},{9,8},{10,9... | collective-permute-start | bytes 393224 | tf_op jit(solution)/shard_map/ppermute | solution.py:298
  50.1 24.3 %copy-start.5 = (s32[32]{0:T(128)S(1)}, s32[32]{0:T(128)}, u32[]{:S(2)}) copy-start(s32[32]{0:T(128)} %rows_ref.1) | copy-start | bytes 388
  50.2 24.3 %copy-start.6 = (s32[32]{0:T(128)S(1)}, s32[32]{0:T(128)}, u32[]{:S(2)}) copy-start(s32[32]{0:T(128)} %cols_ref.1) | copy-start | bytes 388
  50.2 31.9 %all-to-all-start.2 = ((bf16[8,2,64,1024]{3,2,1,0:T(8,128)(2,1)}), bf16[8,2,64,1024]{3,2,1,0:T(8,128)(2,1)S(1)}, u32[]{:S(2)}, u32[]{:S(2)}) async-start(bf16[8,2,64,1024]{3,2,1,0:T(8,128)(2,1)} %copy-done.2), calls=%async_computation.2 | async-start | bytes 4194304 | tf_op jit(solution)/shard_map/all_to_all | solution.py:290
  55.2 6.2 %collective-permute-start.4 = (bf16[2,2,64,256]{3,2,1,0:T(8,128)(2,1)S(1)}, bf16[2,2,64,256]{3,2,1,0:T(8,128)(2,1)S(1)}, u32[]{:S(2)}, u32[]{:S(2)}) collective-permute-start(bf16[2,2,64,256]{3,2,1,0:T(8,128)(2,1)S(1)} %copy-done.9), channel_id=1, source_target_pairs={{0,1},{1,2},{2,3},{3,4},{4,5},{5,6},{6,7},{7,0},{8,9},{9,10},{10,1... | collective-permute-start | bytes 393224 | tf_op jit(solution)/shard_map/ppermute | solution.py:298
  56.6 5.3 %collective-permute-start.7 = (bf16[2,2,64,256]{3,2,1,0:T(8,128)(2,1)}, bf16[2,2,64,256]{3,2,1,0:T(8,128)(2,1)S(1)}, u32[]{:S(2)}, u32[]{:S(2)}) collective-permute-start(bf16[2,2,64,256]{3,2,1,0:T(8,128)(2,1)} %collective-permute-done.2.refs_7_), channel_id=1, source_target_pairs={{0,7},{1,0},{2,1},{3,2},{4,3},{5,4},{6,5},{7,6},{8,15},{9,8},{10,9... | collective-permute-start | bytes 393224 | tf_op jit(solution)/shard_map/ppermute | solution.py:298
  61.4 12.4 %copy-start.10 = (bf16[2,2,64,256]{3,2,1,0:T(8,128)(2,1)}, bf16[2,2,64,256]{3,2,1,0:T(8,128)(2,1)S(1)}, u32[]{:S(2)}) copy-start(bf16[2,2,64,256]{3,2,1,0:T(8,128)(2,1)S(1)} %collective-permute-done.4.refs_2_) | copy-start | bytes 393220
  61.4 6.2 %collective-permute-start.5 = (bf16[2,2,64,256]{3,2,1,0:T(8,128)(2,1)S(1)}, bf16[2,2,64,256]{3,2,1,0:T(8,128)(2,1)S(1)}, u32[]{:S(2)}, u32[]{:S(2)}) collective-permute-start(bf16[2,2,64,256]{3,2,1,0:T(8,128)(2,1)S(1)} %collective-permute-done.4.refs_2_), channel_id=1, source_target_pairs={{0,1},{1,2},{2,3},{3,4},{4,5},{5,6},{6,7},{7,0},{8,9},{9,10},{10,1... | collective-permute-start | bytes 393224 | tf_op jit(solution)/shard_map/ppermute | solution.py:298
  61.9 11.9 %copy-start.11 = (bf16[2,2,64,256]{3,2,1,0:T(8,128)(2,1)}, bf16[2,2,64,256]{3,2,1,0:T(8,128)(2,1)S(1)}, u32[]{:S(2)}) copy-start(bf16[2,2,64,256]{3,2,1,0:T(8,128)(2,1)S(1)} %collective-permute-done.7.refs_6_) | copy-start | bytes 393220
  61.9 6.3 %collective-permute-start.8 = (bf16[2,2,64,256]{3,2,1,0:T(8,128)(2,1)S(1)}, bf16[2,2,64,256]{3,2,1,0:T(8,128)(2,1)S(1)}, u32[]{:S(2)}, u32[]{:S(2)}) collective-permute-start(bf16[2,2,64,256]{3,2,1,0:T(8,128)(2,1)S(1)} %collective-permute-done.7.refs_6_), channel_id=1, source_target_pairs={{0,7},{1,0},{2,1},{3,2},{4,3},{5,4},{6,5},{7,6},{8,15},{9,8},{10,9... | collective-permute-start | bytes 393224 | tf_op jit(solution)/shard_map/ppermute | solution.py:298
  67.6 6.2 %copy-start.12 = (bf16[2,2,64,256]{3,2,1,0:T(8,128)(2,1)}, bf16[2,2,64,256]{3,2,1,0:T(8,128)(2,1)S(1)}, u32[]{:S(2)}) copy-start(bf16[2,2,64,256]{3,2,1,0:T(8,128)(2,1)S(1)} %collective-permute-done.5.refs_3_) | copy-start | bytes 393220
  67.6 6.2 %collective-permute-start.6 = (bf16[2,2,64,256]{3,2,1,0:T(8,128)(2,1)S(1)}, bf16[2,2,64,256]{3,2,1,0:T(8,128)(2,1)S(1)}, u32[]{:S(2)}, u32[]{:S(2)}) collective-permute-start(bf16[2,2,64,256]{3,2,1,0:T(8,128)(2,1)S(1)} %collective-permute-done.5.refs_3_), channel_id=1, source_target_pairs={{0,1},{1,2},{2,3},{3,4},{4,5},{5,6},{6,7},{7,0},{8,9},{9,10},{10,1... | collective-permute-start | bytes 393224 | tf_op jit(solution)/shard_map/ppermute | solution.py:298
  82.0 12.9 %collective-permute-start.9 = (bf16[8,2,64,1024]{3,2,1,0:T(8,128)(2,1)S(1)}, bf16[8,2,64,1024]{3,2,1,0:T(8,128)(2,1)}, u32[]{:S(2)}, u32[]{:S(2)}) collective-permute-start(bf16[8,2,64,1024]{3,2,1,0:T(8,128)(2,1)S(1)} %all-to-all-done.2.came_ref), channel_id=1, source_target_pairs={{0,16},{16,0},{1,17},{17,1},{2,18},{18,2},{3,19},{19,3},{4,20},{20... | collective-permute-start | bytes 6291464 | tf_op jit(solution)/shard_map/ppermute | solution.py:286
  82.0 18.0 %collective-permute-start.10 = (bf16[16,64,128]{2,1,0:T(8,128)(2,1)}, bf16[16,64,128]{2,1,0:T(8,128)(2,1)S(1)}, u32[]{:S(2)}, u32[]{:S(2)}) collective-permute-start(bf16[16,64,128]{2,1,0:T(8,128)(2,1)} %get-tuple-element.49), channel_id=1, source_target_pairs={{0,8},{1,9},{2,10},{3,11},{4,12},{5,13},{6,14},{7,15},{8,0},{9,1},... | collective-permute-start | bytes 786440 | tf_op jit(solution)/shard_map/ppermute | solution.py:368
  84.4 15.6 %collective-permute-start.11 = (bf16[16,64,128]{2,1,0:T(8,128)(2,1)}, bf16[16,64,128]{2,1,0:T(8,128)(2,1)S(1)}, u32[]{:S(2)}, u32[]{:S(2)}) collective-permute-start(bf16[16,64,128]{2,1,0:T(8,128)(2,1)} %get-tuple-element.50), channel_id=1, source_target_pairs={{0,1},{1,0},{2,3},{3,2},{4,5},{5,4},{6,7},{7,6},{8,9},{9,8},{10,11... | collective-permute-start | bytes 786440 | tf_op jit(solution)/shard_map/ppermute | solution.py:368
  84.4 15.6 %collective-permute-start.12 = (bf16[16,64,128]{2,1,0:T(8,128)(2,1)}, bf16[16,64,128]{2,1,0:T(8,128)(2,1)S(1)}, u32[]{:S(2)}, u32[]{:S(2)}) collective-permute-start(bf16[16,64,128]{2,1,0:T(8,128)(2,1)} %get-tuple-element.51), channel_id=1, source_target_pairs={{0,9},{1,8},{2,11},{3,10},{4,13},{5,12},{6,15},{7,14},{8,1},{9,0},... | collective-permute-start | bytes 786440 | tf_op jit(solution)/shard_map/ppermute | solution.py:368
  87.8 17.2 %all-to-all-start.3 = ((bf16[16,32,128]{2,1,0:T(8,128)(2,1)}), bf16[16,32,128]{2,1,0:T(8,128)(2,1)S(1)}, u32[]{:S(2)}, u32[]{:S(2)}) async-start(bf16[16,32,128]{2,1,0:T(8,128)(2,1)} %unpack.1), calls=%async_computation.3 | async-start | bytes 262144 | tf_op jit(solution)/shard_map/all_to_all | solution.py:290
  106.9 20.5 %all-to-all-start.4 = ((bf16[16,128,128]{2,1,0:T(8,128)(2,1)}), bf16[16,128,128]{2,1,0:T(8,128)(2,1)S(1)}, u32[]{:S(2)}, u32[]{:S(2)}) async-start(bf16[16,128,128]{2,1,0:T(8,128)(2,1)} %last_message.1), calls=%async_computation.4 | async-start | bytes 1048576 | tf_op jit(solution)/shard_map/all_to_all | solution.py:290
  (9 other events, 18.6 us)

commit v11 on v10

--- a/solution.py
+++ b/solution.py
@@ -179,21 +179,15 @@
     pot_ref[...] = jnp.concatenate([total[:32], total[32:]], axis=1).astype(bf16)
 
 
-def near(count_ref, rows_ref, cols_ref, low_ref, tiles_hbm, *refs):
+def near(count_ref, rows_ref, cols_ref, low_ref, tiles_ref, *refs):
     pieces, refs = refs[:8], refs[8:]
-    ahead_ref, keep_ref, across_ref, beside_ref, both_ref, acc, behind, drives, tiles_ref, tile_sems, piece_sems = refs
-
-    def tile_copy(index):
-        span = pl.ds(index * 4, 4)
-        return pltpu.make_async_copy(tiles_hbm.at[span], tiles_ref.at[span], tile_sems.at[index])
+    ahead_ref, keep_ref, across_ref, beside_ref, both_ref, acc, behind, drives, piece_sems = refs
 
     arriving = [
         pltpu.make_async_copy(pieces[index], drives.at[index], piece_sems.at[index]) for index in range(8)
     ]
     for copy in arriving:
         copy.start()
-    for index in range(8):
-        tile_copy(index).start()
     acc[...] = jnp.zeros_like(acc)
     behind[...] = jnp.zeros_like(behind)
     for copy in arriving:
@@ -204,7 +198,6 @@
     group = 4
 
     def step(index, carry):
-        tile_copy(index).wait()
         results = []
         for part in range(group):
             slot = index * group + part
@@ -222,14 +215,7 @@
             behind[col] += jnp.where(live, bwd, 0.0)
         return carry
 
-    groups = (count + group - 1) // group
-    lax.fori_loop(0, groups, step, 0)
-
-    def drain(index, carry):
-        tile_copy(index).wait()
-        return carry
-
-    lax.fori_loop(groups, 8, drain, 0)
+    lax.fori_loop(0, (count + group - 1) // group, step, 0)
     for part in range(2):
         ahead_ref[:, part * 256 : part * 256 + 256] = acc[part]
     parity = lax.rem(my_z, 2)
@@ -350,15 +336,13 @@
     ahead, keep, *quarters = call(
         near,
         [((64, 512), f32)] + [((16, 64, 128), bf16)] * 4,
-        [tile_count, tile_rows, tile_cols, low, in_hbm(tiles)]
+        [tile_count, tile_rows, tile_cols, low, tiles]
         + [in_hbm(piece) for piece in (here, up1, up2, up3, up4, down3, down2, down1)],
-        specs=[smem(), smem(), smem(), vmem()] + [hbm()] * 9,
+        specs=[smem(), smem(), smem(), vmem(), vmem()] + [hbm()] * 8,
         scratch=[
             pltpu.VMEM((2, 64, 256), f32),
             pltpu.VMEM((32, 64, 256), f32),
             pltpu.VMEM((8, 2, 2, 64, 256), bf16),
-            pltpu.VMEM((32, 256, 256), bf16),
-            pltpu.SemaphoreType.DMA((8,)),
             pltpu.SemaphoreType.DMA((8,)),
         ],
         name="near",

time: 130 us -> 131 us (level)
  local copies, waits for them, and re-layouts: 7.95 us -> 10.2 us
  Pallas kernels: 27.2 us -> 25 us
    unnamed x30 -> x32, local copies, waits for them, and re-layouts: 7.95 us -> 10.2 us
    pallas_call x11, Pallas kernels: 27.2 us -> 25 us  [call(): pl.pallas_call(kernel, out_shape=[jax.ShapeDtypeStruct(s, d) for s, d in...]
  transfers between devices with their start and end apart: 18 -> 18, of which waited for: 9 -> 10; matrix products, arithmetic and copies ran while one was open for 0% -> 0% of each run, Pallas kernels for 13% -> 11%
where the time goes in v11:
time: 131 us; the launch traced here: 129 us
  starting transfers between devices  52 us (40%)
  waiting for transfers between devices  40.5 us (31%)
  Pallas kernels  25 us (19%)
  local copies, waits for them, and re-layouts  10.2 us (8%)
  between operations  1.51 us (1%)
    all_to_all x5, starting transfers between devices, exchange(): return lax.all_to_all(value, axes, 0, 0, tiled=True)  33.3 us
    all_to_all x5, waiting for transfers between devices, exchange(): return lax.all_to_all(value, axes, 0, 0, tiled=True)  25.5 us
    pallas_call x11, Pallas kernels, call(): pl.pallas_call(kernel, out_shape=[jax.ShapeDtypeStruct(s, d) for s, d in...  25 us
    ppermute x7, waiting for transfers between devices, shift(): return lax.ppermute(value, 'z', [(i, (i + step) % 8) for i in range(8)])  14.9 us
    unnamed x32, local copies, waits for them, and re-layouts  10.2 us
    ppermute x7, starting transfers between devices, shift(): return lax.ppermute(value, 'z', [(i, (i + step) % 8) for i in range(8)])  9.66 us
    ppermute x3, starting transfers between devices, on_device(): lax.ppermute(value, ROWS, [(i, i ^ mask) for i in range(16)])  5.53 us
    ppermute x3, starting transfers between devices, swap(): return lax.ppermute(value, axis, [(0, 1), (1, 0)])  3.53 us
  transfers between devices with their start and end apart: 18, of which 10 were waited for; matrix products, arithmetic and copies ran while one was open for 0% of the time, Pallas kernels for 11%

profile of v11, /device:TPU:8, one launch (start us, length us, event | category | flops | bytes accessed | tf_op | source)
XLA Modules:
  0.0 129.3 jit_solution(14575169948960085871)
XLA Ops:
  0.6 3.0 %prepare.1 = (bf16[2,64,256]{2,1,0:T(8,128)(2,1)S(1)}, bf16[2,64,256]{2,1,0:T(8,128)(2,1)S(1)}, bf16[16,96,128]{2,1,0:T(8,128)(2,1)}) custom-call(f32[64,512]{1,0:T(8,128)} %exc_hbm.1, f32[64,512]{1,0:T(8,128)} %loads_hbm.1, bf16[1024,512]{1,0:T(8,128)(2,1)} %refs_0_.1, bf16[1024,512]{1,0:T(8,128)(2,1)} %refs_1_.1), custom_call_target="tpu_custom_call" | custom-call | flops 1000 | bytes 1000 | tf_op jit(solution)/shard_map/prepare/pallas_call | solution.py:30
  3.6 11.0 %all-to-all-start = ((bf16[16,96,128]{2,1,0:T(8,128)(2,1)}), bf16[16,96,128]{2,1,0:T(8,128)(2,1)S(1)}, u32[]{:S(2)}, u32[]{:S(2)}) async-start(bf16[16,96,128]{2,1,0:T(8,128)(2,1)} %get-tuple-element.34), calls=%async_computation | async-start | bytes 786432 | tf_op jit(solution)/shard_map/all_to_all | solution.py:276
  14.7 3.4 %collective-permute-start = (bf16[2,64,256]{2,1,0:T(8,128)(2,1)S(1)}, bf16[2,64,256]{2,1,0:T(8,128)(2,1)S(1)}, u32[]{:S(2)}, u32[]{:S(2)}) collective-permute-start(bf16[2,64,256]{2,1,0:T(8,128)(2,1)S(1)} %get-tuple-element.35), channel_id=1, source_target_pairs={{0,8},{8,0},{1,9},{9,1},{2,10},{10,2},{3,11},{11,3},{4,12},{12,4},... | collective-permute-start | bytes 196616 | tf_op jit(solution)/shard_map/ppermute | solution.py:272
  18.1 2.2 %split_translation.1.parts_hbm.parts_ref = bf16[15,128,1024]{2,1,0:T(8,128)(2,1)S(1)} custom-call(f32[1,15,64,1024]{3,2,1,0:T(8,128)} %trans_hbm.1), custom_call_target="tpu_custom_call" | custom-call | flops 1000 | bytes 1000 | tf_op jit(solution)/shard_map/split_translation/pallas_call | solution.py:30
  22.2 6.6 %all-to-all-done.msg_ref = bf16[16,96,128]{2,1,0:T(8,128)(2,1)S(1)} async-done(((bf16[16,96,128]{2,1,0:T(8,128)(2,1)}), bf16[16,96,128]{2,1,0:T(8,128)(2,1)S(1)}, u32[]{:S(2)}, u32[]{:S(2)}) %all-to-all-start) | async-done | bytes 393248 | tf_op jit(solution)/shard_map/all_to_all | solution.py:276
  28.8 4.4 %other_terms.1 = (bf16[16,32,128]{2,1,0:T(8,128)(2,1)}, bf16[128,64]{1,0:T(8,128)(2,1)S(1)}, f32[8,64,1024]{2,1,0:T(8,128)}) custom-call(bf16[16,96,128]{2,1,0:T(8,128)(2,1)S(1)} %all-to-all-done.msg_ref, bf16[15,128,1024]{2,1,0:T(8,128)(2,1)} %copy-done), custom_call_target="tpu_custom_call" | custom-call | flops 1000 | bytes 1000 | tf_op jit(solution)/shard_map/other_terms/pallas_call | solution.py:30
  33.2 4.8 %all-to-all-start.1 = ((bf16[16,32,128]{2,1,0:T(8,128)(2,1)}), bf16[16,32,128]{2,1,0:T(8,128)(2,1)S(1)}, u32[]{:S(2)}, u32[]{:S(2)}) async-start(bf16[16,32,128]{2,1,0:T(8,128)(2,1)} %get-tuple-element.38), calls=%async_computation.1 | async-start | bytes 262144 | tf_op jit(solution)/shard_map/all_to_all | solution.py:276
  38.1 2.0 %collective-permute-start.1 = (bf16[2,2,64,256]{3,2,1,0:T(8,128)(2,1)S(1)}, bf16[2,2,64,256]{3,2,1,0:T(8,128)(2,1)S(1)}, u32[]{:S(2)}, u32[]{:S(2)}) collective-permute-start(bf16[2,2,64,256]{3,2,1,0:T(8,128)(2,1)S(1)} %pad_maximum_fusion.refs_0_), channel_id=1, source_target_pairs={{0,1},{1,2},{2,3},{3,4},{4,5},{5,6},{6,7},{7,0},{8,9},{9,10},{10,1... | collective-permute-start | bytes 393224 | tf_op jit(solution)/shard_map/ppermute | solution.py:284
  41.4 3.0 %own_terms.1.own_ref = bf16[8,64,1024]{2,1,0:T(8,128)(2,1)S(1)} custom-call(bf16[128,64]{1,0:T(8,128)(2,1)S(1)} %get-tuple-element.40.grad_ref, f32[8,64,1024]{2,1,0:T(8,128)S(1)} %collective-permute-done.3.came_ref, bf16[15,128,1024]{2,1,0:T(8,128)(2,1)} %copy-done), custom_call_target="tpu_custom_call" | custom-call | flops 1000 | bytes 1000 | tf_op jit(solution)/shard_map/own_terms/pallas_call | solution.py:30
  44.4 3.4 %collective-permute-done.1.refs_1_ = bf16[2,2,64,256]{3,2,1,0:T(8,128)(2,1)S(1)} collective-permute-done((bf16[2,2,64,256]{3,2,1,0:T(8,128)(2,1)S(1)}, bf16[2,2,64,256]{3,2,1,0:T(8,128)(2,1)S(1)}, u32[]{:S(2)}, u32[]{:S(2)}) %collective-permute-start.1) | collective-permute-done | bytes 131104 | tf_op jit(solution)/shard_map/ppermute | solution.py:284
  50.2 5.1 %all-to-all-start.2 = ((bf16[8,2,64,1024]{3,2,1,0:T(8,128)(2,1)}), bf16[8,2,64,1024]{3,2,1,0:T(8,128)(2,1)S(1)}, u32[]{:S(2)}, u32[]{:S(2)}) async-start(bf16[8,2,64,1024]{3,2,1,0:T(8,128)(2,1)} %copy-done.2), calls=%async_computation.2 | async-start | bytes 4194304 | tf_op jit(solution)/shard_map/all_to_all | solution.py:276
  58.5 2.9 %collective-permute-done.4.refs_2_ = bf16[2,2,64,256]{3,2,1,0:T(8,128)(2,1)S(1)} collective-permute-done((bf16[2,2,64,256]{3,2,1,0:T(8,128)(2,1)S(1)}, bf16[2,2,64,256]{3,2,1,0:T(8,128)(2,1)S(1)}, u32[]{:S(2)}, u32[]{:S(2)}) %collective-permute-start.4) | collective-permute-done | bytes 131104 | tf_op jit(solution)/shard_map/ppermute | solution.py:284
  62.0 2.9 %collective-permute-start.8 = (bf16[2,2,64,256]{3,2,1,0:T(8,128)(2,1)S(1)}, bf16[2,2,64,256]{3,2,1,0:T(8,128)(2,1)S(1)}, u32[]{:S(2)}, u32[]{:S(2)}) collective-permute-start(bf16[2,2,64,256]{3,2,1,0:T(8,128)(2,1)S(1)} %collective-permute-done.7.refs_6_), channel_id=1, source_target_pairs={{0,7},{1,0},{2,1},{3,2},{4,3},{5,4},{6,5},{7,6},{8,15},{9,8},{10,9... | collective-permute-start | bytes 393224 | tf_op jit(solution)/shard_map/ppermute | solution.py:284
  64.9 2.7 %collective-permute-done.5.refs_3_ = bf16[2,2,64,256]{3,2,1,0:T(8,128)(2,1)S(1)} collective-permute-done((bf16[2,2,64,256]{3,2,1,0:T(8,128)(2,1)S(1)}, bf16[2,2,64,256]{3,2,1,0:T(8,128)(2,1)S(1)}, u32[]{:S(2)}, u32[]{:S(2)}) %collective-permute-start.5) | collective-permute-done | bytes 131104 | tf_op jit(solution)/shard_map/ppermute | solution.py:284
  68.3 5.5 %collective-permute-done.6.refs_4_ = bf16[2,2,64,256]{3,2,1,0:T(8,128)(2,1)S(1)} collective-permute-done((bf16[2,2,64,256]{3,2,1,0:T(8,128)(2,1)S(1)}, bf16[2,2,64,256]{3,2,1,0:T(8,128)(2,1)S(1)}, u32[]{:S(2)}, u32[]{:S(2)}) %collective-permute-start.6) | collective-permute-done | bytes 131104 | tf_op jit(solution)/shard_map/ppermute | solution.py:284
  74.5 2.2 %copy-done.3 = bf16[32,256,256]{2,1,0:T(8,128)(2,1)S(1)} copy-done((bf16[32,256,256]{2,1,0:T(8,128)(2,1)S(1)}, bf16[32,256,256]{2,1,0:T(8,128)(2,1)}, u32[]{:S(2)}) %copy-start.3) | copy-done | bytes 4194328
  76.7 4.0 %near.1 = (f32[64,512]{1,0:T(8,128)S(1)}, bf16[16,64,128]{2,1,0:T(8,128)(2,1)S(1)}, bf16[16,64,128]{2,1,0:T(8,128)(2,1)}, bf16[16,64,128]{2,1,0:T(8,128)(2,1)}, bf16[16,64,128]{2,1,0:T(8,128)(2,1)}) custom-call(s32[1]{0:T(128)S(6)} %copy.11.count_ref, s32[32]{0:T(128)S(1)} %copy-done.6, s32[32]{0:T(128)S(1)} %copy-done.7, ...), custom_call_target="tpu_custom_call" | custom-call | flops 1000 | bytes 1000 | tf_op jit(solution)/shard_map/near/pallas_call | solution.py:30
  82.1 3.8 %collective-permute-start.10 = (bf16[16,64,128]{2,1,0:T(8,128)(2,1)}, bf16[16,64,128]{2,1,0:T(8,128)(2,1)S(1)}, u32[]{:S(2)}, u32[]{:S(2)}) collective-permute-start(bf16[16,64,128]{2,1,0:T(8,128)(2,1)} %get-tuple-element.49), channel_id=1, source_target_pairs={{0,8},{1,9},{2,10},{3,11},{4,12},{5,13},{6,14},{7,15},{8,0},{9,1},... | collective-permute-start | bytes 786440 | tf_op jit(solution)/shard_map/ppermute | solution.py:352
  88.4 6.6 %all-to-all-start.3 = ((bf16[16,32,128]{2,1,0:T(8,128)(2,1)}), bf16[16,32,128]{2,1,0:T(8,128)(2,1)S(1)}, u32[]{:S(2)}, u32[]{:S(2)}) async-start(bf16[16,32,128]{2,1,0:T(8,128)(2,1)} %unpack.1), calls=%async_computation.3 | async-start | bytes 262144 | tf_op jit(solution)/shard_map/all_to_all | solution.py:276
  95.0 2.1 %copy-done.1 = bf16[15,128,1024]{2,1,0:T(8,128)(2,1)S(1)} copy-done((bf16[15,128,1024]{2,1,0:T(8,128)(2,1)S(1)}, bf16[15,128,1024]{2,1,0:T(8,128)(2,1)}, u32[]{:S(2)}) %copy-start.1) | copy-done | bytes 3932184
  97.1 2.9 %forward.1.pot_ref = bf16[32,128]{1,0:T(8,128)(2,1)S(1)} custom-call(bf16[8,2,64,1024]{3,2,1,0:T(8,128)(2,1)} %collective-permute-done.9.other_ref, bf16[8,2,64,1024]{3,2,1,0:T(8,128)(2,1)S(1)} %all-to-all-done.2.came_ref, bf16[15,128,1024]{2,1,0:T(8,128)(2,1)S(1)} %copy-done.1), custom_call_target="tpu_custom_call" | custom-call | flops 1000 | bytes 1000 | tf_op jit(solution)/shard_map/forward/pallas_call | solution.py:30
  100.1 4.9 %all-to-all-done.3.adj_ref = bf16[16,32,128]{2,1,0:T(8,128)(2,1)S(1)} async-done(((bf16[16,32,128]{2,1,0:T(8,128)(2,1)}), bf16[16,32,128]{2,1,0:T(8,128)(2,1)S(1)}, u32[]{:S(2)}, u32[]{:S(2)}) %all-to-all-start.3) | async-done | bytes 131104 | tf_op jit(solution)/shard_map/all_to_all | solution.py:276
  106.9 5.7 %all-to-all-start.4 = ((bf16[16,128,128]{2,1,0:T(8,128)(2,1)}), bf16[16,128,128]{2,1,0:T(8,128)(2,1)S(1)}, u32[]{:S(2)}, u32[]{:S(2)}) async-start(bf16[16,128,128]{2,1,0:T(8,128)(2,1)} %last_message.1), calls=%async_computation.4 | async-start | bytes 1048576 | tf_op jit(solution)/shard_map/all_to_all | solution.py:276
  114.3 13.9 %all-to-all-done.4.msg_ref = bf16[16,128,128]{2,1,0:T(8,128)(2,1)S(1)} async-done(((bf16[16,128,128]{2,1,0:T(8,128)(2,1)}), bf16[16,128,128]{2,1,0:T(8,128)(2,1)S(1)}, u32[]{:S(2)}, u32[]{:S(2)}) %all-to-all-start.4) | async-done | bytes 524320 | tf_op jit(solution)/shard_map/all_to_all | solution.py:276
  (56 shorter events, 18.6 us)
Async XLA Ops:
  3.6 25.2 %all-to-all-start = ((bf16[16,96,128]{2,1,0:T(8,128)(2,1)}), bf16[16,96,128]{2,1,0:T(8,128)(2,1)S(1)}, u32[]{:S(2)}, u32[]{:S(2)}) async-start(bf16[16,96,128]{2,1,0:T(8,128)(2,1)} %get-tuple-element.34), calls=%async_computation | async-start | bytes 786432 | tf_op jit(solution)/shard_map/all_to_all | solution.py:276
  14.7 7.5 %collective-permute-start = (bf16[2,64,256]{2,1,0:T(8,128)(2,1)S(1)}, bf16[2,64,256]{2,1,0:T(8,128)(2,1)S(1)}, u32[]{:S(2)}, u32[]{:S(2)}) collective-permute-start(bf16[2,64,256]{2,1,0:T(8,128)(2,1)S(1)} %get-tuple-element.35), channel_id=1, source_target_pairs={{0,8},{8,0},{1,9},{9,1},{2,10},{10,2},{3,11},{11,3},{4,12},{12,4},... | collective-permute-start | bytes 196616 | tf_op jit(solution)/shard_map/ppermute | solution.py:272
  33.1 8.3 %collective-permute-start.3 = (f32[8,64,1024]{2,1,0:T(8,128)}, f32[8,64,1024]{2,1,0:T(8,128)S(1)}, u32[]{:S(2)}, u32[]{:S(2)}) collective-permute-start(f32[8,64,1024]{2,1,0:T(8,128)} %get-tuple-element.41), channel_id=1, source_target_pairs={{0,16},{16,0},{1,17},{17,1},{2,18},{18,2},{3,19},{19,3},{4,20},{20... | collective-permute-start | bytes 6291464 | tf_op jit(solution)/shard_map/ppermute | solution.py:272
  33.2 15.4 %all-to-all-start.1 = ((bf16[16,32,128]{2,1,0:T(8,128)(2,1)}), bf16[16,32,128]{2,1,0:T(8,128)(2,1)S(1)}, u32[]{:S(2)}, u32[]{:S(2)}) async-start(bf16[16,32,128]{2,1,0:T(8,128)(2,1)} %get-tuple-element.38), calls=%async_computation.1 | async-start | bytes 262144 | tf_op jit(solution)/shard_map/all_to_all | solution.py:276
  38.1 6.3 %copy-start.8 = (bf16[2,2,64,256]{3,2,1,0:T(8,128)(2,1)}, bf16[2,2,64,256]{3,2,1,0:T(8,128)(2,1)S(1)}, u32[]{:S(2)}) copy-start(bf16[2,2,64,256]{3,2,1,0:T(8,128)(2,1)S(1)} %pad_maximum_fusion.refs_0_) | copy-start | bytes 393220
  38.1 9.7 %collective-permute-start.1 = (bf16[2,2,64,256]{3,2,1,0:T(8,128)(2,1)S(1)}, bf16[2,2,64,256]{3,2,1,0:T(8,128)(2,1)S(1)}, u32[]{:S(2)}, u32[]{:S(2)}) collective-permute-start(bf16[2,2,64,256]{3,2,1,0:T(8,128)(2,1)S(1)} %pad_maximum_fusion.refs_0_), channel_id=1, source_target_pairs={{0,1},{1,2},{2,3},{3,4},{4,5},{5,6},{6,7},{7,0},{8,9},{9,10},{10,1... | collective-permute-start | bytes 393224 | tf_op jit(solution)/shard_map/ppermute | solution.py:284
  40.1 8.4 %collective-permute-start.2 = (bf16[2,2,64,256]{3,2,1,0:T(8,128)(2,1)S(1)}, bf16[2,2,64,256]{3,2,1,0:T(8,128)(2,1)}, u32[]{:S(2)}, u32[]{:S(2)}) collective-permute-start(bf16[2,2,64,256]{3,2,1,0:T(8,128)(2,1)S(1)} %pad_maximum_fusion.refs_0_), channel_id=1, source_target_pairs={{0,7},{1,0},{2,1},{3,2},{4,3},{5,4},{6,5},{7,6},{8,15},{9,8},{10,9... | collective-permute-start | bytes 393224 | tf_op jit(solution)/shard_map/ppermute | solution.py:284
  50.2 24.3 %copy-start.6 = (s32[32]{0:T(128)S(1)}, s32[32]{0:T(128)}, u32[]{:S(2)}) copy-start(s32[32]{0:T(128)} %rows_ref.1) | copy-start | bytes 388
  50.2 24.3 %copy-start.7 = (s32[32]{0:T(128)S(1)}, s32[32]{0:T(128)}, u32[]{:S(2)}) copy-start(s32[32]{0:T(128)} %cols_ref.1) | copy-start | bytes 388
  50.2 31.9 %all-to-all-start.2 = ((bf16[8,2,64,1024]{3,2,1,0:T(8,128)(2,1)}), bf16[8,2,64,1024]{3,2,1,0:T(8,128)(2,1)S(1)}, u32[]{:S(2)}, u32[]{:S(2)}) async-start(bf16[8,2,64,1024]{3,2,1,0:T(8,128)(2,1)} %copy-done.2), calls=%async_computation.2 | async-start | bytes 4194304 | tf_op jit(solution)/shard_map/all_to_all | solution.py:276
  55.3 6.2 %collective-permute-start.4 = (bf16[2,2,64,256]{3,2,1,0:T(8,128)(2,1)S(1)}, bf16[2,2,64,256]{3,2,1,0:T(8,128)(2,1)S(1)}, u32[]{:S(2)}, u32[]{:S(2)}) collective-permute-start(bf16[2,2,64,256]{3,2,1,0:T(8,128)(2,1)S(1)} %copy-done.10), channel_id=1, source_target_pairs={{0,1},{1,2},{2,3},{3,4},{4,5},{5,6},{6,7},{7,0},{8,9},{9,10},{10,1... | collective-permute-start | bytes 393224 | tf_op jit(solution)/shard_map/ppermute | solution.py:284
  56.6 5.3 %collective-permute-start.7 = (bf16[2,2,64,256]{3,2,1,0:T(8,128)(2,1)}, bf16[2,2,64,256]{3,2,1,0:T(8,128)(2,1)S(1)}, u32[]{:S(2)}, u32[]{:S(2)}) collective-permute-start(bf16[2,2,64,256]{3,2,1,0:T(8,128)(2,1)} %collective-permute-done.2.refs_7_), channel_id=1, source_target_pairs={{0,7},{1,0},{2,1},{3,2},{4,3},{5,4},{6,5},{7,6},{8,15},{9,8},{10,9... | collective-permute-start | bytes 393224 | tf_op jit(solution)/shard_map/ppermute | solution.py:284
  61.5 12.4 %copy-start.11 = (bf16[2,2,64,256]{3,2,1,0:T(8,128)(2,1)}, bf16[2,2,64,256]{3,2,1,0:T(8,128)(2,1)S(1)}, u32[]{:S(2)}) copy-start(bf16[2,2,64,256]{3,2,1,0:T(8,128)(2,1)S(1)} %collective-permute-done.4.refs_2_) | copy-start | bytes 393220
  61.5 6.2 %collective-permute-start.5 = (bf16[2,2,64,256]{3,2,1,0:T(8,128)(2,1)S(1)}, bf16[2,2,64,256]{3,2,1,0:T(8,128)(2,1)S(1)}, u32[]{:S(2)}, u32[]{:S(2)}) collective-permute-start(bf16[2,2,64,256]{3,2,1,0:T(8,128)(2,1)S(1)} %collective-permute-done.4.refs_2_), channel_id=1, source_target_pairs={{0,1},{1,2},{2,3},{3,4},{4,5},{5,6},{6,7},{7,0},{8,9},{9,10},{10,1... | collective-permute-start | bytes 393224 | tf_op jit(solution)/shard_map/ppermute | solution.py:284
  62.0 11.9 %copy-start.12 = (bf16[2,2,64,256]{3,2,1,0:T(8,128)(2,1)}, bf16[2,2,64,256]{3,2,1,0:T(8,128)(2,1)S(1)}, u32[]{:S(2)}) copy-start(bf16[2,2,64,256]{3,2,1,0:T(8,128)(2,1)S(1)} %collective-permute-done.7.refs_6_) | copy-start | bytes 393220
  62.0 6.3 %collective-permute-start.8 = (bf16[2,2,64,256]{3,2,1,0:T(8,128)(2,1)S(1)}, bf16[2,2,64,256]{3,2,1,0:T(8,128)(2,1)S(1)}, u32[]{:S(2)}, u32[]{:S(2)}) collective-permute-start(bf16[2,2,64,256]{3,2,1,0:T(8,128)(2,1)S(1)} %collective-permute-done.7.refs_6_), channel_id=1, source_target_pairs={{0,7},{1,0},{2,1},{3,2},{4,3},{5,4},{6,5},{7,6},{8,15},{9,8},{10,9... | collective-permute-start | bytes 393224 | tf_op jit(solution)/shard_map/ppermute | solution.py:284
  67.6 6.2 %copy-start.13 = (bf16[2,2,64,256]{3,2,1,0:T(8,128)(2,1)}, bf16[2,2,64,256]{3,2,1,0:T(8,128)(2,1)S(1)}, u32[]{:S(2)}) copy-start(bf16[2,2,64,256]{3,2,1,0:T(8,128)(2,1)S(1)} %collective-permute-done.5.refs_3_) | copy-start | bytes 393220
  67.6 6.2 %collective-permute-start.6 = (bf16[2,2,64,256]{3,2,1,0:T(8,128)(2,1)S(1)}, bf16[2,2,64,256]{3,2,1,0:T(8,128)(2,1)S(1)}, u32[]{:S(2)}, u32[]{:S(2)}) collective-permute-start(bf16[2,2,64,256]{3,2,1,0:T(8,128)(2,1)S(1)} %collective-permute-done.5.refs_3_), channel_id=1, source_target_pairs={{0,1},{1,2},{2,3},{3,4},{4,5},{5,6},{6,7},{7,0},{8,9},{9,10},{10,1... | collective-permute-start | bytes 393224 | tf_op jit(solution)/shard_map/ppermute | solution.py:284
  82.1 12.9 %collective-permute-start.9 = (bf16[8,2,64,1024]{3,2,1,0:T(8,128)(2,1)S(1)}, bf16[8,2,64,1024]{3,2,1,0:T(8,128)(2,1)}, u32[]{:S(2)}, u32[]{:S(2)}) collective-permute-start(bf16[8,2,64,1024]{3,2,1,0:T(8,128)(2,1)S(1)} %all-to-all-done.2.came_ref), channel_id=1, source_target_pairs={{0,16},{16,0},{1,17},{17,1},{2,18},{18,2},{3,19},{19,3},{4,20},{20... | collective-permute-start | bytes 6291464 | tf_op jit(solution)/shard_map/ppermute | solution.py:272
  82.1 18.0 %collective-permute-start.10 = (bf16[16,64,128]{2,1,0:T(8,128)(2,1)}, bf16[16,64,128]{2,1,0:T(8,128)(2,1)S(1)}, u32[]{:S(2)}, u32[]{:S(2)}) collective-permute-start(bf16[16,64,128]{2,1,0:T(8,128)(2,1)} %get-tuple-element.49), channel_id=1, source_target_pairs={{0,8},{1,9},{2,10},{3,11},{4,12},{5,13},{6,14},{7,15},{8,0},{9,1},... | collective-permute-start | bytes 786440 | tf_op jit(solution)/shard_map/ppermute | solution.py:352
  85.9 14.2 %collective-permute-start.11 = (bf16[16,64,128]{2,1,0:T(8,128)(2,1)}, bf16[16,64,128]{2,1,0:T(8,128)(2,1)S(1)}, u32[]{:S(2)}, u32[]{:S(2)}) collective-permute-start(bf16[16,64,128]{2,1,0:T(8,128)(2,1)} %get-tuple-element.50), channel_id=1, source_target_pairs={{0,1},{1,0},{2,3},{3,2},{4,5},{5,4},{6,7},{7,6},{8,9},{9,8},{10,11... | collective-permute-start | bytes 786440 | tf_op jit(solution)/shard_map/ppermute | solution.py:352
  85.9 14.3 %collective-permute-start.12 = (bf16[16,64,128]{2,1,0:T(8,128)(2,1)}, bf16[16,64,128]{2,1,0:T(8,128)(2,1)S(1)}, u32[]{:S(2)}, u32[]{:S(2)}) collective-permute-start(bf16[16,64,128]{2,1,0:T(8,128)(2,1)} %get-tuple-element.51), channel_id=1, source_target_pairs={{0,9},{1,8},{2,11},{3,10},{4,13},{5,12},{6,15},{7,14},{8,1},{9,0},... | collective-permute-start | bytes 786440 | tf_op jit(solution)/shard_map/ppermute | solution.py:352
  88.4 16.7 %all-to-all-start.3 = ((bf16[16,32,128]{2,1,0:T(8,128)(2,1)}), bf16[16,32,128]{2,1,0:T(8,128)(2,1)S(1)}, u32[]{:S(2)}, u32[]{:S(2)}) async-start(bf16[16,32,128]{2,1,0:T(8,128)(2,1)} %unpack.1), calls=%async_computation.3 | async-start | bytes 262144 | tf_op jit(solution)/shard_map/all_to_all | solution.py:276
  106.9 21.2 %all-to-all-start.4 = ((bf16[16,128,128]{2,1,0:T(8,128)(2,1)}), bf16[16,128,128]{2,1,0:T(8,128)(2,1)S(1)}, u32[]{:S(2)}, u32[]{:S(2)}) async-start(bf16[16,128,128]{2,1,0:T(8,128)(2,1)} %last_message.1), calls=%async_computation.4 | async-start | bytes 1048576 | tf_op jit(solution)/shard_map/all_to_all | solution.py:276
  (10 other events, 20.8 us)

commit v12 on v10

--- a/solution.py
+++ b/solution.py
@@ -188,12 +188,15 @@
         return pltpu.make_async_copy(tiles_hbm.at[span], tiles_ref.at[span], tile_sems.at[index])
 
     arriving = [
-        pltpu.make_async_copy(pieces[index], drives.at[index], piece_sems.at[index]) for index in range(8)
+        pltpu.make_async_copy(pieces[index], drives.at[index], piece_sems.at[index])
+        for index in (0, 1, 2, 3, 6, 7)
     ]
     for copy in arriving:
         copy.start()
     for index in range(8):
         tile_copy(index).start()
+    for index in (4, 5):
+        drives[index] = pieces[index][...]
     acc[...] = jnp.zeros_like(acc)
     behind[...] = jnp.zeros_like(behind)
     for copy in arriving:
@@ -351,8 +354,10 @@
         near,
         [((64, 512), f32)] + [((16, 64, 128), bf16)] * 4,
         [tile_count, tile_rows, tile_cols, low, in_hbm(tiles)]
-        + [in_hbm(piece) for piece in (here, up1, up2, up3, up4, down3, down2, down1)],
-        specs=[smem(), smem(), smem(), vmem()] + [hbm()] * 9,
+        + [in_hbm(piece) for piece in (here, up1, up2, up3)]
+        + [up4, down3]
+        + [in_hbm(piece) for piece in (down2, down1)],
+        specs=[smem(), smem(), smem(), vmem()] + [hbm()] * 5 + [vmem()] * 2 + [hbm()] * 2,
         scratch=[
             pltpu.VMEM((2, 64, 256), f32),
             pltpu.VMEM((32, 64, 256), f32),

time: 130 us -> 129 us (level)
  starting transfers between devices: 50.9 us -> 52.3 us
    all_to_all x5, starting transfers between devices: 32.7 us -> 34.2 us  [exchange(): return lax.all_to_all(value, axes, 0, 0, tiled=True)]
    unnamed x30 -> x26, local copies, waits for them, and re-layouts: 7.95 us -> 7.3 us
  transfers between devices with their start and end apart: 18 -> 18, of which waited for: 9 -> 9; matrix products, arithmetic and copies ran while one was open for 0% -> 0% of each run, Pallas kernels for 13% -> 12%
where the time goes in v12:
time: 129 us; the launch traced here: 128 us
  starting transfers between devices  52.3 us (41%)
  waiting for transfers between devices  41 us (32%)
  Pallas kernels  26.2 us (20%)
  local copies, waits for them, and re-layouts  7.3 us (6%)
  between operations  1.51 us (1%)
    all_to_all x5, starting transfers between devices, exchange(): return lax.all_to_all(value, axes, 0, 0, tiled=True)  34.2 us
    pallas_call x11, Pallas kernels, call(): pl.pallas_call(kernel, out_shape=[jax.ShapeDtypeStruct(s, d) for s, d in...  26.2 us
    all_to_all x5, waiting for transfers between devices, exchange(): return lax.all_to_all(value, axes, 0, 0, tiled=True)  26.1 us
    ppermute x7, waiting for transfers between devices, shift(): return lax.ppermute(value, 'z', [(i, (i + step) % 8) for i in range(8)])  14.9 us
    ppermute x7, starting transfers between devices, shift(): return lax.ppermute(value, 'z', [(i, (i + step) % 8) for i in range(8)])  9.65 us
    unnamed x26, local copies, waits for them, and re-layouts  7.3 us
    ppermute x3, starting transfers between devices, on_device(): lax.ppermute(value, ROWS, [(i, i ^ mask) for i in range(16)])  4.99 us
    ppermute x3, starting transfers between devices, swap(): return lax.ppermute(value, axis, [(0, 1), (1, 0)])  3.53 us
  transfers between devices with their start and end apart: 18, of which 9 were waited for; matrix products, arithmetic and copies ran while one was open for 0% of the time, Pallas kernels for 12%

profile of v12, /device:TPU:8, one launch (start us, length us, event | category | flops | bytes accessed | tf_op | source)
XLA Modules:
  0.0 128.4 jit_solution(17671670628579178365)
XLA Ops:
  0.6 3.0 %prepare.1 = (bf16[2,64,256]{2,1,0:T(8,128)(2,1)S(1)}, bf16[2,64,256]{2,1,0:T(8,128)(2,1)S(1)}, bf16[16,96,128]{2,1,0:T(8,128)(2,1)}) custom-call(f32[64,512]{1,0:T(8,128)} %exc_hbm.1, f32[64,512]{1,0:T(8,128)} %loads_hbm.1, bf16[1024,512]{1,0:T(8,128)(2,1)} %refs_0_.1, bf16[1024,512]{1,0:T(8,128)(2,1)} %refs_1_.1), custom_call_target="tpu_custom_call" | custom-call | flops 1000 | bytes 1000 | tf_op jit(solution)/shard_map/prepare/pallas_call | solution.py:30
  3.6 11.0 %all-to-all-start = ((bf16[16,96,128]{2,1,0:T(8,128)(2,1)}), bf16[16,96,128]{2,1,0:T(8,128)(2,1)S(1)}, u32[]{:S(2)}, u32[]{:S(2)}) async-start(bf16[16,96,128]{2,1,0:T(8,128)(2,1)} %get-tuple-element.34), calls=%async_computation | async-start | bytes 786432 | tf_op jit(solution)/shard_map/all_to_all | solution.py:293
  14.7 3.4 %collective-permute-start = (bf16[2,64,256]{2,1,0:T(8,128)(2,1)S(1)}, bf16[2,64,256]{2,1,0:T(8,128)(2,1)S(1)}, u32[]{:S(2)}, u32[]{:S(2)}) collective-permute-start(bf16[2,64,256]{2,1,0:T(8,128)(2,1)S(1)} %get-tuple-element.35), channel_id=1, source_target_pairs={{0,8},{8,0},{1,9},{9,1},{2,10},{10,2},{3,11},{11,3},{4,12},{12,4},... | collective-permute-start | bytes 196616 | tf_op jit(solution)/shard_map/ppermute | solution.py:289
  18.1 2.2 %split_translation.1.parts_hbm.parts_ref = bf16[15,128,1024]{2,1,0:T(8,128)(2,1)S(1)} custom-call(f32[1,15,64,1024]{3,2,1,0:T(8,128)} %trans_hbm.1), custom_call_target="tpu_custom_call" | custom-call | flops 1000 | bytes 1000 | tf_op jit(solution)/shard_map/split_translation/pallas_call | solution.py:30
  22.2 6.6 %all-to-all-done.msg_ref = bf16[16,96,128]{2,1,0:T(8,128)(2,1)S(1)} async-done(((bf16[16,96,128]{2,1,0:T(8,128)(2,1)}), bf16[16,96,128]{2,1,0:T(8,128)(2,1)S(1)}, u32[]{:S(2)}, u32[]{:S(2)}) %all-to-all-start) | async-done | bytes 393248 | tf_op jit(solution)/shard_map/all_to_all | solution.py:293
  28.8 4.3 %other_terms.1 = (bf16[16,32,128]{2,1,0:T(8,128)(2,1)}, bf16[128,64]{1,0:T(8,128)(2,1)S(1)}, f32[8,64,1024]{2,1,0:T(8,128)}) custom-call(bf16[16,96,128]{2,1,0:T(8,128)(2,1)S(1)} %all-to-all-done.msg_ref, bf16[15,128,1024]{2,1,0:T(8,128)(2,1)} %copy-done), custom_call_target="tpu_custom_call" | custom-call | flops 1000 | bytes 1000 | tf_op jit(solution)/shard_map/other_terms/pallas_call | solution.py:30
  33.2 4.9 %all-to-all-start.1 = ((bf16[16,32,128]{2,1,0:T(8,128)(2,1)}), bf16[16,32,128]{2,1,0:T(8,128)(2,1)S(1)}, u32[]{:S(2)}, u32[]{:S(2)}) async-start(bf16[16,32,128]{2,1,0:T(8,128)(2,1)} %get-tuple-element.38), calls=%async_computation.1 | async-start | bytes 262144 | tf_op jit(solution)/shard_map/all_to_all | solution.py:293
  38.1 2.0 %collective-permute-start.1 = (bf16[2,2,64,256]{3,2,1,0:T(8,128)(2,1)S(1)}, bf16[2,2,64,256]{3,2,1,0:T(8,128)(2,1)S(1)}, u32[]{:S(2)}, u32[]{:S(2)}) collective-permute-start(bf16[2,2,64,256]{3,2,1,0:T(8,128)(2,1)S(1)} %pad_maximum_fusion.refs_0_), channel_id=1, source_target_pairs={{0,1},{1,2},{2,3},{3,4},{4,5},{5,6},{6,7},{7,0},{8,9},{9,10},{10,1... | collective-permute-start | bytes 393224 | tf_op jit(solution)/shard_map/ppermute | solution.py:301
  41.4 3.0 %own_terms.1.own_ref = bf16[8,64,1024]{2,1,0:T(8,128)(2,1)S(1)} custom-call(bf16[128,64]{1,0:T(8,128)(2,1)S(1)} %get-tuple-element.40.grad_ref, f32[8,64,1024]{2,1,0:T(8,128)S(1)} %collective-permute-done.3.came_ref, bf16[15,128,1024]{2,1,0:T(8,128)(2,1)} %copy-done), custom_call_target="tpu_custom_call" | custom-call | flops 1000 | bytes 1000 | tf_op jit(solution)/shard_map/own_terms/pallas_call | solution.py:30
  44.4 3.4 %collective-permute-done.1.refs_1_ = bf16[2,2,64,256]{3,2,1,0:T(8,128)(2,1)S(1)} collective-permute-done((bf16[2,2,64,256]{3,2,1,0:T(8,128)(2,1)S(1)}, bf16[2,2,64,256]{3,2,1,0:T(8,128)(2,1)S(1)}, u32[]{:S(2)}, u32[]{:S(2)}) %collective-permute-start.1) | collective-permute-done | bytes 131104 | tf_op jit(solution)/shard_map/ppermute | solution.py:301
  50.1 5.1 %all-to-all-start.2 = ((bf16[8,2,64,1024]{3,2,1,0:T(8,128)(2,1)}), bf16[8,2,64,1024]{3,2,1,0:T(8,128)(2,1)S(1)}, u32[]{:S(2)}, u32[]{:S(2)}) async-start(bf16[8,2,64,1024]{3,2,1,0:T(8,128)(2,1)} %copy-done.2), calls=%async_computation.2 | async-start | bytes 4194304 | tf_op jit(solution)/shard_map/all_to_all | solution.py:293
  58.5 2.9 %collective-permute-done.4.refs_2_ = bf16[2,2,64,256]{3,2,1,0:T(8,128)(2,1)S(1)} collective-permute-done((bf16[2,2,64,256]{3,2,1,0:T(8,128)(2,1)S(1)}, bf16[2,2,64,256]{3,2,1,0:T(8,128)(2,1)S(1)}, u32[]{:S(2)}, u32[]{:S(2)}) %collective-permute-start.4) | collective-permute-done | bytes 131104 | tf_op jit(solution)/shard_map/ppermute | solution.py:301
  61.9 2.9 %collective-permute-start.8 = (bf16[2,2,64,256]{3,2,1,0:T(8,128)(2,1)S(1)}, bf16[2,2,64,256]{3,2,1,0:T(8,128)(2,1)S(1)}, u32[]{:S(2)}, u32[]{:S(2)}) collective-permute-start(bf16[2,2,64,256]{3,2,1,0:T(8,128)(2,1)S(1)} %collective-permute-done.7.refs_6_), channel_id=1, source_target_pairs={{0,7},{1,0},{2,1},{3,2},{4,3},{5,4},{6,5},{7,6},{8,15},{9,8},{10,9... | collective-permute-start | bytes 393224 | tf_op jit(solution)/shard_map/ppermute | solution.py:301
  64.8 2.7 %collective-permute-done.5.refs_3_ = bf16[2,2,64,256]{3,2,1,0:T(8,128)(2,1)S(1)} collective-permute-done((bf16[2,2,64,256]{3,2,1,0:T(8,128)(2,1)S(1)}, bf16[2,2,64,256]{3,2,1,0:T(8,128)(2,1)S(1)}, u32[]{:S(2)}, u32[]{:S(2)}) %collective-permute-start.5) | collective-permute-done | bytes 131104 | tf_op jit(solution)/shard_map/ppermute | solution.py:301
  68.2 5.5 %collective-permute-done.6.refs_4_ = bf16[2,2,64,256]{3,2,1,0:T(8,128)(2,1)S(1)} collective-permute-done((bf16[2,2,64,256]{3,2,1,0:T(8,128)(2,1)S(1)}, bf16[2,2,64,256]{3,2,1,0:T(8,128)(2,1)S(1)}, u32[]{:S(2)}, u32[]{:S(2)}) %collective-permute-start.6) | collective-permute-done | bytes 131104 | tf_op jit(solution)/shard_map/ppermute | solution.py:301
  73.8 5.3 %near.1 = (f32[64,512]{1,0:T(8,128)S(1)}, bf16[16,64,128]{2,1,0:T(8,128)(2,1)S(1)}, bf16[16,64,128]{2,1,0:T(8,128)(2,1)}, bf16[16,64,128]{2,1,0:T(8,128)(2,1)}, bf16[16,64,128]{2,1,0:T(8,128)(2,1)}) custom-call(s32[1]{0:T(128)S(6)} %copy.11.count_ref, s32[32]{0:T(128)S(1)} %copy-done.5, s32[32]{0:T(128)S(1)} %copy-done.6, ...), custom_call_target="tpu_custom_call" | custom-call | flops 1000 | bytes 1000 | tf_op jit(solution)/shard_map/near/pallas_call | solution.py:30
  80.4 3.1 %collective-permute-start.10 = (bf16[16,64,128]{2,1,0:T(8,128)(2,1)}, bf16[16,64,128]{2,1,0:T(8,128)(2,1)S(1)}, u32[]{:S(2)}, u32[]{:S(2)}) collective-permute-start(bf16[16,64,128]{2,1,0:T(8,128)(2,1)} %get-tuple-element.49), channel_id=1, source_target_pairs={{0,8},{1,9},{2,10},{3,11},{4,12},{5,13},{6,14},{7,15},{8,0},{9,1},... | collective-permute-start | bytes 786440 | tf_op jit(solution)/shard_map/ppermute | solution.py:373
  83.5 1.9 %collective-permute-start.12 = (bf16[16,64,128]{2,1,0:T(8,128)(2,1)}, bf16[16,64,128]{2,1,0:T(8,128)(2,1)S(1)}, u32[]{:S(2)}, u32[]{:S(2)}) collective-permute-start(bf16[16,64,128]{2,1,0:T(8,128)(2,1)} %get-tuple-element.51), channel_id=1, source_target_pairs={{0,9},{1,8},{2,11},{3,10},{4,13},{5,12},{6,15},{7,14},{8,1},{9,0},... | collective-permute-start | bytes 786440 | tf_op jit(solution)/shard_map/ppermute | solution.py:373
  86.2 8.6 %all-to-all-start.3 = ((bf16[16,32,128]{2,1,0:T(8,128)(2,1)}), bf16[16,32,128]{2,1,0:T(8,128)(2,1)S(1)}, u32[]{:S(2)}, u32[]{:S(2)}) async-start(bf16[16,32,128]{2,1,0:T(8,128)(2,1)} %unpack.1), calls=%async_computation.3 | async-start | bytes 262144 | tf_op jit(solution)/shard_map/all_to_all | solution.py:293
  94.8 2.1 %copy-done.1 = bf16[15,128,1024]{2,1,0:T(8,128)(2,1)S(1)} copy-done((bf16[15,128,1024]{2,1,0:T(8,128)(2,1)S(1)}, bf16[15,128,1024]{2,1,0:T(8,128)(2,1)}, u32[]{:S(2)}) %copy-start.1) | copy-done | bytes 3932184
  96.9 2.9 %forward.1.pot_ref = bf16[32,128]{1,0:T(8,128)(2,1)S(1)} custom-call(bf16[8,2,64,1024]{3,2,1,0:T(8,128)(2,1)} %collective-permute-done.9.other_ref, bf16[8,2,64,1024]{3,2,1,0:T(8,128)(2,1)S(1)} %all-to-all-done.2.came_ref, bf16[15,128,1024]{2,1,0:T(8,128)(2,1)S(1)} %copy-done.1), custom_call_target="tpu_custom_call" | custom-call | flops 1000 | bytes 1000 | tf_op jit(solution)/shard_map/forward/pallas_call | solution.py:30
  99.9 5.0 %all-to-all-done.3.adj_ref = bf16[16,32,128]{2,1,0:T(8,128)(2,1)S(1)} async-done(((bf16[16,32,128]{2,1,0:T(8,128)(2,1)}), bf16[16,32,128]{2,1,0:T(8,128)(2,1)S(1)}, u32[]{:S(2)}, u32[]{:S(2)}) %all-to-all-start.3) | async-done | bytes 131104 | tf_op jit(solution)/shard_map/all_to_all | solution.py:293
  106.8 4.6 %all-to-all-start.4 = ((bf16[16,128,128]{2,1,0:T(8,128)(2,1)}), bf16[16,128,128]{2,1,0:T(8,128)(2,1)S(1)}, u32[]{:S(2)}, u32[]{:S(2)}) async-start(bf16[16,128,128]{2,1,0:T(8,128)(2,1)} %last_message.1), calls=%async_computation.4 | async-start | bytes 1048576 | tf_op jit(solution)/shard_map/all_to_all | solution.py:293
  113.0 14.3 %all-to-all-done.4.msg_ref = bf16[16,128,128]{2,1,0:T(8,128)(2,1)S(1)} async-done(((bf16[16,128,128]{2,1,0:T(8,128)(2,1)}), bf16[16,128,128]{2,1,0:T(8,128)(2,1)S(1)}, u32[]{:S(2)}, u32[]{:S(2)}) %all-to-all-start.4) | async-done | bytes 524320 | tf_op jit(solution)/shard_map/all_to_all | solution.py:293
  (50 shorter events, 16.1 us)
Async XLA Ops:
  3.6 25.2 %all-to-all-start = ((bf16[16,96,128]{2,1,0:T(8,128)(2,1)}), bf16[16,96,128]{2,1,0:T(8,128)(2,1)S(1)}, u32[]{:S(2)}, u32[]{:S(2)}) async-start(bf16[16,96,128]{2,1,0:T(8,128)(2,1)} %get-tuple-element.34), calls=%async_computation | async-start | bytes 786432 | tf_op jit(solution)/shard_map/all_to_all | solution.py:293
  14.7 7.5 %collective-permute-start = (bf16[2,64,256]{2,1,0:T(8,128)(2,1)S(1)}, bf16[2,64,256]{2,1,0:T(8,128)(2,1)S(1)}, u32[]{:S(2)}, u32[]{:S(2)}) collective-permute-start(bf16[2,64,256]{2,1,0:T(8,128)(2,1)S(1)} %get-tuple-element.35), channel_id=1, source_target_pairs={{0,8},{8,0},{1,9},{9,1},{2,10},{10,2},{3,11},{11,3},{4,12},{12,4},... | collective-permute-start | bytes 196616 | tf_op jit(solution)/shard_map/ppermute | solution.py:289
  33.1 8.3 %collective-permute-start.3 = (f32[8,64,1024]{2,1,0:T(8,128)}, f32[8,64,1024]{2,1,0:T(8,128)S(1)}, u32[]{:S(2)}, u32[]{:S(2)}) collective-permute-start(f32[8,64,1024]{2,1,0:T(8,128)} %get-tuple-element.41), channel_id=1, source_target_pairs={{0,16},{16,0},{1,17},{17,1},{2,18},{18,2},{3,19},{19,3},{4,20},{20... | collective-permute-start | bytes 6291464 | tf_op jit(solution)/shard_map/ppermute | solution.py:289
  33.2 15.4 %all-to-all-start.1 = ((bf16[16,32,128]{2,1,0:T(8,128)(2,1)}), bf16[16,32,128]{2,1,0:T(8,128)(2,1)S(1)}, u32[]{:S(2)}, u32[]{:S(2)}) async-start(bf16[16,32,128]{2,1,0:T(8,128)(2,1)} %get-tuple-element.38), calls=%async_computation.1 | async-start | bytes 262144 | tf_op jit(solution)/shard_map/all_to_all | solution.py:293
  38.1 6.3 %copy-start.7 = (bf16[2,2,64,256]{3,2,1,0:T(8,128)(2,1)}, bf16[2,2,64,256]{3,2,1,0:T(8,128)(2,1)S(1)}, u32[]{:S(2)}) copy-start(bf16[2,2,64,256]{3,2,1,0:T(8,128)(2,1)S(1)} %pad_maximum_fusion.refs_0_) | copy-start | bytes 393220
  38.1 9.7 %collective-permute-start.1 = (bf16[2,2,64,256]{3,2,1,0:T(8,128)(2,1)S(1)}, bf16[2,2,64,256]{3,2,1,0:T(8,128)(2,1)S(1)}, u32[]{:S(2)}, u32[]{:S(2)}) collective-permute-start(bf16[2,2,64,256]{3,2,1,0:T(8,128)(2,1)S(1)} %pad_maximum_fusion.refs_0_), channel_id=1, source_target_pairs={{0,1},{1,2},{2,3},{3,4},{4,5},{5,6},{6,7},{7,0},{8,9},{9,10},{10,1... | collective-permute-start | bytes 393224 | tf_op jit(solution)/shard_map/ppermute | solution.py:301
  40.1 8.4 %collective-permute-start.2 = (bf16[2,2,64,256]{3,2,1,0:T(8,128)(2,1)S(1)}, bf16[2,2,64,256]{3,2,1,0:T(8,128)(2,1)}, u32[]{:S(2)}, u32[]{:S(2)}) collective-permute-start(bf16[2,2,64,256]{3,2,1,0:T(8,128)(2,1)S(1)} %pad_maximum_fusion.refs_0_), channel_id=1, source_target_pairs={{0,7},{1,0},{2,1},{3,2},{4,3},{5,4},{6,5},{7,6},{8,15},{9,8},{10,9... | collective-permute-start | bytes 393224 | tf_op jit(solution)/shard_map/ppermute | solution.py:301
  50.1 23.6 %copy-start.5 = (s32[32]{0:T(128)S(1)}, s32[32]{0:T(128)}, u32[]{:S(2)}) copy-start(s32[32]{0:T(128)} %rows_ref.1) | copy-start | bytes 388
  50.1 23.6 %copy-start.6 = (s32[32]{0:T(128)S(1)}, s32[32]{0:T(128)}, u32[]{:S(2)}) copy-start(s32[32]{0:T(128)} %cols_ref.1) | copy-start | bytes 388
  50.1 30.3 %all-to-all-start.2 = ((bf16[8,2,64,1024]{3,2,1,0:T(8,128)(2,1)}), bf16[8,2,64,1024]{3,2,1,0:T(8,128)(2,1)S(1)}, u32[]{:S(2)}, u32[]{:S(2)}) async-start(bf16[8,2,64,1024]{3,2,1,0:T(8,128)(2,1)} %copy-done.2), calls=%async_computation.2 | async-start | bytes 4194304 | tf_op jit(solution)/shard_map/all_to_all | solution.py:293
  55.2 6.2 %collective-permute-start.4 = (bf16[2,2,64,256]{3,2,1,0:T(8,128)(2,1)S(1)}, bf16[2,2,64,256]{3,2,1,0:T(8,128)(2,1)S(1)}, u32[]{:S(2)}, u32[]{:S(2)}) collective-permute-start(bf16[2,2,64,256]{3,2,1,0:T(8,128)(2,1)S(1)} %copy-done.9), channel_id=1, source_target_pairs={{0,1},{1,2},{2,3},{3,4},{4,5},{5,6},{6,7},{7,0},{8,9},{9,10},{10,1... | collective-permute-start | bytes 393224 | tf_op jit(solution)/shard_map/ppermute | solution.py:301
  56.6 5.3 %collective-permute-start.7 = (bf16[2,2,64,256]{3,2,1,0:T(8,128)(2,1)}, bf16[2,2,64,256]{3,2,1,0:T(8,128)(2,1)S(1)}, u32[]{:S(2)}, u32[]{:S(2)}) collective-permute-start(bf16[2,2,64,256]{3,2,1,0:T(8,128)(2,1)} %collective-permute-done.2.refs_7_), channel_id=1, source_target_pairs={{0,7},{1,0},{2,1},{3,2},{4,3},{5,4},{6,5},{7,6},{8,15},{9,8},{10,9... | collective-permute-start | bytes 393224 | tf_op jit(solution)/shard_map/ppermute | solution.py:301
  61.4 12.4 %copy-start.10 = (bf16[2,2,64,256]{3,2,1,0:T(8,128)(2,1)}, bf16[2,2,64,256]{3,2,1,0:T(8,128)(2,1)S(1)}, u32[]{:S(2)}) copy-start(bf16[2,2,64,256]{3,2,1,0:T(8,128)(2,1)S(1)} %collective-permute-done.4.refs_2_) | copy-start | bytes 393220
  61.4 6.2 %collective-permute-start.5 = (bf16[2,2,64,256]{3,2,1,0:T(8,128)(2,1)S(1)}, bf16[2,2,64,256]{3,2,1,0:T(8,128)(2,1)S(1)}, u32[]{:S(2)}, u32[]{:S(2)}) collective-permute-start(bf16[2,2,64,256]{3,2,1,0:T(8,128)(2,1)S(1)} %collective-permute-done.4.refs_2_), channel_id=1, source_target_pairs={{0,1},{1,2},{2,3},{3,4},{4,5},{5,6},{6,7},{7,0},{8,9},{9,10},{10,1... | collective-permute-start | bytes 393224 | tf_op jit(solution)/shard_map/ppermute | solution.py:301
  61.9 11.8 %copy-start.11 = (bf16[2,2,64,256]{3,2,1,0:T(8,128)(2,1)}, bf16[2,2,64,256]{3,2,1,0:T(8,128)(2,1)S(1)}, u32[]{:S(2)}) copy-start(bf16[2,2,64,256]{3,2,1,0:T(8,128)(2,1)S(1)} %collective-permute-done.7.refs_6_) | copy-start | bytes 393220
  61.9 6.3 %collective-permute-start.8 = (bf16[2,2,64,256]{3,2,1,0:T(8,128)(2,1)S(1)}, bf16[2,2,64,256]{3,2,1,0:T(8,128)(2,1)S(1)}, u32[]{:S(2)}, u32[]{:S(2)}) collective-permute-start(bf16[2,2,64,256]{3,2,1,0:T(8,128)(2,1)S(1)} %collective-permute-done.7.refs_6_), channel_id=1, source_target_pairs={{0,7},{1,0},{2,1},{3,2},{4,3},{5,4},{6,5},{7,6},{8,15},{9,8},{10,9... | collective-permute-start | bytes 393224 | tf_op jit(solution)/shard_map/ppermute | solution.py:301
  67.6 6.2 %copy-start.12 = (bf16[2,2,64,256]{3,2,1,0:T(8,128)(2,1)}, bf16[2,2,64,256]{3,2,1,0:T(8,128)(2,1)S(1)}, u32[]{:S(2)}) copy-start(bf16[2,2,64,256]{3,2,1,0:T(8,128)(2,1)S(1)} %collective-permute-done.5.refs_3_) | copy-start | bytes 393220
  67.6 6.2 %collective-permute-start.6 = (bf16[2,2,64,256]{3,2,1,0:T(8,128)(2,1)S(1)}, bf16[2,2,64,256]{3,2,1,0:T(8,128)(2,1)S(1)}, u32[]{:S(2)}, u32[]{:S(2)}) collective-permute-start(bf16[2,2,64,256]{3,2,1,0:T(8,128)(2,1)S(1)} %collective-permute-done.5.refs_3_), channel_id=1, source_target_pairs={{0,1},{1,2},{2,3},{3,4},{4,5},{5,6},{6,7},{7,0},{8,9},{9,10},{10,1... | collective-permute-start | bytes 393224 | tf_op jit(solution)/shard_map/ppermute | solution.py:301
  80.4 14.4 %collective-permute-start.9 = (bf16[8,2,64,1024]{3,2,1,0:T(8,128)(2,1)S(1)}, bf16[8,2,64,1024]{3,2,1,0:T(8,128)(2,1)}, u32[]{:S(2)}, u32[]{:S(2)}) collective-permute-start(bf16[8,2,64,1024]{3,2,1,0:T(8,128)(2,1)S(1)} %all-to-all-done.2.came_ref), channel_id=1, source_target_pairs={{0,16},{16,0},{1,17},{17,1},{2,18},{18,2},{3,19},{19,3},{4,20},{20... | collective-permute-start | bytes 6291464 | tf_op jit(solution)/shard_map/ppermute | solution.py:289
  80.4 19.4 %collective-permute-start.10 = (bf16[16,64,128]{2,1,0:T(8,128)(2,1)}, bf16[16,64,128]{2,1,0:T(8,128)(2,1)S(1)}, u32[]{:S(2)}, u32[]{:S(2)}) collective-permute-start(bf16[16,64,128]{2,1,0:T(8,128)(2,1)} %get-tuple-element.49), channel_id=1, source_target_pairs={{0,8},{1,9},{2,10},{3,11},{4,12},{5,13},{6,14},{7,15},{8,0},{9,1},... | collective-permute-start | bytes 786440 | tf_op jit(solution)/shard_map/ppermute | solution.py:373
  83.5 16.4 %collective-permute-start.11 = (bf16[16,64,128]{2,1,0:T(8,128)(2,1)}, bf16[16,64,128]{2,1,0:T(8,128)(2,1)S(1)}, u32[]{:S(2)}, u32[]{:S(2)}) collective-permute-start(bf16[16,64,128]{2,1,0:T(8,128)(2,1)} %get-tuple-element.50), channel_id=1, source_target_pairs={{0,1},{1,0},{2,3},{3,2},{4,5},{5,4},{6,7},{7,6},{8,9},{9,8},{10,11... | collective-permute-start | bytes 786440 | tf_op jit(solution)/shard_map/ppermute | solution.py:373
  83.5 16.4 %collective-permute-start.12 = (bf16[16,64,128]{2,1,0:T(8,128)(2,1)}, bf16[16,64,128]{2,1,0:T(8,128)(2,1)S(1)}, u32[]{:S(2)}, u32[]{:S(2)}) collective-permute-start(bf16[16,64,128]{2,1,0:T(8,128)(2,1)} %get-tuple-element.51), channel_id=1, source_target_pairs={{0,9},{1,8},{2,11},{3,10},{4,13},{5,12},{6,15},{7,14},{8,1},{9,0},... | collective-permute-start | bytes 786440 | tf_op jit(solution)/shard_map/ppermute | solution.py:373
  86.2 18.7 %all-to-all-start.3 = ((bf16[16,32,128]{2,1,0:T(8,128)(2,1)}), bf16[16,32,128]{2,1,0:T(8,128)(2,1)S(1)}, u32[]{:S(2)}, u32[]{:S(2)}) async-start(bf16[16,32,128]{2,1,0:T(8,128)(2,1)} %unpack.1), calls=%async_computation.3 | async-start | bytes 262144 | tf_op jit(solution)/shard_map/all_to_all | solution.py:293
  106.8 20.5 %all-to-all-start.4 = ((bf16[16,128,128]{2,1,0:T(8,128)(2,1)}), bf16[16,128,128]{2,1,0:T(8,128)(2,1)S(1)}, u32[]{:S(2)}, u32[]{:S(2)}) async-start(bf16[16,128,128]{2,1,0:T(8,128)(2,1)} %last_message.1), calls=%async_computation.4 | async-start | bytes 1048576 | tf_op jit(solution)/shard_map/all_to_all | solution.py:293
  (7 other events, 12.4 us)
